TPU v7x, 32 devices: a whole 2x2x4 slice. The times are simulated.
32 devices in a mesh: group: 2 (over x), expert: 8 (over z, y), cuts: 2 (over core).
Axes of the slice: x: 2, y: 2, z: 4, core: 2. Of those that a mesh axis runs over, the one named last changes fastest.
Arguments:
- x_in: bfloat16 [512, 4096], P(('group', 'expert'), 'cuts'), parts along dimension 0, may hold values from -6 to 6
- routes: int32 [512, 2], P(('group', 'expert')), parts along dimension 0, may hold values from 0 to 15, as said below
- conv_state: float32 [64, 3, 4096], P('group', None, ('expert', 'cuts')), parts along dimension 0, may hold values from -6 to 6
- ssm_state: float32 [64, 16, 4096], P('group', None, ('expert', 'cuts')), parts along dimension 0, may hold values from -6 to 6
- mamba_gain: float32 [4096], replicated, may hold values from 0.1 to 1.9
- in_x: bfloat16 [4096, 4096], P(None, ('expert', 'cuts')), may hold values from -0.09375 to 0.09375
- in_z: bfloat16 [4096, 4096], P(None, ('expert', 'cuts')), may hold values from -0.09375 to 0.09375
- conv_w: float32 [4, 4096], P(None, ('expert', 'cuts')), may hold values from -3 to 3
- conv_b: float32 [4096], P(('expert', 'cuts')), may hold values from -3 to 3
- xproj_dt: bfloat16 [4096, 512], P(('expert', 'cuts')), may hold values from -0.09375 to 0.09375
- xproj_bc: bfloat16 [4096, 32], P(('expert', 'cuts')), may hold values from -0.09375 to 0.09375
- dt_proj: bfloat16 [512, 4096], P(None, ('expert', 'cuts')), may hold values from -0.25 to 0.25
- dt_bias: float32 [4096], P(('expert', 'cuts')), may hold values from -4 to 0
- a_rate: float32 [16, 4096], P(None, ('expert', 'cuts')), may hold values from 0.5 to 16
- d_skip: float32 [4096], P(('expert', 'cuts')), may hold values from 0.5 to 1.5
- out_proj: bfloat16 [4096, 4096], P(('expert', 'cuts')), may hold values from -0.09375 to 0.09375
- moe_gain: float32 [4096], replicated, may hold values from 0.1 to 1.9
- router: bfloat16 [4096, 16], replicated, may hold values from -0.09375 to 0.09375
- w_gate: bfloat16 [4096, 12288], P(None, ('expert', 'cuts')), may hold values from -0.09375 to 0.09375
- w_up: bfloat16 [4096, 12288], P(None, ('expert', 'cuts')), may hold values from -0.09375 to 0.09375
- w_down: bfloat16 [12288, 4096], P(('expert', 'cuts')), may hold values from -0.078125 to 0.078125
Outputs:
- stream_out: bfloat16 [512, 4096], P(('group', 'expert'), 'cuts'), parts along dimension 0
- new_state: float32 [64, 16, 4096], P('group', None, ('expert', 'cuts')), parts along dimension 0
There are 2 independent parts, one for each index of `group`. A program takes and returns all parts, laid end to end along the dimension named above; an argument that names none is the same for every part. Nothing has to cross between parts.
Inputs may be any that keep to these rules, and one draw needn't show every extreme that they name: `routes`: each token names 2 different experts. Among the 32 tokens of one index of expert (aligned blocks of rows), at most 16 name any one expert below 2, and in every block one of them is named by exactly 16; no token names two experts below 2.
All inputs are finite; a program needn't handle non-finite values.
Results may differ from a plain program's by a relative error of at most 0.0095.
Values may be sent and summed in bfloat16 or wider, within the bound.
No kernel may reach another device: no remote copies, remote signals or barrier semaphores. Data moves between devices by JAX's collectives and lax.ppermute only.
A program may use at most 128 MiB of HBM per device.

v0:
```python
import jax
import jax.numpy as jnp
from jax import lax
from jax.sharding import PartitionSpec as P

EXPERTS = 2
DRAFT = 8
CAP = 16


def rms_norm(values, gain):
    values = values.astype(jnp.float32)
    scale = lax.rsqrt(jnp.mean(values * values, axis=-1, keepdims=True) + 1e-05)
    return (values * scale * gain).astype(jnp.bfloat16)


def ssm_steps(inputs, steps, b_maps, c_maps, state, a_rate, d_skip):
    outputs = []
    for place in range(inputs.shape[1]):
        decay = jnp.exp(-steps[:, place, None, :] * a_rate[None])
        state = (
            decay * state
            + (steps[:, place] * inputs[:, place])[:, None, :] * b_maps[:, place, :, None]
        )
        outputs.append(
            jnp.sum(c_maps[:, place, :, None] * state, axis=1) + d_skip * inputs[:, place]
        )
    return (jnp.stack(outputs, axis=1), state)


def on_device(
    x_in,
    routes,
    conv_state,
    ssm_state,
    mamba_gain,
    in_x,
    in_z,
    conv_w,
    conv_b,
    xproj_dt,
    xproj_bc,
    dt_proj,
    dt_bias,
    a_rate,
    d_skip,
    out_proj,
    moe_gain,
    router,
    w_gate,
    w_up,
    w_down,
):
    tok_count, half_width = x_in.shape
    requests = conv_state.shape[0]
    channels = in_x.shape[1]
    states = a_rate.shape[0]
    topk = routes.shape[1]
    owners = lax.axis_size("expert")
    pieces = lax.axis_size("cuts")
    full_x = lax.all_gather(x_in, "cuts", axis=1, tiled=True)
    normed = rms_norm(lax.all_gather(full_x, "expert", axis=0, tiled=True), mamba_gain)
    upper = jnp.dot(normed, in_x, preferred_element_type=jnp.float32)
    lower = jnp.dot(normed, in_z, preferred_element_type=jnp.float32)
    both = jnp.stack([upper, lower])
    u_pre = both[0]
    z_gate = both[1]
    seq = jnp.concatenate([conv_state, u_pre.reshape(requests, DRAFT, channels)], axis=1)
    conv = jnp.zeros((requests, DRAFT, channels), jnp.float32) + conv_b
    for tap in range(conv_w.shape[0]):
        conv = conv + conv_w[tap] * seq[:, tap : tap + DRAFT]
    u_act = jax.nn.silu(conv).astype(jnp.bfloat16)
    flat_u = u_act.reshape(requests * DRAFT, channels)
    dt_part = jnp.dot(flat_u, xproj_dt, preferred_element_type=jnp.float32)
    map_part = jnp.dot(flat_u, xproj_bc, preferred_element_type=jnp.float32)
    dt_low, maps = lax.psum((dt_part, map_part), ("expert", "cuts"))
    steps = jax.nn.softplus(
        jnp.dot(dt_low.astype(jnp.bfloat16), dt_proj, preferred_element_type=jnp.float32) + dt_bias
    )
    b_maps = maps[:, :states].reshape(requests, DRAFT, states)
    c_maps = maps[:, states:].reshape(requests, DRAFT, states)
    outputs, new_state = ssm_steps(
        u_act.astype(jnp.float32),
        steps.reshape(requests, DRAFT, channels),
        b_maps,
        c_maps,
        ssm_state,
        a_rate,
        d_skip,
    )
    gated = (outputs.reshape(requests * DRAFT, channels) * jax.nn.silu(z_gate)).astype(jnp.bfloat16)
    term = jnp.einsum(
        "etc,ckf->ektf",
        gated.reshape(owners, tok_count, channels),
        out_proj.reshape(channels, pieces, half_width),
        preferred_element_type=jnp.float32,
    )
    term = term.reshape(owners * pieces * tok_count, half_width)
    mixed_half = lax.psum_scatter(term, ("expert", "cuts"), scatter_dimension=0, tiled=True)
    stream_half = (x_in.astype(jnp.float32) + mixed_half).astype(jnp.bfloat16)
    stream = lax.all_gather(stream_half, "cuts", axis=1, tiled=True)
    normed2 = rms_norm(stream, moe_gain)
    logits = jnp.dot(normed2, router, preferred_element_type=jnp.float32)
    all_labels = jnp.arange(router.shape[1], dtype=jnp.int32)
    pick = (routes[:, :, None] == all_labels).astype(jnp.float32)
    chosen = jnp.sum(logits[:, None, :] * pick, axis=-1)
    weight0 = jax.nn.sigmoid(chosen[:, 0] - chosen[:, 1])
    labels = jnp.arange(EXPERTS, dtype=jnp.int32)
    flat_routes = routes.reshape(tok_count * topk)
    onehot = (flat_routes[:, None] == labels).astype(jnp.int32)
    rank = jnp.cumsum(onehot, axis=0) - 1
    slot = jnp.sum(rank * onehot, axis=-1)
    inside = jnp.sum(onehot, axis=-1)
    dest = jnp.where(inside > 0, flat_routes * CAP + slot, EXPERTS * CAP)
    row_width = normed2.shape[1]
    rows = jnp.repeat(normed2, topk, axis=0)
    buffer = (
        jnp.zeros((EXPERTS * CAP + 1, row_width), jnp.bfloat16).at[dest].set(rows)[: EXPERTS * CAP]
    )
    buffer = buffer.reshape(EXPERTS, CAP, row_width)
    holders = owners // EXPERTS
    outgoing = jnp.repeat(buffer, holders, axis=0)[:, None]
    received = lax.all_to_all(outgoing, "expert", split_axis=0, concat_axis=1, tiled=True)
    local, sources, count, features = received.shape
    tokens = received.reshape(local * sources * count, features)
    gate = jnp.dot(tokens, w_gate, preferred_element_type=jnp.float32)
    upval = jnp.dot(tokens, w_up, preferred_element_type=jnp.float32)
    act = (jax.nn.silu(gate) * upval).astype(jnp.bfloat16)
    partial_out = jnp.dot(act, w_down, preferred_element_type=jnp.float32)
    partial_out = partial_out.reshape(local, sources, count, features)
    returned = lax.all_to_all(
        partial_out.astype(jnp.bfloat16), "expert", split_axis=1, concat_axis=0, tiled=True
    ).astype(partial_out.dtype)
    back_width = returned.shape[3]
    grouped = jnp.sum(returned.reshape(EXPERTS, holders, CAP, back_width), axis=1).reshape(
        EXPERTS * CAP, back_width
    )
    table = jnp.concatenate([grouped, jnp.zeros((1, back_width), jnp.float32)], axis=0)
    picked = table[dest].reshape(tok_count, topk, back_width)
    expert_out = lax.psum_scatter(
        picked.astype(jnp.bfloat16), "cuts", scatter_dimension=2, tiled=True
    )
    expert_out = expert_out.astype(jnp.float32)
    total = (
        stream_half.astype(jnp.float32)
        + weight0[:, None] * expert_out[:, 0]
        + (1.0 - weight0)[:, None] * expert_out[:, 1]
    )
    return (total.astype(jnp.bfloat16), new_state)


def solution(mesh):
    return jax.shard_map(
        on_device,
        mesh=mesh,
        in_specs=(
            P(("group", "expert"), "cuts"),
            P(("group", "expert"), None),
            P("group", None, ("expert", "cuts")),
            P("group", None, ("expert", "cuts")),
            P(),
            P(None, ("expert", "cuts")),
            P(None, ("expert", "cuts")),
            P(None, ("expert", "cuts")),
            P(("expert", "cuts")),
            P(("expert", "cuts"), None),
            P(("expert", "cuts"), None),
            P(None, ("expert", "cuts")),
            P(("expert", "cuts")),
            P(None, ("expert", "cuts")),
            P(("expert", "cuts")),
            P(("expert", "cuts"), None),
            P(),
            P(),
            P(None, ("expert", "cuts")),
            P(None, ("expert", "cuts")),
            P(("expert", "cuts"), None),
        ),
        out_specs=(P(("group", "expert"), "cuts"), P("group", None, ("expert", "cuts"))),
        check_vma=False,
    )
```

profile of v0, /device:TPU:0, one launch (start us, length us, event | category | flops | bytes accessed | tf_op | source)
XLA Modules:
  0.0 318.8 jit_solution(7484145724764435932)
XLA Ops:
  7.2 0.0 copy-start
  7.2 0.0 all-gather.2.cloned.1.call-start
  7.2 4.1 %all_gather.9 = bf16[32,4096]{1,0:T(8,128)(2,1)} all-gather(bf16[32,2048]{1,0:T(8,128)(2,1)} %param.21), channel_id=1, replica_groups=mesh['group'=2,'expert'=8,'cuts'=2] {'cuts'}, dimensions={1}, use_global_device_ids=true | all-gather | bytes 393216 | tf_op jit(solution)/shard_map/all_gather | solution.py:61
  11.3 0.0 all-gather.2.cloned.1.call-update
  11.3 0.0 reduce-scatter.3.cloned.1.call-start
  11.4 1.0 copy.129
  12.3 0.8 fusion.51
  13.2 50.0 %all-gather.2.cloned.1.call-done = bf16[256,4096]{1,0:T(8,128)(2,1)} async-done(((bf16[32,4096]{1,0:T(8,128)(2,1)}), bf16[256,4096]{1,0:T(8,128)(2,1)}) %all-gather.2.cloned.1.call-update) | async-done | bytes 2097168 | tf_op jit(solution)/shard_map/all_gather | solution.py:62
  63.2 2.1 fusion
  65.4 2.4 convolution_bitcast_fusion
  67.8 0.3 fusion.47
  68.0 0.2 fusion.39
  68.3 0.2 fusion.41
  68.4 65.3 %all-reduce.3 = (f32[256,32]{0,1:T(8,128)S(1)}, bf16[256,512]{1,0:T(8,128)(2,1)}) all-reduce(f32[256,32]{0,1:T(8,128)S(1)} %fusion.41, f32[256,512]{1,0:T(8,128)S(1)} %fusion.39), channel_id=1, replica_groups=mesh['group'=2,'expert'=8,'cuts'=2] {'expert','cuts'}, use_global_device_ids=true, to_apply=%region_1.2 | all-reduce | flops 139264 | bytes 851968 | tf_op jit(solution)/shard_map/psum | solution.py:76
  133.8 1.3 fusion.25
  135.1 0.8 slice_negate_fusion.2
  135.9 1.1 slice_multiply_fusion.4
  137.0 0.1 copy.133
  137.1 0.7 fusion.49
  137.8 0.1 copy.130
  137.9 0.1 fusion.48
  138.0 0.8 copy_bitcast_fusion.10
  138.8 0.8 copy_bitcast_fusion.14
  139.6 0.8 copy_bitcast_fusion.11
  140.3 0.8 copy_bitcast_fusion.5
  141.1 0.7 multiply_reduce_fusion.5
  141.8 2.5 multiply_reduce_fusion
  144.3 0.9 multiply_reduce_fusion.1
  145.2 1.0 multiply_add_fusion.8
  146.2 0.4 stack.2
  146.6 3.2 fusion.32
  149.8 2.6 fusion.3
  152.5 0.0 reduce-scatter.3.cloned.1.call-update
  152.5 0.1 copy.165
  152.6 0.1 eq.31
  152.7 0.1 copy.166
  152.8 0.1 mul.724
  152.9 0.1 fusion.43
  153.0 0.1 reduce_window_sum.11
  153.1 0.2 fusion.44
  153.3 69.0 %reduce-scatter.3.cloned.1.call-done = f32[32,2048]{1,0:T(8,128)} async-done(((f32[512,2048]{1,0:T(8,128)}), f32[32,2048]{1,0:T(8,128)}) %reduce-scatter.3.cloned.1.call-update) | async-done | bytes 262160 | tf_op jit(solution)/shard_map/reduce_scatter | solution.py:99
  222.3 1.0 add_convert_fusion
  223.3 2.0 all_gather.11
  225.3 0.2 fusion.9
  225.4 0.1 fusion.11
  225.6 0.5 broadcast_in_dim.11
  226.1 0.2 reshape.222
  226.3 1.4 scatter_custom_fusion
  227.7 0.1 broadcast_in_dim.12
  227.8 29.6 %all_to_all.8 = bf16[8,1,16,4096]{3,2,1,0:T(8,128)(2,1)S(1)} all-to-all(bf16[8,1,16,4096]{3,2,1,0:T(8,128)(2,1)S(1)} %bitcast.143), channel_id=1, replica_groups=mesh['group'=2,'expert'=8,'cuts'=2] {'expert'}, dimensions={0} | all-to-all | bytes 2097152 | tf_op jit(solution)/shard_map/all_to_all | solution.py:123
  257.3 4.5 %fusion.53 = f32[128,768]{1,0:T(8,128)} fusion(bf16[128,4096]{1,0:T(8,128)(2,1)S(1)} %bitcast.139, bf16[4096,768]{1,0:T(8,128)(2,1)} %param.39), kind=kOutput, calls=%fused_computation.141 | convolution fusion | flops 805306368 | bytes 7733248 | tf_op jit(solution)/shard_map/dot_general | solution.py:126
  261.9 8.2 %convolution_convert_fusion = bf16[128,4096]{1,0:T(8,128)(2,1)} fusion(bf16[768,4096]{1,0:T(8,128)(2,1)} %param.41, bf16[128,4096]{1,0:T(8,128)(2,1)S(1)} %bitcast.140, bf16[4096,768]{1,0:T(8,128)(2,1)} %param.40, f32[128,768]{1,0:T(8,128)} %fusion.53), kind=kOutput, calls=%fused_computation.4 | convolution fusion | flops 1611726848 | bytes 15073280 | tf_op jit(solution)/shard_map/dot_general | solution.py:129
  270.0 3.6 %all-to-all-start.1 = ((bf16[1,8,16,4096]{3,2,0,1:T(8,128)(2,1)}), bf16[1,8,16,4096]{3,2,0,1:T(8,128)(2,1)S(1)}, u32[]{:S(2)}, u32[]{:S(2)}) async-start(bf16[1,8,16,4096]{3,2,0,1:T(8,128)(2,1)} %bitcast.141), calls=%async_computation.2 | async-start | bytes 2097152 | tf_op jit(solution)/shard_map/all_to_all | solution.py:131
  273.7 0.0 reduce-scatter.5.cloned.1.call-start
  273.7 25.5 %all-to-all-done.1 = bf16[1,8,16,4096]{3,2,0,1:T(8,128)(2,1)S(1)} async-done(((bf16[1,8,16,4096]{3,2,0,1:T(8,128)(2,1)}), bf16[1,8,16,4096]{3,2,0,1:T(8,128)(2,1)S(1)}, u32[]{:S(2)}, u32[]{:S(2)}) %all-to-all-start.1) | async-done | bytes 1048608 | tf_op jit(solution)/shard_map/all_to_all | solution.py:131
  299.3 0.1 convert_reduce_fusion
  299.5 0.9 gather_fusion
  300.3 1.2 convert_element_type.97
  301.5 2.1 copy.168
  303.6 0.0 reduce-scatter.5.cloned.1.call-update
  303.6 0.2 fusion.52
  303.9 6.7 %reduce-scatter.5.cloned.1.call-done = bf16[32,2,2048]{2,0,1:T(8,128)(2,1)} async-done(((bf16[32,2,4096]{2,0,1:T(8,128)(2,1)}), bf16[32,2,2048]{2,0,1:T(8,128)(2,1)}) %reduce-scatter.5.cloned.1.call-update) | async-done | bytes 262160 | tf_op jit(solution)/shard_map/reduce_scatter | solution.py:140
  310.5 1.0 convert_element_type.98
  311.5 0.8 fusion.28
  (39 shorter events, 0.2 us)
Async XLA Ops:
  7.2 58.2 %copy-start = (bf16[4096,256]{1,0:T(8,128)(2,1)S(1)}, bf16[4096,256]{1,0:T(8,128)(2,1)}, u32[]{:S(2)}) copy-start(bf16[4096,256]{1,0:T(8,128)(2,1)} %param.26) | copy-start | bytes 6291460
  7.2 56.0 %all-gather.2.cloned.1.call-start = ((), (), s32[]{:S(2)}) async-start(), calls=%async_computation.4 | async-start | bytes 2359296 | tf_op jit(solution)/shard_map/all_gather | solution.py:62
  11.3 211.0 %reduce-scatter.3.cloned.1.call-start = ((), (), s32[]{:S(2)}) async-start(), calls=%async_computation.5 | async-start | bytes 4456448 | tf_op jit(solution)/shard_map/reduce_scatter | solution.py:99
  13.2 54.6 %copy-start.10 = (f32[256]{0:T(256)S(1)}, f32[256]{0:T(256)}, u32[]{:S(2)}) copy-start(f32[256]{0:T(256)} %param.29) | copy-start | bytes 3076
  63.2 4.8 %copy-start.4 = (bf16[256,512]{1,0:T(8,128)(2,1)S(1)}, bf16[256,512]{1,0:T(8,128)(2,1)}, u32[]{:S(2)}) copy-start(bf16[256,512]{1,0:T(8,128)(2,1)} %param.30) | copy-start | bytes 786436
  65.3 3.0 copy-start.8
  65.4 2.9 copy-start.11
  65.4 68.4 %copy-start.12 = (f32[256]{0:T(256)S(1)}, f32[256]{0:T(256)}, u32[]{:S(2)}) copy-start(f32[256]{0:T(256)} %param.33) | copy-start | bytes 3076
  67.7 73.4 %copy-start.2 = (f32[32,16,256]{2,1,0:T(8,128)S(1)}, f32[32,16,256]{2,1,0:T(8,128)}, u32[]{:S(2)}) copy-start(f32[32,16,256]{2,1,0:T(8,128)} %param.24) | copy-start | bytes 1572868
  67.8 73.4 %copy-start.5 = (f32[16,256]{1,0:T(8,128)S(1)}, f32[16,256]{1,0:T(8,128)}, u32[]{:S(2)}) copy-start(f32[16,256]{1,0:T(8,128)} %param.34) | copy-start | bytes 49156
  146.6 3.2 %copy-start.1 = (bf16[256,4096]{1,0:T(8,128)(2,1)S(1)}, bf16[256,4096]{1,0:T(8,128)(2,1)}, u32[]{:S(2)}) copy-start(bf16[256,4096]{1,0:T(8,128)(2,1)} %param.36) | copy-start | bytes 6291460
  149.8 2.7 copy-start.9
  149.8 72.5 %copy-start.3 = (bf16[32,2048]{1,0:T(8,128)(2,1)S(1)}, bf16[32,2048]{1,0:T(8,128)(2,1)}, u32[]{:S(2)}) copy-start(bf16[32,2048]{1,0:T(8,128)(2,1)} %param.21) | copy-start | bytes 393220
  152.5 73.0 %copy-start.7 = (f32[4096]{0:T(1024)S(1)}, f32[4096]{0:T(1024)}, u32[]{:S(2)}) copy-start(f32[4096]{0:T(1024)} %param.37) | copy-start | bytes 49156
  270.0 29.2 %all-to-all-start.1 = ((bf16[1,8,16,4096]{3,2,0,1:T(8,128)(2,1)}), bf16[1,8,16,4096]{3,2,0,1:T(8,128)(2,1)S(1)}, u32[]{:S(2)}, u32[]{:S(2)}) async-start(bf16[1,8,16,4096]{3,2,0,1:T(8,128)(2,1)} %bitcast.141), calls=%async_computation.2 | async-start | bytes 2097152 | tf_op jit(solution)/shard_map/all_to_all | solution.py:131
  273.7 36.9 %reduce-scatter.5.cloned.1.call-start = ((), (), s32[]{:S(2)}) async-start(), calls=%async_computation.6 | async-start | bytes 786432 | tf_op jit(solution)/shard_map/reduce_scatter | solution.py:140
  299.4 4.2 %copy-start.6 = (bf16[4096,16]{0,1:T(8,128)(2,1)S(1)}, bf16[4096,16]{0,1:T(8,128)(2,1)}, u32[]{:S(2)}) copy-start(bf16[4096,16]{0,1:T(8,128)(2,1)} %param.38) | copy-start | bytes 393220
Sparse Core Ops, SparseCore 0:
  11.5 51.7 all-gather.1
  152.6 69.6 reduce-scatter.2
  303.7 6.7 reduce-scatter.4
where the time goes:
time: 320 us; the launch traced here: 319 us
  waiting for transfers between devices  151 us (47%)
  blocking collectives  101 us (32%)
  matrix products  22.8 us (7%)
  between operations  14.1 us (4%)
  local copies, waits for them, and re-layouts  13.1 us (4%)
  other arithmetic  12.8 us (4%)
  starting transfers between devices  3.76 us (1%)
    reduce_scatter x1, waiting for transfers between devices, on_device(): lax.psum_scatter(term, ('expert', 'cuts'), scatter_dimension=0, tiled=True)  69 us
    psum x1, blocking collectives, on_device(): dt_low, maps = lax.psum((dt_part, map_part), ('expert', 'cuts'))  65.3 us
    all_gather x1, waiting for transfers between devices, on_device(): lax.all_gather(full_x, 'expert', axis=0, tiled=True)  50 us
    all_to_all x1, blocking collectives, on_device(): lax.all_to_all(outgoing, 'expert', split_axis=0, concat_axis=1, tiled=True)  29.6 us
    all_to_all x1, waiting for transfers between devices, on_device(): lax.all_to_all(partial_out.astype(jnp.bfloat16), 'expert', split_axis=1,...  25.5 us
    dot_general x1, matrix products, on_device(): partial_out = jnp.dot(act, w_down, preferred_element_type=jnp.float32)  8.17 us
    reduce_scatter x1, waiting for transfers between devices, on_device(): lax.psum_scatter(picked.astype(jnp.bfloat16), 'cuts', scatter_dimension=2...  6.68 us
  transfers between devices with their start and end apart: 4, of which 4 were waited for; matrix products, arithmetic and copies ran while one was open for 1% of the time, Pallas kernels for 0%

commit v1 on v0

v1 whole, which is shorter than its diff:
```python
import jax
import jax.numpy as jnp
import numpy as np
from jax import lax
from jax.sharding import PartitionSpec as P

EXPERTS = 2
DRAFT = 8
CAP = 16
F32 = jnp.float32
BF16 = jnp.bfloat16


def ring_order(owners):
    if owners == 8:
        return [0, 2, 4, 6, 7, 5, 3, 1]
    return list(range(owners))


def ring_tables(owners):
    order = ring_order(owners)
    place = {dev: i for i, dev in enumerate(order)}
    half = owners // 2
    ahead = np.zeros((owners, 2, owners), np.int32)
    for p in range(owners):
        for c in range(2):
            step = 1 if c == 0 else -1
            for d in range(owners):
                ahead[p, c, d] = order[(place[p] + step * d) % owners]
    perm = []
    for p in range(owners):
        for c in range(2):
            perm.append((p * 2 + c, int(ahead[p, c, 1]) * 2 + c))
    return ahead, perm, half


def over_cuts(value):
    return lax.ppermute(value, "cuts", [(0, 1), (1, 0)])


def over_expert(value, flip, owners):
    return lax.ppermute(value, "expert", [(i, i ^ flip) for i in range(owners)])


def rms_norm(values, gain):
    values = values.astype(F32)
    scale = lax.rsqrt(jnp.mean(values * values, axis=-1, keepdims=True) + 1e-05)
    return (values * scale * gain).astype(BF16)


def ssm_steps(inputs, steps, b_maps, c_maps, state, a_rate, d_skip):
    outputs = []
    for place in range(inputs.shape[1]):
        decay = jnp.exp(-steps[:, place, None, :] * a_rate[None])
        state = (
            decay * state
            + (steps[:, place] * inputs[:, place])[:, None, :] * b_maps[:, place, :, None]
        )
        outputs.append(
            jnp.sum(c_maps[:, place, :, None] * state, axis=1) + d_skip * inputs[:, place]
        )
    return (jnp.stack(outputs, axis=1), state)


def halves(first, second, core):
    return jnp.concatenate(
        [jnp.where(core == 0, first, second), jnp.where(core == 0, second, first)], axis=-1
    )


def gather_tokens(x_in, owners, core, ahead, perm):
    half = owners // 2
    rows, width = x_in.shape

    def send(value):
        return lax.ppermute(value, ("expert", "cuts"), perm)

    other = over_cuts(x_in)
    part_a, part_b = [x_in], [other]
    for step in range(1, half + 1):
        part_a.append(send(part_a[-1]))
        if step < half:
            part_b.append(send(part_b[-1]))
    mine = [halves(part_a[d], part_b[d], core) for d in range(half)]
    stack = jnp.concatenate(mine[1:], axis=0)
    theirs = over_cuts(stack).reshape(half - 1, rows, 2 * width)
    far = halves(part_a[half], over_cuts(part_a[half]), core)
    out = jnp.zeros((owners * rows, 2 * width), x_in.dtype)

    def put(buffer, block, index):
        return lax.dynamic_update_slice(buffer, block, (index * rows, 0))

    out = put(out, mine[0], ahead[core, 0])
    for d in range(1, half):
        out = put(out, mine[d], ahead[1 - core, d])
        out = put(out, theirs[d - 1], ahead[core, d])
    return put(out, far, ahead[core, half])


def sum_all(part, owners, expert, core):
    def split(value, bit):
        size = value.shape[0] // 2
        return (
            lax.dynamic_slice_in_dim(value, bit * size, size, 0),
            lax.dynamic_slice_in_dim(value, (1 - bit) * size, size, 0),
        )

    def join(mine, theirs, bit):
        size = mine.shape[0]
        out = jnp.zeros((2 * size,) + mine.shape[1:], mine.dtype)
        out = lax.dynamic_update_slice_in_dim(out, mine, bit * size, 0)
        return lax.dynamic_update_slice_in_dim(out, theirs, (1 - bit) * size, 0)

    keep, give = split(part, core)
    keep = keep + over_cuts(give.astype(BF16)).astype(F32)
    low = expert % 2
    keep, give = split(keep, low)
    keep = keep + over_expert(give.astype(BF16), 1, owners).astype(F32)
    flip = 2
    while flip < owners:
        keep = keep + over_expert(keep.astype(BF16), flip, owners).astype(F32)
        flip *= 2
    keep = keep.astype(BF16)
    keep = join(keep, over_expert(keep, 1, owners), low)
    return join(keep, over_cuts(keep), core)


def scatter_sum(term, rows, owners, core, ahead, perm):
    half = owners // 2
    width = term.shape[1] // 2
    here = core * width
    there = (1 - core) * width

    def block(index, start, size):
        return lax.dynamic_slice(term, (index * rows, start), (rows, size))

    def send(value):
        return lax.ppermute(value.astype(BF16), ("expert", "cuts"), perm)

    give = jnp.concatenate(
        [block(ahead[1 - core, d], start, width) for d in range(1, half) for start in (here, there)]
        + [block(ahead[core, half], there, width), block(ahead[core, 0], there, width)],
        axis=0,
    ).astype(BF16)
    got = over_cuts(give).astype(F32).reshape(2 * half, rows, width)
    acc_a = block(ahead[core, half], here, width) + got[2 * half - 2]
    acc_a = send(acc_a).astype(F32)
    acc_b = None
    for d in range(half - 1, 0, -1):
        local_a = block(ahead[core, d], here, width) + got[2 * d - 1]
        local_b = block(ahead[core, d], there, width) + got[2 * d - 2]
        acc_a = send(acc_a + local_a).astype(F32)
        acc_b = send(local_b if acc_b is None else acc_b + local_b).astype(F32)
    cross = over_cuts(acc_b.astype(BF16)).astype(F32)
    return block(ahead[core, 0], here, width) + got[2 * half - 1] + acc_a + cross


def on_device(
    x_in,
    routes,
    conv_state,
    ssm_state,
    mamba_gain,
    in_x,
    in_z,
    conv_w,
    conv_b,
    xproj_dt,
    xproj_bc,
    dt_proj,
    dt_bias,
    a_rate,
    d_skip,
    out_proj,
    moe_gain,
    router,
    w_gate,
    w_up,
    w_down,
):
    tok_count, half_width = x_in.shape
    requests = conv_state.shape[0]
    channels = in_x.shape[1]
    states = a_rate.shape[0]
    topk = routes.shape[1]
    owners = lax.axis_size("expert")
    expert = lax.axis_index("expert")
    core = lax.axis_index("cuts")
    table, perm, half = ring_tables(owners)
    ahead = lax.dynamic_index_in_dim(jnp.asarray(table), expert, 0, keepdims=False)
    full_x = gather_tokens(x_in, owners, core, ahead, perm)
    normed = rms_norm(full_x, mamba_gain)
    u_pre = jnp.dot(normed, in_x, preferred_element_type=F32)
    z_gate = jnp.dot(normed, in_z, preferred_element_type=F32)
    seq = jnp.concatenate([conv_state, u_pre.reshape(requests, DRAFT, channels)], axis=1)
    conv = jnp.zeros((requests, DRAFT, channels), F32) + conv_b
    for tap in range(conv_w.shape[0]):
        conv = conv + conv_w[tap] * seq[:, tap : tap + DRAFT]
    u_act = jax.nn.silu(conv).astype(BF16)
    flat_u = u_act.reshape(requests * DRAFT, channels)
    rank = xproj_dt.shape[1]
    part = jnp.concatenate(
        [
            jnp.dot(flat_u, xproj_dt, preferred_element_type=F32),
            jnp.dot(flat_u, xproj_bc, preferred_element_type=F32),
        ],
        axis=1,
    )
    total = sum_all(part, owners, expert, core)
    dt_low = total[:, :rank]
    maps = total[:, rank:].astype(F32)
    steps = jax.nn.softplus(jnp.dot(dt_low, dt_proj, preferred_element_type=F32) + dt_bias)
    b_maps = maps[:, :states].reshape(requests, DRAFT, states)
    c_maps = maps[:, states:].reshape(requests, DRAFT, states)
    outputs, new_state = ssm_steps(
        u_act.astype(F32),
        steps.reshape(requests, DRAFT, channels),
        b_maps,
        c_maps,
        ssm_state,
        a_rate,
        d_skip,
    )
    gated = (outputs.reshape(requests * DRAFT, channels) * jax.nn.silu(z_gate)).astype(BF16)
    term = jnp.dot(gated, out_proj, preferred_element_type=F32)
    mixed_half = scatter_sum(term, tok_count, owners, core, ahead, perm)
    stream_half = (x_in.astype(F32) + mixed_half).astype(BF16)

    labels = jnp.arange(EXPERTS, dtype=jnp.int32)
    named = jnp.any(routes[:, :, None] == labels, axis=1).astype(BF16)
    earlier = (jnp.arange(tok_count)[:, None] > jnp.arange(tok_count)[None, :]).astype(BF16)
    slot = jnp.dot(earlier, named, preferred_element_type=F32)
    rows = jnp.arange(CAP, dtype=F32)
    pick = ((slot.T[:, None, :] == rows[None, :, None]) & (named.T[:, None, :] > 0)).astype(BF16)
    buffer = (
        jnp.dot(pick.reshape(EXPERTS * CAP, tok_count), stream_half, preferred_element_type=F32)
        .astype(BF16)
        .reshape(EXPERTS, CAP, half_width)
    )
    holders = owners // EXPERTS
    own = expert // holders

    def exchange(value, flip):
        return over_expert(value, flip, owners)

    kept = lax.dynamic_index_in_dim(buffer, own, 0, keepdims=False)
    given = lax.dynamic_index_in_dim(buffer, 1 - own, 0, keepdims=False)
    pair = jnp.concatenate([kept, exchange(given, holders)], axis=0)
    pieces = [pair] + [exchange(pair, flip) for flip in range(1, holders)]
    tokens_half = jnp.concatenate(pieces, axis=0)
    tokens = halves(tokens_half, over_cuts(tokens_half), core)
    normed2 = rms_norm(tokens, moe_gain)
    gate = jnp.dot(normed2, w_gate, preferred_element_type=F32)
    upval = jnp.dot(normed2, w_up, preferred_element_type=F32)
    act = (jax.nn.silu(gate) * upval).astype(BF16)
    partial_out = jnp.dot(act, w_down, preferred_element_type=F32)
    count = partial_out.shape[0]
    mine = lax.dynamic_slice(partial_out, (0, core * half_width), (count, half_width))
    theirs = lax.dynamic_slice(partial_out, (0, (1 - core) * half_width), (count, half_width))
    summed = mine + over_cuts(theirs.astype(BF16)).astype(F32)
    summed = summed.reshape(holders, 2 * CAP, half_width)
    result = summed[0]
    for flip in range(1, holders):
        result = result + exchange(summed[flip].astype(BF16), flip).astype(F32)
    result = result.astype(BF16)
    back = exchange(result[CAP:], holders)

    stream = halves(stream_half, over_cuts(stream_half), core)
    logits = jnp.dot(rms_norm(stream, moe_gain), router, preferred_element_type=F32)
    all_labels = jnp.arange(router.shape[1], dtype=jnp.int32)
    which = (routes[:, :, None] == all_labels).astype(F32)
    chosen = jnp.sum(logits[:, None, :] * which, axis=-1)
    weight0 = jax.nn.sigmoid(chosen[:, 0] - chosen[:, 1])
    weights = jnp.stack([weight0, 1.0 - weight0], axis=1)
    weight = jnp.sum(jnp.where(routes < EXPERTS, weights, 0.0), axis=1)
    table = jnp.concatenate([result[:CAP], back], axis=0)
    pick_own = jnp.where(own == 0, pick, pick[::-1]).reshape(EXPERTS * CAP, tok_count)
    expert_out = lax.dot_general(
        pick_own, table, (((0,), (0,)), ((), ())), preferred_element_type=F32
    )
    out = stream_half.astype(F32) + weight[:, None] * expert_out
    return (out.astype(BF16), new_state)


def solution(mesh):
    return jax.shard_map(
        on_device,
        mesh=mesh,
        in_specs=(
            P(("group", "expert"), "cuts"),
            P(("group", "expert"), None),
            P("group", None, ("expert", "cuts")),
            P("group", None, ("expert", "cuts")),
            P(),
            P(None, ("expert", "cuts")),
            P(None, ("expert", "cuts")),
            P(None, ("expert", "cuts")),
            P(("expert", "cuts")),
            P(("expert", "cuts"), None),
            P(("expert", "cuts"), None),
            P(None, ("expert", "cuts")),
            P(("expert", "cuts")),
            P(None, ("expert", "cuts")),
            P(("expert", "cuts")),
            P(("expert", "cuts"), None),
            P(),
            P(),
            P(None, ("expert", "cuts")),
            P(None, ("expert", "cuts")),
            P(("expert", "cuts"), None),
        ),
        out_specs=(P(("group", "expert"), "cuts"), P("group", None, ("expert", "cuts"))),
        check_vma=False,
    )
```

time: 320 us -> 165 us (0.52)
  blocking collectives: 101 us -> 0 us
  waiting for transfers between devices: 151 us -> 63.9 us
  starting transfers between devices: 3.76 us -> 39.8 us
  between operations: 14.1 us -> 6.35 us
    reduce_scatter x2 -> x0, waiting for transfers between devices: 75.7 us -> none  [the longest x1 69 us: on_device(): lax.psum_scatter(term, ('expert', 'cuts'), scatter_dimension=0, tiled=True)]
    psum x1 -> x0, blocking collectives: 65.3 us -> none  [on_device(): dt_low, maps = lax.psum((dt_part, map_part), ('expert', 'cuts'))]
    ppermute x0 -> x36, waiting for transfers between devices: none -> 63.9 us  [the longest x12 34.7 us: over_expert(): return lax.ppermute(value, 'expert', [(i, i ^ flip) for i in range(owners)])]
    all_gather x1 -> x0, waiting for transfers between devices: 50 us -> none  [on_device(): lax.all_gather(full_x, 'expert', axis=0, tiled=True)]
    ppermute x0 -> x36, starting transfers between devices: none -> 39.8 us  [the longest x12 15.4 us: over_expert(): return lax.ppermute(value, 'expert', [(i, i ^ flip) for i in range(owners)])]
    all_to_all x1 -> x0, blocking collectives: 29.6 us -> none  [on_device(): lax.all_to_all(outgoing, 'expert', split_axis=0, concat_axis=1, tiled=True)]
    all_to_all x1 -> x0, waiting for transfers between devices: 25.5 us -> none  [on_device(): lax.all_to_all(partial_out.astype(jnp.bfloat16), 'expert', split_axis=1,...]
    all_gather x2 -> x0, blocking collectives: 6.07 us -> none  [the longest x1 4.08 us: on_device(): full_x = lax.all_gather(x_in, 'cuts', axis=1, tiled=True)]
  transfers between devices with their start and end apart: 4 -> 36, of which waited for: 4 -> 31; matrix products, arithmetic and copies ran while one was open for 1% -> 4% of each run, Pallas kernels for 0% -> 0%
where the time goes in v1:
time: 165 us
  waiting for transfers between devices  63.9 us (39%)
  starting transfers between devices  39.8 us (24%)
  matrix products  23.6 us (14%)
  local copies, waits for them, and re-layouts  16.2 us (10%)
  other arithmetic  14.7 us (9%)
  between operations  6.35 us (4%)
    ppermute x12, waiting for transfers between devices, over_expert(): return lax.ppermute(value, 'expert', [(i, i ^ flip) for i in range(owners)])  34.7 us
    ppermute x12, starting transfers between devices, over_expert(): return lax.ppermute(value, 'expert', [(i, i ^ flip) for i in range(owners)])  15.4 us
    ppermute x7, waiting for transfers between devices, send(): return lax.ppermute(value.astype(BF16), ('expert', 'cuts'), perm)  13.7 us
    ppermute x7, starting transfers between devices, send(): return lax.ppermute(value, ('expert', 'cuts'), perm)  12.2 us
    ppermute x7, starting transfers between devices, send(): return lax.ppermute(value.astype(BF16), ('expert', 'cuts'), perm)  10.8 us
    unnamed x54, local copies, waits for them, and re-layouts  10.2 us
    ppermute x10, waiting for transfers between devices, over_cuts(): return lax.ppermute(value, 'cuts', [(0, 1), (1, 0)])  8.62 us
    dot_general x1, matrix products, on_device(): partial_out = jnp.dot(act, w_down, preferred_element_type=F32)  8.61 us
  transfers between devices with their start and end apart: 36, of which 31 were waited for; matrix products, arithmetic and copies ran while one was open for 4% of the time, Pallas kernels for 0%

profile of v1, /device:TPU:0, one launch (start us, length us, event | category | flops | bytes accessed | tf_op | source)
XLA Modules:
  0.0 164.5 jit_solution(10659561233583695715)
XLA Ops:
  1.2 2.6 %collective-permute-start.1 = (bf16[32,2048]{1,0:T(8,128)(2,1)}, bf16[32,2048]{1,0:T(8,128)(2,1)S(1)}, u32[]{:S(2)}, u32[]{:S(2)}) collective-permute-start(bf16[32,2048]{1,0:T(8,128)(2,1)} %param.22), channel_id=1, source_target_pairs={{0,4},{1,3},{2,0},{3,7},{4,8},{5,1},{6,2},{7,11},{8,12},{9,5},{10,... | collective-permute-start | bytes 393224 | tf_op jit(solution)/shard_map/ppermute | solution.py:76
  3.8 1.6 constant_dynamic-slice_fusion.1
  12.2 1.6 collective-permute-start.2
  15.1 1.6 collective-permute-start.3
  17.3 1.6 collective-permute-start.4
  18.9 1.2 collective-permute-done.3
  20.1 1.6 collective-permute-start.5
  22.2 1.6 collective-permute-start.6
  23.8 1.2 collective-permute-done.5
  25.1 1.6 collective-permute-start.8
  27.4 2.7 %collective-permute-done.8 = bf16[32,2048]{1,0:T(8,128)(2,1)S(1)} collective-permute-done((bf16[32,2048]{1,0:T(8,128)(2,1)S(1)}, bf16[32,2048]{1,0:T(8,128)(2,1)S(1)}, u32[]{:S(2)}, u32[]{:S(2)}) %collective-permute-start.8) | collective-permute-done | bytes 131104 | tf_op jit(solution)/shard_map/ppermute | solution.py:76
  30.1 1.3 collective-permute-done.9
  32.2 1.6 %copy-done.14 = bf16[4096,256]{1,0:T(8,128)(2,1)S(1)} copy-done((bf16[4096,256]{1,0:T(8,128)(2,1)S(1)}, bf16[4096,256]{1,0:T(8,128)(2,1)}, u32[]{:S(2)}) %copy-start.14) | copy-done | bytes 2097176
  35.6 1.2 collective-permute-done.10
  37.4 4.0 %collective-permute-done.11 = bf16[64,544]{1,0:T(8,128)(2,1)S(1)} collective-permute-done((bf16[64,544]{1,0:T(8,128)(2,1)S(1)}, bf16[64,544]{1,0:T(8,128)(2,1)S(1)}, u32[]{:S(2)}, u32[]{:S(2)}) %collective-permute-start.11) | collective-permute-done | bytes 69664 | tf_op jit(solution)/shard_map/ppermute | solution.py:42
  41.5 1.6 collective-permute-start.12
  43.1 2.9 %collective-permute-done.12 = bf16[64,544]{1,0:T(8,128)(2,1)S(1)} collective-permute-done((bf16[64,544]{1,0:T(8,128)(2,1)S(1)}, bf16[64,544]{1,0:T(8,128)(2,1)S(1)}, u32[]{:S(2)}, u32[]{:S(2)}) %collective-permute-start.12) | collective-permute-done | bytes 69664 | tf_op jit(solution)/shard_map/ppermute | solution.py:42
  46.0 2.6 %collective-permute-start.13 = (bf16[64,544]{1,0:T(8,128)(2,1)S(1)}, bf16[64,544]{1,0:T(8,128)(2,1)S(1)}, u32[]{:S(2)}, u32[]{:S(2)}) collective-permute-start(bf16[64,544]{1,0:T(8,128)(2,1)S(1)} %fusion.84), channel_id=1, source_target_pairs={{0,8},{2,10},{4,12},{6,14},{8,0},{10,2},{12,4},{14,6},{1,9},{3,11}... | collective-permute-start | bytes 208904 | tf_op jit(solution)/shard_map/ppermute | solution.py:42
  48.6 2.8 %collective-permute-done.13 = bf16[64,544]{1,0:T(8,128)(2,1)S(1)} collective-permute-done((bf16[64,544]{1,0:T(8,128)(2,1)S(1)}, bf16[64,544]{1,0:T(8,128)(2,1)S(1)}, u32[]{:S(2)}, u32[]{:S(2)}) %collective-permute-start.13) | collective-permute-done | bytes 69664 | tf_op jit(solution)/shard_map/ppermute | solution.py:42
  52.0 4.0 %collective-permute-done.14 = bf16[64,544]{1,0:T(8,128)(2,1)S(1)} collective-permute-done((bf16[64,544]{1,0:T(8,128)(2,1)S(1)}, bf16[64,544]{1,0:T(8,128)(2,1)S(1)}, u32[]{:S(2)}, u32[]{:S(2)}) %collective-permute-start.14) | collective-permute-done | bytes 69664 | tf_op jit(solution)/shard_map/ppermute | solution.py:42
  56.2 1.3 collective-permute-done.15
  59.6 1.8 %multiply_reduce_fusion = (f32[32,256]{1,0:T(8,128)S(1)}, f32[32,16,256]{2,1,0:T(8,128)}, f32[32,16,256]{2,1,0:T(8,128)S(1)}) fusion(f32[32,16]{1,0:T(8,128)S(1)} %bitcast.126, f32[32,16]{1,0:T(8,128)S(1)} %bitcast.127, f32[32,256]{1,0:T(8,128)S(1)} %get-tuple-element.109, f32[32,16]{1,0:T(8,128)S(1)} %bitcast.114, f32[32,256]{1,0:T(8,128)S(1)} %get-tuple-element.111, ...), kind=kLoop, calls=%fused_computation.36 | loop fusion | flops 4448256 | bytes 2164736 | tf_op jit(solution)/shard_map/reduce_sum | solution.py:60
  63.1 6.6 %fusion.61 = f32[256,4096]{1,0:T(8,128)} fusion(bf16[256,4096]{1,0:T(8,128)(2,1)S(1)} %copy-done, f32[32,8,256]{2,1,0:T(8,128)S(1)} %stack.4, bf16[4096,256]{1,0:T(8,128)(2,1)} %param.28, bf16[256,4096]{1,0:T(8,128)(2,1)} %copy-done.1, f32[4096]{0:T(1024)S(1)} %copy-done.7, f32[256]{0:T(256)S(1)} %add_rsqrt_fusion), kind=kOutput, calls=%fused_computation.126 | convolution fusion | flops 1078329344 | bytes 10765312 | tf_op jit(solution)/shard_map/dot_general | solution.py:225
  70.6 1.0 fusion.67
  71.6 1.0 fusion.68
  75.5 1.0 fusion.72
  76.5 1.0 fusion.73
  77.7 2.5 %collective-permute-done.16 = bf16[256,2048]{1,0:T(8,128)(2,1)S(1)} collective-permute-done((bf16[256,2048]{1,0:T(8,128)(2,1)S(1)}, bf16[256,2048]{1,0:T(8,128)(2,1)S(1)}, u32[]{:S(2)}, u32[]{:S(2)}) %collective-permute-start.16) | collective-permute-done | bytes 1048608 | tf_op jit(solution)/shard_map/ppermute | solution.py:38
  80.5 1.2 fusion.48
  81.7 1.6 collective-permute-start.17
  83.3 3.4 %collective-permute-done.17 = bf16[32,2048]{1,0:T(8,128)(2,1)S(1)} collective-permute-done((bf16[32,2048]{1,0:T(8,128)(2,1)S(1)}, bf16[32,2048]{1,0:T(8,128)(2,1)S(1)}, u32[]{:S(2)}, u32[]{:S(2)}) %collective-permute-start.17) | collective-permute-done | bytes 131104 | tf_op jit(solution)/shard_map/ppermute | solution.py:138
  86.7 1.1 fusion.47
  87.8 1.6 collective-permute-start.18
  89.4 1.5 collective-permute-start.21
  91.0 1.8 %collective-permute-done.18 = bf16[32,2048]{1,0:T(8,128)(2,1)S(1)} collective-permute-done((bf16[32,2048]{1,0:T(8,128)(2,1)S(1)}, bf16[32,2048]{1,0:T(8,128)(2,1)S(1)}, u32[]{:S(2)}, u32[]{:S(2)}) %collective-permute-start.18) | collective-permute-done | bytes 131104 | tf_op jit(solution)/shard_map/ppermute | solution.py:138
  92.8 1.6 collective-permute-done.21
  94.4 1.3 fusion.45
  95.6 1.6 collective-permute-start.19
  97.2 1.4 collective-permute-start.22
  98.7 1.9 %collective-permute-done.19 = bf16[32,2048]{1,0:T(8,128)(2,1)S(1)} collective-permute-done((bf16[32,2048]{1,0:T(8,128)(2,1)S(1)}, bf16[32,2048]{1,0:T(8,128)(2,1)S(1)}, u32[]{:S(2)}, u32[]{:S(2)}) %collective-permute-start.19) | collective-permute-done | bytes 131104 | tf_op jit(solution)/shard_map/ppermute | solution.py:138
  100.6 1.5 collective-permute-done.22
  102.2 1.3 fusion.43
  103.4 1.5 collective-permute-start.23
  105.0 1.6 collective-permute-start.20
  106.5 1.9 %collective-permute-done.23 = bf16[32,2048]{1,0:T(8,128)(2,1)S(1)} collective-permute-done((bf16[32,2048]{1,0:T(8,128)(2,1)S(1)}, bf16[32,2048]{1,0:T(8,128)(2,1)S(1)}, u32[]{:S(2)}, u32[]{:S(2)}) %collective-permute-start.23) | collective-permute-done | bytes 131104 | tf_op jit(solution)/shard_map/ppermute | solution.py:138
  108.5 1.6 collective-permute-done.20
  110.1 1.1 fusion.52
  111.5 2.1 %collective-permute-start.26 = (bf16[16,2048]{1,0:T(8,128)(2,1)S(1)}, bf16[16,2048]{1,0:T(8,128)(2,1)S(1)}, u32[]{:S(2)}, u32[]{:S(2)}) collective-permute-start(bf16[16,2048]{1,0:T(8,128)(2,1)S(1)} %dynamic-slice_bitcast_fusion), channel_id=1, source_target_pairs={{0,8},{2,10},{4,12},{6,14},{8,0},{10,2},{12,4},{14,6},{1,9},{3,11}... | collective-permute-start | bytes 196616 | tf_op jit(solution)/shard_map/ppermute | solution.py:42
  113.6 4.7 %collective-permute-done.26 = bf16[16,2048]{1,0:T(8,128)(2,1)S(1)} collective-permute-done((bf16[16,2048]{1,0:T(8,128)(2,1)S(1)}, bf16[16,2048]{1,0:T(8,128)(2,1)S(1)}, u32[]{:S(2)}, u32[]{:S(2)}) %collective-permute-start.26) | collective-permute-done | bytes 65568 | tf_op jit(solution)/shard_map/ppermute | solution.py:42
  119.0 2.9 %collective-permute-start.29 = (bf16[32,2048]{1,0:T(8,128)(2,1)S(1)}, bf16[32,2048]{1,0:T(8,128)(2,1)S(1)}, u32[]{:S(2)}, u32[]{:S(2)}) collective-permute-start(bf16[32,2048]{1,0:T(8,128)(2,1)S(1)} %pad_maximum_fusion.4), channel_id=1, source_target_pairs={{0,6},{2,4},{4,2},{6,0},{8,14},{10,12},{12,10},{14,8},{1,7},{3,5},... | collective-permute-start | bytes 393224 | tf_op jit(solution)/shard_map/ppermute | solution.py:42
  121.9 2.0 %collective-permute-done.27 = bf16[32,2048]{1,0:T(8,128)(2,1)S(1)} collective-permute-done((bf16[32,2048]{1,0:T(8,128)(2,1)S(1)}, bf16[32,2048]{1,0:T(8,128)(2,1)S(1)}, u32[]{:S(2)}, u32[]{:S(2)}) %collective-permute-start.27) | collective-permute-done | bytes 131104 | tf_op jit(solution)/shard_map/ppermute | solution.py:42
  124.0 1.4 collective-permute-done.28
  125.4 2.1 %collective-permute-done.29 = bf16[32,2048]{1,0:T(8,128)(2,1)S(1)} collective-permute-done((bf16[32,2048]{1,0:T(8,128)(2,1)S(1)}, bf16[32,2048]{1,0:T(8,128)(2,1)S(1)}, u32[]{:S(2)}, u32[]{:S(2)}) %collective-permute-start.29) | collective-permute-done | bytes 131104 | tf_op jit(solution)/shard_map/ppermute | solution.py:42
  127.8 1.7 %collective-permute-done.30 = bf16[128,2048]{1,0:T(8,128)(2,1)S(1)} collective-permute-done((bf16[128,2048]{1,0:T(8,128)(2,1)S(1)}, bf16[128,2048]{1,0:T(8,128)(2,1)S(1)}, u32[]{:S(2)}, u32[]{:S(2)}) %collective-permute-start.30) | collective-permute-done | bytes 524320 | tf_op jit(solution)/shard_map/ppermute | solution.py:38
  130.4 4.6 %fusion.97 = f32[128,768]{1,0:T(8,128)} fusion(bf16[4096,768]{1,0:T(8,128)(2,1)} %param.40, f32[4096]{0:T(1024)S(1)} %copy-done.9, f32[128]{0:T(128)S(1)} %add_rsqrt_fusion.1, bf16[128,2048]{1,0:T(8,128)(2,1)S(1)} %get-tuple-element.29, bf16[128,2048]{1,0:T(8,128)(2,1)S(1)} %get-tuple-element.28), kind=kOutput, calls=%fused_computation.249 | convolution fusion | flops 808976384 | bytes 7750144 | tf_op jit(solution)/shard_map/dot_general | solution.py:253
  135.0 8.6 %fusion.7 = f32[128,4096]{1,0:T(8,128)} fusion(bf16[768,4096]{1,0:T(8,128)(2,1)} %param.42, bf16[4096,768]{1,0:T(8,128)(2,1)} %param.41, f32[128,768]{1,0:T(8,128)} %fusion.97, f32[4096]{0:T(1024)} %param.38, f32[128]{0:T(128)} %copy-done.13, bf16[128,2048]{1,0:T(8,128)(2,1)S(1)} %get-tuple-element.29, bf16[128,2048]{1,0:T(8,128)(2,1)S(1)} %get-tuple-element.28), kind=kOutput, calls=%fused_computation.23 | convolution fusion | flops 1614872576 | bytes 16138752 | tf_op jit(solution)/shard_map/dot_general | solution.py:256
  143.6 1.3 dynamic-slice_convert_fusion
  145.1 1.2 fusion.23
  146.9 1.4 fusion.99
  149.4 2.5 %collective-permute-start.34 = (bf16[32,2048]{1,0:T(8,128)(2,1)S(1)}, bf16[32,2048]{1,0:T(8,128)(2,1)S(1)}, u32[]{:S(2)}, u32[]{:S(2)}) collective-permute-start(bf16[32,2048]{1,0:T(8,128)(2,1)S(1)} %get-tuple-element.31), channel_id=1, source_target_pairs={{0,6},{2,4},{4,2},{6,0},{8,14},{10,12},{12,10},{14,8},{1,7},{3,5},... | collective-permute-start | bytes 393224 | tf_op jit(solution)/shard_map/ppermute | solution.py:42
  151.9 2.0 %collective-permute-done.32 = bf16[32,2048]{1,0:T(8,128)(2,1)S(1)} collective-permute-done((bf16[32,2048]{1,0:T(8,128)(2,1)S(1)}, bf16[32,2048]{1,0:T(8,128)(2,1)S(1)}, u32[]{:S(2)}, u32[]{:S(2)}) %collective-permute-start.32) | collective-permute-done | bytes 131104 | tf_op jit(solution)/shard_map/ppermute | solution.py:42
  153.9 1.6 collective-permute-done.33
  155.5 2.4 %collective-permute-done.34 = bf16[32,2048]{1,0:T(8,128)(2,1)S(1)} collective-permute-done((bf16[32,2048]{1,0:T(8,128)(2,1)S(1)}, bf16[32,2048]{1,0:T(8,128)(2,1)S(1)}, u32[]{:S(2)}, u32[]{:S(2)}) %collective-permute-start.34) | collective-permute-done | bytes 131104 | tf_op jit(solution)/shard_map/ppermute | solution.py:42
  158.9 4.7 %collective-permute-done.35 = bf16[16,2048]{1,0:T(8,128)(2,1)S(1)} collective-permute-done((bf16[16,2048]{1,0:T(8,128)(2,1)S(1)}, bf16[16,2048]{1,0:T(8,128)(2,1)S(1)}, u32[]{:S(2)}, u32[]{:S(2)}) %collective-permute-start.35) | collective-permute-done | bytes 65568 | tf_op jit(solution)/shard_map/ppermute | solution.py:42
  (145 shorter events, 23.3 us)
Async XLA Ops:
  0.6 62.4 %copy-start = (bf16[256,4096]{1,0:T(8,128)(2,1)S(1)}, bf16[256,4096]{1,0:T(8,128)(2,1)}, u32[]{:S(2)}) copy-start(bf16[256,4096]{1,0:T(8,128)(2,1)} %param.37) | copy-start | bytes 6291460
  0.6 11.6 %collective-permute-start = (bf16[32,2048]{1,0:T(8,128)(2,1)}, bf16[32,2048]{1,0:T(8,128)(2,1)S(1)}, u32[]{:S(2)}, u32[]{:S(2)}) collective-permute-start(bf16[32,2048]{1,0:T(8,128)(2,1)} %param.22), channel_id=1, source_target_pairs={{0,1},{1,0},{2,3},{3,2},{4,5},{5,4},{6,7},{7,6},{8,9},{9,8},{10,11... | collective-permute-start | bytes 393224 | tf_op jit(solution)/shard_map/ppermute | solution.py:38
  1.2 13.9 %collective-permute-start.1 = (bf16[32,2048]{1,0:T(8,128)(2,1)}, bf16[32,2048]{1,0:T(8,128)(2,1)S(1)}, u32[]{:S(2)}, u32[]{:S(2)}) collective-permute-start(bf16[32,2048]{1,0:T(8,128)(2,1)} %param.22), channel_id=1, source_target_pairs={{0,4},{1,3},{2,0},{3,7},{4,8},{5,1},{6,2},{7,11},{8,12},{9,5},{10,... | collective-permute-start | bytes 393224 | tf_op jit(solution)/shard_map/ppermute | solution.py:76
  12.2 5.0 %collective-permute-start.2 = (bf16[32,2048]{1,0:T(8,128)(2,1)S(1)}, bf16[32,2048]{1,0:T(8,128)(2,1)S(1)}, u32[]{:S(2)}, u32[]{:S(2)}) collective-permute-start(bf16[32,2048]{1,0:T(8,128)(2,1)S(1)} %collective-permute-done), channel_id=1, source_target_pairs={{0,4},{1,3},{2,0},{3,7},{4,8},{5,1},{6,2},{7,11},{8,12},{9,5},{10,... | collective-permute-start | bytes 393224 | tf_op jit(solution)/shard_map/ppermute | solution.py:76
  15.1 5.0 %collective-permute-start.3 = (bf16[32,2048]{1,0:T(8,128)(2,1)S(1)}, bf16[32,2048]{1,0:T(8,128)(2,1)S(1)}, u32[]{:S(2)}, u32[]{:S(2)}) collective-permute-start(bf16[32,2048]{1,0:T(8,128)(2,1)S(1)} %collective-permute-done.1), channel_id=1, source_target_pairs={{0,4},{1,3},{2,0},{3,7},{4,8},{5,1},{6,2},{7,11},{8,12},{9,5},{10,... | collective-permute-start | bytes 393224 | tf_op jit(solution)/shard_map/ppermute | solution.py:76
  17.3 5.0 %collective-permute-start.4 = (bf16[32,2048]{1,0:T(8,128)(2,1)S(1)}, bf16[32,2048]{1,0:T(8,128)(2,1)S(1)}, u32[]{:S(2)}, u32[]{:S(2)}) collective-permute-start(bf16[32,2048]{1,0:T(8,128)(2,1)S(1)} %collective-permute-done.2), channel_id=1, source_target_pairs={{0,4},{1,3},{2,0},{3,7},{4,8},{5,1},{6,2},{7,11},{8,12},{9,5},{10,... | collective-permute-start | bytes 393224 | tf_op jit(solution)/shard_map/ppermute | solution.py:76
  20.1 5.0 %collective-permute-start.5 = (bf16[32,2048]{1,0:T(8,128)(2,1)S(1)}, bf16[32,2048]{1,0:T(8,128)(2,1)S(1)}, u32[]{:S(2)}, u32[]{:S(2)}) collective-permute-start(bf16[32,2048]{1,0:T(8,128)(2,1)S(1)} %collective-permute-done.3), channel_id=1, source_target_pairs={{0,4},{1,3},{2,0},{3,7},{4,8},{5,1},{6,2},{7,11},{8,12},{9,5},{10,... | collective-permute-start | bytes 393224 | tf_op jit(solution)/shard_map/ppermute | solution.py:76
  22.2 5.0 %collective-permute-start.6 = (bf16[32,2048]{1,0:T(8,128)(2,1)S(1)}, bf16[32,2048]{1,0:T(8,128)(2,1)S(1)}, u32[]{:S(2)}, u32[]{:S(2)}) collective-permute-start(bf16[32,2048]{1,0:T(8,128)(2,1)S(1)} %collective-permute-done.4), channel_id=1, source_target_pairs={{0,4},{1,3},{2,0},{3,7},{4,8},{5,1},{6,2},{7,11},{8,12},{9,5},{10,... | collective-permute-start | bytes 393224 | tf_op jit(solution)/shard_map/ppermute | solution.py:76
  25.1 5.0 %collective-permute-start.8 = (bf16[32,2048]{1,0:T(8,128)(2,1)S(1)}, bf16[32,2048]{1,0:T(8,128)(2,1)S(1)}, u32[]{:S(2)}, u32[]{:S(2)}) collective-permute-start(bf16[32,2048]{1,0:T(8,128)(2,1)S(1)} %collective-permute-done.5), channel_id=1, source_target_pairs={{0,4},{1,3},{2,0},{3,7},{4,8},{5,1},{6,2},{7,11},{8,12},{9,5},{10,... | collective-permute-start | bytes 393224 | tf_op jit(solution)/shard_map/ppermute | solution.py:76
  27.3 4.1 %collective-permute-start.7 = (bf16[96,4096]{1,0:T(8,128)(2,1)S(1)}, bf16[96,4096]{1,0:T(8,128)(2,1)S(1)}, u32[]{:S(2)}, u32[]{:S(2)}) collective-permute-start(bf16[96,4096]{1,0:T(8,128)(2,1)S(1)} %maximum_maximum_fusion), channel_id=1, source_target_pairs={{0,1},{1,0},{2,3},{3,2},{4,5},{5,4},{6,7},{7,6},{8,9},{9,8},{10,11... | collective-permute-start | bytes 2359304 | tf_op jit(solution)/shard_map/ppermute | solution.py:38
  30.0 1.3 collective-permute-start.9
  31.5 0.7 copy-start.7
  31.5 2.4 %copy-start.14 = (bf16[4096,256]{1,0:T(8,128)(2,1)S(1)}, bf16[4096,256]{1,0:T(8,128)(2,1)}, u32[]{:S(2)}) copy-start(bf16[4096,256]{1,0:T(8,128)(2,1)} %param.27) | copy-start | bytes 6291460
  31.6 3.0 %copy-start.1 = (bf16[256,4096]{1,0:T(8,128)(2,1)}, bf16[256,4096]{1,0:T(8,128)(2,1)S(1)}, u32[]{:S(2)}) copy-start(bf16[256,4096]{1,0:T(8,128)(2,1)S(1)} %maximum_dynamic-update-slice_fusion.4) | copy-start | bytes 6291460
  33.9 0.8 copy-start.11
  33.9 1.1 copy-start.5
  33.9 1.3 copy-start.8
  35.3 1.5 collective-permute-start.10
  35.6 22.0 %copy-start.16 = (f32[256]{0:T(256)S(1)}, f32[256]{0:T(256)}, u32[]{:S(2)}) copy-start(f32[256]{0:T(256)} %param.34) | copy-start | bytes 3076
  36.8 20.7 %copy-start.15 = (bf16[512,256]{1,0:T(8,128)(2,1)S(1)}, bf16[512,256]{1,0:T(8,128)(2,1)}, u32[]{:S(2)}) copy-start(bf16[512,256]{1,0:T(8,128)(2,1)} %param.33) | copy-start | bytes 786436
  36.9 4.6 %collective-permute-start.11 = (bf16[64,544]{1,0:T(8,128)(2,1)S(1)}, bf16[64,544]{1,0:T(8,128)(2,1)S(1)}, u32[]{:S(2)}, u32[]{:S(2)}) collective-permute-start(bf16[64,544]{1,0:T(8,128)(2,1)S(1)} %dynamic-slice_convert_fusion.9), channel_id=1, source_target_pairs={{0,2},{2,0},{4,6},{6,4},{8,10},{10,8},{12,14},{14,12},{1,3},{3,1},... | collective-permute-start | bytes 208904 | tf_op jit(solution)/shard_map/ppermute | solution.py:42
  41.5 4.5 %collective-permute-start.12 = (bf16[64,544]{1,0:T(8,128)(2,1)S(1)}, bf16[64,544]{1,0:T(8,128)(2,1)S(1)}, u32[]{:S(2)}, u32[]{:S(2)}) collective-permute-start(bf16[64,544]{1,0:T(8,128)(2,1)S(1)} %fusion.85), channel_id=1, source_target_pairs={{0,4},{2,6},{4,0},{6,2},{8,12},{10,14},{12,8},{14,10},{1,5},{3,7},... | collective-permute-start | bytes 208904 | tf_op jit(solution)/shard_map/ppermute | solution.py:42
  46.0 5.4 %collective-permute-start.13 = (bf16[64,544]{1,0:T(8,128)(2,1)S(1)}, bf16[64,544]{1,0:T(8,128)(2,1)S(1)}, u32[]{:S(2)}, u32[]{:S(2)}) collective-permute-start(bf16[64,544]{1,0:T(8,128)(2,1)S(1)} %fusion.84), channel_id=1, source_target_pairs={{0,8},{2,10},{4,12},{6,14},{8,0},{10,2},{12,4},{14,6},{1,9},{3,11}... | collective-permute-start | bytes 208904 | tf_op jit(solution)/shard_map/ppermute | solution.py:42
  51.5 4.5 %collective-permute-start.14 = (bf16[64,544]{1,0:T(8,128)(2,1)S(1)}, bf16[64,544]{1,0:T(8,128)(2,1)S(1)}, u32[]{:S(2)}, u32[]{:S(2)}) collective-permute-start(bf16[64,544]{1,0:T(8,128)(2,1)S(1)} %get-tuple-element.21), channel_id=1, source_target_pairs={{0,2},{2,0},{4,6},{6,4},{8,10},{10,8},{12,14},{14,12},{1,3},{3,1},... | collective-permute-start | bytes 208904 | tf_op jit(solution)/shard_map/ppermute | solution.py:42
  56.0 1.5 collective-permute-start.15
  57.5 1.4 copy-start.3
  57.6 1.4 copy-start.6
  58.9 3.4 %copy-start.12 = (f32[256]{0:T(256)S(1)}, f32[256]{0:T(256)}, u32[]{:S(2)}) copy-start(f32[256]{0:T(256)} %param.36) | copy-start | bytes 3076
  77.5 13.5 %copy-start.10 = (s32[32,2]{0,1:T(2,128)S(1)}, s32[32,2]{0,1:T(2,128)}, u32[]{:S(2)}) copy-start(s32[32,2]{0,1:T(2,128)} %param.23) | copy-start | bytes 772
  77.5 2.7 %collective-permute-start.16 = (bf16[256,2048]{1,0:T(8,128)(2,1)S(1)}, bf16[256,2048]{1,0:T(8,128)(2,1)S(1)}, u32[]{:S(2)}, u32[]{:S(2)}) collective-permute-start(bf16[256,2048]{1,0:T(8,128)(2,1)S(1)} %fusion.73), channel_id=1, source_target_pairs={{0,1},{1,0},{2,3},{3,2},{4,5},{5,4},{6,7},{7,6},{8,9},{9,8},{10,11... | collective-permute-start | bytes 3145736 | tf_op jit(solution)/shard_map/ppermute | solution.py:38
  80.5 6.2 %copy-start.2 = (f32[256,2048]{1,0:T(8,128)}, f32[256,2048]{1,0:T(8,128)S(1)}, u32[]{:S(2)}) copy-start(f32[256,2048]{1,0:T(8,128)S(1)} %convert_element_type.170) | copy-start | bytes 6291460
  81.6 28.5 %copy-start.4 = (bf16[32,2048]{1,0:T(8,128)(2,1)S(1)}, bf16[32,2048]{1,0:T(8,128)(2,1)}, u32[]{:S(2)}) copy-start(bf16[32,2048]{1,0:T(8,128)(2,1)} %param.22) | copy-start | bytes 393220
  81.7 5.0 %collective-permute-start.17 = (bf16[32,2048]{1,0:T(8,128)(2,1)S(1)}, bf16[32,2048]{1,0:T(8,128)(2,1)S(1)}, u32[]{:S(2)}, u32[]{:S(2)}) collective-permute-start(bf16[32,2048]{1,0:T(8,128)(2,1)S(1)} %fusion.48), channel_id=1, source_target_pairs={{0,4},{1,3},{2,0},{3,7},{4,8},{5,1},{6,2},{7,11},{8,12},{9,5},{10,... | collective-permute-start | bytes 393224 | tf_op jit(solution)/shard_map/ppermute | solution.py:138
  87.8 5.0 %collective-permute-start.18 = (bf16[32,2048]{1,0:T(8,128)(2,1)S(1)}, bf16[32,2048]{1,0:T(8,128)(2,1)S(1)}, u32[]{:S(2)}, u32[]{:S(2)}) collective-permute-start(bf16[32,2048]{1,0:T(8,128)(2,1)S(1)} %get-tuple-element.26), channel_id=1, source_target_pairs={{0,4},{1,3},{2,0},{3,7},{4,8},{5,1},{6,2},{7,11},{8,12},{9,5},{10,... | collective-permute-start | bytes 393224 | tf_op jit(solution)/shard_map/ppermute | solution.py:138
  89.4 5.0 %collective-permute-start.21 = (bf16[32,2048]{1,0:T(8,128)(2,1)S(1)}, bf16[32,2048]{1,0:T(8,128)(2,1)S(1)}, u32[]{:S(2)}, u32[]{:S(2)}) collective-permute-start(bf16[32,2048]{1,0:T(8,128)(2,1)S(1)} %get-tuple-element.27), channel_id=1, source_target_pairs={{0,4},{1,3},{2,0},{3,7},{4,8},{5,1},{6,2},{7,11},{8,12},{9,5},{10,... | collective-permute-start | bytes 393224 | tf_op jit(solution)/shard_map/ppermute | solution.py:138
  95.6 5.0 %collective-permute-start.19 = (bf16[32,2048]{1,0:T(8,128)(2,1)S(1)}, bf16[32,2048]{1,0:T(8,128)(2,1)S(1)}, u32[]{:S(2)}, u32[]{:S(2)}) collective-permute-start(bf16[32,2048]{1,0:T(8,128)(2,1)S(1)} %get-tuple-element.24), channel_id=1, source_target_pairs={{0,4},{1,3},{2,0},{3,7},{4,8},{5,1},{6,2},{7,11},{8,12},{9,5},{10,... | collective-permute-start | bytes 393224 | tf_op jit(solution)/shard_map/ppermute | solution.py:138
  97.2 5.0 %collective-permute-start.22 = (bf16[32,2048]{1,0:T(8,128)(2,1)S(1)}, bf16[32,2048]{1,0:T(8,128)(2,1)S(1)}, u32[]{:S(2)}, u32[]{:S(2)}) collective-permute-start(bf16[32,2048]{1,0:T(8,128)(2,1)S(1)} %get-tuple-element.25), channel_id=1, source_target_pairs={{0,4},{1,3},{2,0},{3,7},{4,8},{5,1},{6,2},{7,11},{8,12},{9,5},{10,... | collective-permute-start | bytes 393224 | tf_op jit(solution)/shard_map/ppermute | solution.py:138
  103.4 5.0 %collective-permute-start.23 = (bf16[32,2048]{1,0:T(8,128)(2,1)S(1)}, bf16[32,2048]{1,0:T(8,128)(2,1)S(1)}, u32[]{:S(2)}, u32[]{:S(2)}) collective-permute-start(bf16[32,2048]{1,0:T(8,128)(2,1)S(1)} %get-tuple-element.23), channel_id=1, source_target_pairs={{0,4},{1,3},{2,0},{3,7},{4,8},{5,1},{6,2},{7,11},{8,12},{9,5},{10,... | collective-permute-start | bytes 393224 | tf_op jit(solution)/shard_map/ppermute | solution.py:138
  105.0 5.1 %collective-permute-start.20 = (bf16[32,2048]{1,0:T(8,128)(2,1)S(1)}, bf16[32,2048]{1,0:T(8,128)(2,1)S(1)}, u32[]{:S(2)}, u32[]{:S(2)}) collective-permute-start(bf16[32,2048]{1,0:T(8,128)(2,1)S(1)} %get-tuple-element.22), channel_id=1, source_target_pairs={{0,4},{1,3},{2,0},{3,7},{4,8},{5,1},{6,2},{7,11},{8,12},{9,5},{10,... | collective-permute-start | bytes 393224 | tf_op jit(solution)/shard_map/ppermute | solution.py:138
  108.4 1.7 %collective-permute-start.24 = (bf16[32,2048]{1,0:T(8,128)(2,1)S(1)}, bf16[32,2048]{1,0:T(8,128)(2,1)S(1)}, u32[]{:S(2)}, u32[]{:S(2)}) collective-permute-start(bf16[32,2048]{1,0:T(8,128)(2,1)S(1)} %collective-permute-done.23), channel_id=1, source_target_pairs={{0,1},{1,0},{2,3},{3,2},{4,5},{5,4},{6,7},{7,6},{8,9},{9,8},{10,11... | collective-permute-start | bytes 393224 | tf_op jit(solution)/shard_map/ppermute | solution.py:38
  111.2 16.4 %collective-permute-start.25 = (bf16[32,2048]{1,0:T(8,128)(2,1)S(1)}, bf16[32,2048]{1,0:T(8,128)(2,1)S(1)}, u32[]{:S(2)}, u32[]{:S(2)}) collective-permute-start(bf16[32,2048]{1,0:T(8,128)(2,1)S(1)} %fusion.52), channel_id=1, source_target_pairs={{0,1},{1,0},{2,3},{3,2},{4,5},{5,4},{6,7},{7,6},{8,9},{9,8},{10,11... | collective-permute-start | bytes 393224 | tf_op jit(solution)/shard_map/ppermute | solution.py:38
  111.5 6.9 %collective-permute-start.26 = (bf16[16,2048]{1,0:T(8,128)(2,1)S(1)}, bf16[16,2048]{1,0:T(8,128)(2,1)S(1)}, u32[]{:S(2)}, u32[]{:S(2)}) collective-permute-start(bf16[16,2048]{1,0:T(8,128)(2,1)S(1)} %dynamic-slice_bitcast_fusion), channel_id=1, source_target_pairs={{0,8},{2,10},{4,12},{6,14},{8,0},{10,2},{12,4},{14,6},{1,9},{3,11}... | collective-permute-start | bytes 196616 | tf_op jit(solution)/shard_map/ppermute | solution.py:42
  118.4 5.6 %collective-permute-start.27 = (bf16[32,2048]{1,0:T(8,128)(2,1)S(1)}, bf16[32,2048]{1,0:T(8,128)(2,1)S(1)}, u32[]{:S(2)}, u32[]{:S(2)}) collective-permute-start(bf16[32,2048]{1,0:T(8,128)(2,1)S(1)} %pad_maximum_fusion.4), channel_id=1, source_target_pairs={{0,2},{2,0},{4,6},{6,4},{8,10},{10,8},{12,14},{14,12},{1,3},{3,1},... | collective-permute-start | bytes 393224 | tf_op jit(solution)/shard_map/ppermute | solution.py:42
  119.0 6.4 %collective-permute-start.28 = (bf16[32,2048]{1,0:T(8,128)(2,1)S(1)}, bf16[32,2048]{1,0:T(8,128)(2,1)S(1)}, u32[]{:S(2)}, u32[]{:S(2)}) collective-permute-start(bf16[32,2048]{1,0:T(8,128)(2,1)S(1)} %pad_maximum_fusion.4), channel_id=1, source_target_pairs={{0,4},{2,6},{4,0},{6,2},{8,12},{10,14},{12,8},{14,10},{1,5},{3,7},... | collective-permute-start | bytes 393224 | tf_op jit(solution)/shard_map/ppermute | solution.py:42
  119.0 8.5 %collective-permute-start.29 = (bf16[32,2048]{1,0:T(8,128)(2,1)S(1)}, bf16[32,2048]{1,0:T(8,128)(2,1)S(1)}, u32[]{:S(2)}, u32[]{:S(2)}) collective-permute-start(bf16[32,2048]{1,0:T(8,128)(2,1)S(1)} %pad_maximum_fusion.4), channel_id=1, source_target_pairs={{0,6},{2,4},{4,2},{6,0},{8,14},{10,12},{12,10},{14,8},{1,7},{3,5},... | collective-permute-start | bytes 393224 | tf_op jit(solution)/shard_map/ppermute | solution.py:42
  125.4 5.0 %copy-start.9 = (f32[4096]{0:T(1024)S(1)}, f32[4096]{0:T(1024)}, u32[]{:S(2)}) copy-start(f32[4096]{0:T(1024)} %param.38) | copy-start | bytes 49156
  127.5 2.0 %collective-permute-start.30 = (bf16[128,2048]{1,0:T(8,128)(2,1)S(1)}, bf16[128,2048]{1,0:T(8,128)(2,1)S(1)}, u32[]{:S(2)}, u32[]{:S(2)}) collective-permute-start(bf16[128,2048]{1,0:T(8,128)(2,1)S(1)} %constant_dynamic-update-slice_fusion), channel_id=1, source_target_pairs={{0,1},{1,0},{2,3},{3,2},{4,5},{5,4},{6,7},{7,6},{8,9},{9,8},{10,11... | collective-permute-start | bytes 1572872 | tf_op jit(solution)/shard_map/ppermute | solution.py:38
  129.9 0.5 copy-start.13
  144.9 2.0 %collective-permute-start.31 = (bf16[128,2048]{1,0:T(8,128)(2,1)S(1)}, bf16[128,2048]{1,0:T(8,128)(2,1)S(1)}, u32[]{:S(2)}, u32[]{:S(2)}) collective-permute-start(bf16[128,2048]{1,0:T(8,128)(2,1)S(1)} %dynamic-slice_convert_fusion), channel_id=1, source_target_pairs={{0,1},{1,0},{2,3},{3,2},{4,5},{5,4},{6,7},{7,6},{8,9},{9,8},{10,11... | collective-permute-start | bytes 1572872 | tf_op jit(solution)/shard_map/ppermute | solution.py:38
  148.3 5.6 %collective-permute-start.32 = (bf16[32,2048]{1,0:T(8,128)(2,1)S(1)}, bf16[32,2048]{1,0:T(8,128)(2,1)S(1)}, u32[]{:S(2)}, u32[]{:S(2)}) collective-permute-start(bf16[32,2048]{1,0:T(8,128)(2,1)S(1)} %get-tuple-element.30), channel_id=1, source_target_pairs={{0,2},{2,0},{4,6},{6,4},{8,10},{10,8},{12,14},{14,12},{1,3},{3,1},... | collective-permute-start | bytes 393224 | tf_op jit(solution)/shard_map/ppermute | solution.py:42
  149.1 6.4 %collective-permute-start.33 = (bf16[32,2048]{1,0:T(8,128)(2,1)S(1)}, bf16[32,2048]{1,0:T(8,128)(2,1)S(1)}, u32[]{:S(2)}, u32[]{:S(2)}) collective-permute-start(bf16[32,2048]{1,0:T(8,128)(2,1)S(1)} %get-tuple-element.32), channel_id=1, source_target_pairs={{0,4},{2,6},{4,0},{6,2},{8,12},{10,14},{12,8},{14,10},{1,5},{3,7},... | collective-permute-start | bytes 393224 | tf_op jit(solution)/shard_map/ppermute | solution.py:42
  149.4 8.5 %collective-permute-start.34 = (bf16[32,2048]{1,0:T(8,128)(2,1)S(1)}, bf16[32,2048]{1,0:T(8,128)(2,1)S(1)}, u32[]{:S(2)}, u32[]{:S(2)}) collective-permute-start(bf16[32,2048]{1,0:T(8,128)(2,1)S(1)} %get-tuple-element.31), channel_id=1, source_target_pairs={{0,6},{2,4},{4,2},{6,0},{8,14},{10,12},{12,10},{14,8},{1,7},{3,5},... | collective-permute-start | bytes 393224 | tf_op jit(solution)/shard_map/ppermute | solution.py:42
  158.0 5.7 %collective-permute-start.35 = (bf16[16,2048]{1,0:T(8,128)(2,1)S(1)}, bf16[16,2048]{1,0:T(8,128)(2,1)S(1)}, u32[]{:S(2)}, u32[]{:S(2)}) collective-permute-start(bf16[16,2048]{1,0:T(8,128)(2,1)S(1)} %get-tuple-element.70), channel_id=1, source_target_pairs={{0,8},{2,10},{4,12},{6,14},{8,0},{10,2},{12,4},{14,6},{1,9},{3,11}... | collective-permute-start | bytes 196616 | tf_op jit(solution)/shard_map/ppermute | solution.py:42

commit v2 on v1

--- a/solution.py
+++ b/solution.py
@@ -1,7 +1,10 @@
+import functools
+
 import jax
 import jax.numpy as jnp
-import numpy as np
 from jax import lax
+from jax.experimental import pallas as pl
+from jax.experimental.pallas import tpu as pltpu
 from jax.sharding import PartitionSpec as P
 
 EXPERTS = 2
@@ -11,27 +14,35 @@
 BF16 = jnp.bfloat16
 
 
-def ring_order(owners):
+def ring_place(index, owners):
     if owners == 8:
-        return [0, 2, 4, 6, 7, 5, 3, 1]
-    return list(range(owners))
-
-
-def ring_tables(owners):
-    order = ring_order(owners)
-    place = {dev: i for i, dev in enumerate(order)}
-    half = owners // 2
-    ahead = np.zeros((owners, 2, owners), np.int32)
-    for p in range(owners):
-        for c in range(2):
-            step = 1 if c == 0 else -1
-            for d in range(owners):
-                ahead[p, c, d] = order[(place[p] + step * d) % owners]
-    perm = []
-    for p in range(owners):
-        for c in range(2):
-            perm.append((p * 2 + c, int(ahead[p, c, 1]) * 2 + c))
-    return ahead, perm, half
+        low = index % 2
+        return index // 2 * (1 - 2 * low) + 7 * low
+    return index
+
+
+def ring_index(place, owners):
+    if owners == 8:
+        low = place // 4
+        return 2 * place * (1 - 2 * low) + 15 * low
+    return place
+
+
+def ring_perm(owners):
+    pairs = []
+    for index in range(owners):
+        for core in range(2):
+            to = ring_index((ring_place(index, owners) + 1 - 2 * core) % owners, owners)
+            pairs.append((2 * index + core, 2 * to + core))
+    return pairs
+
+
+def ring_ahead(expert, core, owners):
+    place = ring_place(expert, owners)
+    return [
+        ring_index(lax.rem(place + (1 - 2 * core) * d + owners, owners), owners)
+        for d in range(owners // 2 + 1)
+    ]
 
 
 def over_cuts(value):
@@ -68,7 +79,7 @@
     )
 
 
-def gather_tokens(x_in, owners, core, ahead, perm):
+def gather_tokens(x_in, owners, core, ahead, behind, perm):
     half = owners // 2
     rows, width = x_in.shape
 
@@ -90,11 +101,11 @@
     def put(buffer, block, index):
         return lax.dynamic_update_slice(buffer, block, (index * rows, 0))
 
-    out = put(out, mine[0], ahead[core, 0])
+    out = put(out, mine[0], ahead[0])
     for d in range(1, half):
-        out = put(out, mine[d], ahead[1 - core, d])
-        out = put(out, theirs[d - 1], ahead[core, d])
-    return put(out, far, ahead[core, half])
+        out = put(out, mine[d], behind[d])
+        out = put(out, theirs[d - 1], ahead[d])
+    return put(out, far, ahead[half])
 
 
 def sum_all(part, owners, expert, core):
@@ -125,34 +136,115 @@
     return join(keep, over_cuts(keep), core)
 
 
-def scatter_sum(term, rows, owners, core, ahead, perm):
+def project_kernel(half, rows, width, place_ref, g_ref, h_ref, wg_ref, wh_ref, near_ref, far_ref, own_ref, other_ref):
+    core = place_ref[half + 1]
+    here = pl.multiple_of(core * width, 128)
+    there = pl.multiple_of((1 - core) * width, 128)
+    picked = [pl.ds(pl.multiple_of(place_ref[d] * rows, rows), rows) for d in range(half + 1)]
+    lhs_g = jnp.concatenate([g_ref[at, :] for at in picked], axis=0)
+    lhs_h = jnp.concatenate([h_ref[at, :] for at in picked], axis=0)
+    tile = 512
+    for start in range(0, width, tile):
+        at = pl.ds(here + start, tile)
+        term = jnp.dot(lhs_g, wg_ref[:, at], preferred_element_type=F32) + jnp.dot(
+            lhs_h, wh_ref[:, at], preferred_element_type=F32
+        )
+        own_ref[:, start : start + tile] = term[:rows]
+        near_ref[:, start : start + tile] = term[rows : half * rows]
+        far_ref[:, start : start + tile] = term[half * rows :].astype(BF16)
+        at = pl.ds(there + start, tile)
+        term = jnp.dot(
+            lhs_g[rows : half * rows], wg_ref[:, at], preferred_element_type=F32
+        ) + jnp.dot(lhs_h[rows : half * rows], wh_ref[:, at], preferred_element_type=F32)
+        other_ref[:, start : start + tile] = term
+
+
+def project_blocks(gated, gated_other, out_proj, out_other, rows, half, places):
+    width = out_proj.shape[1] // 2
+    vmem = pl.BlockSpec(memory_space=pltpu.VMEM)
+    return pl.pallas_call(
+        functools.partial(project_kernel, half, rows, width),
+        out_shape=(
+            jax.ShapeDtypeStruct(((half - 1) * rows, width), F32),
+            jax.ShapeDtypeStruct((rows, width), BF16),
+            jax.ShapeDtypeStruct((rows, width), F32),
+            jax.ShapeDtypeStruct(((half - 1) * rows, width), F32),
+        ),
+        in_specs=[pl.BlockSpec(memory_space=pltpu.SMEM)] + [vmem] * 4,
+        out_specs=[vmem] * 4,
+        compiler_params=pltpu.CompilerParams(vmem_limit_bytes=40 << 20),
+        name="project",
+    )(places, gated, gated_other, out_proj, out_other)
+
+
+def scatter_sum(near, far, own, other, rows, owners, perm):
     half = owners // 2
-    width = term.shape[1] // 2
-    here = core * width
-    there = (1 - core) * width
-
-    def block(index, start, size):
-        return lax.dynamic_slice(term, (index * rows, start), (rows, size))
 
     def send(value):
         return lax.ppermute(value.astype(BF16), ("expert", "cuts"), perm)
 
-    give = jnp.concatenate(
-        [block(ahead[1 - core, d], start, width) for d in range(1, half) for start in (here, there)]
-        + [block(ahead[core, half], there, width), block(ahead[core, 0], there, width)],
-        axis=0,
-    ).astype(BF16)
-    got = over_cuts(give).astype(F32).reshape(2 * half, rows, width)
-    acc_a = block(ahead[core, half], here, width) + got[2 * half - 2]
-    acc_a = send(acc_a).astype(F32)
+    acc_a = send(far)
     acc_b = None
     for d in range(half - 1, 0, -1):
-        local_a = block(ahead[core, d], here, width) + got[2 * d - 1]
-        local_b = block(ahead[core, d], there, width) + got[2 * d - 2]
-        acc_a = send(acc_a + local_a).astype(F32)
-        acc_b = send(local_b if acc_b is None else acc_b + local_b).astype(F32)
-    cross = over_cuts(acc_b.astype(BF16)).astype(F32)
-    return block(ahead[core, 0], here, width) + got[2 * half - 1] + acc_a + cross
+        at = slice((d - 1) * rows, d * rows)
+        acc_a = send(acc_a.astype(F32) + near[at])
+        acc_b = send(other[at] if acc_b is None else acc_b.astype(F32) + other[at])
+    return own + acc_a.astype(F32) + over_cuts(acc_b).astype(F32)
+
+
+def experts_kernel(tiles, x_ref, gain_ref, wg_hbm, wu_hbm, wd_hbm, out_ref, wg, wu, wd, sems):
+    tile = wg.shape[2]
+    copies = []
+    for i in range(tiles):
+        at = pl.ds(i * tile, tile)
+        copies.append(
+            (
+                pltpu.make_async_copy(wg_hbm.at[:, at], wg.at[i], sems.at[0, i]),
+                pltpu.make_async_copy(wu_hbm.at[:, at], wu.at[i], sems.at[1, i]),
+                pltpu.make_async_copy(wd_hbm.at[at, :], wd.at[i], sems.at[2, i]),
+            )
+        )
+    for group in copies:
+        for copy in group:
+            copy.start()
+    values = x_ref[...].astype(F32)
+    scale = lax.rsqrt(jnp.mean(values * values, axis=-1, keepdims=True) + 1e-05)
+    x = (values * scale * gain_ref[...]).astype(BF16)
+    for i in range(tiles):
+        copies[i][0].wait()
+        gate = jnp.dot(x, wg[i], preferred_element_type=F32)
+        copies[i][1].wait()
+        upval = jnp.dot(x, wu[i], preferred_element_type=F32)
+        act = (gate * jax.nn.sigmoid(gate) * upval).astype(BF16)
+        copies[i][2].wait()
+        term = jnp.dot(act, wd[i], preferred_element_type=F32)
+        if i == 0:
+            out_ref[...] = term
+        else:
+            out_ref[...] += term
+
+
+def run_experts(tokens, gain, w_gate, w_up, w_down):
+    count, width = tokens.shape
+    hidden = w_gate.shape[1]
+    tile = 256
+    tiles = hidden // tile
+    vmem = pl.BlockSpec(memory_space=pltpu.VMEM)
+    hbm = pl.BlockSpec(memory_space=pltpu.HBM)
+    return pl.pallas_call(
+        functools.partial(experts_kernel, tiles),
+        out_shape=jax.ShapeDtypeStruct((count, width), F32),
+        in_specs=[vmem, vmem, hbm, hbm, hbm],
+        out_specs=vmem,
+        scratch_shapes=[
+            pltpu.VMEM((tiles, width, tile), BF16),
+            pltpu.VMEM((tiles, width, tile), BF16),
+            pltpu.VMEM((tiles, tile, width), BF16),
+            pltpu.SemaphoreType.DMA((3, tiles)),
+        ],
+        compiler_params=pltpu.CompilerParams(vmem_limit_bytes=48 << 20),
+        name="experts",
+    )(tokens, gain.reshape(1, width), w_gate, w_up, w_down)
 
 
 def on_device(
@@ -186,9 +278,12 @@
     owners = lax.axis_size("expert")
     expert = lax.axis_index("expert")
     core = lax.axis_index("cuts")
-    table, perm, half = ring_tables(owners)
-    ahead = lax.dynamic_index_in_dim(jnp.asarray(table), expert, 0, keepdims=False)
-    full_x = gather_tokens(x_in, owners, core, ahead, perm)
+    half = owners // 2
+    perm = ring_perm(owners)
+    ahead = ring_ahead(expert, core, owners)
+    behind = ring_ahead(expert, 1 - core, owners)
+    out_other = over_cuts(out_proj)
+    full_x = gather_tokens(x_in, owners, core, ahead, behind, perm)
     normed = rms_norm(full_x, mamba_gain)
     u_pre = jnp.dot(normed, in_x, preferred_element_type=F32)
     z_gate = jnp.dot(normed, in_z, preferred_element_type=F32)
@@ -222,8 +317,16 @@
         d_skip,
     )
     gated = (outputs.reshape(requests * DRAFT, channels) * jax.nn.silu(z_gate)).astype(BF16)
-    term = jnp.dot(gated, out_proj, preferred_element_type=F32)
-    mixed_half = scatter_sum(term, tok_count, owners, core, ahead, perm)
+    near, far, own_term, other = project_blocks(
+        gated,
+        over_cuts(gated),
+        out_proj,
+        out_other,
+        tok_count,
+        half,
+        jnp.stack(ahead + [core]).astype(jnp.int32),
+    )
+    mixed_half = scatter_sum(near, far, own_term, other, tok_count, owners, perm)
     stream_half = (x_in.astype(F32) + mixed_half).astype(BF16)
 
     labels = jnp.arange(EXPERTS, dtype=jnp.int32)
@@ -249,11 +352,7 @@
     pieces = [pair] + [exchange(pair, flip) for flip in range(1, holders)]
     tokens_half = jnp.concatenate(pieces, axis=0)
     tokens = halves(tokens_half, over_cuts(tokens_half), core)
-    normed2 = rms_norm(tokens, moe_gain)
-    gate = jnp.dot(normed2, w_gate, preferred_element_type=F32)
-    upval = jnp.dot(normed2, w_up, preferred_element_type=F32)
-    act = (jax.nn.silu(gate) * upval).astype(BF16)
-    partial_out = jnp.dot(act, w_down, preferred_element_type=F32)
+    partial_out = run_experts(tokens, moe_gain, w_gate, w_up, w_down)
     count = partial_out.shape[0]
     mine = lax.dynamic_slice(partial_out, (0, core * half_width), (count, half_width))
     theirs = lax.dynamic_slice(partial_out, (0, (1 - core) * half_width), (count, half_width))

time: 165 us -> 127 us (0.77)
  matrix products: 23.6 us -> 6.77 us
  local copies, waits for them, and re-layouts: 16.2 us -> 3.53 us
  Pallas kernels: 0 us -> 9.93 us
  waiting for transfers between devices: 63.9 us -> 54.9 us
  other arithmetic: 14.7 us -> 7.41 us
  between operations: 6.35 us -> 1.44 us
  starting transfers between devices: 39.8 us -> 42.7 us
    dot_general x3 -> x1, matrix products: 19.8 us -> 3.15 us  [on_device(): z_gate = jnp.dot(normed, in_z, preferred_element_type=F32)]
    pallas_call x0 -> x2, Pallas kernels: none -> 9.93 us  [the longest x1 7.43 us: run_experts(): pl.pallas_call(functools.partial(experts_kernel, tiles), out_shape=jax.Sh...]
    unnamed x54 -> x45, local copies, waits for them, and re-layouts: 10.2 us -> 1.22 us
    ppermute x7, waiting for transfers between devices: 13.7 us -> 8.66 us  [send(): return lax.ppermute(value.astype(BF16), ('expert', 'cuts'), perm)]
    convert_element_type x4 -> x5, other arithmetic: 4.78 us -> 0.13 us  [send(): return lax.ppermute(value.astype(BF16), ('expert', 'cuts'), perm)]
    ppermute x12, waiting for transfers between devices: 34.7 us -> 31.5 us  [over_expert(): return lax.ppermute(value, 'expert', [(i, i ^ flip) for i in range(owners)])]
    ppermute x12, starting transfers between devices: 15.4 us -> 17.7 us  [over_expert(): return lax.ppermute(value, 'expert', [(i, i ^ flip) for i in range(owners)])]
    ppermute x10 -> x11, waiting for transfers between devices: 8.62 us -> 7.9 us  [over_cuts(): return lax.ppermute(value, 'cuts', [(0, 1), (1, 0)])]
  transfers between devices with their start and end apart: 36 -> 37, of which waited for: 31 -> 30; matrix products, arithmetic and copies ran while one was open for 4% -> 11% of each run, Pallas kernels for 0% -> 0%
where the time goes in v2:
time: 127 us
  waiting for transfers between devices  54.9 us (43%)
  starting transfers between devices  42.7 us (34%)
  Pallas kernels  9.93 us (8%)
  other arithmetic  7.41 us (6%)
  matrix products  6.77 us (5%)
  local copies, waits for them, and re-layouts  3.53 us (3%)
  between operations  1.44 us (1%)
    ppermute x12, waiting for transfers between devices, over_expert(): return lax.ppermute(value, 'expert', [(i, i ^ flip) for i in range(owners)])  31.5 us
    ppermute x12, starting transfers between devices, over_expert(): return lax.ppermute(value, 'expert', [(i, i ^ flip) for i in range(owners)])  17.7 us
    ppermute x7, starting transfers between devices, send(): return lax.ppermute(value, ('expert', 'cuts'), perm)  12.2 us
    ppermute x7, starting transfers between devices, send(): return lax.ppermute(value.astype(BF16), ('expert', 'cuts'), perm)  11.4 us
    ppermute x7, waiting for transfers between devices, send(): return lax.ppermute(value.astype(BF16), ('expert', 'cuts'), perm)  8.66 us
    ppermute x11, waiting for transfers between devices, over_cuts(): return lax.ppermute(value, 'cuts', [(0, 1), (1, 0)])  7.9 us
    pallas_call x1, Pallas kernels, run_experts(): pl.pallas_call(functools.partial(experts_kernel, tiles), out_shape=jax.Sh...  7.43 us
    ppermute x7, waiting for transfers between devices, send(): return lax.ppermute(value, ('expert', 'cuts'), perm)  6.8 us
  transfers between devices with their start and end apart: 37, of which 30 were waited for; matrix products, arithmetic and copies ran while one was open for 11% of the time, Pallas kernels for 0%

profile of v2, /device:TPU:0, one launch (start us, length us, event | category | flops | bytes accessed | tf_op | source)
XLA Modules:
  0.0 126.7 jit_solution(12210198898036069441)
XLA Ops:
  0.6 0.5 collective-permute-start
  1.2 2.6 %collective-permute-start.1 = (bf16[32,2048]{1,0:T(8,128)(2,1)}, bf16[32,2048]{1,0:T(8,128)(2,1)S(1)}, u32[]{:S(2)}, u32[]{:S(2)}) collective-permute-start(bf16[32,2048]{1,0:T(8,128)(2,1)} %param.21), channel_id=1, source_target_pairs={{0,4},{1,3},{2,0},{3,7},{4,8},{5,1},{6,2},{7,11},{8,12},{9,5},{10,... | collective-permute-start | bytes 393224 | tf_op jit(solution)/shard_map/ppermute | solution.py:87
  3.8 1.0 copy.33
  4.8 0.8 fusion.60
  5.7 1.6 %collective-permute-start.2 = (bf16[32,2048]{1,0:T(8,128)(2,1)S(1)}, bf16[32,2048]{1,0:T(8,128)(2,1)S(1)}, u32[]{:S(2)}, u32[]{:S(2)}) collective-permute-start(bf16[32,2048]{1,0:T(8,128)(2,1)S(1)} %collective-permute-done), channel_id=1, source_target_pairs={{0,4},{1,3},{2,0},{3,7},{4,8},{5,1},{6,2},{7,11},{8,12},{9,5},{10,... | collective-permute-start | bytes 393224 | tf_op jit(solution)/shard_map/ppermute | solution.py:87
  7.3 0.9 broadcast_select_fusion.13
  8.5 1.6 %collective-permute-start.3 = (bf16[32,2048]{1,0:T(8,128)(2,1)S(1)}, bf16[32,2048]{1,0:T(8,128)(2,1)S(1)}, u32[]{:S(2)}, u32[]{:S(2)}) collective-permute-start(bf16[32,2048]{1,0:T(8,128)(2,1)S(1)} %collective-permute-done.1), channel_id=1, source_target_pairs={{0,4},{1,3},{2,0},{3,7},{4,8},{5,1},{6,2},{7,11},{8,12},{9,5},{10,... | collective-permute-start | bytes 393224 | tf_op jit(solution)/shard_map/ppermute | solution.py:87
  10.1 0.6 collective-permute-done.2
  10.7 1.6 %collective-permute-start.4 = (bf16[32,2048]{1,0:T(8,128)(2,1)S(1)}, bf16[32,2048]{1,0:T(8,128)(2,1)S(1)}, u32[]{:S(2)}, u32[]{:S(2)}) collective-permute-start(bf16[32,2048]{1,0:T(8,128)(2,1)S(1)} %collective-permute-done.2), channel_id=1, source_target_pairs={{0,4},{1,3},{2,0},{3,7},{4,8},{5,1},{6,2},{7,11},{8,12},{9,5},{10,... | collective-permute-start | bytes 393224 | tf_op jit(solution)/shard_map/ppermute | solution.py:87
  12.3 1.2 collective-permute-done.3
  13.5 1.6 %collective-permute-start.5 = (bf16[32,2048]{1,0:T(8,128)(2,1)S(1)}, bf16[32,2048]{1,0:T(8,128)(2,1)S(1)}, u32[]{:S(2)}, u32[]{:S(2)}) collective-permute-start(bf16[32,2048]{1,0:T(8,128)(2,1)S(1)} %collective-permute-done.3), channel_id=1, source_target_pairs={{0,4},{1,3},{2,0},{3,7},{4,8},{5,1},{6,2},{7,11},{8,12},{9,5},{10,... | collective-permute-start | bytes 393224 | tf_op jit(solution)/shard_map/ppermute | solution.py:87
  15.1 0.6 collective-permute-done.4
  15.7 1.6 %collective-permute-start.6 = (bf16[32,2048]{1,0:T(8,128)(2,1)S(1)}, bf16[32,2048]{1,0:T(8,128)(2,1)S(1)}, u32[]{:S(2)}, u32[]{:S(2)}) collective-permute-start(bf16[32,2048]{1,0:T(8,128)(2,1)S(1)} %collective-permute-done.4), channel_id=1, source_target_pairs={{0,4},{1,3},{2,0},{3,7},{4,8},{5,1},{6,2},{7,11},{8,12},{9,5},{10,... | collective-permute-start | bytes 393224 | tf_op jit(solution)/shard_map/ppermute | solution.py:87
  17.3 1.2 collective-permute-done.5
  18.5 1.6 %collective-permute-start.8 = (bf16[32,2048]{1,0:T(8,128)(2,1)S(1)}, bf16[32,2048]{1,0:T(8,128)(2,1)S(1)}, u32[]{:S(2)}, u32[]{:S(2)}) collective-permute-start(bf16[32,2048]{1,0:T(8,128)(2,1)S(1)} %collective-permute-done.5), channel_id=1, source_target_pairs={{0,4},{1,3},{2,0},{3,7},{4,8},{5,1},{6,2},{7,11},{8,12},{9,5},{10,... | collective-permute-start | bytes 393224 | tf_op jit(solution)/shard_map/ppermute | solution.py:87
  20.1 0.6 collective-permute-done.6
  20.8 2.7 %collective-permute-done.8 = bf16[32,2048]{1,0:T(8,128)(2,1)S(1)} collective-permute-done((bf16[32,2048]{1,0:T(8,128)(2,1)S(1)}, bf16[32,2048]{1,0:T(8,128)(2,1)S(1)}, u32[]{:S(2)}, u32[]{:S(2)}) %collective-permute-start.8) | collective-permute-done | bytes 131104 | tf_op jit(solution)/shard_map/ppermute | solution.py:87
  23.5 1.3 %collective-permute-done.9 = bf16[32,2048]{1,0:T(8,128)(2,1)S(1)} collective-permute-done((bf16[32,2048]{1,0:T(8,128)(2,1)S(1)}, bf16[32,2048]{1,0:T(8,128)(2,1)S(1)}, u32[]{:S(2)}, u32[]{:S(2)}) %collective-permute-start.9) | collective-permute-done | bytes 131104 | tf_op jit(solution)/shard_map/ppermute | solution.py:49
  25.6 0.8 convolution_bitcast_fusion
  27.4 1.2 collective-permute-done.10
  28.7 0.5 collective-permute-start.11
  29.2 4.0 %collective-permute-done.11 = bf16[64,544]{1,0:T(8,128)(2,1)S(1)} collective-permute-done((bf16[64,544]{1,0:T(8,128)(2,1)S(1)}, bf16[64,544]{1,0:T(8,128)(2,1)S(1)}, u32[]{:S(2)}, u32[]{:S(2)}) %collective-permute-start.11) | collective-permute-done | bytes 69664 | tf_op jit(solution)/shard_map/ppermute | solution.py:53
  33.3 1.6 %collective-permute-start.12 = (bf16[64,544]{1,0:T(8,128)(2,1)S(1)}, bf16[64,544]{1,0:T(8,128)(2,1)S(1)}, u32[]{:S(2)}, u32[]{:S(2)}) collective-permute-start(bf16[64,544]{1,0:T(8,128)(2,1)S(1)} %fusion.46), channel_id=1, source_target_pairs={{0,4},{2,6},{4,0},{6,2},{8,12},{10,14},{12,8},{14,10},{1,5},{3,7},... | collective-permute-start | bytes 208904 | tf_op jit(solution)/shard_map/ppermute | solution.py:53
  35.0 2.9 %collective-permute-done.12 = bf16[64,544]{1,0:T(8,128)(2,1)S(1)} collective-permute-done((bf16[64,544]{1,0:T(8,128)(2,1)S(1)}, bf16[64,544]{1,0:T(8,128)(2,1)S(1)}, u32[]{:S(2)}, u32[]{:S(2)}) %collective-permute-start.12) | collective-permute-done | bytes 69664 | tf_op jit(solution)/shard_map/ppermute | solution.py:53
  37.8 2.6 %collective-permute-start.13 = (bf16[64,544]{1,0:T(8,128)(2,1)S(1)}, bf16[64,544]{1,0:T(8,128)(2,1)S(1)}, u32[]{:S(2)}, u32[]{:S(2)}) collective-permute-start(bf16[64,544]{1,0:T(8,128)(2,1)S(1)} %fusion.45), channel_id=1, source_target_pairs={{0,8},{2,10},{4,12},{6,14},{8,0},{10,2},{12,4},{14,6},{1,9},{3,11}... | collective-permute-start | bytes 208904 | tf_op jit(solution)/shard_map/ppermute | solution.py:53
  40.4 2.8 %collective-permute-done.13 = bf16[64,544]{1,0:T(8,128)(2,1)S(1)} collective-permute-done((bf16[64,544]{1,0:T(8,128)(2,1)S(1)}, bf16[64,544]{1,0:T(8,128)(2,1)S(1)}, u32[]{:S(2)}, u32[]{:S(2)}) %collective-permute-start.13) | collective-permute-done | bytes 69664 | tf_op jit(solution)/shard_map/ppermute | solution.py:53
  43.9 4.0 %collective-permute-done.14 = bf16[64,544]{1,0:T(8,128)(2,1)S(1)} collective-permute-done((bf16[64,544]{1,0:T(8,128)(2,1)S(1)}, bf16[64,544]{1,0:T(8,128)(2,1)S(1)}, u32[]{:S(2)}, u32[]{:S(2)}) %collective-permute-start.14) | collective-permute-done | bytes 69664 | tf_op jit(solution)/shard_map/ppermute | solution.py:53
  48.2 1.1 collective-permute-done.15
  49.4 1.1 fusion.23
  51.5 0.7 multiply_reduce_fusion.5
  52.2 1.8 %multiply_reduce_fusion = (f32[32,256]{1,0:T(8,128)S(1)}, f32[32,16,256]{2,1,0:T(8,128)}, f32[32,16,256]{2,1,0:T(8,128)S(1)}) fusion(f32[32,16]{1,0:T(8,128)S(1)} %bitcast.120, f32[32,16]{1,0:T(8,128)S(1)} %bitcast.121, f32[32,256]{1,0:T(8,128)S(1)} %get-tuple-element.103, f32[32,16]{1,0:T(8,128)S(1)} %bitcast.108, f32[32,256]{1,0:T(8,128)S(1)} %get-tuple-element.105, ...), kind=kLoop, calls=%fused_computation.28 | loop fusion | flops 4448256 | bytes 2164736 | tf_op jit(solution)/shard_map/reduce_sum | solution.py:71
  54.1 0.9 multiply_reduce_fusion.1
  55.7 3.1 %fusion.29.g_ref = bf16[256,256]{1,0:T(8,128)(2,1)S(1)} fusion(f32[32,8,256]{2,1,0:T(8,128)S(1)} %stack.44, bf16[4096,256]{1,0:T(8,128)(2,1)} %param.27, bf16[256,4096]{1,0:T(8,128)(2,1)} %copy-done.3, f32[4096]{0:T(1024)S(1)} %copy-done.15, f32[256]{0:T(256)S(1)} %add_rsqrt_fusion), kind=kOutput, calls=%fused_computation.78 | convolution fusion | flops 541458432 | bytes 4604928 | tf_op jit(solution)/shard_map/dot_general | solution.py:289
  59.2 1.1 collective-permute-done.16.h_ref
  60.3 2.5 %project.1 = (f32[96,2048]{1,0:T(8,128)S(1)}, bf16[32,2048]{1,0:T(8,128)(2,1)S(1)}, f32[32,2048]{1,0:T(8,128)S(1)}, f32[96,2048]{1,0:T(8,128)S(1)}) custom-call(s32[6]{0:T(128)S(1)} %stack.43.place_ref, bf16[256,256]{1,0:T(8,128)(2,1)S(1)} %fusion.29.g_ref, bf16[256,256]{1,0:T(8,128)(2,1)S(1)} %collective-permute-done.16.h_ref, ...), custom_call_target="tpu_custom_call" | custom-call | tf_op jit(solution)/shard_map/project/pallas_call | solution.py:165
  62.8 1.6 %collective-permute-start.18 = (bf16[32,2048]{1,0:T(8,128)(2,1)S(1)}, bf16[32,2048]{1,0:T(8,128)(2,1)S(1)}, u32[]{:S(2)}, u32[]{:S(2)}) collective-permute-start(bf16[32,2048]{1,0:T(8,128)(2,1)S(1)} %get-tuple-element.7), channel_id=1, source_target_pairs={{0,4},{1,3},{2,0},{3,7},{4,8},{5,1},{6,2},{7,11},{8,12},{9,5},{10,... | collective-permute-start | bytes 393224 | tf_op jit(solution)/shard_map/ppermute | solution.py:184
  64.5 1.6 %collective-permute-start.22 = (bf16[32,2048]{1,0:T(8,128)(2,1)S(1)}, bf16[32,2048]{1,0:T(8,128)(2,1)S(1)}, u32[]{:S(2)}, u32[]{:S(2)}) collective-permute-start(bf16[32,2048]{1,0:T(8,128)(2,1)S(1)} %slice.408), channel_id=1, source_target_pairs={{0,4},{1,3},{2,0},{3,7},{4,8},{5,1},{6,2},{7,11},{8,12},{9,5},{10,... | collective-permute-start | bytes 393224 | tf_op jit(solution)/shard_map/ppermute | solution.py:184
  66.1 1.7 %collective-permute-done.18 = bf16[32,2048]{1,0:T(8,128)(2,1)S(1)} collective-permute-done((bf16[32,2048]{1,0:T(8,128)(2,1)S(1)}, bf16[32,2048]{1,0:T(8,128)(2,1)S(1)}, u32[]{:S(2)}, u32[]{:S(2)}) %collective-permute-start.18) | collective-permute-done | bytes 131104 | tf_op jit(solution)/shard_map/ppermute | solution.py:184
  67.9 1.6 %collective-permute-start.19 = (bf16[32,2048]{1,0:T(8,128)(2,1)S(1)}, bf16[32,2048]{1,0:T(8,128)(2,1)S(1)}, u32[]{:S(2)}, u32[]{:S(2)}) collective-permute-start(bf16[32,2048]{1,0:T(8,128)(2,1)S(1)} %add_convert_fusion.6), channel_id=1, source_target_pairs={{0,4},{1,3},{2,0},{3,7},{4,8},{5,1},{6,2},{7,11},{8,12},{9,5},{10,... | collective-permute-start | bytes 393224 | tf_op jit(solution)/shard_map/ppermute | solution.py:184
  69.6 1.6 %collective-permute-start.23 = (bf16[32,2048]{1,0:T(8,128)(2,1)S(1)}, bf16[32,2048]{1,0:T(8,128)(2,1)S(1)}, u32[]{:S(2)}, u32[]{:S(2)}) collective-permute-start(bf16[32,2048]{1,0:T(8,128)(2,1)S(1)} %add_convert_fusion.3), channel_id=1, source_target_pairs={{0,4},{1,3},{2,0},{3,7},{4,8},{5,1},{6,2},{7,11},{8,12},{9,5},{10,... | collective-permute-start | bytes 393224 | tf_op jit(solution)/shard_map/ppermute | solution.py:184
  71.2 1.7 %collective-permute-done.19 = bf16[32,2048]{1,0:T(8,128)(2,1)S(1)} collective-permute-done((bf16[32,2048]{1,0:T(8,128)(2,1)S(1)}, bf16[32,2048]{1,0:T(8,128)(2,1)S(1)}, u32[]{:S(2)}, u32[]{:S(2)}) %collective-permute-start.19) | collective-permute-done | bytes 131104 | tf_op jit(solution)/shard_map/ppermute | solution.py:184
  72.9 1.6 %collective-permute-start.20 = (bf16[32,2048]{1,0:T(8,128)(2,1)S(1)}, bf16[32,2048]{1,0:T(8,128)(2,1)S(1)}, u32[]{:S(2)}, u32[]{:S(2)}) collective-permute-start(bf16[32,2048]{1,0:T(8,128)(2,1)S(1)} %add_convert_fusion.5), channel_id=1, source_target_pairs={{0,4},{1,3},{2,0},{3,7},{4,8},{5,1},{6,2},{7,11},{8,12},{9,5},{10,... | collective-permute-start | bytes 393224 | tf_op jit(solution)/shard_map/ppermute | solution.py:184
  74.6 1.6 %collective-permute-start.24 = (bf16[32,2048]{1,0:T(8,128)(2,1)S(1)}, bf16[32,2048]{1,0:T(8,128)(2,1)S(1)}, u32[]{:S(2)}, u32[]{:S(2)}) collective-permute-start(bf16[32,2048]{1,0:T(8,128)(2,1)S(1)} %add_convert_fusion.2), channel_id=1, source_target_pairs={{0,4},{1,3},{2,0},{3,7},{4,8},{5,1},{6,2},{7,11},{8,12},{9,5},{10,... | collective-permute-start | bytes 393224 | tf_op jit(solution)/shard_map/ppermute | solution.py:184
  76.2 1.7 %collective-permute-done.20 = bf16[32,2048]{1,0:T(8,128)(2,1)S(1)} collective-permute-done((bf16[32,2048]{1,0:T(8,128)(2,1)S(1)}, bf16[32,2048]{1,0:T(8,128)(2,1)S(1)}, u32[]{:S(2)}, u32[]{:S(2)}) %collective-permute-start.20) | collective-permute-done | bytes 131104 | tf_op jit(solution)/shard_map/ppermute | solution.py:184
  78.0 1.8 %collective-permute-start.21 = (bf16[32,2048]{1,0:T(8,128)(2,1)S(1)}, bf16[32,2048]{1,0:T(8,128)(2,1)S(1)}, u32[]{:S(2)}, u32[]{:S(2)}) collective-permute-start(bf16[32,2048]{1,0:T(8,128)(2,1)S(1)} %add_convert_fusion.4), channel_id=1, source_target_pairs={{0,4},{1,3},{2,0},{3,7},{4,8},{5,1},{6,2},{7,11},{8,12},{9,5},{10,... | collective-permute-start | bytes 393224 | tf_op jit(solution)/shard_map/ppermute | solution.py:184
  79.8 3.4 %collective-permute-done.21 = bf16[32,2048]{1,0:T(8,128)(2,1)S(1)} collective-permute-done((bf16[32,2048]{1,0:T(8,128)(2,1)S(1)}, bf16[32,2048]{1,0:T(8,128)(2,1)S(1)}, u32[]{:S(2)}, u32[]{:S(2)}) %collective-permute-start.21) | collective-permute-done | bytes 131104 | tf_op jit(solution)/shard_map/ppermute | solution.py:184
  83.5 2.6 %collective-permute-start.27 = (bf16[16,2048]{1,0:T(8,128)(2,1)S(1)}, bf16[16,2048]{1,0:T(8,128)(2,1)S(1)}, u32[]{:S(2)}, u32[]{:S(2)}) collective-permute-start(bf16[16,2048]{1,0:T(8,128)(2,1)S(1)} %dynamic-slice_bitcast_fusion), channel_id=1, source_target_pairs={{0,8},{2,10},{4,12},{6,14},{8,0},{10,2},{12,4},{14,6},{1,9},{3,11}... | collective-permute-start | bytes 196616 | tf_op jit(solution)/shard_map/ppermute | solution.py:53
  86.1 4.2 %collective-permute-done.27 = bf16[16,2048]{1,0:T(8,128)(2,1)S(1)} collective-permute-done((bf16[16,2048]{1,0:T(8,128)(2,1)S(1)}, bf16[16,2048]{1,0:T(8,128)(2,1)S(1)}, u32[]{:S(2)}, u32[]{:S(2)}) %collective-permute-start.27) | collective-permute-done | bytes 65568 | tf_op jit(solution)/shard_map/ppermute | solution.py:53
  90.5 1.4 %collective-permute-start.29 = (bf16[32,2048]{1,0:T(8,128)(2,1)S(1)}, bf16[32,2048]{1,0:T(8,128)(2,1)S(1)}, u32[]{:S(2)}, u32[]{:S(2)}) collective-permute-start(bf16[32,2048]{1,0:T(8,128)(2,1)S(1)} %pad_maximum_fusion.4), channel_id=1, source_target_pairs={{0,4},{2,6},{4,0},{6,2},{8,12},{10,14},{12,8},{14,10},{1,5},{3,7},... | collective-permute-start | bytes 393224 | tf_op jit(solution)/shard_map/ppermute | solution.py:53
  91.9 2.1 %collective-permute-start.30 = (bf16[32,2048]{1,0:T(8,128)(2,1)S(1)}, bf16[32,2048]{1,0:T(8,128)(2,1)S(1)}, u32[]{:S(2)}, u32[]{:S(2)}) collective-permute-start(bf16[32,2048]{1,0:T(8,128)(2,1)S(1)} %pad_maximum_fusion.4), channel_id=1, source_target_pairs={{0,6},{2,4},{4,2},{6,0},{8,14},{10,12},{12,10},{14,8},{1,7},{3,5},... | collective-permute-start | bytes 393224 | tf_op jit(solution)/shard_map/ppermute | solution.py:53
  93.9 2.6 %collective-permute-done.28 = bf16[32,2048]{1,0:T(8,128)(2,1)S(1)} collective-permute-done((bf16[32,2048]{1,0:T(8,128)(2,1)S(1)}, bf16[32,2048]{1,0:T(8,128)(2,1)S(1)}, u32[]{:S(2)}, u32[]{:S(2)}) %collective-permute-start.28) | collective-permute-done | bytes 131104 | tf_op jit(solution)/shard_map/ppermute | solution.py:53
  96.8 2.2 %collective-permute-done.30 = bf16[32,2048]{1,0:T(8,128)(2,1)S(1)} collective-permute-done((bf16[32,2048]{1,0:T(8,128)(2,1)S(1)}, bf16[32,2048]{1,0:T(8,128)(2,1)S(1)}, u32[]{:S(2)}, u32[]{:S(2)}) %collective-permute-start.30) | collective-permute-done | bytes 131104 | tf_op jit(solution)/shard_map/ppermute | solution.py:53
  99.4 1.7 %collective-permute-done.31 = bf16[128,2048]{1,0:T(8,128)(2,1)S(1)} collective-permute-done((bf16[128,2048]{1,0:T(8,128)(2,1)S(1)}, bf16[128,2048]{1,0:T(8,128)(2,1)S(1)}, u32[]{:S(2)}, u32[]{:S(2)}) %collective-permute-start.31) | collective-permute-done | bytes 524320 | tf_op jit(solution)/shard_map/ppermute | solution.py:49
  101.2 7.4 %experts.1 = f32[128,4096]{1,0:T(8,128)S(1)} custom-call(bf16[128,4096]{1,0:T(8,128)(2,1)S(1)} %pad_maximum_fusion.x_ref, f32[1,4096]{1,0:T(1,128)S(1)} %bitcast.101, bf16[4096,768]{1,0:T(8,128)(2,1)} %wg_hbm.1, bf16[4096,768]{1,0:T(8,128)(2,1)} %wu_hbm.1, bf16[768,4096]{1,0:T(8,128)(2,1)} %wd_hbm.1), custom_call_target="tpu_custom_call" | custom-call | tf_op jit(solution)/shard_map/experts/pallas_call | solution.py:234
  109.2 1.5 %collective-permute-done.32 = bf16[128,2048]{1,0:T(8,128)(2,1)S(1)} collective-permute-done((bf16[128,2048]{1,0:T(8,128)(2,1)S(1)}, bf16[128,2048]{1,0:T(8,128)(2,1)S(1)}, u32[]{:S(2)}, u32[]{:S(2)}) %collective-permute-start.32) | collective-permute-done | bytes 524320 | tf_op jit(solution)/shard_map/ppermute | solution.py:49
  110.9 0.7 collective-permute-start.33
  111.6 1.6 %collective-permute-start.34 = (bf16[32,2048]{1,0:T(8,128)(2,1)S(1)}, bf16[32,2048]{1,0:T(8,128)(2,1)S(1)}, u32[]{:S(2)}, u32[]{:S(2)}) collective-permute-start(bf16[32,2048]{1,0:T(8,128)(2,1)S(1)} %get-tuple-element.34), channel_id=1, source_target_pairs={{0,4},{2,6},{4,0},{6,2},{8,12},{10,14},{12,8},{14,10},{1,5},{3,7},... | collective-permute-start | bytes 393224 | tf_op jit(solution)/shard_map/ppermute | solution.py:53
  113.2 1.2 collective-permute-start.35
  114.5 2.0 %collective-permute-done.33 = bf16[32,2048]{1,0:T(8,128)(2,1)S(1)} collective-permute-done((bf16[32,2048]{1,0:T(8,128)(2,1)S(1)}, bf16[32,2048]{1,0:T(8,128)(2,1)S(1)}, u32[]{:S(2)}, u32[]{:S(2)}) %collective-permute-start.33) | collective-permute-done | bytes 131104 | tf_op jit(solution)/shard_map/ppermute | solution.py:53
  116.5 1.5 %collective-permute-done.34 = bf16[32,2048]{1,0:T(8,128)(2,1)S(1)} collective-permute-done((bf16[32,2048]{1,0:T(8,128)(2,1)S(1)}, bf16[32,2048]{1,0:T(8,128)(2,1)S(1)}, u32[]{:S(2)}, u32[]{:S(2)}) %collective-permute-start.34) | collective-permute-done | bytes 131104 | tf_op jit(solution)/shard_map/ppermute | solution.py:53
  118.0 2.5 %collective-permute-done.35 = bf16[32,2048]{1,0:T(8,128)(2,1)S(1)} collective-permute-done((bf16[32,2048]{1,0:T(8,128)(2,1)S(1)}, bf16[32,2048]{1,0:T(8,128)(2,1)S(1)}, u32[]{:S(2)}, u32[]{:S(2)}) %collective-permute-start.35) | collective-permute-done | bytes 131104 | tf_op jit(solution)/shard_map/ppermute | solution.py:53
  120.6 2.7 %collective-permute-start.36 = (bf16[16,2048]{1,0:T(8,128)(2,1)S(1)}, bf16[16,2048]{1,0:T(8,128)(2,1)S(1)}, u32[]{:S(2)}, u32[]{:S(2)}) collective-permute-start(bf16[16,2048]{1,0:T(8,128)(2,1)S(1)} %get-tuple-element.72), channel_id=1, source_target_pairs={{0,8},{2,10},{4,12},{6,14},{8,0},{10,2},{12,4},{14,6},{1,9},{3,11}... | collective-permute-start | bytes 196616 | tf_op jit(solution)/shard_map/ppermute | solution.py:53
  123.4 2.5 %collective-permute-done.36 = bf16[16,2048]{1,0:T(8,128)(2,1)S(1)} collective-permute-done((bf16[16,2048]{1,0:T(8,128)(2,1)S(1)}, bf16[16,2048]{1,0:T(8,128)(2,1)S(1)}, u32[]{:S(2)}, u32[]{:S(2)}) %collective-permute-start.36) | collective-permute-done | bytes 65568 | tf_op jit(solution)/shard_map/ppermute | solution.py:53
  125.8 0.9 add_convert_fusion
  (137 shorter events, 7.6 us)
Async XLA Ops:
  0.6 24.9 %copy-start = (bf16[4096,256]{1,0:T(8,128)(2,1)S(1)}, bf16[4096,256]{1,0:T(8,128)(2,1)}, u32[]{:S(2)}) copy-start(bf16[4096,256]{1,0:T(8,128)(2,1)} %param.26) | copy-start | bytes 6291460
  0.6 5.0 %collective-permute-start = (bf16[32,2048]{1,0:T(8,128)(2,1)}, bf16[32,2048]{1,0:T(8,128)(2,1)S(1)}, u32[]{:S(2)}, u32[]{:S(2)}) collective-permute-start(bf16[32,2048]{1,0:T(8,128)(2,1)} %param.21), channel_id=1, source_target_pairs={{0,1},{1,0},{2,3},{3,2},{4,5},{5,4},{6,7},{7,6},{8,9},{9,8},{10,11... | collective-permute-start | bytes 393224 | tf_op jit(solution)/shard_map/ppermute | solution.py:49
  1.2 7.3 %collective-permute-start.1 = (bf16[32,2048]{1,0:T(8,128)(2,1)}, bf16[32,2048]{1,0:T(8,128)(2,1)S(1)}, u32[]{:S(2)}, u32[]{:S(2)}) collective-permute-start(bf16[32,2048]{1,0:T(8,128)(2,1)} %param.21), channel_id=1, source_target_pairs={{0,4},{1,3},{2,0},{3,7},{4,8},{5,1},{6,2},{7,11},{8,12},{9,5},{10,... | collective-permute-start | bytes 393224 | tf_op jit(solution)/shard_map/ppermute | solution.py:87
  5.7 5.0 %collective-permute-start.2 = (bf16[32,2048]{1,0:T(8,128)(2,1)S(1)}, bf16[32,2048]{1,0:T(8,128)(2,1)S(1)}, u32[]{:S(2)}, u32[]{:S(2)}) collective-permute-start(bf16[32,2048]{1,0:T(8,128)(2,1)S(1)} %collective-permute-done), channel_id=1, source_target_pairs={{0,4},{1,3},{2,0},{3,7},{4,8},{5,1},{6,2},{7,11},{8,12},{9,5},{10,... | collective-permute-start | bytes 393224 | tf_op jit(solution)/shard_map/ppermute | solution.py:87
  8.5 5.0 %collective-permute-start.3 = (bf16[32,2048]{1,0:T(8,128)(2,1)S(1)}, bf16[32,2048]{1,0:T(8,128)(2,1)S(1)}, u32[]{:S(2)}, u32[]{:S(2)}) collective-permute-start(bf16[32,2048]{1,0:T(8,128)(2,1)S(1)} %collective-permute-done.1), channel_id=1, source_target_pairs={{0,4},{1,3},{2,0},{3,7},{4,8},{5,1},{6,2},{7,11},{8,12},{9,5},{10,... | collective-permute-start | bytes 393224 | tf_op jit(solution)/shard_map/ppermute | solution.py:87
  10.7 5.0 %collective-permute-start.4 = (bf16[32,2048]{1,0:T(8,128)(2,1)S(1)}, bf16[32,2048]{1,0:T(8,128)(2,1)S(1)}, u32[]{:S(2)}, u32[]{:S(2)}) collective-permute-start(bf16[32,2048]{1,0:T(8,128)(2,1)S(1)} %collective-permute-done.2), channel_id=1, source_target_pairs={{0,4},{1,3},{2,0},{3,7},{4,8},{5,1},{6,2},{7,11},{8,12},{9,5},{10,... | collective-permute-start | bytes 393224 | tf_op jit(solution)/shard_map/ppermute | solution.py:87
  13.5 5.0 %collective-permute-start.5 = (bf16[32,2048]{1,0:T(8,128)(2,1)S(1)}, bf16[32,2048]{1,0:T(8,128)(2,1)S(1)}, u32[]{:S(2)}, u32[]{:S(2)}) collective-permute-start(bf16[32,2048]{1,0:T(8,128)(2,1)S(1)} %collective-permute-done.3), channel_id=1, source_target_pairs={{0,4},{1,3},{2,0},{3,7},{4,8},{5,1},{6,2},{7,11},{8,12},{9,5},{10,... | collective-permute-start | bytes 393224 | tf_op jit(solution)/shard_map/ppermute | solution.py:87
  15.7 5.0 %collective-permute-start.6 = (bf16[32,2048]{1,0:T(8,128)(2,1)S(1)}, bf16[32,2048]{1,0:T(8,128)(2,1)S(1)}, u32[]{:S(2)}, u32[]{:S(2)}) collective-permute-start(bf16[32,2048]{1,0:T(8,128)(2,1)S(1)} %collective-permute-done.4), channel_id=1, source_target_pairs={{0,4},{1,3},{2,0},{3,7},{4,8},{5,1},{6,2},{7,11},{8,12},{9,5},{10,... | collective-permute-start | bytes 393224 | tf_op jit(solution)/shard_map/ppermute | solution.py:87
  18.5 5.0 %collective-permute-start.8 = (bf16[32,2048]{1,0:T(8,128)(2,1)S(1)}, bf16[32,2048]{1,0:T(8,128)(2,1)S(1)}, u32[]{:S(2)}, u32[]{:S(2)}) collective-permute-start(bf16[32,2048]{1,0:T(8,128)(2,1)S(1)} %collective-permute-done.5), channel_id=1, source_target_pairs={{0,4},{1,3},{2,0},{3,7},{4,8},{5,1},{6,2},{7,11},{8,12},{9,5},{10,... | collective-permute-start | bytes 393224 | tf_op jit(solution)/shard_map/ppermute | solution.py:87
  20.7 4.1 %collective-permute-start.7 = (bf16[96,4096]{1,0:T(8,128)(2,1)S(1)}, bf16[96,4096]{1,0:T(8,128)(2,1)S(1)}, u32[]{:S(2)}, u32[]{:S(2)}) collective-permute-start(bf16[96,4096]{1,0:T(8,128)(2,1)S(1)} %maximum_maximum_fusion), channel_id=1, source_target_pairs={{0,1},{1,0},{2,3},{3,2},{4,5},{5,4},{6,7},{7,6},{8,9},{9,8},{10,11... | collective-permute-start | bytes 2359304 | tf_op jit(solution)/shard_map/ppermute | solution.py:49
  23.5 1.3 %collective-permute-start.9 = (bf16[32,2048]{1,0:T(8,128)(2,1)S(1)}, bf16[32,2048]{1,0:T(8,128)(2,1)S(1)}, u32[]{:S(2)}, u32[]{:S(2)}) collective-permute-start(bf16[32,2048]{1,0:T(8,128)(2,1)S(1)} %collective-permute-done.8), channel_id=1, source_target_pairs={{0,1},{1,0},{2,3},{3,2},{4,5},{5,4},{6,7},{7,6},{8,9},{9,8},{10,11... | collective-permute-start | bytes 393224 | tf_op jit(solution)/shard_map/ppermute | solution.py:49
  24.9 0.7 copy-start.14
  25.0 1.4 %copy-start.3 = (bf16[256,4096]{1,0:T(8,128)(2,1)}, bf16[256,4096]{1,0:T(8,128)(2,1)S(1)}, u32[]{:S(2)}) copy-start(bf16[256,4096]{1,0:T(8,128)(2,1)S(1)} %maximum_dynamic-update-slice_fusion.4) | copy-start | bytes 6291460
  25.6 0.8 copy-start.10
  25.6 1.1 copy-start.6
  25.6 1.3 %copy-start.8 = (bf16[256,32]{0,1:T(8,128)(2,1)S(1)}, bf16[256,32]{0,1:T(8,128)(2,1)}, u32[]{:S(2)}) copy-start(bf16[256,32]{0,1:T(8,128)(2,1)} %param.31) | copy-start | bytes 49156
  27.0 21.0 %copy-start.9 = (s32[32,2]{0,1:T(2,128)S(1)}, s32[32,2]{0,1:T(2,128)}, u32[]{:S(2)}) copy-start(s32[32,2]{0,1:T(2,128)} %param.22) | copy-start | bytes 772
  27.2 1.5 %collective-permute-start.10 = (bf16[128,544]{1,0:T(8,128)(2,1)S(1)}, bf16[128,544]{1,0:T(8,128)(2,1)S(1)}, u32[]{:S(2)}, u32[]{:S(2)}) collective-permute-start(bf16[128,544]{1,0:T(8,128)(2,1)S(1)} %fusion.10), channel_id=1, source_target_pairs={{0,1},{1,0},{2,3},{3,2},{4,5},{5,4},{6,7},{7,6},{8,9},{9,8},{10,11... | collective-permute-start | bytes 417800 | tf_op jit(solution)/shard_map/ppermute | solution.py:49
  28.7 20.7 %copy-start.12 = (bf16[512,256]{1,0:T(8,128)(2,1)S(1)}, bf16[512,256]{1,0:T(8,128)(2,1)}, u32[]{:S(2)}) copy-start(bf16[512,256]{1,0:T(8,128)(2,1)} %param.32) | copy-start | bytes 786436
  28.7 4.6 %collective-permute-start.11 = (bf16[64,544]{1,0:T(8,128)(2,1)S(1)}, bf16[64,544]{1,0:T(8,128)(2,1)S(1)}, u32[]{:S(2)}, u32[]{:S(2)}) collective-permute-start(bf16[64,544]{1,0:T(8,128)(2,1)S(1)} %dynamic-slice_convert_fusion.1), channel_id=1, source_target_pairs={{0,2},{2,0},{4,6},{6,4},{8,10},{10,8},{12,14},{14,12},{1,3},{3,1},... | collective-permute-start | bytes 208904 | tf_op jit(solution)/shard_map/ppermute | solution.py:53
  33.3 4.5 %collective-permute-start.12 = (bf16[64,544]{1,0:T(8,128)(2,1)S(1)}, bf16[64,544]{1,0:T(8,128)(2,1)S(1)}, u32[]{:S(2)}, u32[]{:S(2)}) collective-permute-start(bf16[64,544]{1,0:T(8,128)(2,1)S(1)} %fusion.46), channel_id=1, source_target_pairs={{0,4},{2,6},{4,0},{6,2},{8,12},{10,14},{12,8},{14,10},{1,5},{3,7},... | collective-permute-start | bytes 208904 | tf_op jit(solution)/shard_map/ppermute | solution.py:53
  37.8 5.4 %collective-permute-start.13 = (bf16[64,544]{1,0:T(8,128)(2,1)S(1)}, bf16[64,544]{1,0:T(8,128)(2,1)S(1)}, u32[]{:S(2)}, u32[]{:S(2)}) collective-permute-start(bf16[64,544]{1,0:T(8,128)(2,1)S(1)} %fusion.45), channel_id=1, source_target_pairs={{0,8},{2,10},{4,12},{6,14},{8,0},{10,2},{12,4},{14,6},{1,9},{3,11}... | collective-permute-start | bytes 208904 | tf_op jit(solution)/shard_map/ppermute | solution.py:53
  43.3 4.5 %collective-permute-start.14 = (bf16[64,544]{1,0:T(8,128)(2,1)S(1)}, bf16[64,544]{1,0:T(8,128)(2,1)S(1)}, u32[]{:S(2)}, u32[]{:S(2)}) collective-permute-start(bf16[64,544]{1,0:T(8,128)(2,1)S(1)} %get-tuple-element.29), channel_id=1, source_target_pairs={{0,2},{2,0},{4,6},{6,4},{8,10},{10,8},{12,14},{14,12},{1,3},{3,1},... | collective-permute-start | bytes 208904 | tf_op jit(solution)/shard_map/ppermute | solution.py:53
  43.8 16.4 %collective-permute-start.17 = (bf16[256,4096]{1,0:T(8,128)(2,1)}, bf16[256,4096]{1,0:T(8,128)(2,1)}, u32[]{:S(2)}, u32[]{:S(2)}) collective-permute-start(bf16[256,4096]{1,0:T(8,128)(2,1)} %wg_ref.1), channel_id=1, source_target_pairs={{0,1},{1,0},{2,3},{3,2},{4,5},{5,4},{6,7},{7,6},{8,9},{9,8},{10,11... | collective-permute-start | bytes 6291464 | tf_op jit(solution)/shard_map/ppermute | solution.py:49
  47.9 1.5 %collective-permute-start.15 = (bf16[128,544]{1,0:T(8,128)(2,1)S(1)}, bf16[128,544]{1,0:T(8,128)(2,1)S(1)}, u32[]{:S(2)}, u32[]{:S(2)}) collective-permute-start(bf16[128,544]{1,0:T(8,128)(2,1)S(1)} %constant_dynamic-update-slice_fusion.7), channel_id=1, source_target_pairs={{0,1},{1,0},{2,3},{3,2},{4,5},{5,4},{6,7},{7,6},{8,9},{9,8},{10,11... | collective-permute-start | bytes 417800 | tf_op jit(solution)/shard_map/ppermute | solution.py:49
  49.4 2.1 %copy-start.4 = (f32[32,16,256]{2,1,0:T(8,128)S(1)}, f32[32,16,256]{2,1,0:T(8,128)}, u32[]{:S(2)}) copy-start(f32[32,16,256]{2,1,0:T(8,128)} %param.24) | copy-start | bytes 1572868
  49.4 2.1 %copy-start.7 = (f32[16,256]{1,0:T(8,128)S(1)}, f32[16,256]{1,0:T(8,128)}, u32[]{:S(2)}) copy-start(f32[16,256]{1,0:T(8,128)} %param.34) | copy-start | bytes 49156
  52.2 2.8 %copy-start.11 = (f32[256]{0:T(256)S(1)}, f32[256]{0:T(256)}, u32[]{:S(2)}) copy-start(f32[256]{0:T(256)} %param.35) | copy-start | bytes 3076
  52.2 3.5 %copy-start.15 = (f32[4096]{0:T(1024)S(1)}, f32[4096]{0:T(1024)}, u32[]{:S(2)}) copy-start(f32[4096]{0:T(1024)} %param.25) | copy-start | bytes 49156
  55.7 4.6 %copy-start.1 = (bf16[256,4096]{1,0:T(8,128)(2,1)S(1)}, bf16[256,4096]{1,0:T(8,128)(2,1)}, u32[]{:S(2)}) copy-start(bf16[256,4096]{1,0:T(8,128)(2,1)} %wg_ref.1) | copy-start | bytes 6291460
  58.9 1.4 %collective-permute-start.16 = (bf16[256,256]{1,0:T(8,128)(2,1)S(1)}, bf16[256,256]{1,0:T(8,128)(2,1)S(1)}, u32[]{:S(2)}, u32[]{:S(2)}) collective-permute-start(bf16[256,256]{1,0:T(8,128)(2,1)S(1)} %fusion.29.g_ref), channel_id=1, source_target_pairs={{0,1},{1,0},{2,3},{3,2},{4,5},{5,4},{6,7},{7,6},{8,9},{9,8},{10,11... | collective-permute-start | bytes 393224 | tf_op jit(solution)/shard_map/ppermute | solution.py:49
  62.8 20.4 %copy-start.5 = (bf16[32,2048]{1,0:T(8,128)(2,1)S(1)}, bf16[32,2048]{1,0:T(8,128)(2,1)}, u32[]{:S(2)}) copy-start(bf16[32,2048]{1,0:T(8,128)(2,1)} %param.21) | copy-start | bytes 393220
  62.8 5.0 %collective-permute-start.18 = (bf16[32,2048]{1,0:T(8,128)(2,1)S(1)}, bf16[32,2048]{1,0:T(8,128)(2,1)S(1)}, u32[]{:S(2)}, u32[]{:S(2)}) collective-permute-start(bf16[32,2048]{1,0:T(8,128)(2,1)S(1)} %get-tuple-element.7), channel_id=1, source_target_pairs={{0,4},{1,3},{2,0},{3,7},{4,8},{5,1},{6,2},{7,11},{8,12},{9,5},{10,... | collective-permute-start | bytes 393224 | tf_op jit(solution)/shard_map/ppermute | solution.py:184
  64.5 5.0 %collective-permute-start.22 = (bf16[32,2048]{1,0:T(8,128)(2,1)S(1)}, bf16[32,2048]{1,0:T(8,128)(2,1)S(1)}, u32[]{:S(2)}, u32[]{:S(2)}) collective-permute-start(bf16[32,2048]{1,0:T(8,128)(2,1)S(1)} %slice.408), channel_id=1, source_target_pairs={{0,4},{1,3},{2,0},{3,7},{4,8},{5,1},{6,2},{7,11},{8,12},{9,5},{10,... | collective-permute-start | bytes 393224 | tf_op jit(solution)/shard_map/ppermute | solution.py:184
  67.9 5.0 %collective-permute-start.19 = (bf16[32,2048]{1,0:T(8,128)(2,1)S(1)}, bf16[32,2048]{1,0:T(8,128)(2,1)S(1)}, u32[]{:S(2)}, u32[]{:S(2)}) collective-permute-start(bf16[32,2048]{1,0:T(8,128)(2,1)S(1)} %add_convert_fusion.6), channel_id=1, source_target_pairs={{0,4},{1,3},{2,0},{3,7},{4,8},{5,1},{6,2},{7,11},{8,12},{9,5},{10,... | collective-permute-start | bytes 393224 | tf_op jit(solution)/shard_map/ppermute | solution.py:184
  69.6 5.0 %collective-permute-start.23 = (bf16[32,2048]{1,0:T(8,128)(2,1)S(1)}, bf16[32,2048]{1,0:T(8,128)(2,1)S(1)}, u32[]{:S(2)}, u32[]{:S(2)}) collective-permute-start(bf16[32,2048]{1,0:T(8,128)(2,1)S(1)} %add_convert_fusion.3), channel_id=1, source_target_pairs={{0,4},{1,3},{2,0},{3,7},{4,8},{5,1},{6,2},{7,11},{8,12},{9,5},{10,... | collective-permute-start | bytes 393224 | tf_op jit(solution)/shard_map/ppermute | solution.py:184
  72.9 5.0 %collective-permute-start.20 = (bf16[32,2048]{1,0:T(8,128)(2,1)S(1)}, bf16[32,2048]{1,0:T(8,128)(2,1)S(1)}, u32[]{:S(2)}, u32[]{:S(2)}) collective-permute-start(bf16[32,2048]{1,0:T(8,128)(2,1)S(1)} %add_convert_fusion.5), channel_id=1, source_target_pairs={{0,4},{1,3},{2,0},{3,7},{4,8},{5,1},{6,2},{7,11},{8,12},{9,5},{10,... | collective-permute-start | bytes 393224 | tf_op jit(solution)/shard_map/ppermute | solution.py:184
  74.6 5.1 %collective-permute-start.24 = (bf16[32,2048]{1,0:T(8,128)(2,1)S(1)}, bf16[32,2048]{1,0:T(8,128)(2,1)S(1)}, u32[]{:S(2)}, u32[]{:S(2)}) collective-permute-start(bf16[32,2048]{1,0:T(8,128)(2,1)S(1)} %add_convert_fusion.2), channel_id=1, source_target_pairs={{0,4},{1,3},{2,0},{3,7},{4,8},{5,1},{6,2},{7,11},{8,12},{9,5},{10,... | collective-permute-start | bytes 393224 | tf_op jit(solution)/shard_map/ppermute | solution.py:184
  78.0 5.2 %collective-permute-start.21 = (bf16[32,2048]{1,0:T(8,128)(2,1)S(1)}, bf16[32,2048]{1,0:T(8,128)(2,1)S(1)}, u32[]{:S(2)}, u32[]{:S(2)}) collective-permute-start(bf16[32,2048]{1,0:T(8,128)(2,1)S(1)} %add_convert_fusion.4), channel_id=1, source_target_pairs={{0,4},{1,3},{2,0},{3,7},{4,8},{5,1},{6,2},{7,11},{8,12},{9,5},{10,... | collective-permute-start | bytes 393224 | tf_op jit(solution)/shard_map/ppermute | solution.py:184
  79.8 3.4 %collective-permute-start.25 = (bf16[32,2048]{1,0:T(8,128)(2,1)S(1)}, bf16[32,2048]{1,0:T(8,128)(2,1)S(1)}, u32[]{:S(2)}, u32[]{:S(2)}) collective-permute-start(bf16[32,2048]{1,0:T(8,128)(2,1)S(1)} %collective-permute-done.24), channel_id=1, source_target_pairs={{0,1},{1,0},{2,3},{3,2},{4,5},{5,4},{6,7},{7,6},{8,9},{9,8},{10,11... | collective-permute-start | bytes 393224 | tf_op jit(solution)/shard_map/ppermute | solution.py:49
  83.2 15.9 %collective-permute-start.26 = (bf16[32,2048]{1,0:T(8,128)(2,1)S(1)}, bf16[32,2048]{1,0:T(8,128)(2,1)S(1)}, u32[]{:S(2)}, u32[]{:S(2)}) collective-permute-start(bf16[32,2048]{1,0:T(8,128)(2,1)S(1)} %add_convert_fusion.1), channel_id=1, source_target_pairs={{0,1},{1,0},{2,3},{3,2},{4,5},{5,4},{6,7},{7,6},{8,9},{9,8},{10,11... | collective-permute-start | bytes 393224 | tf_op jit(solution)/shard_map/ppermute | solution.py:49
  83.5 6.9 %collective-permute-start.27 = (bf16[16,2048]{1,0:T(8,128)(2,1)S(1)}, bf16[16,2048]{1,0:T(8,128)(2,1)S(1)}, u32[]{:S(2)}, u32[]{:S(2)}) collective-permute-start(bf16[16,2048]{1,0:T(8,128)(2,1)S(1)} %dynamic-slice_bitcast_fusion), channel_id=1, source_target_pairs={{0,8},{2,10},{4,12},{6,14},{8,0},{10,2},{12,4},{14,6},{1,9},{3,11}... | collective-permute-start | bytes 196616 | tf_op jit(solution)/shard_map/ppermute | solution.py:53
  90.4 6.2 %collective-permute-start.28 = (bf16[32,2048]{1,0:T(8,128)(2,1)S(1)}, bf16[32,2048]{1,0:T(8,128)(2,1)S(1)}, u32[]{:S(2)}, u32[]{:S(2)}) collective-permute-start(bf16[32,2048]{1,0:T(8,128)(2,1)S(1)} %pad_maximum_fusion.4), channel_id=1, source_target_pairs={{0,2},{2,0},{4,6},{6,4},{8,10},{10,8},{12,14},{14,12},{1,3},{3,1},... | collective-permute-start | bytes 393224 | tf_op jit(solution)/shard_map/ppermute | solution.py:53
  90.5 6.4 %collective-permute-start.29 = (bf16[32,2048]{1,0:T(8,128)(2,1)S(1)}, bf16[32,2048]{1,0:T(8,128)(2,1)S(1)}, u32[]{:S(2)}, u32[]{:S(2)}) collective-permute-start(bf16[32,2048]{1,0:T(8,128)(2,1)S(1)} %pad_maximum_fusion.4), channel_id=1, source_target_pairs={{0,4},{2,6},{4,0},{6,2},{8,12},{10,14},{12,8},{14,10},{1,5},{3,7},... | collective-permute-start | bytes 393224 | tf_op jit(solution)/shard_map/ppermute | solution.py:53
  91.9 7.2 %collective-permute-start.30 = (bf16[32,2048]{1,0:T(8,128)(2,1)S(1)}, bf16[32,2048]{1,0:T(8,128)(2,1)S(1)}, u32[]{:S(2)}, u32[]{:S(2)}) collective-permute-start(bf16[32,2048]{1,0:T(8,128)(2,1)S(1)} %pad_maximum_fusion.4), channel_id=1, source_target_pairs={{0,6},{2,4},{4,2},{6,0},{8,14},{10,12},{12,10},{14,8},{1,7},{3,5},... | collective-permute-start | bytes 393224 | tf_op jit(solution)/shard_map/ppermute | solution.py:53
  99.1 2.0 %collective-permute-start.31 = (bf16[128,2048]{1,0:T(8,128)(2,1)S(1)}, bf16[128,2048]{1,0:T(8,128)(2,1)S(1)}, u32[]{:S(2)}, u32[]{:S(2)}) collective-permute-start(bf16[128,2048]{1,0:T(8,128)(2,1)S(1)} %constant_dynamic-update-slice_fusion), channel_id=1, source_target_pairs={{0,1},{1,0},{2,3},{3,2},{4,5},{5,4},{6,7},{7,6},{8,9},{9,8},{10,11... | collective-permute-start | bytes 1572872 | tf_op jit(solution)/shard_map/ppermute | solution.py:49
  99.4 1.8 %copy-start.2 = (f32[4096]{0:T(1024)S(1)}, f32[4096]{0:T(1024)}, u32[]{:S(2)}) copy-start(f32[4096]{0:T(1024)} %param.37) | copy-start | bytes 49156
  101.2 7.7 %copy-start.13 = (bf16[4096,16]{0,1:T(8,128)(2,1)S(1)}, bf16[4096,16]{0,1:T(8,128)(2,1)}, u32[]{:S(2)}) copy-start(bf16[4096,16]{0,1:T(8,128)(2,1)} %param.38) | copy-start | bytes 393220
  108.8 2.0 %collective-permute-start.32 = (bf16[128,2048]{1,0:T(8,128)(2,1)S(1)}, bf16[128,2048]{1,0:T(8,128)(2,1)S(1)}, u32[]{:S(2)}, u32[]{:S(2)}) collective-permute-start(bf16[128,2048]{1,0:T(8,128)(2,1)S(1)} %dynamic-slice_convert_fusion), channel_id=1, source_target_pairs={{0,1},{1,0},{2,3},{3,2},{4,5},{5,4},{6,7},{7,6},{8,9},{9,8},{10,11... | collective-permute-start | bytes 1572872 | tf_op jit(solution)/shard_map/ppermute | solution.py:49
  110.9 5.6 %collective-permute-start.33 = (bf16[32,2048]{1,0:T(8,128)(2,1)S(1)}, bf16[32,2048]{1,0:T(8,128)(2,1)S(1)}, u32[]{:S(2)}, u32[]{:S(2)}) collective-permute-start(bf16[32,2048]{1,0:T(8,128)(2,1)S(1)} %get-tuple-element.32), channel_id=1, source_target_pairs={{0,2},{2,0},{4,6},{6,4},{8,10},{10,8},{12,14},{14,12},{1,3},{3,1},... | collective-permute-start | bytes 393224 | tf_op jit(solution)/shard_map/ppermute | solution.py:53
  111.6 6.4 %collective-permute-start.34 = (bf16[32,2048]{1,0:T(8,128)(2,1)S(1)}, bf16[32,2048]{1,0:T(8,128)(2,1)S(1)}, u32[]{:S(2)}, u32[]{:S(2)}) collective-permute-start(bf16[32,2048]{1,0:T(8,128)(2,1)S(1)} %get-tuple-element.34), channel_id=1, source_target_pairs={{0,4},{2,6},{4,0},{6,2},{8,12},{10,14},{12,8},{14,10},{1,5},{3,7},... | collective-permute-start | bytes 393224 | tf_op jit(solution)/shard_map/ppermute | solution.py:53
  113.2 7.3 %collective-permute-start.35 = (bf16[32,2048]{1,0:T(8,128)(2,1)S(1)}, bf16[32,2048]{1,0:T(8,128)(2,1)S(1)}, u32[]{:S(2)}, u32[]{:S(2)}) collective-permute-start(bf16[32,2048]{1,0:T(8,128)(2,1)S(1)} %get-tuple-element.33), channel_id=1, source_target_pairs={{0,6},{2,4},{4,2},{6,0},{8,14},{10,12},{12,10},{14,8},{1,7},{3,5},... | collective-permute-start | bytes 393224 | tf_op jit(solution)/shard_map/ppermute | solution.py:53
  120.6 5.2 %collective-permute-start.36 = (bf16[16,2048]{1,0:T(8,128)(2,1)S(1)}, bf16[16,2048]{1,0:T(8,128)(2,1)S(1)}, u32[]{:S(2)}, u32[]{:S(2)}) collective-permute-start(bf16[16,2048]{1,0:T(8,128)(2,1)S(1)} %get-tuple-element.72), channel_id=1, source_target_pairs={{0,8},{2,10},{4,12},{6,14},{8,0},{10,2},{12,4},{14,6},{1,9},{3,11}... | collective-permute-start | bytes 196616 | tf_op jit(solution)/shard_map/ppermute | solution.py:53

commit v3 on v2

--- a/solution.py
+++ b/solution.py
@@ -12,6 +12,7 @@
 CAP = 16
 F32 = jnp.float32
 BF16 = jnp.bfloat16
+VMEM_LIMIT = 28 << 20
 
 
 def ring_place(index, owners):
@@ -59,20 +60,6 @@
     return (values * scale * gain).astype(BF16)
 
 
-def ssm_steps(inputs, steps, b_maps, c_maps, state, a_rate, d_skip):
-    outputs = []
-    for place in range(inputs.shape[1]):
-        decay = jnp.exp(-steps[:, place, None, :] * a_rate[None])
-        state = (
-            decay * state
-            + (steps[:, place] * inputs[:, place])[:, None, :] * b_maps[:, place, :, None]
-        )
-        outputs.append(
-            jnp.sum(c_maps[:, place, :, None] * state, axis=1) + d_skip * inputs[:, place]
-        )
-    return (jnp.stack(outputs, axis=1), state)
-
-
 def halves(first, second, core):
     return jnp.concatenate(
         [jnp.where(core == 0, first, second), jnp.where(core == 0, second, first)], axis=-1
@@ -92,6 +79,8 @@
         part_a.append(send(part_a[-1]))
         if step < half:
             part_b.append(send(part_b[-1]))
+    part_b, near = lax.optimization_barrier((part_b, part_a[:half]))
+    part_a = [*near, part_a[half]]
     mine = [halves(part_a[d], part_b[d], core) for d in range(half)]
     stack = jnp.concatenate(mine[1:], axis=0)
     theirs = over_cuts(stack).reshape(half - 1, rows, 2 * width)
@@ -108,7 +97,16 @@
     return put(out, far, ahead[half])
 
 
-def sum_all(part, owners, expert, core):
+def sum_all(part, owners, expert, core, under):
+    done = []
+
+    def beside(value):
+        if not under:
+            return value
+        value, extra = lax.optimization_barrier((value, under.pop(0)()))
+        done.append(extra)
+        return value
+
     def split(value, bit):
         size = value.shape[0] // 2
         return (
@@ -126,23 +124,105 @@
     keep = keep + over_cuts(give.astype(BF16)).astype(F32)
     low = expert % 2
     keep, give = split(keep, low)
-    keep = keep + over_expert(give.astype(BF16), 1, owners).astype(F32)
+    keep = keep + beside(over_expert(give.astype(BF16), 1, owners)).astype(F32)
     flip = 2
     while flip < owners:
-        keep = keep + over_expert(keep.astype(BF16), flip, owners).astype(F32)
+        keep = keep + beside(over_expert(keep.astype(BF16), flip, owners)).astype(F32)
         flip *= 2
     keep = keep.astype(BF16)
-    keep = join(keep, over_expert(keep, 1, owners), low)
-    return join(keep, over_cuts(keep), core)
-
-
-def project_kernel(half, rows, width, place_ref, g_ref, h_ref, wg_ref, wh_ref, near_ref, far_ref, own_ref, other_ref):
+    keep = join(keep, beside(over_expert(keep, 1, owners)), low)
+    return join(keep, over_cuts(keep), core), done
+
+
+def scan_kernel(
+    total, dt_proj, dt_bias, u_ref, z_ref, state_ref, a_rate, d_skip, gated, new_state, b_all, c_all, dt_all
+):
+    tokens, channels = u_ref.shape
+    states = a_rate.shape[0]
+    rank = dt_proj.shape[0]
+    raw = jnp.dot(total[:, :rank], dt_proj[...], preferred_element_type=F32) + dt_bias[...]
+    dt_all[...] = jnp.maximum(raw, 0.0) + jnp.log1p(jnp.exp(-jnp.abs(raw)))
+    ones = jnp.ones((states, channels), BF16)
+    diagonal = lax.broadcasted_iota(jnp.int32, (tokens, states, states), 1) == lax.broadcasted_iota(
+        jnp.int32, (tokens, states, states), 2
+    )
+    maps = total[:, rank : rank + 2 * states].astype(F32)
+    for start, dest in ((0, b_all), (states, c_all)):
+        spread = jnp.broadcast_to(
+            maps[:, None, start : start + states], (tokens, states, states)
+        )
+        spread = jnp.where(diagonal, spread, 0.0).reshape(tokens * states, states).astype(BF16)
+        dest[...] = jnp.dot(spread, ones, preferred_element_type=F32)
+    rate = -a_rate[...]
+    skip = d_skip[...]
+
+    def request(r, carry):
+        at = pl.ds(pl.multiple_of(r * DRAFT, DRAFT), DRAFT)
+        dt = dt_all[at, :]
+        u = u_ref[at, :].astype(F32)
+        du = dt * u
+        state = state_ref[r]
+        out = []
+        for p in range(DRAFT):
+            spot = pl.ds(pl.multiple_of((r * DRAFT + p) * states, states), states)
+            state = jnp.exp(dt[p : p + 1] * rate) * state + du[p : p + 1] * b_all[spot, :]
+            out.append(jnp.sum(c_all[spot, :] * state, axis=0, keepdims=True))
+        new_state[r] = state
+        z = z_ref[at, :]
+        y = jnp.concatenate(out, axis=0) + skip * u
+        gated[at, :] = y * (z * jax.nn.sigmoid(z))
+        return carry
+
+    lax.fori_loop(0, tokens // DRAFT, request, 0, unroll=2)
+
+
+def scan(total, dt_proj, dt_bias, u, z, ssm_state, a_rate, d_skip):
+    tokens, channels = u.shape
+    states = a_rate.shape[0]
+    vmem = pl.BlockSpec(memory_space=pltpu.VMEM)
+    return pl.pallas_call(
+        scan_kernel,
+        out_shape=(
+            jax.ShapeDtypeStruct((tokens, channels), F32),
+            jax.ShapeDtypeStruct(ssm_state.shape, F32),
+        ),
+        in_specs=[vmem] * 8,
+        out_specs=[vmem] * 2,
+        scratch_shapes=[
+            pltpu.VMEM((tokens * states, channels), F32),
+            pltpu.VMEM((tokens * states, channels), F32),
+            pltpu.VMEM((tokens, channels), F32),
+        ],
+        compiler_params=pltpu.CompilerParams(vmem_limit_bytes=VMEM_LIMIT),
+        name="scan",
+    )(
+        total,
+        dt_proj,
+        dt_bias.reshape(1, -1),
+        u,
+        z,
+        ssm_state,
+        a_rate,
+        d_skip.reshape(1, -1),
+    )
+
+
+def project_kernel(
+    half, rows, width, place_ref, id_ref, g_ref, h_ref, wg_ref, wh_ref, near_ref, far_ref, own_ref, other_ref
+):
     core = place_ref[half + 1]
+    holders = 2 * half // EXPERTS
+    ids = id_ref[...]
+    column = lax.broadcasted_iota(jnp.int32, (1, (half + 1) * rows), 1)
+    target = jnp.zeros_like(column)
+    for d in range(half + 1):
+        target = jnp.where(column // rows == d, place_ref[d], target)
+    picked = (ids == slot_keys(target, column % rows, holders, rows)).astype(F32).astype(BF16)
     here = pl.multiple_of(core * width, 128)
     there = pl.multiple_of((1 - core) * width, 128)
-    picked = [pl.ds(pl.multiple_of(place_ref[d] * rows, rows), rows) for d in range(half + 1)]
-    lhs_g = jnp.concatenate([g_ref[at, :] for at in picked], axis=0)
-    lhs_h = jnp.concatenate([h_ref[at, :] for at in picked], axis=0)
+    first = (((0,), (0,)), ((), ()))
+    lhs_g = lax.dot_general(picked, g_ref[...], first, preferred_element_type=F32).astype(BF16)
+    lhs_h = lax.dot_general(picked, h_ref[...], first, preferred_element_type=F32).astype(BF16)
     tile = 512
     for start in range(0, width, tile):
         at = pl.ds(here + start, tile)
@@ -159,7 +239,53 @@
         other_ref[:, start : start + tile] = term
 
 
-def project_blocks(gated, gated_other, out_proj, out_other, rows, half, places):
+def slots_kernel(routes_ref, out_ref):
+    routes = routes_ref[...]
+    count = routes.shape[0]
+    named = [
+        jnp.any(routes == label, axis=1, keepdims=True).astype(F32) for label in range(EXPERTS)
+    ]
+    idle = 1.0 - named[0] - named[1]
+    lane = lax.broadcasted_iota(jnp.int32, (count, 128), 1)
+    kinds = jnp.where(lane == 0, named[0], jnp.where(lane == 1, named[1], idle)).astype(BF16)
+    earlier = (
+        lax.broadcasted_iota(jnp.int32, (count, count), 0)
+        > lax.broadcasted_iota(jnp.int32, (count, count), 1)
+    )
+    ranks = jnp.dot(
+        earlier.astype(F32).astype(BF16), kinds, preferred_element_type=F32
+    )
+    first = jnp.sum(named[0], axis=0, keepdims=True)
+    second = jnp.sum(named[1], axis=0, keepdims=True)
+    spare = jnp.where(second < CAP, CAP + second, first)
+    slot = (
+        named[0] * ranks[:, 0:1]
+        + named[1] * (CAP + ranks[:, 1:2])
+        + idle * (spare + ranks[:, 2:3])
+    )
+    both = routes.astype(F32)
+    out_ref[...] = jnp.concatenate([slot, both], axis=1)
+
+
+def find_slots(routes):
+    vmem = pl.BlockSpec(memory_space=pltpu.VMEM)
+    return pl.pallas_call(
+        slots_kernel,
+        out_shape=jax.ShapeDtypeStruct((routes.shape[0], 1 + routes.shape[1]), F32),
+        in_specs=[vmem],
+        out_specs=vmem,
+        compiler_params=pltpu.CompilerParams(vmem_limit_bytes=1 << 20),
+        name="slots",
+    )(routes)
+
+
+def slot_keys(target, row, holders, rows):
+    expert = target // holders
+    block = jnp.where(row < CAP, target, target + holders * (1 - 2 * expert))
+    return block * rows + expert * CAP + row % CAP
+
+
+def project_blocks(ids, gated, gated_other, out_proj, out_other, rows, half, places):
     width = out_proj.shape[1] // 2
     vmem = pl.BlockSpec(memory_space=pltpu.VMEM)
     return pl.pallas_call(
@@ -170,11 +296,11 @@
             jax.ShapeDtypeStruct((rows, width), F32),
             jax.ShapeDtypeStruct(((half - 1) * rows, width), F32),
         ),
-        in_specs=[pl.BlockSpec(memory_space=pltpu.SMEM)] + [vmem] * 4,
+        in_specs=[pl.BlockSpec(memory_space=pltpu.SMEM)] + [vmem] * 5,
         out_specs=[vmem] * 4,
-        compiler_params=pltpu.CompilerParams(vmem_limit_bytes=40 << 20),
+        compiler_params=pltpu.CompilerParams(vmem_limit_bytes=VMEM_LIMIT),
         name="project",
-    )(places, gated, gated_other, out_proj, out_other)
+    )(places, ids, gated, gated_other, out_proj, out_other)
 
 
 def scatter_sum(near, far, own, other, rows, owners, perm):
@@ -273,8 +399,6 @@
     tok_count, half_width = x_in.shape
     requests = conv_state.shape[0]
     channels = in_x.shape[1]
-    states = a_rate.shape[0]
-    topk = routes.shape[1]
     owners = lax.axis_size("expert")
     expert = lax.axis_index("expert")
     core = lax.axis_index("cuts")
@@ -282,11 +406,11 @@
     perm = ring_perm(owners)
     ahead = ring_ahead(expert, core, owners)
     behind = ring_ahead(expert, 1 - core, owners)
+    places = jnp.stack(ahead + [core]).astype(jnp.int32)
     out_other = over_cuts(out_proj)
     full_x = gather_tokens(x_in, owners, core, ahead, behind, perm)
     normed = rms_norm(full_x, mamba_gain)
     u_pre = jnp.dot(normed, in_x, preferred_element_type=F32)
-    z_gate = jnp.dot(normed, in_z, preferred_element_type=F32)
     seq = jnp.concatenate([conv_state, u_pre.reshape(requests, DRAFT, channels)], axis=1)
     conv = jnp.zeros((requests, DRAFT, channels), F32) + conv_b
     for tap in range(conv_w.shape[0]):
@@ -294,65 +418,78 @@
     u_act = jax.nn.silu(conv).astype(BF16)
     flat_u = u_act.reshape(requests * DRAFT, channels)
     rank = xproj_dt.shape[1]
+    carried = xproj_bc.shape[1]
+    notes = find_slots(routes)
+    slot = notes[:, 0]
+    notes = jnp.where(core == 0, notes, 0.0)
+    tokens = flat_u.shape[0]
+    notes = lax.dynamic_update_slice(
+        jnp.zeros((tokens, notes.shape[1]), F32), notes, (expert * tok_count, 0)
+    )
     part = jnp.concatenate(
         [
             jnp.dot(flat_u, xproj_dt, preferred_element_type=F32),
             jnp.dot(flat_u, xproj_bc, preferred_element_type=F32),
+            notes,
         ],
         axis=1,
     )
-    total = sum_all(part, owners, expert, core)
-    dt_low = total[:, :rank]
-    maps = total[:, rank:].astype(F32)
-    steps = jax.nn.softplus(jnp.dot(dt_low, dt_proj, preferred_element_type=F32) + dt_bias)
-    b_maps = maps[:, :states].reshape(requests, DRAFT, states)
-    c_maps = maps[:, states:].reshape(requests, DRAFT, states)
-    outputs, new_state = ssm_steps(
-        u_act.astype(F32),
-        steps.reshape(requests, DRAFT, channels),
-        b_maps,
-        c_maps,
-        ssm_state,
-        a_rate,
-        d_skip,
-    )
-    gated = (outputs.reshape(requests * DRAFT, channels) * jax.nn.silu(z_gate)).astype(BF16)
+    holders = owners // EXPERTS
+    own = expert // holders
+    partner = expert + holders * (1 - 2 * own)
+    x_partner = lax.dynamic_slice(
+        full_x, (partner * tok_count, core * half_width), (tok_count, half_width)
+    )
+    part, x_partner = lax.optimization_barrier((part, x_partner))
+    total, (z_gate,) = sum_all(
+        part,
+        owners,
+        expert,
+        core,
+        [lambda: jnp.dot(normed, in_z, preferred_element_type=F32)],
+    )
+    gated, new_state = scan(
+        total, dt_proj, dt_bias, flat_u, z_gate, ssm_state, a_rate, d_skip
+    )
+    gated = gated.astype(BF16)
+    notes = total[:, rank + carried :]
+    ids = (jnp.arange(tokens) // tok_count * tok_count).astype(jnp.int32)[:, None] + notes[
+        :, :1
+    ].astype(jnp.int32)
     near, far, own_term, other = project_blocks(
+        ids,
         gated,
         over_cuts(gated),
         out_proj,
         out_other,
         tok_count,
         half,
-        jnp.stack(ahead + [core]).astype(jnp.int32),
-    )
+        places,
+    )
+    row = jnp.arange(tok_count, dtype=jnp.int32)
+    rows_here = (slot_keys(expert, row, holders, tok_count)[:, None] == ids[:, 0][None, :]).astype(
+        BF16
+    )
+    x_rows = jnp.dot(
+        lax.dynamic_slice_in_dim(rows_here, expert * tok_count, tok_count, 1),
+        x_in,
+        preferred_element_type=F32,
+    ) + jnp.dot(
+        lax.dynamic_slice_in_dim(rows_here, partner * tok_count, tok_count, 1),
+        x_partner,
+        preferred_element_type=F32,
+    )
+    route_rows = jnp.dot(rows_here, notes[:, 1:], preferred_element_type=F32).astype(jnp.int32)
     mixed_half = scatter_sum(near, far, own_term, other, tok_count, owners, perm)
-    stream_half = (x_in.astype(F32) + mixed_half).astype(BF16)
-
-    labels = jnp.arange(EXPERTS, dtype=jnp.int32)
-    named = jnp.any(routes[:, :, None] == labels, axis=1).astype(BF16)
-    earlier = (jnp.arange(tok_count)[:, None] > jnp.arange(tok_count)[None, :]).astype(BF16)
-    slot = jnp.dot(earlier, named, preferred_element_type=F32)
-    rows = jnp.arange(CAP, dtype=F32)
-    pick = ((slot.T[:, None, :] == rows[None, :, None]) & (named.T[:, None, :] > 0)).astype(BF16)
-    buffer = (
-        jnp.dot(pick.reshape(EXPERTS * CAP, tok_count), stream_half, preferred_element_type=F32)
-        .astype(BF16)
-        .reshape(EXPERTS, CAP, half_width)
-    )
-    holders = owners // EXPERTS
-    own = expert // holders
+    stream_half = (x_rows + mixed_half).astype(BF16)
 
     def exchange(value, flip):
         return over_expert(value, flip, owners)
 
-    kept = lax.dynamic_index_in_dim(buffer, own, 0, keepdims=False)
-    given = lax.dynamic_index_in_dim(buffer, 1 - own, 0, keepdims=False)
-    pair = jnp.concatenate([kept, exchange(given, holders)], axis=0)
-    pieces = [pair] + [exchange(pair, flip) for flip in range(1, holders)]
+    pieces = [stream_half] + [exchange(stream_half, flip) for flip in range(1, holders)]
     tokens_half = jnp.concatenate(pieces, axis=0)
-    tokens = halves(tokens_half, over_cuts(tokens_half), core)
-    partial_out = run_experts(tokens, moe_gain, w_gate, w_up, w_down)
+    routed = halves(tokens_half, over_cuts(tokens_half), core)
+    partial_out = run_experts(routed, moe_gain, w_gate, w_up, w_down)
     count = partial_out.shape[0]
     mine = lax.dynamic_slice(partial_out, (0, core * half_width), (count, half_width))
     theirs = lax.dynamic_slice(partial_out, (0, (1 - core) * half_width), (count, half_width))
@@ -361,24 +498,25 @@
     result = summed[0]
     for flip in range(1, holders):
         result = result + exchange(summed[flip].astype(BF16), flip).astype(F32)
-    result = result.astype(BF16)
-    back = exchange(result[CAP:], holders)
-
-    stream = halves(stream_half, over_cuts(stream_half), core)
-    logits = jnp.dot(rms_norm(stream, moe_gain), router, preferred_element_type=F32)
+    expert_out = result.astype(BF16).astype(F32)
+
+    logits = jnp.dot(
+        rms_norm(routed[:tok_count], moe_gain), router, preferred_element_type=F32
+    )
     all_labels = jnp.arange(router.shape[1], dtype=jnp.int32)
-    which = (routes[:, :, None] == all_labels).astype(F32)
+    which = (route_rows[:, :, None] == all_labels).astype(F32)
     chosen = jnp.sum(logits[:, None, :] * which, axis=-1)
     weight0 = jax.nn.sigmoid(chosen[:, 0] - chosen[:, 1])
     weights = jnp.stack([weight0, 1.0 - weight0], axis=1)
-    weight = jnp.sum(jnp.where(routes < EXPERTS, weights, 0.0), axis=1)
-    table = jnp.concatenate([result[:CAP], back], axis=0)
-    pick_own = jnp.where(own == 0, pick, pick[::-1]).reshape(EXPERTS * CAP, tok_count)
-    expert_out = lax.dot_general(
-        pick_own, table, (((0,), (0,)), ((), ())), preferred_element_type=F32
-    )
-    out = stream_half.astype(F32) + weight[:, None] * expert_out
-    return (out.astype(BF16), new_state)
+    weight = jnp.sum(jnp.where(route_rows < EXPERTS, weights, 0.0), axis=1)
+    done = (stream_half.astype(F32) + weight[:, None] * expert_out).astype(BF16)
+    back = exchange(done[CAP:], holders)
+    table = jnp.concatenate([done[:CAP], back], axis=0)
+    wanted = slot.astype(jnp.int32)
+    wanted = jnp.where(own == 0, wanted, (wanted + CAP) % (EXPERTS * CAP))
+    pick = (wanted[:, None] == row[None, :]).astype(BF16)
+    out = jnp.dot(pick, table, preferred_element_type=F32).astype(BF16)
+    return (out, new_state)
 
 
 def solution(mesh):

time: 127 us -> 120 us (0.945)
  waiting for transfers between devices: 54.9 us -> 44 us
  Pallas kernels: 9.93 us -> 14.9 us
  other arithmetic: 7.41 us -> 4.12 us
  local copies, waits for them, and re-layouts: 3.53 us -> 6.39 us
    ppermute x12 -> x11, waiting for transfers between devices: 31.5 us -> 22.4 us  [over_expert(): return lax.ppermute(value, 'expert', [(i, i ^ flip) for i in range(owners)])]
    pallas_call x0 -> x2, Pallas kernels: none -> 4.18 us  [the longest x1 3.95 us: scan(): pl.pallas_call(scan_kernel, out_shape=(jax.ShapeDtypeStruct((tokens, chan...]
    reduce_sum x4 -> x1, other arithmetic: 3.43 us -> 0.03 us  [on_device(): weight = jnp.sum(jnp.where(route_rows < EXPERTS, weights, 0.0), axis=1)]
    unnamed x45 -> x36, local copies, waits for them, and re-layouts: 1.22 us -> 3.28 us
    ppermute x12 -> x11, starting transfers between devices: 17.7 us -> 17.1 us  [over_expert(): return lax.ppermute(value, 'expert', [(i, i ^ flip) for i in range(owners)])]
    ppermute x11 -> x10, waiting for transfers between devices: 7.9 us -> 7.93 us  [over_cuts(): return lax.ppermute(value, 'cuts', [(0, 1), (1, 0)])]
  transfers between devices with their start and end apart: 37 -> 35, of which waited for: 30 -> 24; matrix products, arithmetic and copies ran while one was open for 11% -> 8% of each run, Pallas kernels for 0% -> 3%
where the time goes in v3:
time: 120 us
  waiting for transfers between devices  44 us (37%)
  starting transfers between devices  42.7 us (36%)
  Pallas kernels  14.9 us (12%)
  matrix products  6.7 us (6%)
  local copies, waits for them, and re-layouts  6.39 us (5%)
  other arithmetic  4.12 us (3%)
  between operations  1.25 us (1%)
    ppermute x11, waiting for transfers between devices, over_expert(): return lax.ppermute(value, 'expert', [(i, i ^ flip) for i in range(owners)])  22.4 us
    ppermute x11, starting transfers between devices, over_expert(): return lax.ppermute(value, 'expert', [(i, i ^ flip) for i in range(owners)])  17.1 us
    ppermute x7, starting transfers between devices, send(): return lax.ppermute(value, ('expert', 'cuts'), perm)  12 us
    ppermute x7, starting transfers between devices, send(): return lax.ppermute(value.astype(BF16), ('expert', 'cuts'), perm)  11.9 us
    ppermute x7, waiting for transfers between devices, send(): return lax.ppermute(value.astype(BF16), ('expert', 'cuts'), perm)  7.96 us
    ppermute x10, waiting for transfers between devices, over_cuts(): return lax.ppermute(value, 'cuts', [(0, 1), (1, 0)])  7.93 us
    pallas_call x1, Pallas kernels, run_experts(): pl.pallas_call(functools.partial(experts_kernel, tiles), out_shape=jax.Sh...  7.43 us
    ppermute x7, waiting for transfers between devices, send(): return lax.ppermute(value, ('expert', 'cuts'), perm)  5.75 us
  transfers between devices with their start and end apart: 35, of which 24 were waited for; matrix products, arithmetic and copies ran while one was open for 8% of the time, Pallas kernels for 3%

profile of v3, /device:TPU:0, one launch (start us, length us, event | category | flops | bytes accessed | tf_op | source)
XLA Modules:
  0.0 120.1 jit_solution(3076590954432637194)
XLA Ops:
  0.7 0.5 collective-permute-start
  1.2 2.6 %collective-permute-start.4 = (bf16[32,2048]{1,0:T(8,128)(2,1)}, bf16[32,2048]{1,0:T(8,128)(2,1)S(1)}, u32[]{:S(2)}, u32[]{:S(2)}) collective-permute-start(bf16[32,2048]{1,0:T(8,128)(2,1)} %param.21), channel_id=1, source_target_pairs={{0,4},{1,3},{2,0},{3,7},{4,8},{5,1},{6,2},{7,11},{8,12},{9,5},{10,... | collective-permute-start | bytes 393224 | tf_op jit(solution)/shard_map/ppermute | solution.py:74
  3.8 1.6 %collective-permute-start.1 = (bf16[32,2048]{1,0:T(8,128)(2,1)S(1)}, bf16[32,2048]{1,0:T(8,128)(2,1)S(1)}, u32[]{:S(2)}, u32[]{:S(2)}) collective-permute-start(bf16[32,2048]{1,0:T(8,128)(2,1)S(1)} %collective-permute-done), channel_id=1, source_target_pairs={{0,4},{1,3},{2,0},{3,7},{4,8},{5,1},{6,2},{7,11},{8,12},{9,5},{10,... | collective-permute-start | bytes 393224 | tf_op jit(solution)/shard_map/ppermute | solution.py:74
  5.4 1.0 copy.34
  6.4 0.8 copy.33.routes_ref
  7.4 1.6 %collective-permute-start.5 = (bf16[32,2048]{1,0:T(8,128)(2,1)S(1)}, bf16[32,2048]{1,0:T(8,128)(2,1)S(1)}, u32[]{:S(2)}, u32[]{:S(2)}) collective-permute-start(bf16[32,2048]{1,0:T(8,128)(2,1)S(1)} %collective-permute-done.4), channel_id=1, source_target_pairs={{0,4},{1,3},{2,0},{3,7},{4,8},{5,1},{6,2},{7,11},{8,12},{9,5},{10,... | collective-permute-start | bytes 393224 | tf_op jit(solution)/shard_map/ppermute | solution.py:74
  9.1 1.5 %collective-permute-start.2 = (bf16[32,2048]{1,0:T(8,128)(2,1)S(1)}, bf16[32,2048]{1,0:T(8,128)(2,1)S(1)}, u32[]{:S(2)}, u32[]{:S(2)}) collective-permute-start(bf16[32,2048]{1,0:T(8,128)(2,1)S(1)} %collective-permute-done.1), channel_id=1, source_target_pairs={{0,4},{1,3},{2,0},{3,7},{4,8},{5,1},{6,2},{7,11},{8,12},{9,5},{10,... | collective-permute-start | bytes 393224 | tf_op jit(solution)/shard_map/ppermute | solution.py:74
  10.6 1.8 %collective-permute-done.5 = bf16[32,2048]{1,0:T(8,128)(2,1)S(1)} collective-permute-done((bf16[32,2048]{1,0:T(8,128)(2,1)S(1)}, bf16[32,2048]{1,0:T(8,128)(2,1)S(1)}, u32[]{:S(2)}, u32[]{:S(2)}) %collective-permute-start.5) | collective-permute-done | bytes 131104 | tf_op jit(solution)/shard_map/ppermute | solution.py:74
  12.4 1.6 %collective-permute-start.6 = (bf16[32,2048]{1,0:T(8,128)(2,1)S(1)}, bf16[32,2048]{1,0:T(8,128)(2,1)S(1)}, u32[]{:S(2)}, u32[]{:S(2)}) collective-permute-start(bf16[32,2048]{1,0:T(8,128)(2,1)S(1)} %collective-permute-done.5), channel_id=1, source_target_pairs={{0,4},{1,3},{2,0},{3,7},{4,8},{5,1},{6,2},{7,11},{8,12},{9,5},{10,... | collective-permute-start | bytes 393224 | tf_op jit(solution)/shard_map/ppermute | solution.py:74
  14.0 1.5 %collective-permute-start.3 = (bf16[32,2048]{1,0:T(8,128)(2,1)S(1)}, bf16[32,2048]{1,0:T(8,128)(2,1)S(1)}, u32[]{:S(2)}, u32[]{:S(2)}) collective-permute-start(bf16[32,2048]{1,0:T(8,128)(2,1)S(1)} %collective-permute-done.2), channel_id=1, source_target_pairs={{0,4},{1,3},{2,0},{3,7},{4,8},{5,1},{6,2},{7,11},{8,12},{9,5},{10,... | collective-permute-start | bytes 393224 | tf_op jit(solution)/shard_map/ppermute | solution.py:74
  15.5 0.8 fusion.60
  16.4 1.0 collective-permute-done.6
  17.4 1.6 %collective-permute-start.8 = (bf16[32,2048]{1,0:T(8,128)(2,1)S(1)}, bf16[32,2048]{1,0:T(8,128)(2,1)S(1)}, u32[]{:S(2)}, u32[]{:S(2)}) collective-permute-start(bf16[32,2048]{1,0:T(8,128)(2,1)S(1)} %collective-permute-done.6), channel_id=1, source_target_pairs={{0,4},{1,3},{2,0},{3,7},{4,8},{5,1},{6,2},{7,11},{8,12},{9,5},{10,... | collective-permute-start | bytes 393224 | tf_op jit(solution)/shard_map/ppermute | solution.py:74
  19.5 2.9 %collective-permute-done.8 = bf16[32,2048]{1,0:T(8,128)(2,1)S(1)} collective-permute-done((bf16[32,2048]{1,0:T(8,128)(2,1)S(1)}, bf16[32,2048]{1,0:T(8,128)(2,1)S(1)}, u32[]{:S(2)}, u32[]{:S(2)}) %collective-permute-start.8) | collective-permute-done | bytes 131104 | tf_op jit(solution)/shard_map/ppermute | solution.py:74
  22.4 1.3 %collective-permute-done.9 = bf16[32,2048]{1,0:T(8,128)(2,1)S(1)} collective-permute-done((bf16[32,2048]{1,0:T(8,128)(2,1)S(1)}, bf16[32,2048]{1,0:T(8,128)(2,1)S(1)}, u32[]{:S(2)}, u32[]{:S(2)}) %collective-permute-start.9) | collective-permute-done | bytes 131104 | tf_op jit(solution)/shard_map/ppermute | solution.py:50
  24.0 0.5 fusion
  24.6 0.8 convolution_bitcast_fusion
  26.1 0.7 dynamic_slice.27
  27.5 0.9 collective-permute-done.10
  28.4 1.5 %collective-permute-start.11 = (bf16[64,547]{1,0:T(8,128)(2,1)S(1)}, bf16[64,547]{1,0:T(8,128)(2,1)S(1)}, u32[]{:S(2)}, u32[]{:S(2)}) collective-permute-start(bf16[64,547]{1,0:T(8,128)(2,1)S(1)} %dynamic-slice_convert_fusion.2), channel_id=1, source_target_pairs={{0,2},{2,0},{4,6},{6,4},{8,10},{10,8},{12,14},{14,12},{1,3},{3,1},... | collective-permute-start | bytes 210056 | tf_op jit(solution)/shard_map/ppermute | solution.py:54
  29.9 3.7 %fusion.3.z_ref = f32[256,256]{1,0:T(8,128)} fusion(bf16[4096,256]{1,0:T(8,128)(2,1)} %param.27, bf16[256,4096]{1,0:T(8,128)(2,1)} %copy-done.8, f32[4096]{0:T(1024)S(1)} %copy-done.16, f32[256]{0:T(256)S(1)} %add_rsqrt_fusion), kind=kOutput, calls=%fused_computation.22 | convolution fusion | flops 541065216 | bytes 4473856 | tf_op jit(solution)/shard_map/dot_general | solution.py:449
  33.7 1.6 %collective-permute-start.12 = (bf16[64,547]{1,0:T(8,128)(2,1)S(1)}, bf16[64,547]{1,0:T(8,128)(2,1)S(1)}, u32[]{:S(2)}, u32[]{:S(2)}) collective-permute-start(bf16[64,547]{1,0:T(8,128)(2,1)S(1)} %fusion.37), channel_id=1, source_target_pairs={{0,4},{2,6},{4,0},{6,2},{8,12},{10,14},{12,8},{14,10},{1,5},{3,7},... | collective-permute-start | bytes 210056 | tf_op jit(solution)/shard_map/ppermute | solution.py:54
  35.3 2.9 %collective-permute-done.12 = bf16[64,547]{1,0:T(8,128)(2,1)S(1)} collective-permute-done((bf16[64,547]{1,0:T(8,128)(2,1)S(1)}, bf16[64,547]{1,0:T(8,128)(2,1)S(1)}, u32[]{:S(2)}, u32[]{:S(2)}) %collective-permute-start.12) | collective-permute-done | bytes 70048 | tf_op jit(solution)/shard_map/ppermute | solution.py:54
  38.2 2.7 %collective-permute-start.13 = (bf16[64,547]{1,0:T(8,128)(2,1)S(1)}, bf16[64,547]{1,0:T(8,128)(2,1)S(1)}, u32[]{:S(2)}, u32[]{:S(2)}) collective-permute-start(bf16[64,547]{1,0:T(8,128)(2,1)S(1)} %fusion.35), channel_id=1, source_target_pairs={{0,8},{2,10},{4,12},{6,14},{8,0},{10,2},{12,4},{14,6},{1,9},{3,11}... | collective-permute-start | bytes 210056 | tf_op jit(solution)/shard_map/ppermute | solution.py:54
  40.9 2.7 %collective-permute-done.13 = bf16[64,547]{1,0:T(8,128)(2,1)S(1)} collective-permute-done((bf16[64,547]{1,0:T(8,128)(2,1)S(1)}, bf16[64,547]{1,0:T(8,128)(2,1)S(1)}, u32[]{:S(2)}, u32[]{:S(2)}) %collective-permute-start.13) | collective-permute-done | bytes 70048 | tf_op jit(solution)/shard_map/ppermute | solution.py:54
  43.7 0.7 constant_dynamic-update-slice_fusion.3
  44.3 0.8 collective-permute-start.14
  45.1 3.9 %collective-permute-done.14 = bf16[64,547]{1,0:T(8,128)(2,1)S(1)} collective-permute-done((bf16[64,547]{1,0:T(8,128)(2,1)}, bf16[64,547]{1,0:T(8,128)(2,1)S(1)}, u32[]{:S(2)}, u32[]{:S(2)}) %collective-permute-start.14) | collective-permute-done | bytes 70048 | tf_op jit(solution)/shard_map/ppermute | solution.py:54
  49.3 1.3 %collective-permute-done.15 = bf16[128,547]{1,0:T(8,128)(2,1)} collective-permute-done((bf16[128,547]{1,0:T(8,128)(2,1)S(1)}, bf16[128,547]{1,0:T(8,128)(2,1)}, u32[]{:S(2)}, u32[]{:S(2)}) %collective-permute-start.15) | collective-permute-done | bytes 140064 | tf_op jit(solution)/shard_map/ppermute | solution.py:50
  50.6 0.9 constant_dynamic-update-slice_fusion.total
  51.6 0.9 copy-done.3
  52.5 4.0 %scan.1 = (f32[256,256]{1,0:T(8,128)S(1)}, f32[32,16,256]{2,1,0:T(8,128)}) custom-call(bf16[256,547]{1,0:T(8,128)(2,1)S(1)} %constant_dynamic-update-slice_fusion.total, bf16[512,256]{1,0:T(8,128)(2,1)S(1)} %copy-done.2, f32[1,256]{1,0:T(1,128)S(1)} %bitcast.27, bf16[256,256]{1,0:T(8,128)(2,1)S(1)} %fusion.34.u_ref, f32[256,256]{1,0:T(8,128)S(1)} %copy-done.3, ...), custom_call_target="tpu_custom_call" | custom-call | tf_op jit(solution)/shard_map/scan/pallas_call | solution.py:183
  56.9 1.0 collective-permute-done.16.h_ref
  57.9 3.3 %project.1 = (f32[96,2048]{1,0:T(8,128)S(1)}, bf16[32,2048]{1,0:T(8,128)(2,1)S(1)}, f32[32,2048]{1,0:T(8,128)S(1)}, f32[96,2048]{1,0:T(8,128)S(1)}) custom-call(s32[6]{0:T(128)S(1)} %stack.32.place_ref, s32[256,1]{1,0:T(8,128)S(1)} %get-tuple-element.52.id_ref, bf16[256,256]{1,0:T(8,128)(2,1)S(1)} %convert_element_type.145.g_ref, ...), custom_call_target="tpu_custom_call" | custom-call | tf_op jit(solution)/shard_map/project/pallas_call | solution.py:291
  61.3 1.7 %collective-permute-start.18 = (bf16[32,2048]{1,0:T(8,128)(2,1)S(1)}, bf16[32,2048]{1,0:T(8,128)(2,1)S(1)}, u32[]{:S(2)}, u32[]{:S(2)}) collective-permute-start(bf16[32,2048]{1,0:T(8,128)(2,1)S(1)} %get-tuple-element.34), channel_id=1, source_target_pairs={{0,4},{1,3},{2,0},{3,7},{4,8},{5,1},{6,2},{7,11},{8,12},{9,5},{10,... | collective-permute-start | bytes 393224 | tf_op jit(solution)/shard_map/ppermute | solution.py:310
  63.0 1.7 %collective-permute-start.22 = (bf16[32,2048]{1,0:T(8,128)(2,1)S(1)}, bf16[32,2048]{1,0:T(8,128)(2,1)S(1)}, u32[]{:S(2)}, u32[]{:S(2)}) collective-permute-start(bf16[32,2048]{1,0:T(8,128)(2,1)S(1)} %slice.221), channel_id=1, source_target_pairs={{0,4},{1,3},{2,0},{3,7},{4,8},{5,1},{6,2},{7,11},{8,12},{9,5},{10,... | collective-permute-start | bytes 393224 | tf_op jit(solution)/shard_map/ppermute | solution.py:310
  64.7 1.6 %collective-permute-done.18 = bf16[32,2048]{1,0:T(8,128)(2,1)S(1)} collective-permute-done((bf16[32,2048]{1,0:T(8,128)(2,1)S(1)}, bf16[32,2048]{1,0:T(8,128)(2,1)S(1)}, u32[]{:S(2)}, u32[]{:S(2)}) %collective-permute-start.18) | collective-permute-done | bytes 131104 | tf_op jit(solution)/shard_map/ppermute | solution.py:310
  66.3 1.7 %collective-permute-start.19 = (bf16[32,2048]{1,0:T(8,128)(2,1)S(1)}, bf16[32,2048]{1,0:T(8,128)(2,1)S(1)}, u32[]{:S(2)}, u32[]{:S(2)}) collective-permute-start(bf16[32,2048]{1,0:T(8,128)(2,1)S(1)} %add_convert_fusion.6), channel_id=1, source_target_pairs={{0,4},{1,3},{2,0},{3,7},{4,8},{5,1},{6,2},{7,11},{8,12},{9,5},{10,... | collective-permute-start | bytes 393224 | tf_op jit(solution)/shard_map/ppermute | solution.py:310
  68.1 1.7 %collective-permute-start.23 = (bf16[32,2048]{1,0:T(8,128)(2,1)S(1)}, bf16[32,2048]{1,0:T(8,128)(2,1)S(1)}, u32[]{:S(2)}, u32[]{:S(2)}) collective-permute-start(bf16[32,2048]{1,0:T(8,128)(2,1)S(1)} %add_convert_fusion.3), channel_id=1, source_target_pairs={{0,4},{1,3},{2,0},{3,7},{4,8},{5,1},{6,2},{7,11},{8,12},{9,5},{10,... | collective-permute-start | bytes 393224 | tf_op jit(solution)/shard_map/ppermute | solution.py:310
  69.8 1.6 %collective-permute-done.19 = bf16[32,2048]{1,0:T(8,128)(2,1)S(1)} collective-permute-done((bf16[32,2048]{1,0:T(8,128)(2,1)S(1)}, bf16[32,2048]{1,0:T(8,128)(2,1)S(1)}, u32[]{:S(2)}, u32[]{:S(2)}) %collective-permute-start.19) | collective-permute-done | bytes 131104 | tf_op jit(solution)/shard_map/ppermute | solution.py:310
  71.4 1.7 %collective-permute-start.20 = (bf16[32,2048]{1,0:T(8,128)(2,1)S(1)}, bf16[32,2048]{1,0:T(8,128)(2,1)S(1)}, u32[]{:S(2)}, u32[]{:S(2)}) collective-permute-start(bf16[32,2048]{1,0:T(8,128)(2,1)S(1)} %add_convert_fusion.5), channel_id=1, source_target_pairs={{0,4},{1,3},{2,0},{3,7},{4,8},{5,1},{6,2},{7,11},{8,12},{9,5},{10,... | collective-permute-start | bytes 393224 | tf_op jit(solution)/shard_map/ppermute | solution.py:310
  73.1 1.7 %collective-permute-start.24 = (bf16[32,2048]{1,0:T(8,128)(2,1)S(1)}, bf16[32,2048]{1,0:T(8,128)(2,1)S(1)}, u32[]{:S(2)}, u32[]{:S(2)}) collective-permute-start(bf16[32,2048]{1,0:T(8,128)(2,1)S(1)} %add_convert_fusion.2), channel_id=1, source_target_pairs={{0,4},{1,3},{2,0},{3,7},{4,8},{5,1},{6,2},{7,11},{8,12},{9,5},{10,... | collective-permute-start | bytes 393224 | tf_op jit(solution)/shard_map/ppermute | solution.py:310
  74.8 1.6 %collective-permute-done.20 = bf16[32,2048]{1,0:T(8,128)(2,1)S(1)} collective-permute-done((bf16[32,2048]{1,0:T(8,128)(2,1)S(1)}, bf16[32,2048]{1,0:T(8,128)(2,1)S(1)}, u32[]{:S(2)}, u32[]{:S(2)}) %collective-permute-start.20) | collective-permute-done | bytes 131104 | tf_op jit(solution)/shard_map/ppermute | solution.py:310
  76.4 1.8 %collective-permute-start.21 = (bf16[32,2048]{1,0:T(8,128)(2,1)S(1)}, bf16[32,2048]{1,0:T(8,128)(2,1)S(1)}, u32[]{:S(2)}, u32[]{:S(2)}) collective-permute-start(bf16[32,2048]{1,0:T(8,128)(2,1)S(1)} %add_convert_fusion.4), channel_id=1, source_target_pairs={{0,4},{1,3},{2,0},{3,7},{4,8},{5,1},{6,2},{7,11},{8,12},{9,5},{10,... | collective-permute-start | bytes 393224 | tf_op jit(solution)/shard_map/ppermute | solution.py:310
  78.5 3.1 %collective-permute-done.21 = bf16[32,2048]{1,0:T(8,128)(2,1)S(1)} collective-permute-done((bf16[32,2048]{1,0:T(8,128)(2,1)S(1)}, bf16[32,2048]{1,0:T(8,128)(2,1)S(1)}, u32[]{:S(2)}, u32[]{:S(2)}) %collective-permute-start.21) | collective-permute-done | bytes 131104 | tf_op jit(solution)/shard_map/ppermute | solution.py:310
  81.9 0.8 collective-permute-start.26
  82.7 1.6 %collective-permute-start.27 = (bf16[32,2048]{1,0:T(8,128)(2,1)S(1)}, bf16[32,2048]{1,0:T(8,128)(2,1)S(1)}, u32[]{:S(2)}, u32[]{:S(2)}) collective-permute-start(bf16[32,2048]{1,0:T(8,128)(2,1)S(1)} %add_convert_fusion.1), channel_id=1, source_target_pairs={{0,4},{2,6},{4,0},{6,2},{8,12},{10,14},{12,8},{14,10},{1,5},{3,7},... | collective-permute-start | bytes 393224 | tf_op jit(solution)/shard_map/ppermute | solution.py:54
  84.3 1.1 collective-permute-start.28
  85.4 2.6 %collective-permute-done.26 = bf16[32,2048]{1,0:T(8,128)(2,1)S(1)} collective-permute-done((bf16[32,2048]{1,0:T(8,128)(2,1)S(1)}, bf16[32,2048]{1,0:T(8,128)(2,1)S(1)}, u32[]{:S(2)}, u32[]{:S(2)}) %collective-permute-start.26) | collective-permute-done | bytes 131104 | tf_op jit(solution)/shard_map/ppermute | solution.py:54
  88.1 2.1 %collective-permute-done.28 = bf16[32,2048]{1,0:T(8,128)(2,1)S(1)} collective-permute-done((bf16[32,2048]{1,0:T(8,128)(2,1)S(1)}, bf16[32,2048]{1,0:T(8,128)(2,1)S(1)}, u32[]{:S(2)}, u32[]{:S(2)}) %collective-permute-start.28) | collective-permute-done | bytes 131104 | tf_op jit(solution)/shard_map/ppermute | solution.py:54
  90.2 0.8 pad_maximum_fusion.2
  91.3 1.9 %collective-permute-done.29 = bf16[128,2048]{1,0:T(8,128)(2,1)S(1)} collective-permute-done((bf16[128,2048]{1,0:T(8,128)(2,1)}, bf16[128,2048]{1,0:T(8,128)(2,1)S(1)}, u32[]{:S(2)}, u32[]{:S(2)}) %collective-permute-start.29) | collective-permute-done | bytes 524320 | tf_op jit(solution)/shard_map/ppermute | solution.py:50
  93.7 0.4 copy-done.5
  94.1 7.4 %experts.1 = f32[128,4096]{1,0:T(8,128)S(1)} custom-call(bf16[128,4096]{1,0:T(8,128)(2,1)S(1)} %pad_maximum_fusion.x_ref, f32[1,4096]{1,0:T(1,128)S(1)} %bitcast.26, bf16[4096,768]{1,0:T(8,128)(2,1)} %wg_hbm.1, bf16[4096,768]{1,0:T(8,128)(2,1)} %wu_hbm.1, bf16[768,4096]{1,0:T(8,128)(2,1)} %wd_hbm.1), custom_call_target="tpu_custom_call" | custom-call | tf_op jit(solution)/shard_map/experts/pallas_call | solution.py:360
  102.1 1.5 %collective-permute-done.30 = bf16[128,2048]{1,0:T(8,128)(2,1)S(1)} collective-permute-done((bf16[128,2048]{1,0:T(8,128)(2,1)S(1)}, bf16[128,2048]{1,0:T(8,128)(2,1)S(1)}, u32[]{:S(2)}, u32[]{:S(2)}) %collective-permute-start.30) | collective-permute-done | bytes 524320 | tf_op jit(solution)/shard_map/ppermute | solution.py:50
  103.8 1.3 %collective-permute-start.31 = (bf16[32,2048]{1,0:T(8,128)(2,1)S(1)}, bf16[32,2048]{1,0:T(8,128)(2,1)S(1)}, u32[]{:S(2)}, u32[]{:S(2)}) collective-permute-start(bf16[32,2048]{1,0:T(8,128)(2,1)S(1)} %get-tuple-element.48), channel_id=1, source_target_pairs={{0,2},{2,0},{4,6},{6,4},{8,10},{10,8},{12,14},{14,12},{1,3},{3,1},... | collective-permute-start | bytes 393224 | tf_op jit(solution)/shard_map/ppermute | solution.py:54
  105.1 0.7 collective-permute-start.32
  105.8 1.5 %collective-permute-start.33 = (bf16[32,2048]{1,0:T(8,128)(2,1)S(1)}, bf16[32,2048]{1,0:T(8,128)(2,1)S(1)}, u32[]{:S(2)}, u32[]{:S(2)}) collective-permute-start(bf16[32,2048]{1,0:T(8,128)(2,1)S(1)} %get-tuple-element.49), channel_id=1, source_target_pairs={{0,6},{2,4},{4,2},{6,0},{8,14},{10,12},{12,10},{14,8},{1,7},{3,5},... | collective-permute-start | bytes 393224 | tf_op jit(solution)/shard_map/ppermute | solution.py:54
  107.4 2.0 %collective-permute-done.31 = bf16[32,2048]{1,0:T(8,128)(2,1)S(1)} collective-permute-done((bf16[32,2048]{1,0:T(8,128)(2,1)S(1)}, bf16[32,2048]{1,0:T(8,128)(2,1)S(1)}, u32[]{:S(2)}, u32[]{:S(2)}) %collective-permute-start.31) | collective-permute-done | bytes 131104 | tf_op jit(solution)/shard_map/ppermute | solution.py:54
  109.4 2.1 %collective-permute-done.32 = bf16[32,2048]{1,0:T(8,128)(2,1)S(1)} collective-permute-done((bf16[32,2048]{1,0:T(8,128)(2,1)S(1)}, bf16[32,2048]{1,0:T(8,128)(2,1)S(1)}, u32[]{:S(2)}, u32[]{:S(2)}) %collective-permute-start.32) | collective-permute-done | bytes 131104 | tf_op jit(solution)/shard_map/ppermute | solution.py:54
  111.5 1.9 %collective-permute-done.33 = bf16[32,2048]{1,0:T(8,128)(2,1)S(1)} collective-permute-done((bf16[32,2048]{1,0:T(8,128)(2,1)S(1)}, bf16[32,2048]{1,0:T(8,128)(2,1)S(1)}, u32[]{:S(2)}, u32[]{:S(2)}) %collective-permute-start.33) | collective-permute-done | bytes 131104 | tf_op jit(solution)/shard_map/ppermute | solution.py:54
  113.5 3.4 %collective-permute-start.34 = (bf16[16,2048]{1,0:T(8,128)(2,1)S(1)}, bf16[16,2048]{1,0:T(8,128)(2,1)S(1)}, u32[]{:S(2)}, u32[]{:S(2)}) collective-permute-start(bf16[16,2048]{1,0:T(8,128)(2,1)S(1)} %get-tuple-element.64), channel_id=1, source_target_pairs={{0,8},{2,10},{4,12},{6,14},{8,0},{10,2},{12,4},{14,6},{1,9},{3,11}... | collective-permute-start | bytes 196616 | tf_op jit(solution)/shard_map/ppermute | solution.py:54
  117.1 2.1 %collective-permute-done.34 = bf16[16,2048]{1,0:T(8,128)(2,1)S(1)} collective-permute-done((bf16[16,2048]{1,0:T(8,128)(2,1)S(1)}, bf16[16,2048]{1,0:T(8,128)(2,1)S(1)}, u32[]{:S(2)}, u32[]{:S(2)}) %collective-permute-start.34) | collective-permute-done | bytes 65568 | tf_op jit(solution)/shard_map/ppermute | solution.py:54
  119.2 0.9 convolution_convert_fusion
  (112 shorter events, 5.8 us)
Async XLA Ops:
  0.6 23.9 %copy-start = (bf16[4096,256]{1,0:T(8,128)(2,1)S(1)}, bf16[4096,256]{1,0:T(8,128)(2,1)}, u32[]{:S(2)}) copy-start(bf16[4096,256]{1,0:T(8,128)(2,1)} %param.26) | copy-start | bytes 6291460
  0.6 18.4 %copy-start.9 = (bf16[32,2048]{1,0:T(8,128)(2,1)S(1)}, bf16[32,2048]{1,0:T(8,128)(2,1)}, u32[]{:S(2)}) copy-start(bf16[32,2048]{1,0:T(8,128)(2,1)} %param.21) | copy-start | bytes 393220
  0.7 3.2 %collective-permute-start = (bf16[32,2048]{1,0:T(8,128)(2,1)}, bf16[32,2048]{1,0:T(8,128)(2,1)S(1)}, u32[]{:S(2)}, u32[]{:S(2)}) collective-permute-start(bf16[32,2048]{1,0:T(8,128)(2,1)} %param.21), channel_id=1, source_target_pairs={{0,1},{1,0},{2,3},{3,2},{4,5},{5,4},{6,7},{7,6},{8,9},{9,8},{10,11... | collective-permute-start | bytes 393224 | tf_op jit(solution)/shard_map/ppermute | solution.py:50
  1.2 6.2 %collective-permute-start.4 = (bf16[32,2048]{1,0:T(8,128)(2,1)}, bf16[32,2048]{1,0:T(8,128)(2,1)S(1)}, u32[]{:S(2)}, u32[]{:S(2)}) collective-permute-start(bf16[32,2048]{1,0:T(8,128)(2,1)} %param.21), channel_id=1, source_target_pairs={{0,4},{1,3},{2,0},{3,7},{4,8},{5,1},{6,2},{7,11},{8,12},{9,5},{10,... | collective-permute-start | bytes 393224 | tf_op jit(solution)/shard_map/ppermute | solution.py:74
  3.8 5.2 %collective-permute-start.1 = (bf16[32,2048]{1,0:T(8,128)(2,1)S(1)}, bf16[32,2048]{1,0:T(8,128)(2,1)S(1)}, u32[]{:S(2)}, u32[]{:S(2)}) collective-permute-start(bf16[32,2048]{1,0:T(8,128)(2,1)S(1)} %collective-permute-done), channel_id=1, source_target_pairs={{0,4},{1,3},{2,0},{3,7},{4,8},{5,1},{6,2},{7,11},{8,12},{9,5},{10,... | collective-permute-start | bytes 393224 | tf_op jit(solution)/shard_map/ppermute | solution.py:74
  7.4 5.0 %collective-permute-start.5 = (bf16[32,2048]{1,0:T(8,128)(2,1)S(1)}, bf16[32,2048]{1,0:T(8,128)(2,1)S(1)}, u32[]{:S(2)}, u32[]{:S(2)}) collective-permute-start(bf16[32,2048]{1,0:T(8,128)(2,1)S(1)} %collective-permute-done.4), channel_id=1, source_target_pairs={{0,4},{1,3},{2,0},{3,7},{4,8},{5,1},{6,2},{7,11},{8,12},{9,5},{10,... | collective-permute-start | bytes 393224 | tf_op jit(solution)/shard_map/ppermute | solution.py:74
  9.1 5.0 %collective-permute-start.2 = (bf16[32,2048]{1,0:T(8,128)(2,1)S(1)}, bf16[32,2048]{1,0:T(8,128)(2,1)S(1)}, u32[]{:S(2)}, u32[]{:S(2)}) collective-permute-start(bf16[32,2048]{1,0:T(8,128)(2,1)S(1)} %collective-permute-done.1), channel_id=1, source_target_pairs={{0,4},{1,3},{2,0},{3,7},{4,8},{5,1},{6,2},{7,11},{8,12},{9,5},{10,... | collective-permute-start | bytes 393224 | tf_op jit(solution)/shard_map/ppermute | solution.py:74
  12.4 5.0 %collective-permute-start.6 = (bf16[32,2048]{1,0:T(8,128)(2,1)S(1)}, bf16[32,2048]{1,0:T(8,128)(2,1)S(1)}, u32[]{:S(2)}, u32[]{:S(2)}) collective-permute-start(bf16[32,2048]{1,0:T(8,128)(2,1)S(1)} %collective-permute-done.5), channel_id=1, source_target_pairs={{0,4},{1,3},{2,0},{3,7},{4,8},{5,1},{6,2},{7,11},{8,12},{9,5},{10,... | collective-permute-start | bytes 393224 | tf_op jit(solution)/shard_map/ppermute | solution.py:74
  14.0 5.0 %collective-permute-start.3 = (bf16[32,2048]{1,0:T(8,128)(2,1)S(1)}, bf16[32,2048]{1,0:T(8,128)(2,1)S(1)}, u32[]{:S(2)}, u32[]{:S(2)}) collective-permute-start(bf16[32,2048]{1,0:T(8,128)(2,1)S(1)} %collective-permute-done.2), channel_id=1, source_target_pairs={{0,4},{1,3},{2,0},{3,7},{4,8},{5,1},{6,2},{7,11},{8,12},{9,5},{10,... | collective-permute-start | bytes 393224 | tf_op jit(solution)/shard_map/ppermute | solution.py:74
  17.4 5.0 %collective-permute-start.8 = (bf16[32,2048]{1,0:T(8,128)(2,1)S(1)}, bf16[32,2048]{1,0:T(8,128)(2,1)S(1)}, u32[]{:S(2)}, u32[]{:S(2)}) collective-permute-start(bf16[32,2048]{1,0:T(8,128)(2,1)S(1)} %collective-permute-done.6), channel_id=1, source_target_pairs={{0,4},{1,3},{2,0},{3,7},{4,8},{5,1},{6,2},{7,11},{8,12},{9,5},{10,... | collective-permute-start | bytes 393224 | tf_op jit(solution)/shard_map/ppermute | solution.py:74
  19.2 4.6 %collective-permute-start.7 = (bf16[96,4096]{1,0:T(8,128)(2,1)S(1)}, bf16[96,4096]{1,0:T(8,128)(2,1)S(1)}, u32[]{:S(2)}, u32[]{:S(2)}) collective-permute-start(bf16[96,4096]{1,0:T(8,128)(2,1)S(1)} %maximum_maximum_fusion), channel_id=1, source_target_pairs={{0,1},{1,0},{2,3},{3,2},{4,5},{5,4},{6,7},{7,6},{8,9},{9,8},{10,11... | collective-permute-start | bytes 2359304 | tf_op jit(solution)/shard_map/ppermute | solution.py:50
  22.4 1.3 %collective-permute-start.9 = (bf16[32,2048]{1,0:T(8,128)(2,1)S(1)}, bf16[32,2048]{1,0:T(8,128)(2,1)S(1)}, u32[]{:S(2)}, u32[]{:S(2)}) collective-permute-start(bf16[32,2048]{1,0:T(8,128)(2,1)S(1)} %collective-permute-done.8), channel_id=1, source_target_pairs={{0,1},{1,0},{2,3},{3,2},{4,5},{5,4},{6,7},{7,6},{8,9},{9,8},{10,11... | collective-permute-start | bytes 393224 | tf_op jit(solution)/shard_map/ppermute | solution.py:50
  23.8 0.7 copy-start.16
  24.0 2.1 %copy-start.8 = (bf16[256,4096]{1,0:T(8,128)(2,1)}, bf16[256,4096]{1,0:T(8,128)(2,1)S(1)}, u32[]{:S(2)}) copy-start(bf16[256,4096]{1,0:T(8,128)(2,1)S(1)} %maximum_dynamic-update-slice_fusion.4) | copy-start | bytes 6291460
  24.6 0.8 copy-start.14
  24.6 1.1 copy-start.12
  24.6 1.3 %copy-start.13 = (bf16[256,32]{0,1:T(8,128)(2,1)S(1)}, bf16[256,32]{0,1:T(8,128)(2,1)}, u32[]{:S(2)}) copy-start(bf16[256,32]{0,1:T(8,128)(2,1)} %param.31) | copy-start | bytes 49156
  26.9 1.5 %collective-permute-start.10 = (bf16[128,547]{1,0:T(8,128)(2,1)S(1)}, bf16[128,547]{1,0:T(8,128)(2,1)S(1)}, u32[]{:S(2)}, u32[]{:S(2)}) collective-permute-start(bf16[128,547]{1,0:T(8,128)(2,1)S(1)} %dynamic-slice_convert_fusion.1), channel_id=1, source_target_pairs={{0,1},{1,0},{2,3},{3,2},{4,5},{5,4},{6,7},{7,6},{8,9},{9,8},{10,11... | collective-permute-start | bytes 420104 | tf_op jit(solution)/shard_map/ppermute | solution.py:50
  27.1 30.8 %collective-permute-start.17 = (bf16[256,4096]{1,0:T(8,128)(2,1)}, bf16[256,4096]{1,0:T(8,128)(2,1)}, u32[]{:S(2)}, u32[]{:S(2)}) collective-permute-start(bf16[256,4096]{1,0:T(8,128)(2,1)} %wg_ref.1), channel_id=1, source_target_pairs={{0,1},{1,0},{2,3},{3,2},{4,5},{5,4},{6,7},{7,6},{8,9},{9,8},{10,11... | collective-permute-start | bytes 6291464 | tf_op jit(solution)/shard_map/ppermute | solution.py:50
  28.4 5.2 %collective-permute-start.11 = (bf16[64,547]{1,0:T(8,128)(2,1)S(1)}, bf16[64,547]{1,0:T(8,128)(2,1)S(1)}, u32[]{:S(2)}, u32[]{:S(2)}) collective-permute-start(bf16[64,547]{1,0:T(8,128)(2,1)S(1)} %dynamic-slice_convert_fusion.2), channel_id=1, source_target_pairs={{0,2},{2,0},{4,6},{6,4},{8,10},{10,8},{12,14},{14,12},{1,3},{3,1},... | collective-permute-start | bytes 210056 | tf_op jit(solution)/shard_map/ppermute | solution.py:54
  33.6 17.9 %copy-start.1 = (f32[32,16,256]{2,1,0:T(8,128)S(1)}, f32[32,16,256]{2,1,0:T(8,128)}, u32[]{:S(2)}) copy-start(f32[32,16,256]{2,1,0:T(8,128)} %state_ref.1) | copy-start | bytes 1572868
  33.6 17.9 %copy-start.2 = (bf16[512,256]{1,0:T(8,128)(2,1)S(1)}, bf16[512,256]{1,0:T(8,128)(2,1)}, u32[]{:S(2)}) copy-start(bf16[512,256]{1,0:T(8,128)(2,1)} %dt_proj.1) | copy-start | bytes 786436
  33.6 17.9 %copy-start.4 = (f32[16,256]{1,0:T(8,128)S(1)}, f32[16,256]{1,0:T(8,128)}, u32[]{:S(2)}) copy-start(f32[16,256]{1,0:T(8,128)} %a_rate.1) | copy-start | bytes 49156
  33.6 17.9 %copy-start.6 = (f32[256]{0:T(256)S(1)}, f32[256]{0:T(256)}, u32[]{:S(2)}) copy-start(f32[256]{0:T(256)} %param.33) | copy-start | bytes 3076
  33.6 17.9 %copy-start.7 = (f32[256]{0:T(256)S(1)}, f32[256]{0:T(256)}, u32[]{:S(2)}) copy-start(f32[256]{0:T(256)} %param.35) | copy-start | bytes 3076
  33.7 4.5 %collective-permute-start.12 = (bf16[64,547]{1,0:T(8,128)(2,1)S(1)}, bf16[64,547]{1,0:T(8,128)(2,1)S(1)}, u32[]{:S(2)}, u32[]{:S(2)}) collective-permute-start(bf16[64,547]{1,0:T(8,128)(2,1)S(1)} %fusion.37), channel_id=1, source_target_pairs={{0,4},{2,6},{4,0},{6,2},{8,12},{10,14},{12,8},{14,10},{1,5},{3,7},... | collective-permute-start | bytes 210056 | tf_op jit(solution)/shard_map/ppermute | solution.py:54
  38.2 5.4 %collective-permute-start.13 = (bf16[64,547]{1,0:T(8,128)(2,1)S(1)}, bf16[64,547]{1,0:T(8,128)(2,1)S(1)}, u32[]{:S(2)}, u32[]{:S(2)}) collective-permute-start(bf16[64,547]{1,0:T(8,128)(2,1)S(1)} %fusion.35), channel_id=1, source_target_pairs={{0,8},{2,10},{4,12},{6,14},{8,0},{10,2},{12,4},{14,6},{1,9},{3,11}... | collective-permute-start | bytes 210056 | tf_op jit(solution)/shard_map/ppermute | solution.py:54
  44.3 4.7 %collective-permute-start.14 = (bf16[64,547]{1,0:T(8,128)(2,1)}, bf16[64,547]{1,0:T(8,128)(2,1)S(1)}, u32[]{:S(2)}, u32[]{:S(2)}) collective-permute-start(bf16[64,547]{1,0:T(8,128)(2,1)} %get-tuple-element.45), channel_id=1, source_target_pairs={{0,2},{2,0},{4,6},{6,4},{8,10},{10,8},{12,14},{14,12},{1,3},{3,1},... | collective-permute-start | bytes 210056 | tf_op jit(solution)/shard_map/ppermute | solution.py:54
  49.0 1.6 %collective-permute-start.15 = (bf16[128,547]{1,0:T(8,128)(2,1)S(1)}, bf16[128,547]{1,0:T(8,128)(2,1)}, u32[]{:S(2)}, u32[]{:S(2)}) collective-permute-start(bf16[128,547]{1,0:T(8,128)(2,1)S(1)} %constant_dynamic-update-slice_fusion.2), channel_id=1, source_target_pairs={{0,1},{1,0},{2,3},{3,2},{4,5},{5,4},{6,7},{7,6},{8,9},{9,8},{10,11... | collective-permute-start | bytes 420104 | tf_op jit(solution)/shard_map/ppermute | solution.py:50
  51.6 1.0 copy-start.3
  56.5 1.4 %collective-permute-start.16 = (bf16[256,256]{1,0:T(8,128)(2,1)S(1)}, bf16[256,256]{1,0:T(8,128)(2,1)S(1)}, u32[]{:S(2)}, u32[]{:S(2)}) collective-permute-start(bf16[256,256]{1,0:T(8,128)(2,1)S(1)} %convert_element_type.145.g_ref), channel_id=1, source_target_pairs={{0,1},{1,0},{2,3},{3,2},{4,5},{5,4},{6,7},{7,6},{8,9},{9,8},{10,11... | collective-permute-start | bytes 393224 | tf_op jit(solution)/shard_map/ppermute | solution.py:50
  61.2 17.0 %copy-start.10 = (bf16[32,2048]{1,0:T(8,128)(2,1)S(1)}, bf16[32,2048]{1,0:T(8,128)(2,1)}, u32[]{:S(2)}) copy-start(bf16[32,2048]{1,0:T(8,128)(2,1)} %param.21) | copy-start | bytes 393220
  61.3 20.4 %copy-start.11 = (bf16[32,2048]{1,0:T(8,128)(2,1)S(1)}, bf16[32,2048]{1,0:T(8,128)(2,1)}, u32[]{:S(2)}) copy-start(bf16[32,2048]{1,0:T(8,128)(2,1)} %dynamic_slice.27) | copy-start | bytes 393220
  61.3 5.0 %collective-permute-start.18 = (bf16[32,2048]{1,0:T(8,128)(2,1)S(1)}, bf16[32,2048]{1,0:T(8,128)(2,1)S(1)}, u32[]{:S(2)}, u32[]{:S(2)}) collective-permute-start(bf16[32,2048]{1,0:T(8,128)(2,1)S(1)} %get-tuple-element.34), channel_id=1, source_target_pairs={{0,4},{1,3},{2,0},{3,7},{4,8},{5,1},{6,2},{7,11},{8,12},{9,5},{10,... | collective-permute-start | bytes 393224 | tf_op jit(solution)/shard_map/ppermute | solution.py:310
  63.0 5.0 %collective-permute-start.22 = (bf16[32,2048]{1,0:T(8,128)(2,1)S(1)}, bf16[32,2048]{1,0:T(8,128)(2,1)S(1)}, u32[]{:S(2)}, u32[]{:S(2)}) collective-permute-start(bf16[32,2048]{1,0:T(8,128)(2,1)S(1)} %slice.221), channel_id=1, source_target_pairs={{0,4},{1,3},{2,0},{3,7},{4,8},{5,1},{6,2},{7,11},{8,12},{9,5},{10,... | collective-permute-start | bytes 393224 | tf_op jit(solution)/shard_map/ppermute | solution.py:310
  66.3 5.0 %collective-permute-start.19 = (bf16[32,2048]{1,0:T(8,128)(2,1)S(1)}, bf16[32,2048]{1,0:T(8,128)(2,1)S(1)}, u32[]{:S(2)}, u32[]{:S(2)}) collective-permute-start(bf16[32,2048]{1,0:T(8,128)(2,1)S(1)} %add_convert_fusion.6), channel_id=1, source_target_pairs={{0,4},{1,3},{2,0},{3,7},{4,8},{5,1},{6,2},{7,11},{8,12},{9,5},{10,... | collective-permute-start | bytes 393224 | tf_op jit(solution)/shard_map/ppermute | solution.py:310
  68.1 5.0 %collective-permute-start.23 = (bf16[32,2048]{1,0:T(8,128)(2,1)S(1)}, bf16[32,2048]{1,0:T(8,128)(2,1)S(1)}, u32[]{:S(2)}, u32[]{:S(2)}) collective-permute-start(bf16[32,2048]{1,0:T(8,128)(2,1)S(1)} %add_convert_fusion.3), channel_id=1, source_target_pairs={{0,4},{1,3},{2,0},{3,7},{4,8},{5,1},{6,2},{7,11},{8,12},{9,5},{10,... | collective-permute-start | bytes 393224 | tf_op jit(solution)/shard_map/ppermute | solution.py:310
  71.4 5.0 %collective-permute-start.20 = (bf16[32,2048]{1,0:T(8,128)(2,1)S(1)}, bf16[32,2048]{1,0:T(8,128)(2,1)S(1)}, u32[]{:S(2)}, u32[]{:S(2)}) collective-permute-start(bf16[32,2048]{1,0:T(8,128)(2,1)S(1)} %add_convert_fusion.5), channel_id=1, source_target_pairs={{0,4},{1,3},{2,0},{3,7},{4,8},{5,1},{6,2},{7,11},{8,12},{9,5},{10,... | collective-permute-start | bytes 393224 | tf_op jit(solution)/shard_map/ppermute | solution.py:310
  73.1 5.1 %collective-permute-start.24 = (bf16[32,2048]{1,0:T(8,128)(2,1)S(1)}, bf16[32,2048]{1,0:T(8,128)(2,1)S(1)}, u32[]{:S(2)}, u32[]{:S(2)}) collective-permute-start(bf16[32,2048]{1,0:T(8,128)(2,1)S(1)} %add_convert_fusion.2), channel_id=1, source_target_pairs={{0,4},{1,3},{2,0},{3,7},{4,8},{5,1},{6,2},{7,11},{8,12},{9,5},{10,... | collective-permute-start | bytes 393224 | tf_op jit(solution)/shard_map/ppermute | solution.py:310
  76.4 5.2 %collective-permute-start.21 = (bf16[32,2048]{1,0:T(8,128)(2,1)S(1)}, bf16[32,2048]{1,0:T(8,128)(2,1)S(1)}, u32[]{:S(2)}, u32[]{:S(2)}) collective-permute-start(bf16[32,2048]{1,0:T(8,128)(2,1)S(1)} %add_convert_fusion.4), channel_id=1, source_target_pairs={{0,4},{1,3},{2,0},{3,7},{4,8},{5,1},{6,2},{7,11},{8,12},{9,5},{10,... | collective-permute-start | bytes 393224 | tf_op jit(solution)/shard_map/ppermute | solution.py:310
  78.3 3.4 %collective-permute-start.25 = (bf16[32,2048]{1,0:T(8,128)(2,1)S(1)}, bf16[32,2048]{1,0:T(8,128)(2,1)S(1)}, u32[]{:S(2)}, u32[]{:S(2)}) collective-permute-start(bf16[32,2048]{1,0:T(8,128)(2,1)S(1)} %collective-permute-done.24), channel_id=1, source_target_pairs={{0,1},{1,0},{2,3},{3,2},{4,5},{5,4},{6,7},{7,6},{8,9},{9,8},{10,11... | collective-permute-start | bytes 393224 | tf_op jit(solution)/shard_map/ppermute | solution.py:50
  81.9 6.2 %collective-permute-start.26 = (bf16[32,2048]{1,0:T(8,128)(2,1)S(1)}, bf16[32,2048]{1,0:T(8,128)(2,1)S(1)}, u32[]{:S(2)}, u32[]{:S(2)}) collective-permute-start(bf16[32,2048]{1,0:T(8,128)(2,1)S(1)} %add_convert_fusion.1), channel_id=1, source_target_pairs={{0,2},{2,0},{4,6},{6,4},{8,10},{10,8},{12,14},{14,12},{1,3},{3,1},... | collective-permute-start | bytes 393224 | tf_op jit(solution)/shard_map/ppermute | solution.py:54
  82.7 5.4 %collective-permute-start.27 = (bf16[32,2048]{1,0:T(8,128)(2,1)S(1)}, bf16[32,2048]{1,0:T(8,128)(2,1)S(1)}, u32[]{:S(2)}, u32[]{:S(2)}) collective-permute-start(bf16[32,2048]{1,0:T(8,128)(2,1)S(1)} %add_convert_fusion.1), channel_id=1, source_target_pairs={{0,4},{2,6},{4,0},{6,2},{8,12},{10,14},{12,8},{14,10},{1,5},{3,7},... | collective-permute-start | bytes 393224 | tf_op jit(solution)/shard_map/ppermute | solution.py:54
  84.3 5.9 %collective-permute-start.28 = (bf16[32,2048]{1,0:T(8,128)(2,1)S(1)}, bf16[32,2048]{1,0:T(8,128)(2,1)S(1)}, u32[]{:S(2)}, u32[]{:S(2)}) collective-permute-start(bf16[32,2048]{1,0:T(8,128)(2,1)S(1)} %add_convert_fusion.1), channel_id=1, source_target_pairs={{0,6},{2,4},{4,2},{6,0},{8,14},{10,12},{12,10},{14,8},{1,7},{3,5},... | collective-permute-start | bytes 393224 | tf_op jit(solution)/shard_map/ppermute | solution.py:54
  91.0 2.1 %collective-permute-start.29 = (bf16[128,2048]{1,0:T(8,128)(2,1)}, bf16[128,2048]{1,0:T(8,128)(2,1)S(1)}, u32[]{:S(2)}, u32[]{:S(2)}) collective-permute-start(bf16[128,2048]{1,0:T(8,128)(2,1)} %pad_maximum_fusion.2), channel_id=1, source_target_pairs={{0,1},{1,0},{2,3},{3,2},{4,5},{5,4},{6,7},{7,6},{8,9},{9,8},{10,11... | collective-permute-start | bytes 1572872 | tf_op jit(solution)/shard_map/ppermute | solution.py:50
  93.4 0.7 copy-start.5
  94.1 7.7 %copy-start.15 = (bf16[4096,16]{0,1:T(8,128)(2,1)S(1)}, bf16[4096,16]{0,1:T(8,128)(2,1)}, u32[]{:S(2)}) copy-start(bf16[4096,16]{0,1:T(8,128)(2,1)} %param.38) | copy-start | bytes 393220
  101.6 2.0 %collective-permute-start.30 = (bf16[128,2048]{1,0:T(8,128)(2,1)S(1)}, bf16[128,2048]{1,0:T(8,128)(2,1)S(1)}, u32[]{:S(2)}, u32[]{:S(2)}) collective-permute-start(bf16[128,2048]{1,0:T(8,128)(2,1)S(1)} %dynamic-slice_convert_fusion), channel_id=1, source_target_pairs={{0,1},{1,0},{2,3},{3,2},{4,5},{5,4},{6,7},{7,6},{8,9},{9,8},{10,11... | collective-permute-start | bytes 1572872 | tf_op jit(solution)/shard_map/ppermute | solution.py:50
  103.8 5.6 %collective-permute-start.31 = (bf16[32,2048]{1,0:T(8,128)(2,1)S(1)}, bf16[32,2048]{1,0:T(8,128)(2,1)S(1)}, u32[]{:S(2)}, u32[]{:S(2)}) collective-permute-start(bf16[32,2048]{1,0:T(8,128)(2,1)S(1)} %get-tuple-element.48), channel_id=1, source_target_pairs={{0,2},{2,0},{4,6},{6,4},{8,10},{10,8},{12,14},{14,12},{1,3},{3,1},... | collective-permute-start | bytes 393224 | tf_op jit(solution)/shard_map/ppermute | solution.py:54
  105.1 6.4 %collective-permute-start.32 = (bf16[32,2048]{1,0:T(8,128)(2,1)S(1)}, bf16[32,2048]{1,0:T(8,128)(2,1)S(1)}, u32[]{:S(2)}, u32[]{:S(2)}) collective-permute-start(bf16[32,2048]{1,0:T(8,128)(2,1)S(1)} %get-tuple-element.50), channel_id=1, source_target_pairs={{0,4},{2,6},{4,0},{6,2},{8,12},{10,14},{12,8},{14,10},{1,5},{3,7},... | collective-permute-start | bytes 393224 | tf_op jit(solution)/shard_map/ppermute | solution.py:54
  105.8 7.6 %collective-permute-start.33 = (bf16[32,2048]{1,0:T(8,128)(2,1)S(1)}, bf16[32,2048]{1,0:T(8,128)(2,1)S(1)}, u32[]{:S(2)}, u32[]{:S(2)}) collective-permute-start(bf16[32,2048]{1,0:T(8,128)(2,1)S(1)} %get-tuple-element.49), channel_id=1, source_target_pairs={{0,6},{2,4},{4,2},{6,0},{8,14},{10,12},{12,10},{14,8},{1,7},{3,5},... | collective-permute-start | bytes 393224 | tf_op jit(solution)/shard_map/ppermute | solution.py:54
  113.5 5.7 %collective-permute-start.34 = (bf16[16,2048]{1,0:T(8,128)(2,1)S(1)}, bf16[16,2048]{1,0:T(8,128)(2,1)S(1)}, u32[]{:S(2)}, u32[]{:S(2)}) collective-permute-start(bf16[16,2048]{1,0:T(8,128)(2,1)S(1)} %get-tuple-element.64), channel_id=1, source_target_pairs={{0,8},{2,10},{4,12},{6,14},{8,0},{10,2},{12,4},{14,6},{1,9},{3,11}... | collective-permute-start | bytes 196616 | tf_op jit(solution)/shard_map/ppermute | solution.py:54

commit v4 on v3

--- a/solution.py
+++ b/solution.py
@@ -131,17 +131,47 @@
         flip *= 2
     keep = keep.astype(BF16)
     keep = join(keep, beside(over_expert(keep, 1, owners)), low)
-    return join(keep, over_cuts(keep), core), done
+    return (keep, over_cuts(keep)), done
 
 
 def scan_kernel(
-    total, dt_proj, dt_bias, u_ref, z_ref, state_ref, a_rate, d_skip, gated, new_state, b_all, c_all, dt_all
+    place_ref,
+    mine,
+    theirs,
+    dt_proj,
+    dt_bias,
+    u_ref,
+    z_hbm,
+    state_hbm,
+    a_rate,
+    d_skip,
+    gated,
+    new_state,
+    notes,
+    total,
+    z_ref,
+    state_ref,
+    b_all,
+    c_all,
+    dt_all,
+    sems,
 ):
+    fetches = [
+        pltpu.make_async_copy(state_hbm, state_ref, sems.at[0]),
+        pltpu.make_async_copy(z_hbm, z_ref, sems.at[1]),
+    ]
+    for fetch in fetches:
+        fetch.start()
     tokens, channels = u_ref.shape
     states = a_rate.shape[0]
     rank = dt_proj.shape[0]
+    count = tokens // 2
+    core = place_ref[place_ref.shape[0] - 1]
+    total[pl.ds(pl.multiple_of(core * count, count), count), :] = mine[...]
+    total[pl.ds(pl.multiple_of((1 - core) * count, count), count), :] = theirs[...]
     raw = jnp.dot(total[:, :rank], dt_proj[...], preferred_element_type=F32) + dt_bias[...]
     dt_all[...] = jnp.maximum(raw, 0.0) + jnp.log1p(jnp.exp(-jnp.abs(raw)))
+    notes[...] = total[:, rank + 2 * states :].astype(F32)
     ones = jnp.ones((states, channels), BF16)
     diagonal = lax.broadcasted_iota(jnp.int32, (tokens, states, states), 1) == lax.broadcasted_iota(
         jnp.int32, (tokens, states, states), 2
@@ -153,6 +183,8 @@
         )
         spread = jnp.where(diagonal, spread, 0.0).reshape(tokens * states, states).astype(BF16)
         dest[...] = jnp.dot(spread, ones, preferred_element_type=F32)
+    for fetch in fetches:
+        fetch.wait()
     rate = -a_rate[...]
     skip = d_skip[...]
 
@@ -176,27 +208,38 @@
     lax.fori_loop(0, tokens // DRAFT, request, 0, unroll=2)
 
 
-def scan(total, dt_proj, dt_bias, u, z, ssm_state, a_rate, d_skip):
+def scan(places, total, dt_proj, dt_bias, u, z, ssm_state, a_rate, d_skip):
     tokens, channels = u.shape
     states = a_rate.shape[0]
+    columns = total[0].shape[1]
+    extra = columns - dt_proj.shape[0] - 2 * states
     vmem = pl.BlockSpec(memory_space=pltpu.VMEM)
     return pl.pallas_call(
         scan_kernel,
         out_shape=(
             jax.ShapeDtypeStruct((tokens, channels), F32),
             jax.ShapeDtypeStruct(ssm_state.shape, F32),
+            jax.ShapeDtypeStruct((tokens, extra), F32),
         ),
-        in_specs=[vmem] * 8,
-        out_specs=[vmem] * 2,
+        in_specs=[pl.BlockSpec(memory_space=pltpu.SMEM)]
+        + [vmem] * 5
+        + [pl.BlockSpec(memory_space=pltpu.HBM)] * 2
+        + [vmem] * 2,
+        out_specs=[vmem] * 3,
         scratch_shapes=[
+            pltpu.VMEM((tokens, columns), BF16),
+            pltpu.VMEM((tokens, channels), F32),
+            pltpu.VMEM(ssm_state.shape, F32),
             pltpu.VMEM((tokens * states, channels), F32),
             pltpu.VMEM((tokens * states, channels), F32),
             pltpu.VMEM((tokens, channels), F32),
+            pltpu.SemaphoreType.DMA((2,)),
         ],
         compiler_params=pltpu.CompilerParams(vmem_limit_bytes=VMEM_LIMIT),
         name="scan",
     )(
-        total,
+        places,
+        *total,
         dt_proj,
         dt_bias.reshape(1, -1),
         u,
@@ -318,7 +361,10 @@
     return own + acc_a.astype(F32) + over_cuts(acc_b).astype(F32)
 
 
-def experts_kernel(tiles, x_ref, gain_ref, wg_hbm, wu_hbm, wd_hbm, out_ref, wg, wu, wd, sems):
+def experts_kernel(tiles, pieces, place_ref, *refs):
+    own, refs = refs[:pieces], refs[pieces:]
+    other, refs = refs[:pieces], refs[pieces:]
+    gain_ref, wg_hbm, wu_hbm, wd_hbm, out_ref, x_ref, wg, wu, wd, sems = refs
     tile = wg.shape[2]
     copies = []
     for i in range(tiles):
@@ -331,38 +377,51 @@
             )
         )
     for group in copies:
-        for copy in group:
-            copy.start()
+        group[0].start()
+        group[1].start()
+    for group in copies:
+        group[2].start()
+    rows, width = own[0].shape
+    core = place_ref[place_ref.shape[0] - 1]
+    here = pl.ds(pl.multiple_of(core * width, 128), width)
+    there = pl.ds(pl.multiple_of((1 - core) * width, 128), width)
+    for i in range(pieces):
+        x_ref[i * rows : (i + 1) * rows, here] = own[i][...]
+        x_ref[i * rows : (i + 1) * rows, there] = other[i][...]
     values = x_ref[...].astype(F32)
     scale = lax.rsqrt(jnp.mean(values * values, axis=-1, keepdims=True) + 1e-05)
     x = (values * scale * gain_ref[...]).astype(BF16)
+    acts = []
     for i in range(tiles):
         copies[i][0].wait()
         gate = jnp.dot(x, wg[i], preferred_element_type=F32)
         copies[i][1].wait()
         upval = jnp.dot(x, wu[i], preferred_element_type=F32)
-        act = (gate * jax.nn.sigmoid(gate) * upval).astype(BF16)
+        acts.append((gate * jax.nn.sigmoid(gate) * upval).astype(BF16))
+    for i in range(tiles):
         copies[i][2].wait()
-        term = jnp.dot(act, wd[i], preferred_element_type=F32)
+        term = jnp.dot(acts[i], wd[i], preferred_element_type=F32)
         if i == 0:
             out_ref[...] = term
         else:
             out_ref[...] += term
 
 
-def run_experts(tokens, gain, w_gate, w_up, w_down):
-    count, width = tokens.shape
+def run_experts(places, own, other, gain, w_gate, w_up, w_down):
+    pieces = len(own)
+    count, width = pieces * own[0].shape[0], 2 * own[0].shape[1]
     hidden = w_gate.shape[1]
     tile = 256
     tiles = hidden // tile
     vmem = pl.BlockSpec(memory_space=pltpu.VMEM)
     hbm = pl.BlockSpec(memory_space=pltpu.HBM)
     return pl.pallas_call(
-        functools.partial(experts_kernel, tiles),
+        functools.partial(experts_kernel, tiles, pieces),
         out_shape=jax.ShapeDtypeStruct((count, width), F32),
-        in_specs=[vmem, vmem, hbm, hbm, hbm],
+        in_specs=[pl.BlockSpec(memory_space=pltpu.SMEM)] + [vmem] * (2 * pieces + 1) + [hbm] * 3,
         out_specs=vmem,
         scratch_shapes=[
+            pltpu.VMEM((count, width), BF16),
             pltpu.VMEM((tiles, width, tile), BF16),
             pltpu.VMEM((tiles, width, tile), BF16),
             pltpu.VMEM((tiles, tile, width), BF16),
@@ -370,7 +429,7 @@
         ],
         compiler_params=pltpu.CompilerParams(vmem_limit_bytes=48 << 20),
         name="experts",
-    )(tokens, gain.reshape(1, width), w_gate, w_up, w_down)
+    )(places, *own, *other, gain.reshape(1, width), w_gate, w_up, w_down)
 
 
 def on_device(
@@ -418,7 +477,6 @@
     u_act = jax.nn.silu(conv).astype(BF16)
     flat_u = u_act.reshape(requests * DRAFT, channels)
     rank = xproj_dt.shape[1]
-    carried = xproj_bc.shape[1]
     notes = find_slots(routes)
     slot = notes[:, 0]
     notes = jnp.where(core == 0, notes, 0.0)
@@ -448,11 +506,10 @@
         core,
         [lambda: jnp.dot(normed, in_z, preferred_element_type=F32)],
     )
-    gated, new_state = scan(
-        total, dt_proj, dt_bias, flat_u, z_gate, ssm_state, a_rate, d_skip
+    gated, new_state, notes = scan(
+        places, total, dt_proj, dt_bias, flat_u, z_gate, ssm_state, a_rate, d_skip
     )
     gated = gated.astype(BF16)
-    notes = total[:, rank + carried :]
     ids = (jnp.arange(tokens) // tok_count * tok_count).astype(jnp.int32)[:, None] + notes[
         :, :1
     ].astype(jnp.int32)
@@ -479,7 +536,7 @@
         x_partner,
         preferred_element_type=F32,
     )
-    route_rows = jnp.dot(rows_here, notes[:, 1:], preferred_element_type=F32).astype(jnp.int32)
+    route_rows = jnp.dot(rows_here, notes[:, 1:].astype(BF16), preferred_element_type=F32).astype(jnp.int32)
     mixed_half = scatter_sum(near, far, own_term, other, tok_count, owners, perm)
     stream_half = (x_rows + mixed_half).astype(BF16)
 
@@ -487,9 +544,8 @@
         return over_expert(value, flip, owners)
 
     pieces = [stream_half] + [exchange(stream_half, flip) for flip in range(1, holders)]
-    tokens_half = jnp.concatenate(pieces, axis=0)
-    routed = halves(tokens_half, over_cuts(tokens_half), core)
-    partial_out = run_experts(routed, moe_gain, w_gate, w_up, w_down)
+    others = [over_cuts(piece) for piece in pieces]
+    partial_out = run_experts(places, pieces, others, moe_gain, w_gate, w_up, w_down)
     count = partial_out.shape[0]
     mine = lax.dynamic_slice(partial_out, (0, core * half_width), (count, half_width))
     theirs = lax.dynamic_slice(partial_out, (0, (1 - core) * half_width), (count, half_width))
@@ -501,7 +557,7 @@
     expert_out = result.astype(BF16).astype(F32)
 
     logits = jnp.dot(
-        rms_norm(routed[:tok_count], moe_gain), router, preferred_element_type=F32
+        rms_norm(halves(stream_half, others[0], core), moe_gain), router, preferred_element_type=F32
     )
     all_labels = jnp.arange(router.shape[1], dtype=jnp.int32)
     which = (route_rows[:, :, None] == all_labels).astype(F32)

time: 120 us -> 117 us (0.975)
  local copies, waits for them, and re-layouts: 6.39 us -> 4.04 us
  waiting for transfers between devices: 44 us -> 42.3 us
  Pallas kernels: 14.9 us -> 16.2 us
    unnamed x36 -> x32, local copies, waits for them, and re-layouts: 3.28 us -> 1.92 us
    ppermute x10 -> x13, waiting for transfers between devices: 7.93 us -> 8.34 us  [over_cuts(): return lax.ppermute(value, 'cuts', [(0, 1), (1, 0)])]
  transfers between devices with their start and end apart: 35 -> 38, of which waited for: 24 -> 27; matrix products, arithmetic and copies ran while one was open for 8% -> 8% of each run, Pallas kernels for 3% -> 4%
where the time goes in v4:
time: 117 us
  starting transfers between devices  43.6 us (37%)
  waiting for transfers between devices  42.3 us (36%)
  Pallas kernels  16.2 us (14%)
  matrix products  5.99 us (5%)
  local copies, waits for them, and re-layouts  4.04 us (3%)
  other arithmetic  3.22 us (3%)
  between operations  1.22 us (1%)
    ppermute x11, waiting for transfers between devices, over_expert(): return lax.ppermute(value, 'expert', [(i, i ^ flip) for i in range(owners)])  22.3 us
    ppermute x11, starting transfers between devices, over_expert(): return lax.ppermute(value, 'expert', [(i, i ^ flip) for i in range(owners)])  17.8 us
    ppermute x7, starting transfers between devices, send(): return lax.ppermute(value, ('expert', 'cuts'), perm)  12 us
    ppermute x7, starting transfers between devices, send(): return lax.ppermute(value.astype(BF16), ('expert', 'cuts'), perm)  11.7 us
    ppermute x13, waiting for transfers between devices, over_cuts(): return lax.ppermute(value, 'cuts', [(0, 1), (1, 0)])  8.34 us
    pallas_call x1, Pallas kernels, run_experts(): pl.pallas_call(functools.partial(experts_kernel, tiles, pieces), out_shap...  7.69 us
    ppermute x7, waiting for transfers between devices, send(): return lax.ppermute(value.astype(BF16), ('expert', 'cuts'), perm)  6.89 us
    pallas_call x1, Pallas kernels, scan(): pl.pallas_call(scan_kernel, out_shape=(jax.ShapeDtypeStruct((tokens, chan...  5 us
  transfers between devices with their start and end apart: 38, of which 27 were waited for; matrix products, arithmetic and copies ran while one was open for 8% of the time, Pallas kernels for 4%

profile of v4, /device:TPU:0, one launch (start us, length us, event | category | flops | bytes accessed | tf_op | source)
XLA Modules:
  0.0 116.7 jit_solution(12493082260244165929)
XLA Ops:
  0.6 0.5 collective-permute-start
  1.2 2.6 %collective-permute-start.4 = (bf16[32,2048]{1,0:T(8,128)(2,1)}, bf16[32,2048]{1,0:T(8,128)(2,1)S(1)}, u32[]{:S(2)}, u32[]{:S(2)}) collective-permute-start(bf16[32,2048]{1,0:T(8,128)(2,1)} %param.21), channel_id=1, source_target_pairs={{0,4},{1,3},{2,0},{3,7},{4,8},{5,1},{6,2},{7,11},{8,12},{9,5},{10,... | collective-permute-start | bytes 393224 | tf_op jit(solution)/shard_map/ppermute | solution.py:74
  3.8 1.6 %collective-permute-start.1 = (bf16[32,2048]{1,0:T(8,128)(2,1)S(1)}, bf16[32,2048]{1,0:T(8,128)(2,1)S(1)}, u32[]{:S(2)}, u32[]{:S(2)}) collective-permute-start(bf16[32,2048]{1,0:T(8,128)(2,1)S(1)} %collective-permute-done), channel_id=1, source_target_pairs={{0,4},{1,3},{2,0},{3,7},{4,8},{5,1},{6,2},{7,11},{8,12},{9,5},{10,... | collective-permute-start | bytes 393224 | tf_op jit(solution)/shard_map/ppermute | solution.py:74
  5.4 0.8 copy.33.routes_ref
  6.4 1.0 copy.34
  7.5 1.6 %collective-permute-start.5 = (bf16[32,2048]{1,0:T(8,128)(2,1)S(1)}, bf16[32,2048]{1,0:T(8,128)(2,1)S(1)}, u32[]{:S(2)}, u32[]{:S(2)}) collective-permute-start(bf16[32,2048]{1,0:T(8,128)(2,1)S(1)} %collective-permute-done.4), channel_id=1, source_target_pairs={{0,4},{1,3},{2,0},{3,7},{4,8},{5,1},{6,2},{7,11},{8,12},{9,5},{10,... | collective-permute-start | bytes 393224 | tf_op jit(solution)/shard_map/ppermute | solution.py:74
  9.1 1.5 %collective-permute-start.2 = (bf16[32,2048]{1,0:T(8,128)(2,1)S(1)}, bf16[32,2048]{1,0:T(8,128)(2,1)S(1)}, u32[]{:S(2)}, u32[]{:S(2)}) collective-permute-start(bf16[32,2048]{1,0:T(8,128)(2,1)S(1)} %collective-permute-done.1), channel_id=1, source_target_pairs={{0,4},{1,3},{2,0},{3,7},{4,8},{5,1},{6,2},{7,11},{8,12},{9,5},{10,... | collective-permute-start | bytes 393224 | tf_op jit(solution)/shard_map/ppermute | solution.py:74
  10.6 1.8 %collective-permute-done.5 = bf16[32,2048]{1,0:T(8,128)(2,1)S(1)} collective-permute-done((bf16[32,2048]{1,0:T(8,128)(2,1)S(1)}, bf16[32,2048]{1,0:T(8,128)(2,1)S(1)}, u32[]{:S(2)}, u32[]{:S(2)}) %collective-permute-start.5) | collective-permute-done | bytes 131104 | tf_op jit(solution)/shard_map/ppermute | solution.py:74
  12.5 1.6 %collective-permute-start.6 = (bf16[32,2048]{1,0:T(8,128)(2,1)S(1)}, bf16[32,2048]{1,0:T(8,128)(2,1)S(1)}, u32[]{:S(2)}, u32[]{:S(2)}) collective-permute-start(bf16[32,2048]{1,0:T(8,128)(2,1)S(1)} %collective-permute-done.5), channel_id=1, source_target_pairs={{0,4},{1,3},{2,0},{3,7},{4,8},{5,1},{6,2},{7,11},{8,12},{9,5},{10,... | collective-permute-start | bytes 393224 | tf_op jit(solution)/shard_map/ppermute | solution.py:74
  14.1 1.5 %collective-permute-start.3 = (bf16[32,2048]{1,0:T(8,128)(2,1)S(1)}, bf16[32,2048]{1,0:T(8,128)(2,1)S(1)}, u32[]{:S(2)}, u32[]{:S(2)}) collective-permute-start(bf16[32,2048]{1,0:T(8,128)(2,1)S(1)} %collective-permute-done.2), channel_id=1, source_target_pairs={{0,4},{1,3},{2,0},{3,7},{4,8},{5,1},{6,2},{7,11},{8,12},{9,5},{10,... | collective-permute-start | bytes 393224 | tf_op jit(solution)/shard_map/ppermute | solution.py:74
  15.6 0.8 fusion.57
  16.4 1.0 collective-permute-done.6
  17.4 1.6 %collective-permute-start.8 = (bf16[32,2048]{1,0:T(8,128)(2,1)S(1)}, bf16[32,2048]{1,0:T(8,128)(2,1)S(1)}, u32[]{:S(2)}, u32[]{:S(2)}) collective-permute-start(bf16[32,2048]{1,0:T(8,128)(2,1)S(1)} %collective-permute-done.6), channel_id=1, source_target_pairs={{0,4},{1,3},{2,0},{3,7},{4,8},{5,1},{6,2},{7,11},{8,12},{9,5},{10,... | collective-permute-start | bytes 393224 | tf_op jit(solution)/shard_map/ppermute | solution.py:74
  19.0 0.9 broadcast_select_fusion.9
  20.4 2.0 %collective-permute-done.8 = bf16[32,2048]{1,0:T(8,128)(2,1)S(1)} collective-permute-done((bf16[32,2048]{1,0:T(8,128)(2,1)S(1)}, bf16[32,2048]{1,0:T(8,128)(2,1)S(1)}, u32[]{:S(2)}, u32[]{:S(2)}) %collective-permute-start.8) | collective-permute-done | bytes 131104 | tf_op jit(solution)/shard_map/ppermute | solution.py:74
  22.4 1.3 %collective-permute-done.9 = bf16[32,2048]{1,0:T(8,128)(2,1)S(1)} collective-permute-done((bf16[32,2048]{1,0:T(8,128)(2,1)S(1)}, bf16[32,2048]{1,0:T(8,128)(2,1)S(1)}, u32[]{:S(2)}, u32[]{:S(2)}) %collective-permute-start.9) | collective-permute-done | bytes 131104 | tf_op jit(solution)/shard_map/ppermute | solution.py:50
  24.0 0.5 fusion
  24.6 0.8 convolution_bitcast_fusion
  26.1 0.7 dynamic_slice.27
  27.1 0.4 collective-permute-start.17
  27.5 0.9 collective-permute-done.10
  28.5 1.5 %collective-permute-start.11 = (bf16[64,547]{1,0:T(8,128)(2,1)S(1)}, bf16[64,547]{1,0:T(8,128)(2,1)S(1)}, u32[]{:S(2)}, u32[]{:S(2)}) collective-permute-start(bf16[64,547]{1,0:T(8,128)(2,1)S(1)} %dynamic-slice_convert_fusion.2), channel_id=1, source_target_pairs={{0,2},{2,0},{4,6},{6,4},{8,10},{10,8},{12,14},{14,12},{1,3},{3,1},... | collective-permute-start | bytes 210056 | tf_op jit(solution)/shard_map/ppermute | solution.py:54
  30.0 3.0 %fusion.3.z_hbm = f32[256,256]{1,0:T(8,128)S(1)} fusion(bf16[4096,256]{1,0:T(8,128)(2,1)} %param.27, bf16[256,4096]{1,0:T(8,128)(2,1)} %copy-done.7, f32[4096]{0:T(1024)S(1)} %copy-done.14, f32[256]{0:T(256)S(1)} %add_rsqrt_fusion), kind=kOutput, calls=%fused_computation.19 | convolution fusion | flops 541065216 | bytes 4473856 | tf_op jit(solution)/shard_map/dot_general | solution.py:507
  33.1 1.6 %collective-permute-start.12 = (bf16[64,547]{1,0:T(8,128)(2,1)S(1)}, bf16[64,547]{1,0:T(8,128)(2,1)S(1)}, u32[]{:S(2)}, u32[]{:S(2)}) collective-permute-start(bf16[64,547]{1,0:T(8,128)(2,1)S(1)} %fusion.35), channel_id=1, source_target_pairs={{0,4},{2,6},{4,0},{6,2},{8,12},{10,14},{12,8},{14,10},{1,5},{3,7},... | collective-permute-start | bytes 210056 | tf_op jit(solution)/shard_map/ppermute | solution.py:54
  34.7 2.9 %collective-permute-done.12 = bf16[64,547]{1,0:T(8,128)(2,1)S(1)} collective-permute-done((bf16[64,547]{1,0:T(8,128)(2,1)S(1)}, bf16[64,547]{1,0:T(8,128)(2,1)S(1)}, u32[]{:S(2)}, u32[]{:S(2)}) %collective-permute-start.12) | collective-permute-done | bytes 70048 | tf_op jit(solution)/shard_map/ppermute | solution.py:54
  37.6 2.6 %collective-permute-start.13 = (bf16[64,547]{1,0:T(8,128)(2,1)S(1)}, bf16[64,547]{1,0:T(8,128)(2,1)S(1)}, u32[]{:S(2)}, u32[]{:S(2)}) collective-permute-start(bf16[64,547]{1,0:T(8,128)(2,1)S(1)} %fusion.34), channel_id=1, source_target_pairs={{0,8},{2,10},{4,12},{6,14},{8,0},{10,2},{12,4},{14,6},{1,9},{3,11}... | collective-permute-start | bytes 210056 | tf_op jit(solution)/shard_map/ppermute | solution.py:54
  40.2 2.8 %collective-permute-done.13 = bf16[64,547]{1,0:T(8,128)(2,1)S(1)} collective-permute-done((bf16[64,547]{1,0:T(8,128)(2,1)S(1)}, bf16[64,547]{1,0:T(8,128)(2,1)S(1)}, u32[]{:S(2)}, u32[]{:S(2)}) %collective-permute-start.13) | collective-permute-done | bytes 70048 | tf_op jit(solution)/shard_map/ppermute | solution.py:54
  43.1 1.5 %collective-permute-start.14 = (bf16[64,547]{1,0:T(8,128)(2,1)S(1)}, bf16[64,547]{1,0:T(8,128)(2,1)S(1)}, u32[]{:S(2)}, u32[]{:S(2)}) collective-permute-start(bf16[64,547]{1,0:T(8,128)(2,1)S(1)} %get-tuple-element.47), channel_id=1, source_target_pairs={{0,2},{2,0},{4,6},{6,4},{8,10},{10,8},{12,14},{14,12},{1,3},{3,1},... | collective-permute-start | bytes 210056 | tf_op jit(solution)/shard_map/ppermute | solution.py:54
  44.6 3.0 %collective-permute-done.14 = bf16[64,547]{1,0:T(8,128)(2,1)S(1)} collective-permute-done((bf16[64,547]{1,0:T(8,128)(2,1)S(1)}, bf16[64,547]{1,0:T(8,128)(2,1)S(1)}, u32[]{:S(2)}, u32[]{:S(2)}) %collective-permute-start.14) | collective-permute-done | bytes 70048 | tf_op jit(solution)/shard_map/ppermute | solution.py:54
  47.8 1.4 %collective-permute-done.15.theirs = bf16[128,547]{1,0:T(8,128)(2,1)} collective-permute-done((bf16[128,547]{1,0:T(8,128)(2,1)S(1)}, bf16[128,547]{1,0:T(8,128)(2,1)}, u32[]{:S(2)}, u32[]{:S(2)}) %collective-permute-start.15) | collective-permute-done | bytes 140064 | tf_op jit(solution)/shard_map/ppermute | solution.py:50
  49.2 5.0 %scan.1 = (f32[256,256]{1,0:T(8,128)S(1)}, f32[32,16,256]{2,1,0:T(8,128)}, f32[256,3]{1,0:T(8,128)S(1)}) custom-call(s32[6]{0:T(128)S(1)} %stack.32.place_ref, bf16[128,547]{1,0:T(8,128)(2,1)S(1)} %constant_dynamic-update-slice_fusion.mine, bf16[128,547]{1,0:T(8,128)(2,1)} %collective-permute-done.15.theirs, bf16[512,256]{1,0:T(8,128)(2,1)S(1)} %copy-done.2, ...), custom_call_target="tpu_custom_call" | custom-call | tf_op jit(solution)/shard_map/scan/pallas_call | solution.py:217
  54.7 1.0 collective-permute-done.16.h_ref
  55.7 3.3 %project.1 = (f32[96,2048]{1,0:T(8,128)S(1)}, bf16[32,2048]{1,0:T(8,128)(2,1)S(1)}, f32[32,2048]{1,0:T(8,128)S(1)}, f32[96,2048]{1,0:T(8,128)S(1)}) custom-call(s32[6]{0:T(128)S(1)} %stack.32.place_ref, s32[256,1]{1,0:T(8,128)S(1)} %get-tuple-element.45.id_ref, bf16[256,256]{1,0:T(8,128)(2,1)S(1)} %convert_element_type.146.g_ref, ...), custom_call_target="tpu_custom_call" | custom-call | tf_op jit(solution)/shard_map/project/pallas_call | solution.py:334
  59.0 1.6 %collective-permute-start.18 = (bf16[32,2048]{1,0:T(8,128)(2,1)S(1)}, bf16[32,2048]{1,0:T(8,128)(2,1)S(1)}, u32[]{:S(2)}, u32[]{:S(2)}) collective-permute-start(bf16[32,2048]{1,0:T(8,128)(2,1)S(1)} %get-tuple-element.36), channel_id=1, source_target_pairs={{0,4},{1,3},{2,0},{3,7},{4,8},{5,1},{6,2},{7,11},{8,12},{9,5},{10,... | collective-permute-start | bytes 393224 | tf_op jit(solution)/shard_map/ppermute | solution.py:353
  60.9 1.7 %collective-permute-start.22 = (bf16[32,2048]{1,0:T(8,128)(2,1)S(1)}, bf16[32,2048]{1,0:T(8,128)(2,1)S(1)}, u32[]{:S(2)}, u32[]{:S(2)}) collective-permute-start(bf16[32,2048]{1,0:T(8,128)(2,1)S(1)} %slice.204), channel_id=1, source_target_pairs={{0,4},{1,3},{2,0},{3,7},{4,8},{5,1},{6,2},{7,11},{8,12},{9,5},{10,... | collective-permute-start | bytes 393224 | tf_op jit(solution)/shard_map/ppermute | solution.py:353
  62.6 1.5 %collective-permute-done.18 = bf16[32,2048]{1,0:T(8,128)(2,1)S(1)} collective-permute-done((bf16[32,2048]{1,0:T(8,128)(2,1)S(1)}, bf16[32,2048]{1,0:T(8,128)(2,1)S(1)}, u32[]{:S(2)}, u32[]{:S(2)}) %collective-permute-start.18) | collective-permute-done | bytes 131104 | tf_op jit(solution)/shard_map/ppermute | solution.py:353
  64.1 1.6 %collective-permute-start.19 = (bf16[32,2048]{1,0:T(8,128)(2,1)S(1)}, bf16[32,2048]{1,0:T(8,128)(2,1)S(1)}, u32[]{:S(2)}, u32[]{:S(2)}) collective-permute-start(bf16[32,2048]{1,0:T(8,128)(2,1)S(1)} %add_convert_fusion.6), channel_id=1, source_target_pairs={{0,4},{1,3},{2,0},{3,7},{4,8},{5,1},{6,2},{7,11},{8,12},{9,5},{10,... | collective-permute-start | bytes 393224 | tf_op jit(solution)/shard_map/ppermute | solution.py:353
  66.0 1.7 %collective-permute-start.23 = (bf16[32,2048]{1,0:T(8,128)(2,1)S(1)}, bf16[32,2048]{1,0:T(8,128)(2,1)S(1)}, u32[]{:S(2)}, u32[]{:S(2)}) collective-permute-start(bf16[32,2048]{1,0:T(8,128)(2,1)S(1)} %add_convert_fusion.3), channel_id=1, source_target_pairs={{0,4},{1,3},{2,0},{3,7},{4,8},{5,1},{6,2},{7,11},{8,12},{9,5},{10,... | collective-permute-start | bytes 393224 | tf_op jit(solution)/shard_map/ppermute | solution.py:353
  67.7 1.5 %collective-permute-done.19 = bf16[32,2048]{1,0:T(8,128)(2,1)S(1)} collective-permute-done((bf16[32,2048]{1,0:T(8,128)(2,1)S(1)}, bf16[32,2048]{1,0:T(8,128)(2,1)S(1)}, u32[]{:S(2)}, u32[]{:S(2)}) %collective-permute-start.19) | collective-permute-done | bytes 131104 | tf_op jit(solution)/shard_map/ppermute | solution.py:353
  69.1 1.6 %collective-permute-start.20 = (bf16[32,2048]{1,0:T(8,128)(2,1)S(1)}, bf16[32,2048]{1,0:T(8,128)(2,1)S(1)}, u32[]{:S(2)}, u32[]{:S(2)}) collective-permute-start(bf16[32,2048]{1,0:T(8,128)(2,1)S(1)} %add_convert_fusion.5), channel_id=1, source_target_pairs={{0,4},{1,3},{2,0},{3,7},{4,8},{5,1},{6,2},{7,11},{8,12},{9,5},{10,... | collective-permute-start | bytes 393224 | tf_op jit(solution)/shard_map/ppermute | solution.py:353
  71.0 1.7 %collective-permute-start.24 = (bf16[32,2048]{1,0:T(8,128)(2,1)S(1)}, bf16[32,2048]{1,0:T(8,128)(2,1)S(1)}, u32[]{:S(2)}, u32[]{:S(2)}) collective-permute-start(bf16[32,2048]{1,0:T(8,128)(2,1)S(1)} %add_convert_fusion.2), channel_id=1, source_target_pairs={{0,4},{1,3},{2,0},{3,7},{4,8},{5,1},{6,2},{7,11},{8,12},{9,5},{10,... | collective-permute-start | bytes 393224 | tf_op jit(solution)/shard_map/ppermute | solution.py:353
  72.7 1.5 %collective-permute-done.20 = bf16[32,2048]{1,0:T(8,128)(2,1)S(1)} collective-permute-done((bf16[32,2048]{1,0:T(8,128)(2,1)S(1)}, bf16[32,2048]{1,0:T(8,128)(2,1)S(1)}, u32[]{:S(2)}, u32[]{:S(2)}) %collective-permute-start.20) | collective-permute-done | bytes 131104 | tf_op jit(solution)/shard_map/ppermute | solution.py:353
  74.2 1.8 %collective-permute-start.21 = (bf16[32,2048]{1,0:T(8,128)(2,1)S(1)}, bf16[32,2048]{1,0:T(8,128)(2,1)S(1)}, u32[]{:S(2)}, u32[]{:S(2)}) collective-permute-start(bf16[32,2048]{1,0:T(8,128)(2,1)S(1)} %add_convert_fusion.4), channel_id=1, source_target_pairs={{0,4},{1,3},{2,0},{3,7},{4,8},{5,1},{6,2},{7,11},{8,12},{9,5},{10,... | collective-permute-start | bytes 393224 | tf_op jit(solution)/shard_map/ppermute | solution.py:353
  76.3 1.1 collective-permute-done.25
  77.4 2.0 %collective-permute-done.21 = bf16[32,2048]{1,0:T(8,128)(2,1)S(1)} collective-permute-done((bf16[32,2048]{1,0:T(8,128)(2,1)S(1)}, bf16[32,2048]{1,0:T(8,128)(2,1)S(1)}, u32[]{:S(2)}, u32[]{:S(2)}) %collective-permute-start.21) | collective-permute-done | bytes 131104 | tf_op jit(solution)/shard_map/ppermute | solution.py:353
  79.4 1.5 %collective-permute-start.27 = (bf16[32,2048]{1,0:T(8,128)(2,1)S(1)}, bf16[32,2048]{1,0:T(8,128)(2,1)S(1)}, u32[]{:S(2)}, u32[]{:S(2)}) collective-permute-start(bf16[32,2048]{1,0:T(8,128)(2,1)S(1)} %add_convert_fusion.1.refs_0_), channel_id=1, source_target_pairs={{0,2},{2,0},{4,6},{6,4},{8,10},{10,8},{12,14},{14,12},{1,3},{3,1},... | collective-permute-start | bytes 393224 | tf_op jit(solution)/shard_map/ppermute | solution.py:54
  80.9 1.6 %collective-permute-start.28 = (bf16[32,2048]{1,0:T(8,128)(2,1)S(1)}, bf16[32,2048]{1,0:T(8,128)(2,1)S(1)}, u32[]{:S(2)}, u32[]{:S(2)}) collective-permute-start(bf16[32,2048]{1,0:T(8,128)(2,1)S(1)} %add_convert_fusion.1.refs_0_), channel_id=1, source_target_pairs={{0,4},{2,6},{4,0},{6,2},{8,12},{10,14},{12,8},{14,10},{1,5},{3,7},... | collective-permute-start | bytes 393224 | tf_op jit(solution)/shard_map/ppermute | solution.py:54
  82.5 0.5 collective-permute-start.29
  83.2 2.6 %collective-permute-done.27.refs_1_ = bf16[32,2048]{1,0:T(8,128)(2,1)S(1)} collective-permute-done((bf16[32,2048]{1,0:T(8,128)(2,1)S(1)}, bf16[32,2048]{1,0:T(8,128)(2,1)S(1)}, u32[]{:S(2)}, u32[]{:S(2)}) %collective-permute-start.27) | collective-permute-done | bytes 131104 | tf_op jit(solution)/shard_map/ppermute | solution.py:54
  85.9 0.5 collective-permute-start.31
  86.4 2.0 %collective-permute-done.29.refs_3_ = bf16[32,2048]{1,0:T(8,128)(2,1)S(1)} collective-permute-done((bf16[32,2048]{1,0:T(8,128)(2,1)S(1)}, bf16[32,2048]{1,0:T(8,128)(2,1)S(1)}, u32[]{:S(2)}, u32[]{:S(2)}) %collective-permute-start.29) | collective-permute-done | bytes 131104 | tf_op jit(solution)/shard_map/ppermute | solution.py:54
  88.6 1.1 collective-permute-done.32.refs_7_
  89.7 7.7 %experts.1 = f32[128,4096]{1,0:T(8,128)S(1)} custom-call(s32[6]{0:T(128)S(1)} %stack.32.place_ref, bf16[32,2048]{1,0:T(8,128)(2,1)S(1)} %add_convert_fusion.1.refs_0_, bf16[32,2048]{1,0:T(8,128)(2,1)S(1)} %collective-permute-done.27.refs_1_, bf16[32,2048]{1,0:T(8,128)(2,1)S(1)} %collective-permute-done.28.refs_2_, ...), custom_call_target="tpu_custom_call" | custom-call | tf_op jit(solution)/shard_map/experts/pallas_call | solution.py:418
  97.7 0.3 fusion.9
  98.0 1.5 %collective-permute-done.33 = bf16[128,2048]{1,0:T(8,128)(2,1)S(1)} collective-permute-done((bf16[128,2048]{1,0:T(8,128)(2,1)S(1)}, bf16[128,2048]{1,0:T(8,128)(2,1)S(1)}, u32[]{:S(2)}, u32[]{:S(2)}) %collective-permute-start.33) | collective-permute-done | bytes 524320 | tf_op jit(solution)/shard_map/ppermute | solution.py:50
  99.7 1.5 %collective-permute-start.36 = (bf16[32,2048]{1,0:T(8,128)(2,1)S(1)}, bf16[32,2048]{1,0:T(8,128)(2,1)S(1)}, u32[]{:S(2)}, u32[]{:S(2)}) collective-permute-start(bf16[32,2048]{1,0:T(8,128)(2,1)S(1)} %get-tuple-element.49), channel_id=1, source_target_pairs={{0,6},{2,4},{4,2},{6,0},{8,14},{10,12},{12,10},{14,8},{1,7},{3,5},... | collective-permute-start | bytes 393224 | tf_op jit(solution)/shard_map/ppermute | solution.py:54
  101.1 0.7 collective-permute-start.35
  101.8 1.4 %collective-permute-start.34 = (bf16[32,2048]{1,0:T(8,128)(2,1)S(1)}, bf16[32,2048]{1,0:T(8,128)(2,1)S(1)}, u32[]{:S(2)}, u32[]{:S(2)}) collective-permute-start(bf16[32,2048]{1,0:T(8,128)(2,1)S(1)} %get-tuple-element.48), channel_id=1, source_target_pairs={{0,2},{2,0},{4,6},{6,4},{8,10},{10,8},{12,14},{14,12},{1,3},{3,1},... | collective-permute-start | bytes 393224 | tf_op jit(solution)/shard_map/ppermute | solution.py:54
  103.3 3.7 %collective-permute-done.36 = bf16[32,2048]{1,0:T(8,128)(2,1)S(1)} collective-permute-done((bf16[32,2048]{1,0:T(8,128)(2,1)S(1)}, bf16[32,2048]{1,0:T(8,128)(2,1)S(1)}, u32[]{:S(2)}, u32[]{:S(2)}) %collective-permute-start.36) | collective-permute-done | bytes 131104 | tf_op jit(solution)/shard_map/ppermute | solution.py:54
  107.0 1.2 collective-permute-done.35
  108.1 0.9 collective-permute-done.34
  109.1 3.4 %collective-permute-start.37 = (bf16[16,2048]{1,0:T(8,128)(2,1)S(1)}, bf16[16,2048]{1,0:T(8,128)(2,1)S(1)}, u32[]{:S(2)}, u32[]{:S(2)}) collective-permute-start(bf16[16,2048]{1,0:T(8,128)(2,1)S(1)} %get-tuple-element.64), channel_id=1, source_target_pairs={{0,8},{2,10},{4,12},{6,14},{8,0},{10,2},{12,4},{14,6},{1,9},{3,11}... | collective-permute-start | bytes 196616 | tf_op jit(solution)/shard_map/ppermute | solution.py:54
  112.7 3.1 %collective-permute-done.37 = bf16[16,2048]{1,0:T(8,128)(2,1)S(1)} collective-permute-done((bf16[16,2048]{1,0:T(8,128)(2,1)S(1)}, bf16[16,2048]{1,0:T(8,128)(2,1)S(1)}, u32[]{:S(2)}, u32[]{:S(2)}) %collective-permute-start.37) | collective-permute-done | bytes 65568 | tf_op jit(solution)/shard_map/ppermute | solution.py:54
  115.8 0.9 convolution_convert_fusion
  (110 shorter events, 5.3 us)
Async XLA Ops:
  0.6 23.9 %copy-start = (bf16[4096,256]{1,0:T(8,128)(2,1)S(1)}, bf16[4096,256]{1,0:T(8,128)(2,1)}, u32[]{:S(2)}) copy-start(bf16[4096,256]{1,0:T(8,128)(2,1)} %param.26) | copy-start | bytes 6291460
  0.6 3.2 %collective-permute-start = (bf16[32,2048]{1,0:T(8,128)(2,1)}, bf16[32,2048]{1,0:T(8,128)(2,1)S(1)}, u32[]{:S(2)}, u32[]{:S(2)}) collective-permute-start(bf16[32,2048]{1,0:T(8,128)(2,1)} %param.21), channel_id=1, source_target_pairs={{0,1},{1,0},{2,3},{3,2},{4,5},{5,4},{6,7},{7,6},{8,9},{9,8},{10,11... | collective-permute-start | bytes 393224 | tf_op jit(solution)/shard_map/ppermute | solution.py:50
  1.2 6.3 %collective-permute-start.4 = (bf16[32,2048]{1,0:T(8,128)(2,1)}, bf16[32,2048]{1,0:T(8,128)(2,1)S(1)}, u32[]{:S(2)}, u32[]{:S(2)}) collective-permute-start(bf16[32,2048]{1,0:T(8,128)(2,1)} %param.21), channel_id=1, source_target_pairs={{0,4},{1,3},{2,0},{3,7},{4,8},{5,1},{6,2},{7,11},{8,12},{9,5},{10,... | collective-permute-start | bytes 393224 | tf_op jit(solution)/shard_map/ppermute | solution.py:74
  3.8 5.3 %collective-permute-start.1 = (bf16[32,2048]{1,0:T(8,128)(2,1)S(1)}, bf16[32,2048]{1,0:T(8,128)(2,1)S(1)}, u32[]{:S(2)}, u32[]{:S(2)}) collective-permute-start(bf16[32,2048]{1,0:T(8,128)(2,1)S(1)} %collective-permute-done), channel_id=1, source_target_pairs={{0,4},{1,3},{2,0},{3,7},{4,8},{5,1},{6,2},{7,11},{8,12},{9,5},{10,... | collective-permute-start | bytes 393224 | tf_op jit(solution)/shard_map/ppermute | solution.py:74
  7.5 5.0 %collective-permute-start.5 = (bf16[32,2048]{1,0:T(8,128)(2,1)S(1)}, bf16[32,2048]{1,0:T(8,128)(2,1)S(1)}, u32[]{:S(2)}, u32[]{:S(2)}) collective-permute-start(bf16[32,2048]{1,0:T(8,128)(2,1)S(1)} %collective-permute-done.4), channel_id=1, source_target_pairs={{0,4},{1,3},{2,0},{3,7},{4,8},{5,1},{6,2},{7,11},{8,12},{9,5},{10,... | collective-permute-start | bytes 393224 | tf_op jit(solution)/shard_map/ppermute | solution.py:74
  9.1 5.0 %collective-permute-start.2 = (bf16[32,2048]{1,0:T(8,128)(2,1)S(1)}, bf16[32,2048]{1,0:T(8,128)(2,1)S(1)}, u32[]{:S(2)}, u32[]{:S(2)}) collective-permute-start(bf16[32,2048]{1,0:T(8,128)(2,1)S(1)} %collective-permute-done.1), channel_id=1, source_target_pairs={{0,4},{1,3},{2,0},{3,7},{4,8},{5,1},{6,2},{7,11},{8,12},{9,5},{10,... | collective-permute-start | bytes 393224 | tf_op jit(solution)/shard_map/ppermute | solution.py:74
  12.5 5.0 %collective-permute-start.6 = (bf16[32,2048]{1,0:T(8,128)(2,1)S(1)}, bf16[32,2048]{1,0:T(8,128)(2,1)S(1)}, u32[]{:S(2)}, u32[]{:S(2)}) collective-permute-start(bf16[32,2048]{1,0:T(8,128)(2,1)S(1)} %collective-permute-done.5), channel_id=1, source_target_pairs={{0,4},{1,3},{2,0},{3,7},{4,8},{5,1},{6,2},{7,11},{8,12},{9,5},{10,... | collective-permute-start | bytes 393224 | tf_op jit(solution)/shard_map/ppermute | solution.py:74
  14.1 5.0 %collective-permute-start.3 = (bf16[32,2048]{1,0:T(8,128)(2,1)S(1)}, bf16[32,2048]{1,0:T(8,128)(2,1)S(1)}, u32[]{:S(2)}, u32[]{:S(2)}) collective-permute-start(bf16[32,2048]{1,0:T(8,128)(2,1)S(1)} %collective-permute-done.2), channel_id=1, source_target_pairs={{0,4},{1,3},{2,0},{3,7},{4,8},{5,1},{6,2},{7,11},{8,12},{9,5},{10,... | collective-permute-start | bytes 393224 | tf_op jit(solution)/shard_map/ppermute | solution.py:74
  17.4 5.0 %collective-permute-start.8 = (bf16[32,2048]{1,0:T(8,128)(2,1)S(1)}, bf16[32,2048]{1,0:T(8,128)(2,1)S(1)}, u32[]{:S(2)}, u32[]{:S(2)}) collective-permute-start(bf16[32,2048]{1,0:T(8,128)(2,1)S(1)} %collective-permute-done.6), channel_id=1, source_target_pairs={{0,4},{1,3},{2,0},{3,7},{4,8},{5,1},{6,2},{7,11},{8,12},{9,5},{10,... | collective-permute-start | bytes 393224 | tf_op jit(solution)/shard_map/ppermute | solution.py:74
  20.1 3.7 %collective-permute-start.7 = (bf16[96,4096]{1,0:T(8,128)(2,1)S(1)}, bf16[96,4096]{1,0:T(8,128)(2,1)S(1)}, u32[]{:S(2)}, u32[]{:S(2)}) collective-permute-start(bf16[96,4096]{1,0:T(8,128)(2,1)S(1)} %maximum_maximum_fusion), channel_id=1, source_target_pairs={{0,1},{1,0},{2,3},{3,2},{4,5},{5,4},{6,7},{7,6},{8,9},{9,8},{10,11... | collective-permute-start | bytes 2359304 | tf_op jit(solution)/shard_map/ppermute | solution.py:50
  22.4 1.3 %collective-permute-start.9 = (bf16[32,2048]{1,0:T(8,128)(2,1)S(1)}, bf16[32,2048]{1,0:T(8,128)(2,1)S(1)}, u32[]{:S(2)}, u32[]{:S(2)}) collective-permute-start(bf16[32,2048]{1,0:T(8,128)(2,1)S(1)} %collective-permute-done.8), channel_id=1, source_target_pairs={{0,1},{1,0},{2,3},{3,2},{4,5},{5,4},{6,7},{7,6},{8,9},{9,8},{10,11... | collective-permute-start | bytes 393224 | tf_op jit(solution)/shard_map/ppermute | solution.py:50
  23.9 0.7 copy-start.14
  24.0 2.1 %copy-start.7 = (bf16[256,4096]{1,0:T(8,128)(2,1)}, bf16[256,4096]{1,0:T(8,128)(2,1)S(1)}, u32[]{:S(2)}) copy-start(bf16[256,4096]{1,0:T(8,128)(2,1)S(1)} %maximum_dynamic-update-slice_fusion.4) | copy-start | bytes 6291460
  24.6 0.8 copy-start.12
  24.6 1.1 copy-start.11
  24.6 1.2 %copy-start.10 = (bf16[256,512]{1,0:T(8,128)(2,1)S(1)}, bf16[256,512]{1,0:T(8,128)(2,1)}, u32[]{:S(2)}) copy-start(bf16[256,512]{1,0:T(8,128)(2,1)} %param.30) | copy-start | bytes 786436
  26.9 1.5 %collective-permute-start.10 = (bf16[128,547]{1,0:T(8,128)(2,1)S(1)}, bf16[128,547]{1,0:T(8,128)(2,1)S(1)}, u32[]{:S(2)}, u32[]{:S(2)}) collective-permute-start(bf16[128,547]{1,0:T(8,128)(2,1)S(1)} %dynamic-slice_convert_fusion.1), channel_id=1, source_target_pairs={{0,1},{1,0},{2,3},{3,2},{4,5},{5,4},{6,7},{7,6},{8,9},{9,8},{10,11... | collective-permute-start | bytes 420104 | tf_op jit(solution)/shard_map/ppermute | solution.py:50
  27.1 28.6 %collective-permute-start.17 = (bf16[256,4096]{1,0:T(8,128)(2,1)}, bf16[256,4096]{1,0:T(8,128)(2,1)}, u32[]{:S(2)}, u32[]{:S(2)}) collective-permute-start(bf16[256,4096]{1,0:T(8,128)(2,1)} %wg_ref.1), channel_id=1, source_target_pairs={{0,1},{1,0},{2,3},{3,2},{4,5},{5,4},{6,7},{7,6},{8,9},{9,8},{10,11... | collective-permute-start | bytes 6291464 | tf_op jit(solution)/shard_map/ppermute | solution.py:50
  28.4 20.8 %copy-start.1 = (f32[32,16,256]{2,1,0:T(8,128)S(1)}, f32[32,16,256]{2,1,0:T(8,128)}, u32[]{:S(2)}) copy-start(f32[32,16,256]{2,1,0:T(8,128)} %state_hbm.1) | copy-start | bytes 1572868
  28.4 20.8 %copy-start.2 = (bf16[512,256]{1,0:T(8,128)(2,1)S(1)}, bf16[512,256]{1,0:T(8,128)(2,1)}, u32[]{:S(2)}) copy-start(bf16[512,256]{1,0:T(8,128)(2,1)} %dt_proj.1) | copy-start | bytes 786436
  28.4 20.8 %copy-start.3 = (f32[16,256]{1,0:T(8,128)S(1)}, f32[16,256]{1,0:T(8,128)}, u32[]{:S(2)}) copy-start(f32[16,256]{1,0:T(8,128)} %a_rate.1) | copy-start | bytes 49156
  28.5 20.8 %copy-start.5 = (f32[256]{0:T(256)S(1)}, f32[256]{0:T(256)}, u32[]{:S(2)}) copy-start(f32[256]{0:T(256)} %param.33) | copy-start | bytes 3076
  28.5 20.8 %copy-start.6 = (f32[256]{0:T(256)S(1)}, f32[256]{0:T(256)}, u32[]{:S(2)}) copy-start(f32[256]{0:T(256)} %param.35) | copy-start | bytes 3076
  28.5 4.6 %collective-permute-start.11 = (bf16[64,547]{1,0:T(8,128)(2,1)S(1)}, bf16[64,547]{1,0:T(8,128)(2,1)S(1)}, u32[]{:S(2)}, u32[]{:S(2)}) collective-permute-start(bf16[64,547]{1,0:T(8,128)(2,1)S(1)} %dynamic-slice_convert_fusion.2), channel_id=1, source_target_pairs={{0,2},{2,0},{4,6},{6,4},{8,10},{10,8},{12,14},{14,12},{1,3},{3,1},... | collective-permute-start | bytes 210056 | tf_op jit(solution)/shard_map/ppermute | solution.py:54
  33.1 4.5 %collective-permute-start.12 = (bf16[64,547]{1,0:T(8,128)(2,1)S(1)}, bf16[64,547]{1,0:T(8,128)(2,1)S(1)}, u32[]{:S(2)}, u32[]{:S(2)}) collective-permute-start(bf16[64,547]{1,0:T(8,128)(2,1)S(1)} %fusion.35), channel_id=1, source_target_pairs={{0,4},{2,6},{4,0},{6,2},{8,12},{10,14},{12,8},{14,10},{1,5},{3,7},... | collective-permute-start | bytes 210056 | tf_op jit(solution)/shard_map/ppermute | solution.py:54
  37.6 5.4 %collective-permute-start.13 = (bf16[64,547]{1,0:T(8,128)(2,1)S(1)}, bf16[64,547]{1,0:T(8,128)(2,1)S(1)}, u32[]{:S(2)}, u32[]{:S(2)}) collective-permute-start(bf16[64,547]{1,0:T(8,128)(2,1)S(1)} %fusion.34), channel_id=1, source_target_pairs={{0,8},{2,10},{4,12},{6,14},{8,0},{10,2},{12,4},{14,6},{1,9},{3,11}... | collective-permute-start | bytes 210056 | tf_op jit(solution)/shard_map/ppermute | solution.py:54
  43.1 4.5 %collective-permute-start.14 = (bf16[64,547]{1,0:T(8,128)(2,1)S(1)}, bf16[64,547]{1,0:T(8,128)(2,1)S(1)}, u32[]{:S(2)}, u32[]{:S(2)}) collective-permute-start(bf16[64,547]{1,0:T(8,128)(2,1)S(1)} %get-tuple-element.47), channel_id=1, source_target_pairs={{0,2},{2,0},{4,6},{6,4},{8,10},{10,8},{12,14},{14,12},{1,3},{3,1},... | collective-permute-start | bytes 210056 | tf_op jit(solution)/shard_map/ppermute | solution.py:54
  47.6 1.6 %collective-permute-start.15 = (bf16[128,547]{1,0:T(8,128)(2,1)S(1)}, bf16[128,547]{1,0:T(8,128)(2,1)}, u32[]{:S(2)}, u32[]{:S(2)}) collective-permute-start(bf16[128,547]{1,0:T(8,128)(2,1)S(1)} %constant_dynamic-update-slice_fusion.mine), channel_id=1, source_target_pairs={{0,1},{1,0},{2,3},{3,2},{4,5},{5,4},{6,7},{7,6},{8,9},{9,8},{10,11... | collective-permute-start | bytes 420104 | tf_op jit(solution)/shard_map/ppermute | solution.py:50
  54.3 1.4 %collective-permute-start.16 = (bf16[256,256]{1,0:T(8,128)(2,1)S(1)}, bf16[256,256]{1,0:T(8,128)(2,1)S(1)}, u32[]{:S(2)}, u32[]{:S(2)}) collective-permute-start(bf16[256,256]{1,0:T(8,128)(2,1)S(1)} %convert_element_type.146.g_ref), channel_id=1, source_target_pairs={{0,1},{1,0},{2,3},{3,2},{4,5},{5,4},{6,7},{7,6},{8,9},{9,8},{10,11... | collective-permute-start | bytes 393224 | tf_op jit(solution)/shard_map/ppermute | solution.py:50
  55.7 5.0 %copy-start.9 = (bf16[32,2048]{1,0:T(8,128)(2,1)S(1)}, bf16[32,2048]{1,0:T(8,128)(2,1)}, u32[]{:S(2)}) copy-start(bf16[32,2048]{1,0:T(8,128)(2,1)} %param.21) | copy-start | bytes 393220
  59.0 17.0 %copy-start.8 = (bf16[32,2048]{1,0:T(8,128)(2,1)S(1)}, bf16[32,2048]{1,0:T(8,128)(2,1)}, u32[]{:S(2)}) copy-start(bf16[32,2048]{1,0:T(8,128)(2,1)} %dynamic_slice.27) | copy-start | bytes 393220
  59.0 5.0 %collective-permute-start.18 = (bf16[32,2048]{1,0:T(8,128)(2,1)S(1)}, bf16[32,2048]{1,0:T(8,128)(2,1)S(1)}, u32[]{:S(2)}, u32[]{:S(2)}) collective-permute-start(bf16[32,2048]{1,0:T(8,128)(2,1)S(1)} %get-tuple-element.36), channel_id=1, source_target_pairs={{0,4},{1,3},{2,0},{3,7},{4,8},{5,1},{6,2},{7,11},{8,12},{9,5},{10,... | collective-permute-start | bytes 393224 | tf_op jit(solution)/shard_map/ppermute | solution.py:353
  60.9 5.0 %collective-permute-start.22 = (bf16[32,2048]{1,0:T(8,128)(2,1)S(1)}, bf16[32,2048]{1,0:T(8,128)(2,1)S(1)}, u32[]{:S(2)}, u32[]{:S(2)}) collective-permute-start(bf16[32,2048]{1,0:T(8,128)(2,1)S(1)} %slice.204), channel_id=1, source_target_pairs={{0,4},{1,3},{2,0},{3,7},{4,8},{5,1},{6,2},{7,11},{8,12},{9,5},{10,... | collective-permute-start | bytes 393224 | tf_op jit(solution)/shard_map/ppermute | solution.py:353
  64.1 5.0 %collective-permute-start.19 = (bf16[32,2048]{1,0:T(8,128)(2,1)S(1)}, bf16[32,2048]{1,0:T(8,128)(2,1)S(1)}, u32[]{:S(2)}, u32[]{:S(2)}) collective-permute-start(bf16[32,2048]{1,0:T(8,128)(2,1)S(1)} %add_convert_fusion.6), channel_id=1, source_target_pairs={{0,4},{1,3},{2,0},{3,7},{4,8},{5,1},{6,2},{7,11},{8,12},{9,5},{10,... | collective-permute-start | bytes 393224 | tf_op jit(solution)/shard_map/ppermute | solution.py:353
  66.0 23.8 %copy-start.4 = (f32[4096]{0:T(1024)S(1)}, f32[4096]{0:T(1024)}, u32[]{:S(2)}) copy-start(f32[4096]{0:T(1024)} %param.37) | copy-start | bytes 49156
  66.0 5.0 %collective-permute-start.23 = (bf16[32,2048]{1,0:T(8,128)(2,1)S(1)}, bf16[32,2048]{1,0:T(8,128)(2,1)S(1)}, u32[]{:S(2)}, u32[]{:S(2)}) collective-permute-start(bf16[32,2048]{1,0:T(8,128)(2,1)S(1)} %add_convert_fusion.3), channel_id=1, source_target_pairs={{0,4},{1,3},{2,0},{3,7},{4,8},{5,1},{6,2},{7,11},{8,12},{9,5},{10,... | collective-permute-start | bytes 393224 | tf_op jit(solution)/shard_map/ppermute | solution.py:353
  69.1 5.0 %collective-permute-start.20 = (bf16[32,2048]{1,0:T(8,128)(2,1)S(1)}, bf16[32,2048]{1,0:T(8,128)(2,1)S(1)}, u32[]{:S(2)}, u32[]{:S(2)}) collective-permute-start(bf16[32,2048]{1,0:T(8,128)(2,1)S(1)} %add_convert_fusion.5), channel_id=1, source_target_pairs={{0,4},{1,3},{2,0},{3,7},{4,8},{5,1},{6,2},{7,11},{8,12},{9,5},{10,... | collective-permute-start | bytes 393224 | tf_op jit(solution)/shard_map/ppermute | solution.py:353
  71.0 5.0 %collective-permute-start.24 = (bf16[32,2048]{1,0:T(8,128)(2,1)S(1)}, bf16[32,2048]{1,0:T(8,128)(2,1)S(1)}, u32[]{:S(2)}, u32[]{:S(2)}) collective-permute-start(bf16[32,2048]{1,0:T(8,128)(2,1)S(1)} %add_convert_fusion.2), channel_id=1, source_target_pairs={{0,4},{1,3},{2,0},{3,7},{4,8},{5,1},{6,2},{7,11},{8,12},{9,5},{10,... | collective-permute-start | bytes 393224 | tf_op jit(solution)/shard_map/ppermute | solution.py:353
  74.2 5.2 %collective-permute-start.21 = (bf16[32,2048]{1,0:T(8,128)(2,1)S(1)}, bf16[32,2048]{1,0:T(8,128)(2,1)S(1)}, u32[]{:S(2)}, u32[]{:S(2)}) collective-permute-start(bf16[32,2048]{1,0:T(8,128)(2,1)S(1)} %add_convert_fusion.4), channel_id=1, source_target_pairs={{0,4},{1,3},{2,0},{3,7},{4,8},{5,1},{6,2},{7,11},{8,12},{9,5},{10,... | collective-permute-start | bytes 393224 | tf_op jit(solution)/shard_map/ppermute | solution.py:353
  76.1 1.3 %collective-permute-start.25 = (bf16[32,2048]{1,0:T(8,128)(2,1)S(1)}, bf16[32,2048]{1,0:T(8,128)(2,1)S(1)}, u32[]{:S(2)}, u32[]{:S(2)}) collective-permute-start(bf16[32,2048]{1,0:T(8,128)(2,1)S(1)} %collective-permute-done.24), channel_id=1, source_target_pairs={{0,1},{1,0},{2,3},{3,2},{4,5},{5,4},{6,7},{7,6},{8,9},{9,8},{10,11... | collective-permute-start | bytes 393224 | tf_op jit(solution)/shard_map/ppermute | solution.py:50
  79.4 6.4 %collective-permute-start.27 = (bf16[32,2048]{1,0:T(8,128)(2,1)S(1)}, bf16[32,2048]{1,0:T(8,128)(2,1)S(1)}, u32[]{:S(2)}, u32[]{:S(2)}) collective-permute-start(bf16[32,2048]{1,0:T(8,128)(2,1)S(1)} %add_convert_fusion.1.refs_0_), channel_id=1, source_target_pairs={{0,2},{2,0},{4,6},{6,4},{8,10},{10,8},{12,14},{14,12},{1,3},{3,1},... | collective-permute-start | bytes 393224 | tf_op jit(solution)/shard_map/ppermute | solution.py:54
  80.9 5.0 %collective-permute-start.28 = (bf16[32,2048]{1,0:T(8,128)(2,1)S(1)}, bf16[32,2048]{1,0:T(8,128)(2,1)S(1)}, u32[]{:S(2)}, u32[]{:S(2)}) collective-permute-start(bf16[32,2048]{1,0:T(8,128)(2,1)S(1)} %add_convert_fusion.1.refs_0_), channel_id=1, source_target_pairs={{0,4},{2,6},{4,0},{6,2},{8,12},{10,14},{12,8},{14,10},{1,5},{3,7},... | collective-permute-start | bytes 393224 | tf_op jit(solution)/shard_map/ppermute | solution.py:54
  82.5 5.9 %collective-permute-start.29 = (bf16[32,2048]{1,0:T(8,128)(2,1)S(1)}, bf16[32,2048]{1,0:T(8,128)(2,1)S(1)}, u32[]{:S(2)}, u32[]{:S(2)}) collective-permute-start(bf16[32,2048]{1,0:T(8,128)(2,1)S(1)} %add_convert_fusion.1.refs_0_), channel_id=1, source_target_pairs={{0,6},{2,4},{4,2},{6,0},{8,14},{10,12},{12,10},{14,8},{1,7},{3,5},... | collective-permute-start | bytes 393224 | tf_op jit(solution)/shard_map/ppermute | solution.py:54
  83.0 5.4 %collective-permute-start.26 = (bf16[32,2048]{1,0:T(8,128)(2,1)S(1)}, bf16[32,2048]{1,0:T(8,128)(2,1)S(1)}, u32[]{:S(2)}, u32[]{:S(2)}) collective-permute-start(bf16[32,2048]{1,0:T(8,128)(2,1)S(1)} %add_convert_fusion.1.refs_0_), channel_id=1, source_target_pairs={{0,1},{1,0},{2,3},{3,2},{4,5},{5,4},{6,7},{7,6},{8,9},{9,8},{10,11... | collective-permute-start | bytes 393224 | tf_op jit(solution)/shard_map/ppermute | solution.py:50
  85.9 2.7 %collective-permute-start.30 = (bf16[32,2048]{1,0:T(8,128)(2,1)S(1)}, bf16[32,2048]{1,0:T(8,128)(2,1)S(1)}, u32[]{:S(2)}, u32[]{:S(2)}) collective-permute-start(bf16[32,2048]{1,0:T(8,128)(2,1)S(1)} %collective-permute-done.27.refs_1_), channel_id=1, source_target_pairs={{0,1},{1,0},{2,3},{3,2},{4,5},{5,4},{6,7},{7,6},{8,9},{9,8},{10,11... | collective-permute-start | bytes 393224 | tf_op jit(solution)/shard_map/ppermute | solution.py:50
  85.9 2.7 %collective-permute-start.31 = (bf16[32,2048]{1,0:T(8,128)(2,1)S(1)}, bf16[32,2048]{1,0:T(8,128)(2,1)S(1)}, u32[]{:S(2)}, u32[]{:S(2)}) collective-permute-start(bf16[32,2048]{1,0:T(8,128)(2,1)S(1)} %collective-permute-done.28.refs_2_), channel_id=1, source_target_pairs={{0,1},{1,0},{2,3},{3,2},{4,5},{5,4},{6,7},{7,6},{8,9},{9,8},{10,11... | collective-permute-start | bytes 393224 | tf_op jit(solution)/shard_map/ppermute | solution.py:50
  88.4 1.3 %collective-permute-start.32 = (bf16[32,2048]{1,0:T(8,128)(2,1)S(1)}, bf16[32,2048]{1,0:T(8,128)(2,1)S(1)}, u32[]{:S(2)}, u32[]{:S(2)}) collective-permute-start(bf16[32,2048]{1,0:T(8,128)(2,1)S(1)} %collective-permute-done.29.refs_3_), channel_id=1, source_target_pairs={{0,1},{1,0},{2,3},{3,2},{4,5},{5,4},{6,7},{7,6},{8,9},{9,8},{10,11... | collective-permute-start | bytes 393224 | tf_op jit(solution)/shard_map/ppermute | solution.py:50
  89.7 8.0 %copy-start.13 = (bf16[4096,16]{0,1:T(8,128)(2,1)S(1)}, bf16[4096,16]{0,1:T(8,128)(2,1)}, u32[]{:S(2)}) copy-start(bf16[4096,16]{0,1:T(8,128)(2,1)} %param.38) | copy-start | bytes 393220
  97.5 2.0 %collective-permute-start.33 = (bf16[128,2048]{1,0:T(8,128)(2,1)S(1)}, bf16[128,2048]{1,0:T(8,128)(2,1)S(1)}, u32[]{:S(2)}, u32[]{:S(2)}) collective-permute-start(bf16[128,2048]{1,0:T(8,128)(2,1)S(1)} %dynamic-slice_convert_fusion), channel_id=1, source_target_pairs={{0,1},{1,0},{2,3},{3,2},{4,5},{5,4},{6,7},{7,6},{8,9},{9,8},{10,11... | collective-permute-start | bytes 1572872 | tf_op jit(solution)/shard_map/ppermute | solution.py:50
  99.7 7.3 %collective-permute-start.36 = (bf16[32,2048]{1,0:T(8,128)(2,1)S(1)}, bf16[32,2048]{1,0:T(8,128)(2,1)S(1)}, u32[]{:S(2)}, u32[]{:S(2)}) collective-permute-start(bf16[32,2048]{1,0:T(8,128)(2,1)S(1)} %get-tuple-element.49), channel_id=1, source_target_pairs={{0,6},{2,4},{4,2},{6,0},{8,14},{10,12},{12,10},{14,8},{1,7},{3,5},... | collective-permute-start | bytes 393224 | tf_op jit(solution)/shard_map/ppermute | solution.py:54
  101.1 7.0 %collective-permute-start.35 = (bf16[32,2048]{1,0:T(8,128)(2,1)S(1)}, bf16[32,2048]{1,0:T(8,128)(2,1)S(1)}, u32[]{:S(2)}, u32[]{:S(2)}) collective-permute-start(bf16[32,2048]{1,0:T(8,128)(2,1)S(1)} %get-tuple-element.50), channel_id=1, source_target_pairs={{0,4},{2,6},{4,0},{6,2},{8,12},{10,14},{12,8},{14,10},{1,5},{3,7},... | collective-permute-start | bytes 393224 | tf_op jit(solution)/shard_map/ppermute | solution.py:54
  101.8 7.2 %collective-permute-start.34 = (bf16[32,2048]{1,0:T(8,128)(2,1)S(1)}, bf16[32,2048]{1,0:T(8,128)(2,1)S(1)}, u32[]{:S(2)}, u32[]{:S(2)}) collective-permute-start(bf16[32,2048]{1,0:T(8,128)(2,1)S(1)} %get-tuple-element.48), channel_id=1, source_target_pairs={{0,2},{2,0},{4,6},{6,4},{8,10},{10,8},{12,14},{14,12},{1,3},{3,1},... | collective-permute-start | bytes 393224 | tf_op jit(solution)/shard_map/ppermute | solution.py:54
  109.1 6.7 %collective-permute-start.37 = (bf16[16,2048]{1,0:T(8,128)(2,1)S(1)}, bf16[16,2048]{1,0:T(8,128)(2,1)S(1)}, u32[]{:S(2)}, u32[]{:S(2)}) collective-permute-start(bf16[16,2048]{1,0:T(8,128)(2,1)S(1)} %get-tuple-element.64), channel_id=1, source_target_pairs={{0,8},{2,10},{4,12},{6,14},{8,0},{10,2},{12,4},{14,6},{1,9},{3,11}... | collective-permute-start | bytes 196616 | tf_op jit(solution)/shard_map/ppermute | solution.py:54

commit v5 on v4

--- a/solution.py
+++ b/solution.py
@@ -205,7 +205,7 @@
         gated[at, :] = y * (z * jax.nn.sigmoid(z))
         return carry
 
-    lax.fori_loop(0, tokens // DRAFT, request, 0, unroll=2)
+    lax.fori_loop(0, tokens // DRAFT, request, 0, unroll=4)
 
 
 def scan(places, total, dt_proj, dt_bias, u, z, ssm_state, a_rate, d_skip):
@@ -341,7 +341,7 @@
         ),
         in_specs=[pl.BlockSpec(memory_space=pltpu.SMEM)] + [vmem] * 5,
         out_specs=[vmem] * 4,
-        compiler_params=pltpu.CompilerParams(vmem_limit_bytes=VMEM_LIMIT),
+        compiler_params=pltpu.CompilerParams(vmem_limit_bytes=14 << 20),
         name="project",
     )(places, ids, gated, gated_other, out_proj, out_other)
 
@@ -365,22 +365,24 @@
     own, refs = refs[:pieces], refs[pieces:]
     other, refs = refs[:pieces], refs[pieces:]
     gain_ref, wg_hbm, wu_hbm, wd_hbm, out_ref, x_ref, wg, wu, wd, sems = refs
-    tile = wg.shape[2]
-    copies = []
+    depth = wg.shape[0] // tiles
+    inner = wd.shape[0] // tiles
+
+    def fetch(kind, src, dst, size):
+        parts = [pl.ds(i * size, size) for i in range(tiles)]
+        return [
+            pltpu.make_async_copy(src.at[at, :], dst.at[at, :], sems.at[kind, i])
+            for i, at in enumerate(parts)
+        ]
+
+    gates = fetch(0, wg_hbm, wg, depth)
+    ups = fetch(1, wu_hbm, wu, depth)
+    downs = fetch(2, wd_hbm, wd, inner)
     for i in range(tiles):
-        at = pl.ds(i * tile, tile)
-        copies.append(
-            (
-                pltpu.make_async_copy(wg_hbm.at[:, at], wg.at[i], sems.at[0, i]),
-                pltpu.make_async_copy(wu_hbm.at[:, at], wu.at[i], sems.at[1, i]),
-                pltpu.make_async_copy(wd_hbm.at[at, :], wd.at[i], sems.at[2, i]),
-            )
-        )
-    for group in copies:
-        group[0].start()
-        group[1].start()
-    for group in copies:
-        group[2].start()
+        gates[i].start()
+        ups[i].start()
+    for copy in downs:
+        copy.start()
     rows, width = own[0].shape
     core = place_ref[place_ref.shape[0] - 1]
     here = pl.ds(pl.multiple_of(core * width, 128), width)
@@ -390,17 +392,21 @@
         x_ref[i * rows : (i + 1) * rows, there] = other[i][...]
     values = x_ref[...].astype(F32)
     scale = lax.rsqrt(jnp.mean(values * values, axis=-1, keepdims=True) + 1e-05)
-    x = (values * scale * gain_ref[...]).astype(BF16)
-    acts = []
+    x_ref[...] = (values * scale * gain_ref[...]).astype(BF16)
+    gate = upval = None
     for i in range(tiles):
-        copies[i][0].wait()
-        gate = jnp.dot(x, wg[i], preferred_element_type=F32)
-        copies[i][1].wait()
-        upval = jnp.dot(x, wu[i], preferred_element_type=F32)
-        acts.append((gate * jax.nn.sigmoid(gate) * upval).astype(BF16))
+        at = slice(i * depth, (i + 1) * depth)
+        gates[i].wait()
+        term = jnp.dot(x_ref[:, at], wg[at, :], preferred_element_type=F32)
+        gate = term if gate is None else gate + term
+        ups[i].wait()
+        term = jnp.dot(x_ref[:, at], wu[at, :], preferred_element_type=F32)
+        upval = term if upval is None else upval + term
+    act = (gate * jax.nn.sigmoid(gate) * upval).astype(BF16)
     for i in range(tiles):
-        copies[i][2].wait()
-        term = jnp.dot(acts[i], wd[i], preferred_element_type=F32)
+        at = slice(i * inner, (i + 1) * inner)
+        downs[i].wait()
+        term = jnp.dot(act[:, at], wd[at, :], preferred_element_type=F32)
         if i == 0:
             out_ref[...] = term
         else:
@@ -410,9 +416,7 @@
 def run_experts(places, own, other, gain, w_gate, w_up, w_down):
     pieces = len(own)
     count, width = pieces * own[0].shape[0], 2 * own[0].shape[1]
-    hidden = w_gate.shape[1]
-    tile = 256
-    tiles = hidden // tile
+    tiles = 4
     vmem = pl.BlockSpec(memory_space=pltpu.VMEM)
     hbm = pl.BlockSpec(memory_space=pltpu.HBM)
     return pl.pallas_call(
@@ -422,14 +426,20 @@
         out_specs=vmem,
         scratch_shapes=[
             pltpu.VMEM((count, width), BF16),
-            pltpu.VMEM((tiles, width, tile), BF16),
-            pltpu.VMEM((tiles, width, tile), BF16),
-            pltpu.VMEM((tiles, tile, width), BF16),
+            pltpu.VMEM(w_gate.shape, BF16),
+            pltpu.VMEM(w_up.shape, BF16),
+            pltpu.VMEM(w_down.shape, BF16),
             pltpu.SemaphoreType.DMA((3, tiles)),
         ],
-        compiler_params=pltpu.CompilerParams(vmem_limit_bytes=48 << 20),
+        compiler_params=pltpu.CompilerParams(vmem_limit_bytes=28 << 20),
         name="experts",
-    )(places, *own, *other, gain.reshape(1, width), w_gate, w_up, w_down)
+    )(
+        places,
+        *own,
+        *other,
+        gain.reshape(1, width),
+        *(pltpu.with_memory_space_constraint(w, pltpu.HBM) for w in (w_gate, w_up, w_down)),
+    )
 
 
 def on_device(

time: 117 us -> 117 us (level)
  no operation moved by 1% of the time
where the time goes in v5:
time: 117 us
  starting transfers between devices  43.7 us (37%)
  waiting for transfers between devices  42.3 us (36%)
  Pallas kernels  16.1 us (14%)
  matrix products  5.98 us (5%)
  local copies, waits for them, and re-layouts  4.04 us (3%)
  other arithmetic  3.27 us (3%)
  between operations  1.22 us (1%)
    ppermute x11, waiting for transfers between devices, over_expert(): return lax.ppermute(value, 'expert', [(i, i ^ flip) for i in range(owners)])  22.2 us
    ppermute x11, starting transfers between devices, over_expert(): return lax.ppermute(value, 'expert', [(i, i ^ flip) for i in range(owners)])  17.8 us
    ppermute x7, starting transfers between devices, send(): return lax.ppermute(value, ('expert', 'cuts'), perm)  12 us
    ppermute x7, starting transfers between devices, send(): return lax.ppermute(value.astype(BF16), ('expert', 'cuts'), perm)  11.7 us
    ppermute x13, waiting for transfers between devices, over_cuts(): return lax.ppermute(value, 'cuts', [(0, 1), (1, 0)])  8.35 us
    pallas_call x1, Pallas kernels, run_experts(): pl.pallas_call(functools.partial(experts_kernel, tiles, pieces), out_shap...  7.61 us
    ppermute x7, waiting for transfers between devices, send(): return lax.ppermute(value.astype(BF16), ('expert', 'cuts'), perm)  6.88 us
    pallas_call x1, Pallas kernels, scan(): pl.pallas_call(scan_kernel, out_shape=(jax.ShapeDtypeStruct((tokens, chan...  4.94 us
  transfers between devices with their start and end apart: 38, of which 27 were waited for; matrix products, arithmetic and copies ran while one was open for 8% of the time, Pallas kernels for 4%

profile of v5, /device:TPU:0, one launch (start us, length us, event | category | flops | bytes accessed | tf_op | source)
XLA Modules:
  0.0 116.6 jit_solution(15252360721843394736)
XLA Ops:
  0.6 0.5 collective-permute-start
  1.2 2.6 %collective-permute-start.4 = (bf16[32,2048]{1,0:T(8,128)(2,1)}, bf16[32,2048]{1,0:T(8,128)(2,1)S(1)}, u32[]{:S(2)}, u32[]{:S(2)}) collective-permute-start(bf16[32,2048]{1,0:T(8,128)(2,1)} %param.21), channel_id=1, source_target_pairs={{0,4},{1,3},{2,0},{3,7},{4,8},{5,1},{6,2},{7,11},{8,12},{9,5},{10,... | collective-permute-start | bytes 393224 | tf_op jit(solution)/shard_map/ppermute | solution.py:74
  3.8 1.6 %collective-permute-start.1 = (bf16[32,2048]{1,0:T(8,128)(2,1)S(1)}, bf16[32,2048]{1,0:T(8,128)(2,1)S(1)}, u32[]{:S(2)}, u32[]{:S(2)}) collective-permute-start(bf16[32,2048]{1,0:T(8,128)(2,1)S(1)} %collective-permute-done), channel_id=1, source_target_pairs={{0,4},{1,3},{2,0},{3,7},{4,8},{5,1},{6,2},{7,11},{8,12},{9,5},{10,... | collective-permute-start | bytes 393224 | tf_op jit(solution)/shard_map/ppermute | solution.py:74
  5.4 0.8 copy.33.routes_ref
  6.4 1.0 copy.34
  7.5 1.6 %collective-permute-start.5 = (bf16[32,2048]{1,0:T(8,128)(2,1)S(1)}, bf16[32,2048]{1,0:T(8,128)(2,1)S(1)}, u32[]{:S(2)}, u32[]{:S(2)}) collective-permute-start(bf16[32,2048]{1,0:T(8,128)(2,1)S(1)} %collective-permute-done.4), channel_id=1, source_target_pairs={{0,4},{1,3},{2,0},{3,7},{4,8},{5,1},{6,2},{7,11},{8,12},{9,5},{10,... | collective-permute-start | bytes 393224 | tf_op jit(solution)/shard_map/ppermute | solution.py:74
  9.1 1.5 %collective-permute-start.2 = (bf16[32,2048]{1,0:T(8,128)(2,1)S(1)}, bf16[32,2048]{1,0:T(8,128)(2,1)S(1)}, u32[]{:S(2)}, u32[]{:S(2)}) collective-permute-start(bf16[32,2048]{1,0:T(8,128)(2,1)S(1)} %collective-permute-done.1), channel_id=1, source_target_pairs={{0,4},{1,3},{2,0},{3,7},{4,8},{5,1},{6,2},{7,11},{8,12},{9,5},{10,... | collective-permute-start | bytes 393224 | tf_op jit(solution)/shard_map/ppermute | solution.py:74
  10.6 1.8 %collective-permute-done.5 = bf16[32,2048]{1,0:T(8,128)(2,1)S(1)} collective-permute-done((bf16[32,2048]{1,0:T(8,128)(2,1)S(1)}, bf16[32,2048]{1,0:T(8,128)(2,1)S(1)}, u32[]{:S(2)}, u32[]{:S(2)}) %collective-permute-start.5) | collective-permute-done | bytes 131104 | tf_op jit(solution)/shard_map/ppermute | solution.py:74
  12.5 1.6 %collective-permute-start.6 = (bf16[32,2048]{1,0:T(8,128)(2,1)S(1)}, bf16[32,2048]{1,0:T(8,128)(2,1)S(1)}, u32[]{:S(2)}, u32[]{:S(2)}) collective-permute-start(bf16[32,2048]{1,0:T(8,128)(2,1)S(1)} %collective-permute-done.5), channel_id=1, source_target_pairs={{0,4},{1,3},{2,0},{3,7},{4,8},{5,1},{6,2},{7,11},{8,12},{9,5},{10,... | collective-permute-start | bytes 393224 | tf_op jit(solution)/shard_map/ppermute | solution.py:74
  14.1 1.5 %collective-permute-start.3 = (bf16[32,2048]{1,0:T(8,128)(2,1)S(1)}, bf16[32,2048]{1,0:T(8,128)(2,1)S(1)}, u32[]{:S(2)}, u32[]{:S(2)}) collective-permute-start(bf16[32,2048]{1,0:T(8,128)(2,1)S(1)} %collective-permute-done.2), channel_id=1, source_target_pairs={{0,4},{1,3},{2,0},{3,7},{4,8},{5,1},{6,2},{7,11},{8,12},{9,5},{10,... | collective-permute-start | bytes 393224 | tf_op jit(solution)/shard_map/ppermute | solution.py:74
  15.6 0.8 fusion.57
  16.4 1.0 collective-permute-done.6
  17.4 1.6 %collective-permute-start.8 = (bf16[32,2048]{1,0:T(8,128)(2,1)S(1)}, bf16[32,2048]{1,0:T(8,128)(2,1)S(1)}, u32[]{:S(2)}, u32[]{:S(2)}) collective-permute-start(bf16[32,2048]{1,0:T(8,128)(2,1)S(1)} %collective-permute-done.6), channel_id=1, source_target_pairs={{0,4},{1,3},{2,0},{3,7},{4,8},{5,1},{6,2},{7,11},{8,12},{9,5},{10,... | collective-permute-start | bytes 393224 | tf_op jit(solution)/shard_map/ppermute | solution.py:74
  19.0 0.9 broadcast_select_fusion.9
  20.4 2.0 %collective-permute-done.8 = bf16[32,2048]{1,0:T(8,128)(2,1)S(1)} collective-permute-done((bf16[32,2048]{1,0:T(8,128)(2,1)S(1)}, bf16[32,2048]{1,0:T(8,128)(2,1)S(1)}, u32[]{:S(2)}, u32[]{:S(2)}) %collective-permute-start.8) | collective-permute-done | bytes 131104 | tf_op jit(solution)/shard_map/ppermute | solution.py:74
  22.4 1.3 %collective-permute-done.9 = bf16[32,2048]{1,0:T(8,128)(2,1)S(1)} collective-permute-done((bf16[32,2048]{1,0:T(8,128)(2,1)S(1)}, bf16[32,2048]{1,0:T(8,128)(2,1)S(1)}, u32[]{:S(2)}, u32[]{:S(2)}) %collective-permute-start.9) | collective-permute-done | bytes 131104 | tf_op jit(solution)/shard_map/ppermute | solution.py:50
  24.0 0.5 fusion
  24.6 0.8 convolution_bitcast_fusion
  26.1 0.7 dynamic_slice.27
  27.1 0.4 collective-permute-start.17
  27.5 0.9 collective-permute-done.10
  28.5 1.5 %collective-permute-start.11 = (bf16[64,547]{1,0:T(8,128)(2,1)S(1)}, bf16[64,547]{1,0:T(8,128)(2,1)S(1)}, u32[]{:S(2)}, u32[]{:S(2)}) collective-permute-start(bf16[64,547]{1,0:T(8,128)(2,1)S(1)} %dynamic-slice_convert_fusion.2), channel_id=1, source_target_pairs={{0,2},{2,0},{4,6},{6,4},{8,10},{10,8},{12,14},{14,12},{1,3},{3,1},... | collective-permute-start | bytes 210056 | tf_op jit(solution)/shard_map/ppermute | solution.py:54
  30.0 3.0 %fusion.3.z_hbm = f32[256,256]{1,0:T(8,128)S(1)} fusion(bf16[4096,256]{1,0:T(8,128)(2,1)} %param.27, bf16[256,4096]{1,0:T(8,128)(2,1)} %copy-done.7, f32[4096]{0:T(1024)S(1)} %copy-done.14, f32[256]{0:T(256)S(1)} %add_rsqrt_fusion), kind=kOutput, calls=%fused_computation.19 | convolution fusion | flops 541065216 | bytes 4473856 | tf_op jit(solution)/shard_map/dot_general | solution.py:517
  33.1 1.6 %collective-permute-start.12 = (bf16[64,547]{1,0:T(8,128)(2,1)S(1)}, bf16[64,547]{1,0:T(8,128)(2,1)S(1)}, u32[]{:S(2)}, u32[]{:S(2)}) collective-permute-start(bf16[64,547]{1,0:T(8,128)(2,1)S(1)} %fusion.35), channel_id=1, source_target_pairs={{0,4},{2,6},{4,0},{6,2},{8,12},{10,14},{12,8},{14,10},{1,5},{3,7},... | collective-permute-start | bytes 210056 | tf_op jit(solution)/shard_map/ppermute | solution.py:54
  34.7 2.9 %collective-permute-done.12 = bf16[64,547]{1,0:T(8,128)(2,1)S(1)} collective-permute-done((bf16[64,547]{1,0:T(8,128)(2,1)S(1)}, bf16[64,547]{1,0:T(8,128)(2,1)S(1)}, u32[]{:S(2)}, u32[]{:S(2)}) %collective-permute-start.12) | collective-permute-done | bytes 70048 | tf_op jit(solution)/shard_map/ppermute | solution.py:54
  37.6 2.6 %collective-permute-start.13 = (bf16[64,547]{1,0:T(8,128)(2,1)S(1)}, bf16[64,547]{1,0:T(8,128)(2,1)S(1)}, u32[]{:S(2)}, u32[]{:S(2)}) collective-permute-start(bf16[64,547]{1,0:T(8,128)(2,1)S(1)} %fusion.34), channel_id=1, source_target_pairs={{0,8},{2,10},{4,12},{6,14},{8,0},{10,2},{12,4},{14,6},{1,9},{3,11}... | collective-permute-start | bytes 210056 | tf_op jit(solution)/shard_map/ppermute | solution.py:54
  40.2 2.8 %collective-permute-done.13 = bf16[64,547]{1,0:T(8,128)(2,1)S(1)} collective-permute-done((bf16[64,547]{1,0:T(8,128)(2,1)S(1)}, bf16[64,547]{1,0:T(8,128)(2,1)S(1)}, u32[]{:S(2)}, u32[]{:S(2)}) %collective-permute-start.13) | collective-permute-done | bytes 70048 | tf_op jit(solution)/shard_map/ppermute | solution.py:54
  43.1 1.5 %collective-permute-start.14 = (bf16[64,547]{1,0:T(8,128)(2,1)S(1)}, bf16[64,547]{1,0:T(8,128)(2,1)S(1)}, u32[]{:S(2)}, u32[]{:S(2)}) collective-permute-start(bf16[64,547]{1,0:T(8,128)(2,1)S(1)} %get-tuple-element.47), channel_id=1, source_target_pairs={{0,2},{2,0},{4,6},{6,4},{8,10},{10,8},{12,14},{14,12},{1,3},{3,1},... | collective-permute-start | bytes 210056 | tf_op jit(solution)/shard_map/ppermute | solution.py:54
  44.6 3.0 %collective-permute-done.14 = bf16[64,547]{1,0:T(8,128)(2,1)S(1)} collective-permute-done((bf16[64,547]{1,0:T(8,128)(2,1)S(1)}, bf16[64,547]{1,0:T(8,128)(2,1)S(1)}, u32[]{:S(2)}, u32[]{:S(2)}) %collective-permute-start.14) | collective-permute-done | bytes 70048 | tf_op jit(solution)/shard_map/ppermute | solution.py:54
  47.8 1.4 %collective-permute-done.15.theirs = bf16[128,547]{1,0:T(8,128)(2,1)} collective-permute-done((bf16[128,547]{1,0:T(8,128)(2,1)S(1)}, bf16[128,547]{1,0:T(8,128)(2,1)}, u32[]{:S(2)}, u32[]{:S(2)}) %collective-permute-start.15) | collective-permute-done | bytes 140064 | tf_op jit(solution)/shard_map/ppermute | solution.py:50
  49.2 4.9 %scan.1 = (f32[256,256]{1,0:T(8,128)S(1)}, f32[32,16,256]{2,1,0:T(8,128)}, f32[256,3]{1,0:T(8,128)S(1)}) custom-call(s32[6]{0:T(128)S(1)} %stack.32.place_ref, bf16[128,547]{1,0:T(8,128)(2,1)S(1)} %constant_dynamic-update-slice_fusion.mine, bf16[128,547]{1,0:T(8,128)(2,1)} %collective-permute-done.15.theirs, bf16[512,256]{1,0:T(8,128)(2,1)S(1)} %copy-done.2, ...), custom_call_target="tpu_custom_call" | custom-call | tf_op jit(solution)/shard_map/scan/pallas_call | solution.py:217
  54.6 1.0 collective-permute-done.16.h_ref
  55.6 3.4 %project.1 = (f32[96,2048]{1,0:T(8,128)S(1)}, bf16[32,2048]{1,0:T(8,128)(2,1)S(1)}, f32[32,2048]{1,0:T(8,128)S(1)}, f32[96,2048]{1,0:T(8,128)S(1)}) custom-call(s32[6]{0:T(128)S(1)} %stack.32.place_ref, s32[256,1]{1,0:T(8,128)S(1)} %get-tuple-element.45.id_ref, bf16[256,256]{1,0:T(8,128)(2,1)S(1)} %convert_element_type.146.g_ref, ...), custom_call_target="tpu_custom_call" | custom-call | tf_op jit(solution)/shard_map/project/pallas_call | solution.py:334
  59.0 1.6 %collective-permute-start.18 = (bf16[32,2048]{1,0:T(8,128)(2,1)S(1)}, bf16[32,2048]{1,0:T(8,128)(2,1)S(1)}, u32[]{:S(2)}, u32[]{:S(2)}) collective-permute-start(bf16[32,2048]{1,0:T(8,128)(2,1)S(1)} %get-tuple-element.36), channel_id=1, source_target_pairs={{0,4},{1,3},{2,0},{3,7},{4,8},{5,1},{6,2},{7,11},{8,12},{9,5},{10,... | collective-permute-start | bytes 393224 | tf_op jit(solution)/shard_map/ppermute | solution.py:353
  60.9 1.7 %collective-permute-start.22 = (bf16[32,2048]{1,0:T(8,128)(2,1)S(1)}, bf16[32,2048]{1,0:T(8,128)(2,1)S(1)}, u32[]{:S(2)}, u32[]{:S(2)}) collective-permute-start(bf16[32,2048]{1,0:T(8,128)(2,1)S(1)} %slice.204), channel_id=1, source_target_pairs={{0,4},{1,3},{2,0},{3,7},{4,8},{5,1},{6,2},{7,11},{8,12},{9,5},{10,... | collective-permute-start | bytes 393224 | tf_op jit(solution)/shard_map/ppermute | solution.py:353
  62.6 1.5 %collective-permute-done.18 = bf16[32,2048]{1,0:T(8,128)(2,1)S(1)} collective-permute-done((bf16[32,2048]{1,0:T(8,128)(2,1)S(1)}, bf16[32,2048]{1,0:T(8,128)(2,1)S(1)}, u32[]{:S(2)}, u32[]{:S(2)}) %collective-permute-start.18) | collective-permute-done | bytes 131104 | tf_op jit(solution)/shard_map/ppermute | solution.py:353
  64.1 1.6 %collective-permute-start.19 = (bf16[32,2048]{1,0:T(8,128)(2,1)S(1)}, bf16[32,2048]{1,0:T(8,128)(2,1)S(1)}, u32[]{:S(2)}, u32[]{:S(2)}) collective-permute-start(bf16[32,2048]{1,0:T(8,128)(2,1)S(1)} %add_convert_fusion.6), channel_id=1, source_target_pairs={{0,4},{1,3},{2,0},{3,7},{4,8},{5,1},{6,2},{7,11},{8,12},{9,5},{10,... | collective-permute-start | bytes 393224 | tf_op jit(solution)/shard_map/ppermute | solution.py:353
  66.0 1.7 %collective-permute-start.23 = (bf16[32,2048]{1,0:T(8,128)(2,1)S(1)}, bf16[32,2048]{1,0:T(8,128)(2,1)S(1)}, u32[]{:S(2)}, u32[]{:S(2)}) collective-permute-start(bf16[32,2048]{1,0:T(8,128)(2,1)S(1)} %add_convert_fusion.3), channel_id=1, source_target_pairs={{0,4},{1,3},{2,0},{3,7},{4,8},{5,1},{6,2},{7,11},{8,12},{9,5},{10,... | collective-permute-start | bytes 393224 | tf_op jit(solution)/shard_map/ppermute | solution.py:353
  67.6 1.5 %collective-permute-done.19 = bf16[32,2048]{1,0:T(8,128)(2,1)S(1)} collective-permute-done((bf16[32,2048]{1,0:T(8,128)(2,1)S(1)}, bf16[32,2048]{1,0:T(8,128)(2,1)S(1)}, u32[]{:S(2)}, u32[]{:S(2)}) %collective-permute-start.19) | collective-permute-done | bytes 131104 | tf_op jit(solution)/shard_map/ppermute | solution.py:353
  69.1 1.6 %collective-permute-start.20 = (bf16[32,2048]{1,0:T(8,128)(2,1)S(1)}, bf16[32,2048]{1,0:T(8,128)(2,1)S(1)}, u32[]{:S(2)}, u32[]{:S(2)}) collective-permute-start(bf16[32,2048]{1,0:T(8,128)(2,1)S(1)} %add_convert_fusion.5), channel_id=1, source_target_pairs={{0,4},{1,3},{2,0},{3,7},{4,8},{5,1},{6,2},{7,11},{8,12},{9,5},{10,... | collective-permute-start | bytes 393224 | tf_op jit(solution)/shard_map/ppermute | solution.py:353
  71.0 1.7 %collective-permute-start.24 = (bf16[32,2048]{1,0:T(8,128)(2,1)S(1)}, bf16[32,2048]{1,0:T(8,128)(2,1)S(1)}, u32[]{:S(2)}, u32[]{:S(2)}) collective-permute-start(bf16[32,2048]{1,0:T(8,128)(2,1)S(1)} %add_convert_fusion.2), channel_id=1, source_target_pairs={{0,4},{1,3},{2,0},{3,7},{4,8},{5,1},{6,2},{7,11},{8,12},{9,5},{10,... | collective-permute-start | bytes 393224 | tf_op jit(solution)/shard_map/ppermute | solution.py:353
  72.7 1.5 %collective-permute-done.20 = bf16[32,2048]{1,0:T(8,128)(2,1)S(1)} collective-permute-done((bf16[32,2048]{1,0:T(8,128)(2,1)S(1)}, bf16[32,2048]{1,0:T(8,128)(2,1)S(1)}, u32[]{:S(2)}, u32[]{:S(2)}) %collective-permute-start.20) | collective-permute-done | bytes 131104 | tf_op jit(solution)/shard_map/ppermute | solution.py:353
  74.2 1.8 %collective-permute-start.21 = (bf16[32,2048]{1,0:T(8,128)(2,1)S(1)}, bf16[32,2048]{1,0:T(8,128)(2,1)S(1)}, u32[]{:S(2)}, u32[]{:S(2)}) collective-permute-start(bf16[32,2048]{1,0:T(8,128)(2,1)S(1)} %add_convert_fusion.4), channel_id=1, source_target_pairs={{0,4},{1,3},{2,0},{3,7},{4,8},{5,1},{6,2},{7,11},{8,12},{9,5},{10,... | collective-permute-start | bytes 393224 | tf_op jit(solution)/shard_map/ppermute | solution.py:353
  76.3 1.1 collective-permute-done.25
  77.4 2.0 %collective-permute-done.21 = bf16[32,2048]{1,0:T(8,128)(2,1)S(1)} collective-permute-done((bf16[32,2048]{1,0:T(8,128)(2,1)S(1)}, bf16[32,2048]{1,0:T(8,128)(2,1)S(1)}, u32[]{:S(2)}, u32[]{:S(2)}) %collective-permute-start.21) | collective-permute-done | bytes 131104 | tf_op jit(solution)/shard_map/ppermute | solution.py:353
  79.4 1.5 %collective-permute-start.27 = (bf16[32,2048]{1,0:T(8,128)(2,1)S(1)}, bf16[32,2048]{1,0:T(8,128)(2,1)S(1)}, u32[]{:S(2)}, u32[]{:S(2)}) collective-permute-start(bf16[32,2048]{1,0:T(8,128)(2,1)S(1)} %add_convert_fusion.1.refs_0_), channel_id=1, source_target_pairs={{0,2},{2,0},{4,6},{6,4},{8,10},{10,8},{12,14},{14,12},{1,3},{3,1},... | collective-permute-start | bytes 393224 | tf_op jit(solution)/shard_map/ppermute | solution.py:54
  80.9 1.6 %collective-permute-start.28 = (bf16[32,2048]{1,0:T(8,128)(2,1)S(1)}, bf16[32,2048]{1,0:T(8,128)(2,1)S(1)}, u32[]{:S(2)}, u32[]{:S(2)}) collective-permute-start(bf16[32,2048]{1,0:T(8,128)(2,1)S(1)} %add_convert_fusion.1.refs_0_), channel_id=1, source_target_pairs={{0,4},{2,6},{4,0},{6,2},{8,12},{10,14},{12,8},{14,10},{1,5},{3,7},... | collective-permute-start | bytes 393224 | tf_op jit(solution)/shard_map/ppermute | solution.py:54
  82.5 0.5 collective-permute-start.29
  83.3 2.6 %collective-permute-done.27.refs_1_ = bf16[32,2048]{1,0:T(8,128)(2,1)S(1)} collective-permute-done((bf16[32,2048]{1,0:T(8,128)(2,1)S(1)}, bf16[32,2048]{1,0:T(8,128)(2,1)S(1)}, u32[]{:S(2)}, u32[]{:S(2)}) %collective-permute-start.27) | collective-permute-done | bytes 131104 | tf_op jit(solution)/shard_map/ppermute | solution.py:54
  85.9 0.5 collective-permute-start.31
  86.4 2.0 %collective-permute-done.29.refs_3_ = bf16[32,2048]{1,0:T(8,128)(2,1)S(1)} collective-permute-done((bf16[32,2048]{1,0:T(8,128)(2,1)S(1)}, bf16[32,2048]{1,0:T(8,128)(2,1)S(1)}, u32[]{:S(2)}, u32[]{:S(2)}) %collective-permute-start.29) | collective-permute-done | bytes 131104 | tf_op jit(solution)/shard_map/ppermute | solution.py:54
  88.6 1.1 collective-permute-done.32.refs_7_
  89.7 7.6 %experts.1 = f32[128,4096]{1,0:T(8,128)S(1)} custom-call(s32[6]{0:T(128)S(1)} %stack.32.place_ref, bf16[32,2048]{1,0:T(8,128)(2,1)S(1)} %add_convert_fusion.1.refs_0_, bf16[32,2048]{1,0:T(8,128)(2,1)S(1)} %collective-permute-done.27.refs_1_, bf16[32,2048]{1,0:T(8,128)(2,1)S(1)} %collective-permute-done.28.refs_2_, ...), custom_call_target="tpu_custom_call" | custom-call | tf_op jit(solution)/shard_map/experts/pallas_call | solution.py:422
  97.6 0.3 fusion.9
  97.9 1.5 %collective-permute-done.33 = bf16[128,2048]{1,0:T(8,128)(2,1)S(1)} collective-permute-done((bf16[128,2048]{1,0:T(8,128)(2,1)S(1)}, bf16[128,2048]{1,0:T(8,128)(2,1)S(1)}, u32[]{:S(2)}, u32[]{:S(2)}) %collective-permute-start.33) | collective-permute-done | bytes 524320 | tf_op jit(solution)/shard_map/ppermute | solution.py:50
  99.6 1.5 %collective-permute-start.36 = (bf16[32,2048]{1,0:T(8,128)(2,1)S(1)}, bf16[32,2048]{1,0:T(8,128)(2,1)S(1)}, u32[]{:S(2)}, u32[]{:S(2)}) collective-permute-start(bf16[32,2048]{1,0:T(8,128)(2,1)S(1)} %get-tuple-element.49), channel_id=1, source_target_pairs={{0,6},{2,4},{4,2},{6,0},{8,14},{10,12},{12,10},{14,8},{1,7},{3,5},... | collective-permute-start | bytes 393224 | tf_op jit(solution)/shard_map/ppermute | solution.py:54
  101.0 0.7 collective-permute-start.35
  101.7 1.4 %collective-permute-start.34 = (bf16[32,2048]{1,0:T(8,128)(2,1)S(1)}, bf16[32,2048]{1,0:T(8,128)(2,1)S(1)}, u32[]{:S(2)}, u32[]{:S(2)}) collective-permute-start(bf16[32,2048]{1,0:T(8,128)(2,1)S(1)} %get-tuple-element.48), channel_id=1, source_target_pairs={{0,2},{2,0},{4,6},{6,4},{8,10},{10,8},{12,14},{14,12},{1,3},{3,1},... | collective-permute-start | bytes 393224 | tf_op jit(solution)/shard_map/ppermute | solution.py:54
  103.2 3.7 %collective-permute-done.36 = bf16[32,2048]{1,0:T(8,128)(2,1)S(1)} collective-permute-done((bf16[32,2048]{1,0:T(8,128)(2,1)S(1)}, bf16[32,2048]{1,0:T(8,128)(2,1)S(1)}, u32[]{:S(2)}, u32[]{:S(2)}) %collective-permute-start.36) | collective-permute-done | bytes 131104 | tf_op jit(solution)/shard_map/ppermute | solution.py:54
  106.9 1.2 %collective-permute-done.35 = bf16[32,2048]{1,0:T(8,128)(2,1)S(1)} collective-permute-done((bf16[32,2048]{1,0:T(8,128)(2,1)S(1)}, bf16[32,2048]{1,0:T(8,128)(2,1)S(1)}, u32[]{:S(2)}, u32[]{:S(2)}) %collective-permute-start.35) | collective-permute-done | bytes 131104 | tf_op jit(solution)/shard_map/ppermute | solution.py:54
  108.1 0.8 collective-permute-done.34
  109.0 3.4 %collective-permute-start.37 = (bf16[16,2048]{1,0:T(8,128)(2,1)S(1)}, bf16[16,2048]{1,0:T(8,128)(2,1)S(1)}, u32[]{:S(2)}, u32[]{:S(2)}) collective-permute-start(bf16[16,2048]{1,0:T(8,128)(2,1)S(1)} %get-tuple-element.64), channel_id=1, source_target_pairs={{0,8},{2,10},{4,12},{6,14},{8,0},{10,2},{12,4},{14,6},{1,9},{3,11}... | collective-permute-start | bytes 196616 | tf_op jit(solution)/shard_map/ppermute | solution.py:54
  112.6 3.1 %collective-permute-done.37 = bf16[16,2048]{1,0:T(8,128)(2,1)S(1)} collective-permute-done((bf16[16,2048]{1,0:T(8,128)(2,1)S(1)}, bf16[16,2048]{1,0:T(8,128)(2,1)S(1)}, u32[]{:S(2)}, u32[]{:S(2)}) %collective-permute-start.37) | collective-permute-done | bytes 65568 | tf_op jit(solution)/shard_map/ppermute | solution.py:54
  115.7 0.9 convolution_convert_fusion
  (110 shorter events, 5.3 us)
Async XLA Ops:
  0.6 23.9 %copy-start = (bf16[4096,256]{1,0:T(8,128)(2,1)S(1)}, bf16[4096,256]{1,0:T(8,128)(2,1)}, u32[]{:S(2)}) copy-start(bf16[4096,256]{1,0:T(8,128)(2,1)} %param.26) | copy-start | bytes 6291460
  0.6 3.2 %collective-permute-start = (bf16[32,2048]{1,0:T(8,128)(2,1)}, bf16[32,2048]{1,0:T(8,128)(2,1)S(1)}, u32[]{:S(2)}, u32[]{:S(2)}) collective-permute-start(bf16[32,2048]{1,0:T(8,128)(2,1)} %param.21), channel_id=1, source_target_pairs={{0,1},{1,0},{2,3},{3,2},{4,5},{5,4},{6,7},{7,6},{8,9},{9,8},{10,11... | collective-permute-start | bytes 393224 | tf_op jit(solution)/shard_map/ppermute | solution.py:50
  1.2 6.3 %collective-permute-start.4 = (bf16[32,2048]{1,0:T(8,128)(2,1)}, bf16[32,2048]{1,0:T(8,128)(2,1)S(1)}, u32[]{:S(2)}, u32[]{:S(2)}) collective-permute-start(bf16[32,2048]{1,0:T(8,128)(2,1)} %param.21), channel_id=1, source_target_pairs={{0,4},{1,3},{2,0},{3,7},{4,8},{5,1},{6,2},{7,11},{8,12},{9,5},{10,... | collective-permute-start | bytes 393224 | tf_op jit(solution)/shard_map/ppermute | solution.py:74
  3.8 5.3 %collective-permute-start.1 = (bf16[32,2048]{1,0:T(8,128)(2,1)S(1)}, bf16[32,2048]{1,0:T(8,128)(2,1)S(1)}, u32[]{:S(2)}, u32[]{:S(2)}) collective-permute-start(bf16[32,2048]{1,0:T(8,128)(2,1)S(1)} %collective-permute-done), channel_id=1, source_target_pairs={{0,4},{1,3},{2,0},{3,7},{4,8},{5,1},{6,2},{7,11},{8,12},{9,5},{10,... | collective-permute-start | bytes 393224 | tf_op jit(solution)/shard_map/ppermute | solution.py:74
  7.5 5.0 %collective-permute-start.5 = (bf16[32,2048]{1,0:T(8,128)(2,1)S(1)}, bf16[32,2048]{1,0:T(8,128)(2,1)S(1)}, u32[]{:S(2)}, u32[]{:S(2)}) collective-permute-start(bf16[32,2048]{1,0:T(8,128)(2,1)S(1)} %collective-permute-done.4), channel_id=1, source_target_pairs={{0,4},{1,3},{2,0},{3,7},{4,8},{5,1},{6,2},{7,11},{8,12},{9,5},{10,... | collective-permute-start | bytes 393224 | tf_op jit(solution)/shard_map/ppermute | solution.py:74
  9.1 5.0 %collective-permute-start.2 = (bf16[32,2048]{1,0:T(8,128)(2,1)S(1)}, bf16[32,2048]{1,0:T(8,128)(2,1)S(1)}, u32[]{:S(2)}, u32[]{:S(2)}) collective-permute-start(bf16[32,2048]{1,0:T(8,128)(2,1)S(1)} %collective-permute-done.1), channel_id=1, source_target_pairs={{0,4},{1,3},{2,0},{3,7},{4,8},{5,1},{6,2},{7,11},{8,12},{9,5},{10,... | collective-permute-start | bytes 393224 | tf_op jit(solution)/shard_map/ppermute | solution.py:74
  12.5 5.0 %collective-permute-start.6 = (bf16[32,2048]{1,0:T(8,128)(2,1)S(1)}, bf16[32,2048]{1,0:T(8,128)(2,1)S(1)}, u32[]{:S(2)}, u32[]{:S(2)}) collective-permute-start(bf16[32,2048]{1,0:T(8,128)(2,1)S(1)} %collective-permute-done.5), channel_id=1, source_target_pairs={{0,4},{1,3},{2,0},{3,7},{4,8},{5,1},{6,2},{7,11},{8,12},{9,5},{10,... | collective-permute-start | bytes 393224 | tf_op jit(solution)/shard_map/ppermute | solution.py:74
  14.1 5.0 %collective-permute-start.3 = (bf16[32,2048]{1,0:T(8,128)(2,1)S(1)}, bf16[32,2048]{1,0:T(8,128)(2,1)S(1)}, u32[]{:S(2)}, u32[]{:S(2)}) collective-permute-start(bf16[32,2048]{1,0:T(8,128)(2,1)S(1)} %collective-permute-done.2), channel_id=1, source_target_pairs={{0,4},{1,3},{2,0},{3,7},{4,8},{5,1},{6,2},{7,11},{8,12},{9,5},{10,... | collective-permute-start | bytes 393224 | tf_op jit(solution)/shard_map/ppermute | solution.py:74
  17.4 5.0 %collective-permute-start.8 = (bf16[32,2048]{1,0:T(8,128)(2,1)S(1)}, bf16[32,2048]{1,0:T(8,128)(2,1)S(1)}, u32[]{:S(2)}, u32[]{:S(2)}) collective-permute-start(bf16[32,2048]{1,0:T(8,128)(2,1)S(1)} %collective-permute-done.6), channel_id=1, source_target_pairs={{0,4},{1,3},{2,0},{3,7},{4,8},{5,1},{6,2},{7,11},{8,12},{9,5},{10,... | collective-permute-start | bytes 393224 | tf_op jit(solution)/shard_map/ppermute | solution.py:74
  20.1 3.7 %collective-permute-start.7 = (bf16[96,4096]{1,0:T(8,128)(2,1)S(1)}, bf16[96,4096]{1,0:T(8,128)(2,1)S(1)}, u32[]{:S(2)}, u32[]{:S(2)}) collective-permute-start(bf16[96,4096]{1,0:T(8,128)(2,1)S(1)} %maximum_maximum_fusion), channel_id=1, source_target_pairs={{0,1},{1,0},{2,3},{3,2},{4,5},{5,4},{6,7},{7,6},{8,9},{9,8},{10,11... | collective-permute-start | bytes 2359304 | tf_op jit(solution)/shard_map/ppermute | solution.py:50
  22.4 1.3 %collective-permute-start.9 = (bf16[32,2048]{1,0:T(8,128)(2,1)S(1)}, bf16[32,2048]{1,0:T(8,128)(2,1)S(1)}, u32[]{:S(2)}, u32[]{:S(2)}) collective-permute-start(bf16[32,2048]{1,0:T(8,128)(2,1)S(1)} %collective-permute-done.8), channel_id=1, source_target_pairs={{0,1},{1,0},{2,3},{3,2},{4,5},{5,4},{6,7},{7,6},{8,9},{9,8},{10,11... | collective-permute-start | bytes 393224 | tf_op jit(solution)/shard_map/ppermute | solution.py:50
  23.9 0.7 copy-start.14
  24.0 2.1 %copy-start.7 = (bf16[256,4096]{1,0:T(8,128)(2,1)}, bf16[256,4096]{1,0:T(8,128)(2,1)S(1)}, u32[]{:S(2)}) copy-start(bf16[256,4096]{1,0:T(8,128)(2,1)S(1)} %maximum_dynamic-update-slice_fusion.4) | copy-start | bytes 6291460
  24.6 0.8 copy-start.12
  24.6 1.1 copy-start.11
  24.6 1.2 %copy-start.10 = (bf16[256,512]{1,0:T(8,128)(2,1)S(1)}, bf16[256,512]{1,0:T(8,128)(2,1)}, u32[]{:S(2)}) copy-start(bf16[256,512]{1,0:T(8,128)(2,1)} %param.30) | copy-start | bytes 786436
  26.9 1.5 %collective-permute-start.10 = (bf16[128,547]{1,0:T(8,128)(2,1)S(1)}, bf16[128,547]{1,0:T(8,128)(2,1)S(1)}, u32[]{:S(2)}, u32[]{:S(2)}) collective-permute-start(bf16[128,547]{1,0:T(8,128)(2,1)S(1)} %dynamic-slice_convert_fusion.1), channel_id=1, source_target_pairs={{0,1},{1,0},{2,3},{3,2},{4,5},{5,4},{6,7},{7,6},{8,9},{9,8},{10,11... | collective-permute-start | bytes 420104 | tf_op jit(solution)/shard_map/ppermute | solution.py:50
  27.1 28.5 %collective-permute-start.17 = (bf16[256,4096]{1,0:T(8,128)(2,1)}, bf16[256,4096]{1,0:T(8,128)(2,1)}, u32[]{:S(2)}, u32[]{:S(2)}) collective-permute-start(bf16[256,4096]{1,0:T(8,128)(2,1)} %wg_ref.1), channel_id=1, source_target_pairs={{0,1},{1,0},{2,3},{3,2},{4,5},{5,4},{6,7},{7,6},{8,9},{9,8},{10,11... | collective-permute-start | bytes 6291464 | tf_op jit(solution)/shard_map/ppermute | solution.py:50
  28.4 20.8 %copy-start.1 = (f32[32,16,256]{2,1,0:T(8,128)S(1)}, f32[32,16,256]{2,1,0:T(8,128)}, u32[]{:S(2)}) copy-start(f32[32,16,256]{2,1,0:T(8,128)} %state_hbm.1) | copy-start | bytes 1572868
  28.4 20.8 %copy-start.2 = (bf16[512,256]{1,0:T(8,128)(2,1)S(1)}, bf16[512,256]{1,0:T(8,128)(2,1)}, u32[]{:S(2)}) copy-start(bf16[512,256]{1,0:T(8,128)(2,1)} %dt_proj.1) | copy-start | bytes 786436
  28.4 20.8 %copy-start.3 = (f32[16,256]{1,0:T(8,128)S(1)}, f32[16,256]{1,0:T(8,128)}, u32[]{:S(2)}) copy-start(f32[16,256]{1,0:T(8,128)} %a_rate.1) | copy-start | bytes 49156
  28.5 20.8 %copy-start.5 = (f32[256]{0:T(256)S(1)}, f32[256]{0:T(256)}, u32[]{:S(2)}) copy-start(f32[256]{0:T(256)} %param.33) | copy-start | bytes 3076
  28.5 20.8 %copy-start.6 = (f32[256]{0:T(256)S(1)}, f32[256]{0:T(256)}, u32[]{:S(2)}) copy-start(f32[256]{0:T(256)} %param.35) | copy-start | bytes 3076
  28.5 4.6 %collective-permute-start.11 = (bf16[64,547]{1,0:T(8,128)(2,1)S(1)}, bf16[64,547]{1,0:T(8,128)(2,1)S(1)}, u32[]{:S(2)}, u32[]{:S(2)}) collective-permute-start(bf16[64,547]{1,0:T(8,128)(2,1)S(1)} %dynamic-slice_convert_fusion.2), channel_id=1, source_target_pairs={{0,2},{2,0},{4,6},{6,4},{8,10},{10,8},{12,14},{14,12},{1,3},{3,1},... | collective-permute-start | bytes 210056 | tf_op jit(solution)/shard_map/ppermute | solution.py:54
  33.1 4.5 %collective-permute-start.12 = (bf16[64,547]{1,0:T(8,128)(2,1)S(1)}, bf16[64,547]{1,0:T(8,128)(2,1)S(1)}, u32[]{:S(2)}, u32[]{:S(2)}) collective-permute-start(bf16[64,547]{1,0:T(8,128)(2,1)S(1)} %fusion.35), channel_id=1, source_target_pairs={{0,4},{2,6},{4,0},{6,2},{8,12},{10,14},{12,8},{14,10},{1,5},{3,7},... | collective-permute-start | bytes 210056 | tf_op jit(solution)/shard_map/ppermute | solution.py:54
  37.6 5.4 %collective-permute-start.13 = (bf16[64,547]{1,0:T(8,128)(2,1)S(1)}, bf16[64,547]{1,0:T(8,128)(2,1)S(1)}, u32[]{:S(2)}, u32[]{:S(2)}) collective-permute-start(bf16[64,547]{1,0:T(8,128)(2,1)S(1)} %fusion.34), channel_id=1, source_target_pairs={{0,8},{2,10},{4,12},{6,14},{8,0},{10,2},{12,4},{14,6},{1,9},{3,11}... | collective-permute-start | bytes 210056 | tf_op jit(solution)/shard_map/ppermute | solution.py:54
  43.1 4.5 %collective-permute-start.14 = (bf16[64,547]{1,0:T(8,128)(2,1)S(1)}, bf16[64,547]{1,0:T(8,128)(2,1)S(1)}, u32[]{:S(2)}, u32[]{:S(2)}) collective-permute-start(bf16[64,547]{1,0:T(8,128)(2,1)S(1)} %get-tuple-element.47), channel_id=1, source_target_pairs={{0,2},{2,0},{4,6},{6,4},{8,10},{10,8},{12,14},{14,12},{1,3},{3,1},... | collective-permute-start | bytes 210056 | tf_op jit(solution)/shard_map/ppermute | solution.py:54
  47.6 1.6 %collective-permute-start.15 = (bf16[128,547]{1,0:T(8,128)(2,1)S(1)}, bf16[128,547]{1,0:T(8,128)(2,1)}, u32[]{:S(2)}, u32[]{:S(2)}) collective-permute-start(bf16[128,547]{1,0:T(8,128)(2,1)S(1)} %constant_dynamic-update-slice_fusion.mine), channel_id=1, source_target_pairs={{0,1},{1,0},{2,3},{3,2},{4,5},{5,4},{6,7},{7,6},{8,9},{9,8},{10,11... | collective-permute-start | bytes 420104 | tf_op jit(solution)/shard_map/ppermute | solution.py:50
  54.2 1.4 %collective-permute-start.16 = (bf16[256,256]{1,0:T(8,128)(2,1)S(1)}, bf16[256,256]{1,0:T(8,128)(2,1)S(1)}, u32[]{:S(2)}, u32[]{:S(2)}) collective-permute-start(bf16[256,256]{1,0:T(8,128)(2,1)S(1)} %convert_element_type.146.g_ref), channel_id=1, source_target_pairs={{0,1},{1,0},{2,3},{3,2},{4,5},{5,4},{6,7},{7,6},{8,9},{9,8},{10,11... | collective-permute-start | bytes 393224 | tf_op jit(solution)/shard_map/ppermute | solution.py:50
  55.6 5.0 %copy-start.9 = (bf16[32,2048]{1,0:T(8,128)(2,1)S(1)}, bf16[32,2048]{1,0:T(8,128)(2,1)}, u32[]{:S(2)}) copy-start(bf16[32,2048]{1,0:T(8,128)(2,1)} %param.21) | copy-start | bytes 393220
  59.0 17.1 %copy-start.8 = (bf16[32,2048]{1,0:T(8,128)(2,1)S(1)}, bf16[32,2048]{1,0:T(8,128)(2,1)}, u32[]{:S(2)}) copy-start(bf16[32,2048]{1,0:T(8,128)(2,1)} %dynamic_slice.27) | copy-start | bytes 393220
  59.0 5.0 %collective-permute-start.18 = (bf16[32,2048]{1,0:T(8,128)(2,1)S(1)}, bf16[32,2048]{1,0:T(8,128)(2,1)S(1)}, u32[]{:S(2)}, u32[]{:S(2)}) collective-permute-start(bf16[32,2048]{1,0:T(8,128)(2,1)S(1)} %get-tuple-element.36), channel_id=1, source_target_pairs={{0,4},{1,3},{2,0},{3,7},{4,8},{5,1},{6,2},{7,11},{8,12},{9,5},{10,... | collective-permute-start | bytes 393224 | tf_op jit(solution)/shard_map/ppermute | solution.py:353
  60.9 5.0 %collective-permute-start.22 = (bf16[32,2048]{1,0:T(8,128)(2,1)S(1)}, bf16[32,2048]{1,0:T(8,128)(2,1)S(1)}, u32[]{:S(2)}, u32[]{:S(2)}) collective-permute-start(bf16[32,2048]{1,0:T(8,128)(2,1)S(1)} %slice.204), channel_id=1, source_target_pairs={{0,4},{1,3},{2,0},{3,7},{4,8},{5,1},{6,2},{7,11},{8,12},{9,5},{10,... | collective-permute-start | bytes 393224 | tf_op jit(solution)/shard_map/ppermute | solution.py:353
  64.1 5.0 %collective-permute-start.19 = (bf16[32,2048]{1,0:T(8,128)(2,1)S(1)}, bf16[32,2048]{1,0:T(8,128)(2,1)S(1)}, u32[]{:S(2)}, u32[]{:S(2)}) collective-permute-start(bf16[32,2048]{1,0:T(8,128)(2,1)S(1)} %add_convert_fusion.6), channel_id=1, source_target_pairs={{0,4},{1,3},{2,0},{3,7},{4,8},{5,1},{6,2},{7,11},{8,12},{9,5},{10,... | collective-permute-start | bytes 393224 | tf_op jit(solution)/shard_map/ppermute | solution.py:353
  66.0 23.8 %copy-start.4 = (f32[4096]{0:T(1024)S(1)}, f32[4096]{0:T(1024)}, u32[]{:S(2)}) copy-start(f32[4096]{0:T(1024)} %param.37) | copy-start | bytes 49156
  66.0 5.0 %collective-permute-start.23 = (bf16[32,2048]{1,0:T(8,128)(2,1)S(1)}, bf16[32,2048]{1,0:T(8,128)(2,1)S(1)}, u32[]{:S(2)}, u32[]{:S(2)}) collective-permute-start(bf16[32,2048]{1,0:T(8,128)(2,1)S(1)} %add_convert_fusion.3), channel_id=1, source_target_pairs={{0,4},{1,3},{2,0},{3,7},{4,8},{5,1},{6,2},{7,11},{8,12},{9,5},{10,... | collective-permute-start | bytes 393224 | tf_op jit(solution)/shard_map/ppermute | solution.py:353
  69.1 5.0 %collective-permute-start.20 = (bf16[32,2048]{1,0:T(8,128)(2,1)S(1)}, bf16[32,2048]{1,0:T(8,128)(2,1)S(1)}, u32[]{:S(2)}, u32[]{:S(2)}) collective-permute-start(bf16[32,2048]{1,0:T(8,128)(2,1)S(1)} %add_convert_fusion.5), channel_id=1, source_target_pairs={{0,4},{1,3},{2,0},{3,7},{4,8},{5,1},{6,2},{7,11},{8,12},{9,5},{10,... | collective-permute-start | bytes 393224 | tf_op jit(solution)/shard_map/ppermute | solution.py:353
  71.0 5.0 %collective-permute-start.24 = (bf16[32,2048]{1,0:T(8,128)(2,1)S(1)}, bf16[32,2048]{1,0:T(8,128)(2,1)S(1)}, u32[]{:S(2)}, u32[]{:S(2)}) collective-permute-start(bf16[32,2048]{1,0:T(8,128)(2,1)S(1)} %add_convert_fusion.2), channel_id=1, source_target_pairs={{0,4},{1,3},{2,0},{3,7},{4,8},{5,1},{6,2},{7,11},{8,12},{9,5},{10,... | collective-permute-start | bytes 393224 | tf_op jit(solution)/shard_map/ppermute | solution.py:353
  74.2 5.2 %collective-permute-start.21 = (bf16[32,2048]{1,0:T(8,128)(2,1)S(1)}, bf16[32,2048]{1,0:T(8,128)(2,1)S(1)}, u32[]{:S(2)}, u32[]{:S(2)}) collective-permute-start(bf16[32,2048]{1,0:T(8,128)(2,1)S(1)} %add_convert_fusion.4), channel_id=1, source_target_pairs={{0,4},{1,3},{2,0},{3,7},{4,8},{5,1},{6,2},{7,11},{8,12},{9,5},{10,... | collective-permute-start | bytes 393224 | tf_op jit(solution)/shard_map/ppermute | solution.py:353
  76.0 1.3 %collective-permute-start.25 = (bf16[32,2048]{1,0:T(8,128)(2,1)S(1)}, bf16[32,2048]{1,0:T(8,128)(2,1)S(1)}, u32[]{:S(2)}, u32[]{:S(2)}) collective-permute-start(bf16[32,2048]{1,0:T(8,128)(2,1)S(1)} %collective-permute-done.24), channel_id=1, source_target_pairs={{0,1},{1,0},{2,3},{3,2},{4,5},{5,4},{6,7},{7,6},{8,9},{9,8},{10,11... | collective-permute-start | bytes 393224 | tf_op jit(solution)/shard_map/ppermute | solution.py:50
  79.4 6.4 %collective-permute-start.27 = (bf16[32,2048]{1,0:T(8,128)(2,1)S(1)}, bf16[32,2048]{1,0:T(8,128)(2,1)S(1)}, u32[]{:S(2)}, u32[]{:S(2)}) collective-permute-start(bf16[32,2048]{1,0:T(8,128)(2,1)S(1)} %add_convert_fusion.1.refs_0_), channel_id=1, source_target_pairs={{0,2},{2,0},{4,6},{6,4},{8,10},{10,8},{12,14},{14,12},{1,3},{3,1},... | collective-permute-start | bytes 393224 | tf_op jit(solution)/shard_map/ppermute | solution.py:54
  80.9 5.0 %collective-permute-start.28 = (bf16[32,2048]{1,0:T(8,128)(2,1)S(1)}, bf16[32,2048]{1,0:T(8,128)(2,1)S(1)}, u32[]{:S(2)}, u32[]{:S(2)}) collective-permute-start(bf16[32,2048]{1,0:T(8,128)(2,1)S(1)} %add_convert_fusion.1.refs_0_), channel_id=1, source_target_pairs={{0,4},{2,6},{4,0},{6,2},{8,12},{10,14},{12,8},{14,10},{1,5},{3,7},... | collective-permute-start | bytes 393224 | tf_op jit(solution)/shard_map/ppermute | solution.py:54
  82.5 5.9 %collective-permute-start.29 = (bf16[32,2048]{1,0:T(8,128)(2,1)S(1)}, bf16[32,2048]{1,0:T(8,128)(2,1)S(1)}, u32[]{:S(2)}, u32[]{:S(2)}) collective-permute-start(bf16[32,2048]{1,0:T(8,128)(2,1)S(1)} %add_convert_fusion.1.refs_0_), channel_id=1, source_target_pairs={{0,6},{2,4},{4,2},{6,0},{8,14},{10,12},{12,10},{14,8},{1,7},{3,5},... | collective-permute-start | bytes 393224 | tf_op jit(solution)/shard_map/ppermute | solution.py:54
  83.0 5.4 %collective-permute-start.26 = (bf16[32,2048]{1,0:T(8,128)(2,1)S(1)}, bf16[32,2048]{1,0:T(8,128)(2,1)S(1)}, u32[]{:S(2)}, u32[]{:S(2)}) collective-permute-start(bf16[32,2048]{1,0:T(8,128)(2,1)S(1)} %add_convert_fusion.1.refs_0_), channel_id=1, source_target_pairs={{0,1},{1,0},{2,3},{3,2},{4,5},{5,4},{6,7},{7,6},{8,9},{9,8},{10,11... | collective-permute-start | bytes 393224 | tf_op jit(solution)/shard_map/ppermute | solution.py:50
  85.9 2.7 %collective-permute-start.30 = (bf16[32,2048]{1,0:T(8,128)(2,1)S(1)}, bf16[32,2048]{1,0:T(8,128)(2,1)S(1)}, u32[]{:S(2)}, u32[]{:S(2)}) collective-permute-start(bf16[32,2048]{1,0:T(8,128)(2,1)S(1)} %collective-permute-done.27.refs_1_), channel_id=1, source_target_pairs={{0,1},{1,0},{2,3},{3,2},{4,5},{5,4},{6,7},{7,6},{8,9},{9,8},{10,11... | collective-permute-start | bytes 393224 | tf_op jit(solution)/shard_map/ppermute | solution.py:50
  85.9 2.7 %collective-permute-start.31 = (bf16[32,2048]{1,0:T(8,128)(2,1)S(1)}, bf16[32,2048]{1,0:T(8,128)(2,1)S(1)}, u32[]{:S(2)}, u32[]{:S(2)}) collective-permute-start(bf16[32,2048]{1,0:T(8,128)(2,1)S(1)} %collective-permute-done.28.refs_2_), channel_id=1, source_target_pairs={{0,1},{1,0},{2,3},{3,2},{4,5},{5,4},{6,7},{7,6},{8,9},{9,8},{10,11... | collective-permute-start | bytes 393224 | tf_op jit(solution)/shard_map/ppermute | solution.py:50
  88.4 1.3 %collective-permute-start.32 = (bf16[32,2048]{1,0:T(8,128)(2,1)S(1)}, bf16[32,2048]{1,0:T(8,128)(2,1)S(1)}, u32[]{:S(2)}, u32[]{:S(2)}) collective-permute-start(bf16[32,2048]{1,0:T(8,128)(2,1)S(1)} %collective-permute-done.29.refs_3_), channel_id=1, source_target_pairs={{0,1},{1,0},{2,3},{3,2},{4,5},{5,4},{6,7},{7,6},{8,9},{9,8},{10,11... | collective-permute-start | bytes 393224 | tf_op jit(solution)/shard_map/ppermute | solution.py:50
  89.7 7.9 %copy-start.13 = (bf16[4096,16]{0,1:T(8,128)(2,1)S(1)}, bf16[4096,16]{0,1:T(8,128)(2,1)}, u32[]{:S(2)}) copy-start(bf16[4096,16]{0,1:T(8,128)(2,1)} %param.38) | copy-start | bytes 393220
  97.4 2.0 %collective-permute-start.33 = (bf16[128,2048]{1,0:T(8,128)(2,1)S(1)}, bf16[128,2048]{1,0:T(8,128)(2,1)S(1)}, u32[]{:S(2)}, u32[]{:S(2)}) collective-permute-start(bf16[128,2048]{1,0:T(8,128)(2,1)S(1)} %dynamic-slice_convert_fusion), channel_id=1, source_target_pairs={{0,1},{1,0},{2,3},{3,2},{4,5},{5,4},{6,7},{7,6},{8,9},{9,8},{10,11... | collective-permute-start | bytes 1572872 | tf_op jit(solution)/shard_map/ppermute | solution.py:50
  99.6 7.3 %collective-permute-start.36 = (bf16[32,2048]{1,0:T(8,128)(2,1)S(1)}, bf16[32,2048]{1,0:T(8,128)(2,1)S(1)}, u32[]{:S(2)}, u32[]{:S(2)}) collective-permute-start(bf16[32,2048]{1,0:T(8,128)(2,1)S(1)} %get-tuple-element.49), channel_id=1, source_target_pairs={{0,6},{2,4},{4,2},{6,0},{8,14},{10,12},{12,10},{14,8},{1,7},{3,5},... | collective-permute-start | bytes 393224 | tf_op jit(solution)/shard_map/ppermute | solution.py:54
  101.0 7.0 %collective-permute-start.35 = (bf16[32,2048]{1,0:T(8,128)(2,1)S(1)}, bf16[32,2048]{1,0:T(8,128)(2,1)S(1)}, u32[]{:S(2)}, u32[]{:S(2)}) collective-permute-start(bf16[32,2048]{1,0:T(8,128)(2,1)S(1)} %get-tuple-element.50), channel_id=1, source_target_pairs={{0,4},{2,6},{4,0},{6,2},{8,12},{10,14},{12,8},{14,10},{1,5},{3,7},... | collective-permute-start | bytes 393224 | tf_op jit(solution)/shard_map/ppermute | solution.py:54
  101.7 7.2 %collective-permute-start.34 = (bf16[32,2048]{1,0:T(8,128)(2,1)S(1)}, bf16[32,2048]{1,0:T(8,128)(2,1)S(1)}, u32[]{:S(2)}, u32[]{:S(2)}) collective-permute-start(bf16[32,2048]{1,0:T(8,128)(2,1)S(1)} %get-tuple-element.48), channel_id=1, source_target_pairs={{0,2},{2,0},{4,6},{6,4},{8,10},{10,8},{12,14},{14,12},{1,3},{3,1},... | collective-permute-start | bytes 393224 | tf_op jit(solution)/shard_map/ppermute | solution.py:54
  109.0 6.7 %collective-permute-start.37 = (bf16[16,2048]{1,0:T(8,128)(2,1)S(1)}, bf16[16,2048]{1,0:T(8,128)(2,1)S(1)}, u32[]{:S(2)}, u32[]{:S(2)}) collective-permute-start(bf16[16,2048]{1,0:T(8,128)(2,1)S(1)} %get-tuple-element.64), channel_id=1, source_target_pairs={{0,8},{2,10},{4,12},{6,14},{8,0},{10,2},{12,4},{14,6},{1,9},{3,11}... | collective-permute-start | bytes 196616 | tf_op jit(solution)/shard_map/ppermute | solution.py:54

commit v6 on v5

--- a/solution.py
+++ b/solution.py
@@ -205,7 +205,7 @@
         gated[at, :] = y * (z * jax.nn.sigmoid(z))
         return carry
 
-    lax.fori_loop(0, tokens // DRAFT, request, 0, unroll=4)
+    lax.fori_loop(0, tokens // DRAFT, request, 0, unroll=8)
 
 
 def scan(places, total, dt_proj, dt_bias, u, z, ssm_state, a_rate, d_skip):

time: 117 us -> 117 us (level)
  no operation moved by 1% of the time
where the time goes in v6:
time: 117 us
  starting transfers between devices  43.6 us (37%)
  waiting for transfers between devices  42.3 us (36%)
  Pallas kernels  16.1 us (14%)
  matrix products  5.98 us (5%)
  local copies, waits for them, and re-layouts  4.04 us (3%)
  other arithmetic  3.27 us (3%)
  between operations  1.22 us (1%)
    ppermute x11, waiting for transfers between devices, over_expert(): return lax.ppermute(value, 'expert', [(i, i ^ flip) for i in range(owners)])  22.3 us
    ppermute x11, starting transfers between devices, over_expert(): return lax.ppermute(value, 'expert', [(i, i ^ flip) for i in range(owners)])  17.8 us
    ppermute x7, starting transfers between devices, send(): return lax.ppermute(value, ('expert', 'cuts'), perm)  12 us
    ppermute x7, starting transfers between devices, send(): return lax.ppermute(value.astype(BF16), ('expert', 'cuts'), perm)  11.7 us
    ppermute x13, waiting for transfers between devices, over_cuts(): return lax.ppermute(value, 'cuts', [(0, 1), (1, 0)])  8.35 us
    pallas_call x1, Pallas kernels, run_experts(): pl.pallas_call(functools.partial(experts_kernel, tiles, pieces), out_shap...  7.61 us
    ppermute x7, waiting for transfers between devices, send(): return lax.ppermute(value.astype(BF16), ('expert', 'cuts'), perm)  6.87 us
    pallas_call x1, Pallas kernels, scan(): pl.pallas_call(scan_kernel, out_shape=(jax.ShapeDtypeStruct((tokens, chan...  4.91 us
  transfers between devices with their start and end apart: 38, of which 27 were waited for; matrix products, arithmetic and copies ran while one was open for 8% of the time, Pallas kernels for 4%

profile of v6, /device:TPU:0, one launch (start us, length us, event | category | flops | bytes accessed | tf_op | source)
XLA Modules:
  0.0 116.6 jit_solution(13337339330688329836)
XLA Ops:
  0.6 0.5 collective-permute-start
  1.2 2.6 %collective-permute-start.4 = (bf16[32,2048]{1,0:T(8,128)(2,1)}, bf16[32,2048]{1,0:T(8,128)(2,1)S(1)}, u32[]{:S(2)}, u32[]{:S(2)}) collective-permute-start(bf16[32,2048]{1,0:T(8,128)(2,1)} %param.21), channel_id=1, source_target_pairs={{0,4},{1,3},{2,0},{3,7},{4,8},{5,1},{6,2},{7,11},{8,12},{9,5},{10,... | collective-permute-start | bytes 393224 | tf_op jit(solution)/shard_map/ppermute | solution.py:74
  3.8 1.6 %collective-permute-start.1 = (bf16[32,2048]{1,0:T(8,128)(2,1)S(1)}, bf16[32,2048]{1,0:T(8,128)(2,1)S(1)}, u32[]{:S(2)}, u32[]{:S(2)}) collective-permute-start(bf16[32,2048]{1,0:T(8,128)(2,1)S(1)} %collective-permute-done), channel_id=1, source_target_pairs={{0,4},{1,3},{2,0},{3,7},{4,8},{5,1},{6,2},{7,11},{8,12},{9,5},{10,... | collective-permute-start | bytes 393224 | tf_op jit(solution)/shard_map/ppermute | solution.py:74
  5.4 0.8 copy.33.routes_ref
  6.4 1.0 copy.34
  7.5 1.6 %collective-permute-start.5 = (bf16[32,2048]{1,0:T(8,128)(2,1)S(1)}, bf16[32,2048]{1,0:T(8,128)(2,1)S(1)}, u32[]{:S(2)}, u32[]{:S(2)}) collective-permute-start(bf16[32,2048]{1,0:T(8,128)(2,1)S(1)} %collective-permute-done.4), channel_id=1, source_target_pairs={{0,4},{1,3},{2,0},{3,7},{4,8},{5,1},{6,2},{7,11},{8,12},{9,5},{10,... | collective-permute-start | bytes 393224 | tf_op jit(solution)/shard_map/ppermute | solution.py:74
  9.1 1.5 %collective-permute-start.2 = (bf16[32,2048]{1,0:T(8,128)(2,1)S(1)}, bf16[32,2048]{1,0:T(8,128)(2,1)S(1)}, u32[]{:S(2)}, u32[]{:S(2)}) collective-permute-start(bf16[32,2048]{1,0:T(8,128)(2,1)S(1)} %collective-permute-done.1), channel_id=1, source_target_pairs={{0,4},{1,3},{2,0},{3,7},{4,8},{5,1},{6,2},{7,11},{8,12},{9,5},{10,... | collective-permute-start | bytes 393224 | tf_op jit(solution)/shard_map/ppermute | solution.py:74
  10.6 1.8 %collective-permute-done.5 = bf16[32,2048]{1,0:T(8,128)(2,1)S(1)} collective-permute-done((bf16[32,2048]{1,0:T(8,128)(2,1)S(1)}, bf16[32,2048]{1,0:T(8,128)(2,1)S(1)}, u32[]{:S(2)}, u32[]{:S(2)}) %collective-permute-start.5) | collective-permute-done | bytes 131104 | tf_op jit(solution)/shard_map/ppermute | solution.py:74
  12.5 1.6 %collective-permute-start.6 = (bf16[32,2048]{1,0:T(8,128)(2,1)S(1)}, bf16[32,2048]{1,0:T(8,128)(2,1)S(1)}, u32[]{:S(2)}, u32[]{:S(2)}) collective-permute-start(bf16[32,2048]{1,0:T(8,128)(2,1)S(1)} %collective-permute-done.5), channel_id=1, source_target_pairs={{0,4},{1,3},{2,0},{3,7},{4,8},{5,1},{6,2},{7,11},{8,12},{9,5},{10,... | collective-permute-start | bytes 393224 | tf_op jit(solution)/shard_map/ppermute | solution.py:74
  14.1 1.5 %collective-permute-start.3 = (bf16[32,2048]{1,0:T(8,128)(2,1)S(1)}, bf16[32,2048]{1,0:T(8,128)(2,1)S(1)}, u32[]{:S(2)}, u32[]{:S(2)}) collective-permute-start(bf16[32,2048]{1,0:T(8,128)(2,1)S(1)} %collective-permute-done.2), channel_id=1, source_target_pairs={{0,4},{1,3},{2,0},{3,7},{4,8},{5,1},{6,2},{7,11},{8,12},{9,5},{10,... | collective-permute-start | bytes 393224 | tf_op jit(solution)/shard_map/ppermute | solution.py:74
  15.6 0.8 fusion.57
  16.4 1.0 collective-permute-done.6
  17.4 1.6 %collective-permute-start.8 = (bf16[32,2048]{1,0:T(8,128)(2,1)S(1)}, bf16[32,2048]{1,0:T(8,128)(2,1)S(1)}, u32[]{:S(2)}, u32[]{:S(2)}) collective-permute-start(bf16[32,2048]{1,0:T(8,128)(2,1)S(1)} %collective-permute-done.6), channel_id=1, source_target_pairs={{0,4},{1,3},{2,0},{3,7},{4,8},{5,1},{6,2},{7,11},{8,12},{9,5},{10,... | collective-permute-start | bytes 393224 | tf_op jit(solution)/shard_map/ppermute | solution.py:74
  19.0 0.9 broadcast_select_fusion.9
  20.4 2.0 %collective-permute-done.8 = bf16[32,2048]{1,0:T(8,128)(2,1)S(1)} collective-permute-done((bf16[32,2048]{1,0:T(8,128)(2,1)S(1)}, bf16[32,2048]{1,0:T(8,128)(2,1)S(1)}, u32[]{:S(2)}, u32[]{:S(2)}) %collective-permute-start.8) | collective-permute-done | bytes 131104 | tf_op jit(solution)/shard_map/ppermute | solution.py:74
  22.4 1.3 %collective-permute-done.9 = bf16[32,2048]{1,0:T(8,128)(2,1)S(1)} collective-permute-done((bf16[32,2048]{1,0:T(8,128)(2,1)S(1)}, bf16[32,2048]{1,0:T(8,128)(2,1)S(1)}, u32[]{:S(2)}, u32[]{:S(2)}) %collective-permute-start.9) | collective-permute-done | bytes 131104 | tf_op jit(solution)/shard_map/ppermute | solution.py:50
  24.0 0.5 fusion
  24.6 0.8 convolution_bitcast_fusion
  26.1 0.7 dynamic_slice.27
  27.1 0.4 collective-permute-start.17
  27.5 0.9 collective-permute-done.10
  28.5 1.5 %collective-permute-start.11 = (bf16[64,547]{1,0:T(8,128)(2,1)S(1)}, bf16[64,547]{1,0:T(8,128)(2,1)S(1)}, u32[]{:S(2)}, u32[]{:S(2)}) collective-permute-start(bf16[64,547]{1,0:T(8,128)(2,1)S(1)} %dynamic-slice_convert_fusion.2), channel_id=1, source_target_pairs={{0,2},{2,0},{4,6},{6,4},{8,10},{10,8},{12,14},{14,12},{1,3},{3,1},... | collective-permute-start | bytes 210056 | tf_op jit(solution)/shard_map/ppermute | solution.py:54
  30.0 3.0 %fusion.3.z_hbm = f32[256,256]{1,0:T(8,128)S(1)} fusion(bf16[4096,256]{1,0:T(8,128)(2,1)} %param.27, bf16[256,4096]{1,0:T(8,128)(2,1)} %copy-done.7, f32[4096]{0:T(1024)S(1)} %copy-done.14, f32[256]{0:T(256)S(1)} %add_rsqrt_fusion), kind=kOutput, calls=%fused_computation.19 | convolution fusion | flops 541065216 | bytes 4473856 | tf_op jit(solution)/shard_map/dot_general | solution.py:517
  33.1 1.6 %collective-permute-start.12 = (bf16[64,547]{1,0:T(8,128)(2,1)S(1)}, bf16[64,547]{1,0:T(8,128)(2,1)S(1)}, u32[]{:S(2)}, u32[]{:S(2)}) collective-permute-start(bf16[64,547]{1,0:T(8,128)(2,1)S(1)} %fusion.35), channel_id=1, source_target_pairs={{0,4},{2,6},{4,0},{6,2},{8,12},{10,14},{12,8},{14,10},{1,5},{3,7},... | collective-permute-start | bytes 210056 | tf_op jit(solution)/shard_map/ppermute | solution.py:54
  34.7 2.9 %collective-permute-done.12 = bf16[64,547]{1,0:T(8,128)(2,1)S(1)} collective-permute-done((bf16[64,547]{1,0:T(8,128)(2,1)S(1)}, bf16[64,547]{1,0:T(8,128)(2,1)S(1)}, u32[]{:S(2)}, u32[]{:S(2)}) %collective-permute-start.12) | collective-permute-done | bytes 70048 | tf_op jit(solution)/shard_map/ppermute | solution.py:54
  37.6 2.6 %collective-permute-start.13 = (bf16[64,547]{1,0:T(8,128)(2,1)S(1)}, bf16[64,547]{1,0:T(8,128)(2,1)S(1)}, u32[]{:S(2)}, u32[]{:S(2)}) collective-permute-start(bf16[64,547]{1,0:T(8,128)(2,1)S(1)} %fusion.34), channel_id=1, source_target_pairs={{0,8},{2,10},{4,12},{6,14},{8,0},{10,2},{12,4},{14,6},{1,9},{3,11}... | collective-permute-start | bytes 210056 | tf_op jit(solution)/shard_map/ppermute | solution.py:54
  40.2 2.8 %collective-permute-done.13 = bf16[64,547]{1,0:T(8,128)(2,1)S(1)} collective-permute-done((bf16[64,547]{1,0:T(8,128)(2,1)S(1)}, bf16[64,547]{1,0:T(8,128)(2,1)S(1)}, u32[]{:S(2)}, u32[]{:S(2)}) %collective-permute-start.13) | collective-permute-done | bytes 70048 | tf_op jit(solution)/shard_map/ppermute | solution.py:54
  43.1 1.5 %collective-permute-start.14 = (bf16[64,547]{1,0:T(8,128)(2,1)S(1)}, bf16[64,547]{1,0:T(8,128)(2,1)S(1)}, u32[]{:S(2)}, u32[]{:S(2)}) collective-permute-start(bf16[64,547]{1,0:T(8,128)(2,1)S(1)} %get-tuple-element.47), channel_id=1, source_target_pairs={{0,2},{2,0},{4,6},{6,4},{8,10},{10,8},{12,14},{14,12},{1,3},{3,1},... | collective-permute-start | bytes 210056 | tf_op jit(solution)/shard_map/ppermute | solution.py:54
  44.6 3.0 %collective-permute-done.14 = bf16[64,547]{1,0:T(8,128)(2,1)S(1)} collective-permute-done((bf16[64,547]{1,0:T(8,128)(2,1)S(1)}, bf16[64,547]{1,0:T(8,128)(2,1)S(1)}, u32[]{:S(2)}, u32[]{:S(2)}) %collective-permute-start.14) | collective-permute-done | bytes 70048 | tf_op jit(solution)/shard_map/ppermute | solution.py:54
  47.8 1.4 %collective-permute-done.15.theirs = bf16[128,547]{1,0:T(8,128)(2,1)} collective-permute-done((bf16[128,547]{1,0:T(8,128)(2,1)S(1)}, bf16[128,547]{1,0:T(8,128)(2,1)}, u32[]{:S(2)}, u32[]{:S(2)}) %collective-permute-start.15) | collective-permute-done | bytes 140064 | tf_op jit(solution)/shard_map/ppermute | solution.py:50
  49.2 4.9 %scan.1 = (f32[256,256]{1,0:T(8,128)S(1)}, f32[32,16,256]{2,1,0:T(8,128)}, f32[256,3]{1,0:T(8,128)S(1)}) custom-call(s32[6]{0:T(128)S(1)} %stack.32.place_ref, bf16[128,547]{1,0:T(8,128)(2,1)S(1)} %constant_dynamic-update-slice_fusion.mine, bf16[128,547]{1,0:T(8,128)(2,1)} %collective-permute-done.15.theirs, bf16[512,256]{1,0:T(8,128)(2,1)S(1)} %copy-done.2, ...), custom_call_target="tpu_custom_call" | custom-call | tf_op jit(solution)/shard_map/scan/pallas_call | solution.py:217
  54.6 1.0 collective-permute-done.16.h_ref
  55.6 3.3 %project.1 = (f32[96,2048]{1,0:T(8,128)S(1)}, bf16[32,2048]{1,0:T(8,128)(2,1)S(1)}, f32[32,2048]{1,0:T(8,128)S(1)}, f32[96,2048]{1,0:T(8,128)S(1)}) custom-call(s32[6]{0:T(128)S(1)} %stack.32.place_ref, s32[256,1]{1,0:T(8,128)S(1)} %get-tuple-element.45.id_ref, bf16[256,256]{1,0:T(8,128)(2,1)S(1)} %convert_element_type.146.g_ref, ...), custom_call_target="tpu_custom_call" | custom-call | tf_op jit(solution)/shard_map/project/pallas_call | solution.py:334
  59.0 1.6 %collective-permute-start.18 = (bf16[32,2048]{1,0:T(8,128)(2,1)S(1)}, bf16[32,2048]{1,0:T(8,128)(2,1)S(1)}, u32[]{:S(2)}, u32[]{:S(2)}) collective-permute-start(bf16[32,2048]{1,0:T(8,128)(2,1)S(1)} %get-tuple-element.36), channel_id=1, source_target_pairs={{0,4},{1,3},{2,0},{3,7},{4,8},{5,1},{6,2},{7,11},{8,12},{9,5},{10,... | collective-permute-start | bytes 393224 | tf_op jit(solution)/shard_map/ppermute | solution.py:353
  60.8 1.7 %collective-permute-start.22 = (bf16[32,2048]{1,0:T(8,128)(2,1)S(1)}, bf16[32,2048]{1,0:T(8,128)(2,1)S(1)}, u32[]{:S(2)}, u32[]{:S(2)}) collective-permute-start(bf16[32,2048]{1,0:T(8,128)(2,1)S(1)} %slice.204), channel_id=1, source_target_pairs={{0,4},{1,3},{2,0},{3,7},{4,8},{5,1},{6,2},{7,11},{8,12},{9,5},{10,... | collective-permute-start | bytes 393224 | tf_op jit(solution)/shard_map/ppermute | solution.py:353
  62.5 1.5 %collective-permute-done.18 = bf16[32,2048]{1,0:T(8,128)(2,1)S(1)} collective-permute-done((bf16[32,2048]{1,0:T(8,128)(2,1)S(1)}, bf16[32,2048]{1,0:T(8,128)(2,1)S(1)}, u32[]{:S(2)}, u32[]{:S(2)}) %collective-permute-start.18) | collective-permute-done | bytes 131104 | tf_op jit(solution)/shard_map/ppermute | solution.py:353
  64.0 1.6 %collective-permute-start.19 = (bf16[32,2048]{1,0:T(8,128)(2,1)S(1)}, bf16[32,2048]{1,0:T(8,128)(2,1)S(1)}, u32[]{:S(2)}, u32[]{:S(2)}) collective-permute-start(bf16[32,2048]{1,0:T(8,128)(2,1)S(1)} %add_convert_fusion.6), channel_id=1, source_target_pairs={{0,4},{1,3},{2,0},{3,7},{4,8},{5,1},{6,2},{7,11},{8,12},{9,5},{10,... | collective-permute-start | bytes 393224 | tf_op jit(solution)/shard_map/ppermute | solution.py:353
  65.9 1.7 %collective-permute-start.23 = (bf16[32,2048]{1,0:T(8,128)(2,1)S(1)}, bf16[32,2048]{1,0:T(8,128)(2,1)S(1)}, u32[]{:S(2)}, u32[]{:S(2)}) collective-permute-start(bf16[32,2048]{1,0:T(8,128)(2,1)S(1)} %add_convert_fusion.3), channel_id=1, source_target_pairs={{0,4},{1,3},{2,0},{3,7},{4,8},{5,1},{6,2},{7,11},{8,12},{9,5},{10,... | collective-permute-start | bytes 393224 | tf_op jit(solution)/shard_map/ppermute | solution.py:353
  67.6 1.5 %collective-permute-done.19 = bf16[32,2048]{1,0:T(8,128)(2,1)S(1)} collective-permute-done((bf16[32,2048]{1,0:T(8,128)(2,1)S(1)}, bf16[32,2048]{1,0:T(8,128)(2,1)S(1)}, u32[]{:S(2)}, u32[]{:S(2)}) %collective-permute-start.19) | collective-permute-done | bytes 131104 | tf_op jit(solution)/shard_map/ppermute | solution.py:353
  69.1 1.6 %collective-permute-start.20 = (bf16[32,2048]{1,0:T(8,128)(2,1)S(1)}, bf16[32,2048]{1,0:T(8,128)(2,1)S(1)}, u32[]{:S(2)}, u32[]{:S(2)}) collective-permute-start(bf16[32,2048]{1,0:T(8,128)(2,1)S(1)} %add_convert_fusion.5), channel_id=1, source_target_pairs={{0,4},{1,3},{2,0},{3,7},{4,8},{5,1},{6,2},{7,11},{8,12},{9,5},{10,... | collective-permute-start | bytes 393224 | tf_op jit(solution)/shard_map/ppermute | solution.py:353
  71.0 1.7 %collective-permute-start.24 = (bf16[32,2048]{1,0:T(8,128)(2,1)S(1)}, bf16[32,2048]{1,0:T(8,128)(2,1)S(1)}, u32[]{:S(2)}, u32[]{:S(2)}) collective-permute-start(bf16[32,2048]{1,0:T(8,128)(2,1)S(1)} %add_convert_fusion.2), channel_id=1, source_target_pairs={{0,4},{1,3},{2,0},{3,7},{4,8},{5,1},{6,2},{7,11},{8,12},{9,5},{10,... | collective-permute-start | bytes 393224 | tf_op jit(solution)/shard_map/ppermute | solution.py:353
  72.6 1.5 %collective-permute-done.20 = bf16[32,2048]{1,0:T(8,128)(2,1)S(1)} collective-permute-done((bf16[32,2048]{1,0:T(8,128)(2,1)S(1)}, bf16[32,2048]{1,0:T(8,128)(2,1)S(1)}, u32[]{:S(2)}, u32[]{:S(2)}) %collective-permute-start.20) | collective-permute-done | bytes 131104 | tf_op jit(solution)/shard_map/ppermute | solution.py:353
  74.1 1.8 %collective-permute-start.21 = (bf16[32,2048]{1,0:T(8,128)(2,1)S(1)}, bf16[32,2048]{1,0:T(8,128)(2,1)S(1)}, u32[]{:S(2)}, u32[]{:S(2)}) collective-permute-start(bf16[32,2048]{1,0:T(8,128)(2,1)S(1)} %add_convert_fusion.4), channel_id=1, source_target_pairs={{0,4},{1,3},{2,0},{3,7},{4,8},{5,1},{6,2},{7,11},{8,12},{9,5},{10,... | collective-permute-start | bytes 393224 | tf_op jit(solution)/shard_map/ppermute | solution.py:353
  76.2 1.1 collective-permute-done.25
  77.3 2.0 %collective-permute-done.21 = bf16[32,2048]{1,0:T(8,128)(2,1)S(1)} collective-permute-done((bf16[32,2048]{1,0:T(8,128)(2,1)S(1)}, bf16[32,2048]{1,0:T(8,128)(2,1)S(1)}, u32[]{:S(2)}, u32[]{:S(2)}) %collective-permute-start.21) | collective-permute-done | bytes 131104 | tf_op jit(solution)/shard_map/ppermute | solution.py:353
  79.4 1.5 %collective-permute-start.27 = (bf16[32,2048]{1,0:T(8,128)(2,1)S(1)}, bf16[32,2048]{1,0:T(8,128)(2,1)S(1)}, u32[]{:S(2)}, u32[]{:S(2)}) collective-permute-start(bf16[32,2048]{1,0:T(8,128)(2,1)S(1)} %add_convert_fusion.1.refs_0_), channel_id=1, source_target_pairs={{0,2},{2,0},{4,6},{6,4},{8,10},{10,8},{12,14},{14,12},{1,3},{3,1},... | collective-permute-start | bytes 393224 | tf_op jit(solution)/shard_map/ppermute | solution.py:54
  80.9 1.6 %collective-permute-start.28 = (bf16[32,2048]{1,0:T(8,128)(2,1)S(1)}, bf16[32,2048]{1,0:T(8,128)(2,1)S(1)}, u32[]{:S(2)}, u32[]{:S(2)}) collective-permute-start(bf16[32,2048]{1,0:T(8,128)(2,1)S(1)} %add_convert_fusion.1.refs_0_), channel_id=1, source_target_pairs={{0,4},{2,6},{4,0},{6,2},{8,12},{10,14},{12,8},{14,10},{1,5},{3,7},... | collective-permute-start | bytes 393224 | tf_op jit(solution)/shard_map/ppermute | solution.py:54
  82.5 0.5 collective-permute-start.29
  83.2 2.6 %collective-permute-done.27.refs_1_ = bf16[32,2048]{1,0:T(8,128)(2,1)S(1)} collective-permute-done((bf16[32,2048]{1,0:T(8,128)(2,1)S(1)}, bf16[32,2048]{1,0:T(8,128)(2,1)S(1)}, u32[]{:S(2)}, u32[]{:S(2)}) %collective-permute-start.27) | collective-permute-done | bytes 131104 | tf_op jit(solution)/shard_map/ppermute | solution.py:54
  85.9 0.5 collective-permute-start.31
  86.3 2.0 %collective-permute-done.29.refs_3_ = bf16[32,2048]{1,0:T(8,128)(2,1)S(1)} collective-permute-done((bf16[32,2048]{1,0:T(8,128)(2,1)S(1)}, bf16[32,2048]{1,0:T(8,128)(2,1)S(1)}, u32[]{:S(2)}, u32[]{:S(2)}) %collective-permute-start.29) | collective-permute-done | bytes 131104 | tf_op jit(solution)/shard_map/ppermute | solution.py:54
  88.6 1.1 collective-permute-done.32.refs_7_
  89.7 7.6 %experts.1 = f32[128,4096]{1,0:T(8,128)S(1)} custom-call(s32[6]{0:T(128)S(1)} %stack.32.place_ref, bf16[32,2048]{1,0:T(8,128)(2,1)S(1)} %add_convert_fusion.1.refs_0_, bf16[32,2048]{1,0:T(8,128)(2,1)S(1)} %collective-permute-done.27.refs_1_, bf16[32,2048]{1,0:T(8,128)(2,1)S(1)} %collective-permute-done.28.refs_2_, ...), custom_call_target="tpu_custom_call" | custom-call | tf_op jit(solution)/shard_map/experts/pallas_call | solution.py:422
  97.6 0.3 fusion.9
  97.9 1.5 %collective-permute-done.33 = bf16[128,2048]{1,0:T(8,128)(2,1)S(1)} collective-permute-done((bf16[128,2048]{1,0:T(8,128)(2,1)S(1)}, bf16[128,2048]{1,0:T(8,128)(2,1)S(1)}, u32[]{:S(2)}, u32[]{:S(2)}) %collective-permute-start.33) | collective-permute-done | bytes 524320 | tf_op jit(solution)/shard_map/ppermute | solution.py:50
  99.6 1.5 %collective-permute-start.36 = (bf16[32,2048]{1,0:T(8,128)(2,1)S(1)}, bf16[32,2048]{1,0:T(8,128)(2,1)S(1)}, u32[]{:S(2)}, u32[]{:S(2)}) collective-permute-start(bf16[32,2048]{1,0:T(8,128)(2,1)S(1)} %get-tuple-element.49), channel_id=1, source_target_pairs={{0,6},{2,4},{4,2},{6,0},{8,14},{10,12},{12,10},{14,8},{1,7},{3,5},... | collective-permute-start | bytes 393224 | tf_op jit(solution)/shard_map/ppermute | solution.py:54
  101.0 0.6 collective-permute-start.35
  101.7 1.4 %collective-permute-start.34 = (bf16[32,2048]{1,0:T(8,128)(2,1)S(1)}, bf16[32,2048]{1,0:T(8,128)(2,1)S(1)}, u32[]{:S(2)}, u32[]{:S(2)}) collective-permute-start(bf16[32,2048]{1,0:T(8,128)(2,1)S(1)} %get-tuple-element.48), channel_id=1, source_target_pairs={{0,2},{2,0},{4,6},{6,4},{8,10},{10,8},{12,14},{14,12},{1,3},{3,1},... | collective-permute-start | bytes 393224 | tf_op jit(solution)/shard_map/ppermute | solution.py:54
  103.2 3.7 %collective-permute-done.36 = bf16[32,2048]{1,0:T(8,128)(2,1)S(1)} collective-permute-done((bf16[32,2048]{1,0:T(8,128)(2,1)S(1)}, bf16[32,2048]{1,0:T(8,128)(2,1)S(1)}, u32[]{:S(2)}, u32[]{:S(2)}) %collective-permute-start.36) | collective-permute-done | bytes 131104 | tf_op jit(solution)/shard_map/ppermute | solution.py:54
  106.9 1.1 collective-permute-done.35
  108.0 0.9 collective-permute-done.34
  109.0 3.4 %collective-permute-start.37 = (bf16[16,2048]{1,0:T(8,128)(2,1)S(1)}, bf16[16,2048]{1,0:T(8,128)(2,1)S(1)}, u32[]{:S(2)}, u32[]{:S(2)}) collective-permute-start(bf16[16,2048]{1,0:T(8,128)(2,1)S(1)} %get-tuple-element.64), channel_id=1, source_target_pairs={{0,8},{2,10},{4,12},{6,14},{8,0},{10,2},{12,4},{14,6},{1,9},{3,11}... | collective-permute-start | bytes 196616 | tf_op jit(solution)/shard_map/ppermute | solution.py:54
  112.6 3.1 %collective-permute-done.37 = bf16[16,2048]{1,0:T(8,128)(2,1)S(1)} collective-permute-done((bf16[16,2048]{1,0:T(8,128)(2,1)S(1)}, bf16[16,2048]{1,0:T(8,128)(2,1)S(1)}, u32[]{:S(2)}, u32[]{:S(2)}) %collective-permute-start.37) | collective-permute-done | bytes 65568 | tf_op jit(solution)/shard_map/ppermute | solution.py:54
  115.7 0.9 convolution_convert_fusion
  (110 shorter events, 5.3 us)
Async XLA Ops:
  0.6 23.9 %copy-start = (bf16[4096,256]{1,0:T(8,128)(2,1)S(1)}, bf16[4096,256]{1,0:T(8,128)(2,1)}, u32[]{:S(2)}) copy-start(bf16[4096,256]{1,0:T(8,128)(2,1)} %param.26) | copy-start | bytes 6291460
  0.6 3.2 %collective-permute-start = (bf16[32,2048]{1,0:T(8,128)(2,1)}, bf16[32,2048]{1,0:T(8,128)(2,1)S(1)}, u32[]{:S(2)}, u32[]{:S(2)}) collective-permute-start(bf16[32,2048]{1,0:T(8,128)(2,1)} %param.21), channel_id=1, source_target_pairs={{0,1},{1,0},{2,3},{3,2},{4,5},{5,4},{6,7},{7,6},{8,9},{9,8},{10,11... | collective-permute-start | bytes 393224 | tf_op jit(solution)/shard_map/ppermute | solution.py:50
  1.2 6.3 %collective-permute-start.4 = (bf16[32,2048]{1,0:T(8,128)(2,1)}, bf16[32,2048]{1,0:T(8,128)(2,1)S(1)}, u32[]{:S(2)}, u32[]{:S(2)}) collective-permute-start(bf16[32,2048]{1,0:T(8,128)(2,1)} %param.21), channel_id=1, source_target_pairs={{0,4},{1,3},{2,0},{3,7},{4,8},{5,1},{6,2},{7,11},{8,12},{9,5},{10,... | collective-permute-start | bytes 393224 | tf_op jit(solution)/shard_map/ppermute | solution.py:74
  3.8 5.3 %collective-permute-start.1 = (bf16[32,2048]{1,0:T(8,128)(2,1)S(1)}, bf16[32,2048]{1,0:T(8,128)(2,1)S(1)}, u32[]{:S(2)}, u32[]{:S(2)}) collective-permute-start(bf16[32,2048]{1,0:T(8,128)(2,1)S(1)} %collective-permute-done), channel_id=1, source_target_pairs={{0,4},{1,3},{2,0},{3,7},{4,8},{5,1},{6,2},{7,11},{8,12},{9,5},{10,... | collective-permute-start | bytes 393224 | tf_op jit(solution)/shard_map/ppermute | solution.py:74
  7.5 5.0 %collective-permute-start.5 = (bf16[32,2048]{1,0:T(8,128)(2,1)S(1)}, bf16[32,2048]{1,0:T(8,128)(2,1)S(1)}, u32[]{:S(2)}, u32[]{:S(2)}) collective-permute-start(bf16[32,2048]{1,0:T(8,128)(2,1)S(1)} %collective-permute-done.4), channel_id=1, source_target_pairs={{0,4},{1,3},{2,0},{3,7},{4,8},{5,1},{6,2},{7,11},{8,12},{9,5},{10,... | collective-permute-start | bytes 393224 | tf_op jit(solution)/shard_map/ppermute | solution.py:74
  9.1 5.0 %collective-permute-start.2 = (bf16[32,2048]{1,0:T(8,128)(2,1)S(1)}, bf16[32,2048]{1,0:T(8,128)(2,1)S(1)}, u32[]{:S(2)}, u32[]{:S(2)}) collective-permute-start(bf16[32,2048]{1,0:T(8,128)(2,1)S(1)} %collective-permute-done.1), channel_id=1, source_target_pairs={{0,4},{1,3},{2,0},{3,7},{4,8},{5,1},{6,2},{7,11},{8,12},{9,5},{10,... | collective-permute-start | bytes 393224 | tf_op jit(solution)/shard_map/ppermute | solution.py:74
  12.5 5.0 %collective-permute-start.6 = (bf16[32,2048]{1,0:T(8,128)(2,1)S(1)}, bf16[32,2048]{1,0:T(8,128)(2,1)S(1)}, u32[]{:S(2)}, u32[]{:S(2)}) collective-permute-start(bf16[32,2048]{1,0:T(8,128)(2,1)S(1)} %collective-permute-done.5), channel_id=1, source_target_pairs={{0,4},{1,3},{2,0},{3,7},{4,8},{5,1},{6,2},{7,11},{8,12},{9,5},{10,... | collective-permute-start | bytes 393224 | tf_op jit(solution)/shard_map/ppermute | solution.py:74
  14.1 5.0 %collective-permute-start.3 = (bf16[32,2048]{1,0:T(8,128)(2,1)S(1)}, bf16[32,2048]{1,0:T(8,128)(2,1)S(1)}, u32[]{:S(2)}, u32[]{:S(2)}) collective-permute-start(bf16[32,2048]{1,0:T(8,128)(2,1)S(1)} %collective-permute-done.2), channel_id=1, source_target_pairs={{0,4},{1,3},{2,0},{3,7},{4,8},{5,1},{6,2},{7,11},{8,12},{9,5},{10,... | collective-permute-start | bytes 393224 | tf_op jit(solution)/shard_map/ppermute | solution.py:74
  17.4 5.0 %collective-permute-start.8 = (bf16[32,2048]{1,0:T(8,128)(2,1)S(1)}, bf16[32,2048]{1,0:T(8,128)(2,1)S(1)}, u32[]{:S(2)}, u32[]{:S(2)}) collective-permute-start(bf16[32,2048]{1,0:T(8,128)(2,1)S(1)} %collective-permute-done.6), channel_id=1, source_target_pairs={{0,4},{1,3},{2,0},{3,7},{4,8},{5,1},{6,2},{7,11},{8,12},{9,5},{10,... | collective-permute-start | bytes 393224 | tf_op jit(solution)/shard_map/ppermute | solution.py:74
  20.1 3.7 %collective-permute-start.7 = (bf16[96,4096]{1,0:T(8,128)(2,1)S(1)}, bf16[96,4096]{1,0:T(8,128)(2,1)S(1)}, u32[]{:S(2)}, u32[]{:S(2)}) collective-permute-start(bf16[96,4096]{1,0:T(8,128)(2,1)S(1)} %maximum_maximum_fusion), channel_id=1, source_target_pairs={{0,1},{1,0},{2,3},{3,2},{4,5},{5,4},{6,7},{7,6},{8,9},{9,8},{10,11... | collective-permute-start | bytes 2359304 | tf_op jit(solution)/shard_map/ppermute | solution.py:50
  22.4 1.3 %collective-permute-start.9 = (bf16[32,2048]{1,0:T(8,128)(2,1)S(1)}, bf16[32,2048]{1,0:T(8,128)(2,1)S(1)}, u32[]{:S(2)}, u32[]{:S(2)}) collective-permute-start(bf16[32,2048]{1,0:T(8,128)(2,1)S(1)} %collective-permute-done.8), channel_id=1, source_target_pairs={{0,1},{1,0},{2,3},{3,2},{4,5},{5,4},{6,7},{7,6},{8,9},{9,8},{10,11... | collective-permute-start | bytes 393224 | tf_op jit(solution)/shard_map/ppermute | solution.py:50
  23.9 0.7 copy-start.14
  24.0 2.1 %copy-start.7 = (bf16[256,4096]{1,0:T(8,128)(2,1)}, bf16[256,4096]{1,0:T(8,128)(2,1)S(1)}, u32[]{:S(2)}) copy-start(bf16[256,4096]{1,0:T(8,128)(2,1)S(1)} %maximum_dynamic-update-slice_fusion.4) | copy-start | bytes 6291460
  24.6 0.8 copy-start.12
  24.6 1.1 copy-start.11
  24.6 1.2 %copy-start.10 = (bf16[256,512]{1,0:T(8,128)(2,1)S(1)}, bf16[256,512]{1,0:T(8,128)(2,1)}, u32[]{:S(2)}) copy-start(bf16[256,512]{1,0:T(8,128)(2,1)} %param.30) | copy-start | bytes 786436
  26.9 1.5 %collective-permute-start.10 = (bf16[128,547]{1,0:T(8,128)(2,1)S(1)}, bf16[128,547]{1,0:T(8,128)(2,1)S(1)}, u32[]{:S(2)}, u32[]{:S(2)}) collective-permute-start(bf16[128,547]{1,0:T(8,128)(2,1)S(1)} %dynamic-slice_convert_fusion.1), channel_id=1, source_target_pairs={{0,1},{1,0},{2,3},{3,2},{4,5},{5,4},{6,7},{7,6},{8,9},{9,8},{10,11... | collective-permute-start | bytes 420104 | tf_op jit(solution)/shard_map/ppermute | solution.py:50
  27.1 28.5 %collective-permute-start.17 = (bf16[256,4096]{1,0:T(8,128)(2,1)}, bf16[256,4096]{1,0:T(8,128)(2,1)}, u32[]{:S(2)}, u32[]{:S(2)}) collective-permute-start(bf16[256,4096]{1,0:T(8,128)(2,1)} %wg_ref.1), channel_id=1, source_target_pairs={{0,1},{1,0},{2,3},{3,2},{4,5},{5,4},{6,7},{7,6},{8,9},{9,8},{10,11... | collective-permute-start | bytes 6291464 | tf_op jit(solution)/shard_map/ppermute | solution.py:50
  28.4 20.8 %copy-start.1 = (f32[32,16,256]{2,1,0:T(8,128)S(1)}, f32[32,16,256]{2,1,0:T(8,128)}, u32[]{:S(2)}) copy-start(f32[32,16,256]{2,1,0:T(8,128)} %state_hbm.1) | copy-start | bytes 1572868
  28.4 20.8 %copy-start.2 = (bf16[512,256]{1,0:T(8,128)(2,1)S(1)}, bf16[512,256]{1,0:T(8,128)(2,1)}, u32[]{:S(2)}) copy-start(bf16[512,256]{1,0:T(8,128)(2,1)} %dt_proj.1) | copy-start | bytes 786436
  28.4 20.8 %copy-start.3 = (f32[16,256]{1,0:T(8,128)S(1)}, f32[16,256]{1,0:T(8,128)}, u32[]{:S(2)}) copy-start(f32[16,256]{1,0:T(8,128)} %a_rate.1) | copy-start | bytes 49156
  28.5 20.8 %copy-start.5 = (f32[256]{0:T(256)S(1)}, f32[256]{0:T(256)}, u32[]{:S(2)}) copy-start(f32[256]{0:T(256)} %param.33) | copy-start | bytes 3076
  28.5 20.8 %copy-start.6 = (f32[256]{0:T(256)S(1)}, f32[256]{0:T(256)}, u32[]{:S(2)}) copy-start(f32[256]{0:T(256)} %param.35) | copy-start | bytes 3076
  28.5 4.6 %collective-permute-start.11 = (bf16[64,547]{1,0:T(8,128)(2,1)S(1)}, bf16[64,547]{1,0:T(8,128)(2,1)S(1)}, u32[]{:S(2)}, u32[]{:S(2)}) collective-permute-start(bf16[64,547]{1,0:T(8,128)(2,1)S(1)} %dynamic-slice_convert_fusion.2), channel_id=1, source_target_pairs={{0,2},{2,0},{4,6},{6,4},{8,10},{10,8},{12,14},{14,12},{1,3},{3,1},... | collective-permute-start | bytes 210056 | tf_op jit(solution)/shard_map/ppermute | solution.py:54
  33.1 4.5 %collective-permute-start.12 = (bf16[64,547]{1,0:T(8,128)(2,1)S(1)}, bf16[64,547]{1,0:T(8,128)(2,1)S(1)}, u32[]{:S(2)}, u32[]{:S(2)}) collective-permute-start(bf16[64,547]{1,0:T(8,128)(2,1)S(1)} %fusion.35), channel_id=1, source_target_pairs={{0,4},{2,6},{4,0},{6,2},{8,12},{10,14},{12,8},{14,10},{1,5},{3,7},... | collective-permute-start | bytes 210056 | tf_op jit(solution)/shard_map/ppermute | solution.py:54
  37.6 5.4 %collective-permute-start.13 = (bf16[64,547]{1,0:T(8,128)(2,1)S(1)}, bf16[64,547]{1,0:T(8,128)(2,1)S(1)}, u32[]{:S(2)}, u32[]{:S(2)}) collective-permute-start(bf16[64,547]{1,0:T(8,128)(2,1)S(1)} %fusion.34), channel_id=1, source_target_pairs={{0,8},{2,10},{4,12},{6,14},{8,0},{10,2},{12,4},{14,6},{1,9},{3,11}... | collective-permute-start | bytes 210056 | tf_op jit(solution)/shard_map/ppermute | solution.py:54
  43.1 4.5 %collective-permute-start.14 = (bf16[64,547]{1,0:T(8,128)(2,1)S(1)}, bf16[64,547]{1,0:T(8,128)(2,1)S(1)}, u32[]{:S(2)}, u32[]{:S(2)}) collective-permute-start(bf16[64,547]{1,0:T(8,128)(2,1)S(1)} %get-tuple-element.47), channel_id=1, source_target_pairs={{0,2},{2,0},{4,6},{6,4},{8,10},{10,8},{12,14},{14,12},{1,3},{3,1},... | collective-permute-start | bytes 210056 | tf_op jit(solution)/shard_map/ppermute | solution.py:54
  47.6 1.6 %collective-permute-start.15 = (bf16[128,547]{1,0:T(8,128)(2,1)S(1)}, bf16[128,547]{1,0:T(8,128)(2,1)}, u32[]{:S(2)}, u32[]{:S(2)}) collective-permute-start(bf16[128,547]{1,0:T(8,128)(2,1)S(1)} %constant_dynamic-update-slice_fusion.mine), channel_id=1, source_target_pairs={{0,1},{1,0},{2,3},{3,2},{4,5},{5,4},{6,7},{7,6},{8,9},{9,8},{10,11... | collective-permute-start | bytes 420104 | tf_op jit(solution)/shard_map/ppermute | solution.py:50
  54.2 1.4 %collective-permute-start.16 = (bf16[256,256]{1,0:T(8,128)(2,1)S(1)}, bf16[256,256]{1,0:T(8,128)(2,1)S(1)}, u32[]{:S(2)}, u32[]{:S(2)}) collective-permute-start(bf16[256,256]{1,0:T(8,128)(2,1)S(1)} %convert_element_type.146.g_ref), channel_id=1, source_target_pairs={{0,1},{1,0},{2,3},{3,2},{4,5},{5,4},{6,7},{7,6},{8,9},{9,8},{10,11... | collective-permute-start | bytes 393224 | tf_op jit(solution)/shard_map/ppermute | solution.py:50
  55.6 5.0 %copy-start.9 = (bf16[32,2048]{1,0:T(8,128)(2,1)S(1)}, bf16[32,2048]{1,0:T(8,128)(2,1)}, u32[]{:S(2)}) copy-start(bf16[32,2048]{1,0:T(8,128)(2,1)} %param.21) | copy-start | bytes 393220
  58.9 17.1 %copy-start.8 = (bf16[32,2048]{1,0:T(8,128)(2,1)S(1)}, bf16[32,2048]{1,0:T(8,128)(2,1)}, u32[]{:S(2)}) copy-start(bf16[32,2048]{1,0:T(8,128)(2,1)} %dynamic_slice.27) | copy-start | bytes 393220
  59.0 5.0 %collective-permute-start.18 = (bf16[32,2048]{1,0:T(8,128)(2,1)S(1)}, bf16[32,2048]{1,0:T(8,128)(2,1)S(1)}, u32[]{:S(2)}, u32[]{:S(2)}) collective-permute-start(bf16[32,2048]{1,0:T(8,128)(2,1)S(1)} %get-tuple-element.36), channel_id=1, source_target_pairs={{0,4},{1,3},{2,0},{3,7},{4,8},{5,1},{6,2},{7,11},{8,12},{9,5},{10,... | collective-permute-start | bytes 393224 | tf_op jit(solution)/shard_map/ppermute | solution.py:353
  60.8 5.0 %collective-permute-start.22 = (bf16[32,2048]{1,0:T(8,128)(2,1)S(1)}, bf16[32,2048]{1,0:T(8,128)(2,1)S(1)}, u32[]{:S(2)}, u32[]{:S(2)}) collective-permute-start(bf16[32,2048]{1,0:T(8,128)(2,1)S(1)} %slice.204), channel_id=1, source_target_pairs={{0,4},{1,3},{2,0},{3,7},{4,8},{5,1},{6,2},{7,11},{8,12},{9,5},{10,... | collective-permute-start | bytes 393224 | tf_op jit(solution)/shard_map/ppermute | solution.py:353
  64.0 5.0 %collective-permute-start.19 = (bf16[32,2048]{1,0:T(8,128)(2,1)S(1)}, bf16[32,2048]{1,0:T(8,128)(2,1)S(1)}, u32[]{:S(2)}, u32[]{:S(2)}) collective-permute-start(bf16[32,2048]{1,0:T(8,128)(2,1)S(1)} %add_convert_fusion.6), channel_id=1, source_target_pairs={{0,4},{1,3},{2,0},{3,7},{4,8},{5,1},{6,2},{7,11},{8,12},{9,5},{10,... | collective-permute-start | bytes 393224 | tf_op jit(solution)/shard_map/ppermute | solution.py:353
  65.9 23.8 %copy-start.4 = (f32[4096]{0:T(1024)S(1)}, f32[4096]{0:T(1024)}, u32[]{:S(2)}) copy-start(f32[4096]{0:T(1024)} %param.37) | copy-start | bytes 49156
  65.9 5.0 %collective-permute-start.23 = (bf16[32,2048]{1,0:T(8,128)(2,1)S(1)}, bf16[32,2048]{1,0:T(8,128)(2,1)S(1)}, u32[]{:S(2)}, u32[]{:S(2)}) collective-permute-start(bf16[32,2048]{1,0:T(8,128)(2,1)S(1)} %add_convert_fusion.3), channel_id=1, source_target_pairs={{0,4},{1,3},{2,0},{3,7},{4,8},{5,1},{6,2},{7,11},{8,12},{9,5},{10,... | collective-permute-start | bytes 393224 | tf_op jit(solution)/shard_map/ppermute | solution.py:353
  69.1 5.0 %collective-permute-start.20 = (bf16[32,2048]{1,0:T(8,128)(2,1)S(1)}, bf16[32,2048]{1,0:T(8,128)(2,1)S(1)}, u32[]{:S(2)}, u32[]{:S(2)}) collective-permute-start(bf16[32,2048]{1,0:T(8,128)(2,1)S(1)} %add_convert_fusion.5), channel_id=1, source_target_pairs={{0,4},{1,3},{2,0},{3,7},{4,8},{5,1},{6,2},{7,11},{8,12},{9,5},{10,... | collective-permute-start | bytes 393224 | tf_op jit(solution)/shard_map/ppermute | solution.py:353
  71.0 5.0 %collective-permute-start.24 = (bf16[32,2048]{1,0:T(8,128)(2,1)S(1)}, bf16[32,2048]{1,0:T(8,128)(2,1)S(1)}, u32[]{:S(2)}, u32[]{:S(2)}) collective-permute-start(bf16[32,2048]{1,0:T(8,128)(2,1)S(1)} %add_convert_fusion.2), channel_id=1, source_target_pairs={{0,4},{1,3},{2,0},{3,7},{4,8},{5,1},{6,2},{7,11},{8,12},{9,5},{10,... | collective-permute-start | bytes 393224 | tf_op jit(solution)/shard_map/ppermute | solution.py:353
  74.1 5.2 %collective-permute-start.21 = (bf16[32,2048]{1,0:T(8,128)(2,1)S(1)}, bf16[32,2048]{1,0:T(8,128)(2,1)S(1)}, u32[]{:S(2)}, u32[]{:S(2)}) collective-permute-start(bf16[32,2048]{1,0:T(8,128)(2,1)S(1)} %add_convert_fusion.4), channel_id=1, source_target_pairs={{0,4},{1,3},{2,0},{3,7},{4,8},{5,1},{6,2},{7,11},{8,12},{9,5},{10,... | collective-permute-start | bytes 393224 | tf_op jit(solution)/shard_map/ppermute | solution.py:353
  76.0 1.3 %collective-permute-start.25 = (bf16[32,2048]{1,0:T(8,128)(2,1)S(1)}, bf16[32,2048]{1,0:T(8,128)(2,1)S(1)}, u32[]{:S(2)}, u32[]{:S(2)}) collective-permute-start(bf16[32,2048]{1,0:T(8,128)(2,1)S(1)} %collective-permute-done.24), channel_id=1, source_target_pairs={{0,1},{1,0},{2,3},{3,2},{4,5},{5,4},{6,7},{7,6},{8,9},{9,8},{10,11... | collective-permute-start | bytes 393224 | tf_op jit(solution)/shard_map/ppermute | solution.py:50
  79.4 6.4 %collective-permute-start.27 = (bf16[32,2048]{1,0:T(8,128)(2,1)S(1)}, bf16[32,2048]{1,0:T(8,128)(2,1)S(1)}, u32[]{:S(2)}, u32[]{:S(2)}) collective-permute-start(bf16[32,2048]{1,0:T(8,128)(2,1)S(1)} %add_convert_fusion.1.refs_0_), channel_id=1, source_target_pairs={{0,2},{2,0},{4,6},{6,4},{8,10},{10,8},{12,14},{14,12},{1,3},{3,1},... | collective-permute-start | bytes 393224 | tf_op jit(solution)/shard_map/ppermute | solution.py:54
  80.9 5.0 %collective-permute-start.28 = (bf16[32,2048]{1,0:T(8,128)(2,1)S(1)}, bf16[32,2048]{1,0:T(8,128)(2,1)S(1)}, u32[]{:S(2)}, u32[]{:S(2)}) collective-permute-start(bf16[32,2048]{1,0:T(8,128)(2,1)S(1)} %add_convert_fusion.1.refs_0_), channel_id=1, source_target_pairs={{0,4},{2,6},{4,0},{6,2},{8,12},{10,14},{12,8},{14,10},{1,5},{3,7},... | collective-permute-start | bytes 393224 | tf_op jit(solution)/shard_map/ppermute | solution.py:54
  82.5 5.9 %collective-permute-start.29 = (bf16[32,2048]{1,0:T(8,128)(2,1)S(1)}, bf16[32,2048]{1,0:T(8,128)(2,1)S(1)}, u32[]{:S(2)}, u32[]{:S(2)}) collective-permute-start(bf16[32,2048]{1,0:T(8,128)(2,1)S(1)} %add_convert_fusion.1.refs_0_), channel_id=1, source_target_pairs={{0,6},{2,4},{4,2},{6,0},{8,14},{10,12},{12,10},{14,8},{1,7},{3,5},... | collective-permute-start | bytes 393224 | tf_op jit(solution)/shard_map/ppermute | solution.py:54
  83.0 5.4 %collective-permute-start.26 = (bf16[32,2048]{1,0:T(8,128)(2,1)S(1)}, bf16[32,2048]{1,0:T(8,128)(2,1)S(1)}, u32[]{:S(2)}, u32[]{:S(2)}) collective-permute-start(bf16[32,2048]{1,0:T(8,128)(2,1)S(1)} %add_convert_fusion.1.refs_0_), channel_id=1, source_target_pairs={{0,1},{1,0},{2,3},{3,2},{4,5},{5,4},{6,7},{7,6},{8,9},{9,8},{10,11... | collective-permute-start | bytes 393224 | tf_op jit(solution)/shard_map/ppermute | solution.py:50
  85.8 2.7 %collective-permute-start.30 = (bf16[32,2048]{1,0:T(8,128)(2,1)S(1)}, bf16[32,2048]{1,0:T(8,128)(2,1)S(1)}, u32[]{:S(2)}, u32[]{:S(2)}) collective-permute-start(bf16[32,2048]{1,0:T(8,128)(2,1)S(1)} %collective-permute-done.27.refs_1_), channel_id=1, source_target_pairs={{0,1},{1,0},{2,3},{3,2},{4,5},{5,4},{6,7},{7,6},{8,9},{9,8},{10,11... | collective-permute-start | bytes 393224 | tf_op jit(solution)/shard_map/ppermute | solution.py:50
  85.9 2.7 %collective-permute-start.31 = (bf16[32,2048]{1,0:T(8,128)(2,1)S(1)}, bf16[32,2048]{1,0:T(8,128)(2,1)S(1)}, u32[]{:S(2)}, u32[]{:S(2)}) collective-permute-start(bf16[32,2048]{1,0:T(8,128)(2,1)S(1)} %collective-permute-done.28.refs_2_), channel_id=1, source_target_pairs={{0,1},{1,0},{2,3},{3,2},{4,5},{5,4},{6,7},{7,6},{8,9},{9,8},{10,11... | collective-permute-start | bytes 393224 | tf_op jit(solution)/shard_map/ppermute | solution.py:50
  88.3 1.3 %collective-permute-start.32 = (bf16[32,2048]{1,0:T(8,128)(2,1)S(1)}, bf16[32,2048]{1,0:T(8,128)(2,1)S(1)}, u32[]{:S(2)}, u32[]{:S(2)}) collective-permute-start(bf16[32,2048]{1,0:T(8,128)(2,1)S(1)} %collective-permute-done.29.refs_3_), channel_id=1, source_target_pairs={{0,1},{1,0},{2,3},{3,2},{4,5},{5,4},{6,7},{7,6},{8,9},{9,8},{10,11... | collective-permute-start | bytes 393224 | tf_op jit(solution)/shard_map/ppermute | solution.py:50
  89.7 7.9 %copy-start.13 = (bf16[4096,16]{0,1:T(8,128)(2,1)S(1)}, bf16[4096,16]{0,1:T(8,128)(2,1)}, u32[]{:S(2)}) copy-start(bf16[4096,16]{0,1:T(8,128)(2,1)} %param.38) | copy-start | bytes 393220
  97.4 2.0 %collective-permute-start.33 = (bf16[128,2048]{1,0:T(8,128)(2,1)S(1)}, bf16[128,2048]{1,0:T(8,128)(2,1)S(1)}, u32[]{:S(2)}, u32[]{:S(2)}) collective-permute-start(bf16[128,2048]{1,0:T(8,128)(2,1)S(1)} %dynamic-slice_convert_fusion), channel_id=1, source_target_pairs={{0,1},{1,0},{2,3},{3,2},{4,5},{5,4},{6,7},{7,6},{8,9},{9,8},{10,11... | collective-permute-start | bytes 1572872 | tf_op jit(solution)/shard_map/ppermute | solution.py:50
  99.6 7.3 %collective-permute-start.36 = (bf16[32,2048]{1,0:T(8,128)(2,1)S(1)}, bf16[32,2048]{1,0:T(8,128)(2,1)S(1)}, u32[]{:S(2)}, u32[]{:S(2)}) collective-permute-start(bf16[32,2048]{1,0:T(8,128)(2,1)S(1)} %get-tuple-element.49), channel_id=1, source_target_pairs={{0,6},{2,4},{4,2},{6,0},{8,14},{10,12},{12,10},{14,8},{1,7},{3,5},... | collective-permute-start | bytes 393224 | tf_op jit(solution)/shard_map/ppermute | solution.py:54
  101.0 7.0 %collective-permute-start.35 = (bf16[32,2048]{1,0:T(8,128)(2,1)S(1)}, bf16[32,2048]{1,0:T(8,128)(2,1)S(1)}, u32[]{:S(2)}, u32[]{:S(2)}) collective-permute-start(bf16[32,2048]{1,0:T(8,128)(2,1)S(1)} %get-tuple-element.50), channel_id=1, source_target_pairs={{0,4},{2,6},{4,0},{6,2},{8,12},{10,14},{12,8},{14,10},{1,5},{3,7},... | collective-permute-start | bytes 393224 | tf_op jit(solution)/shard_map/ppermute | solution.py:54
  101.7 7.2 %collective-permute-start.34 = (bf16[32,2048]{1,0:T(8,128)(2,1)S(1)}, bf16[32,2048]{1,0:T(8,128)(2,1)S(1)}, u32[]{:S(2)}, u32[]{:S(2)}) collective-permute-start(bf16[32,2048]{1,0:T(8,128)(2,1)S(1)} %get-tuple-element.48), channel_id=1, source_target_pairs={{0,2},{2,0},{4,6},{6,4},{8,10},{10,8},{12,14},{14,12},{1,3},{3,1},... | collective-permute-start | bytes 393224 | tf_op jit(solution)/shard_map/ppermute | solution.py:54
  109.0 6.7 %collective-permute-start.37 = (bf16[16,2048]{1,0:T(8,128)(2,1)S(1)}, bf16[16,2048]{1,0:T(8,128)(2,1)S(1)}, u32[]{:S(2)}, u32[]{:S(2)}) collective-permute-start(bf16[16,2048]{1,0:T(8,128)(2,1)S(1)} %get-tuple-element.64), channel_id=1, source_target_pairs={{0,8},{2,10},{4,12},{6,14},{8,0},{10,2},{12,4},{14,6},{1,9},{3,11}... | collective-permute-start | bytes 196616 | tf_op jit(solution)/shard_map/ppermute | solution.py:54
